TPU v7x, 32 devices: a whole 2x2x4 slice. The times are simulated.
32 devices in a mesh: dp: 8 (over y, x, core), fsdp: 4 (over z).
Axes of the slice: x: 2, y: 2, z: 4, core: 2. Of those that a mesh axis runs over, the one named last changes fastest.
Arguments:
- inputs: bfloat16 [32, 8, 12, 6, 6, 256], P(('dp', 'fsdp')), may hold values from -6 to 6
- cotangent: bfloat16 [32, 8, 12, 6, 6, 256], P(('dp', 'fsdp')), may hold values from -6 to 6
- lengths: int32 [32], P(('dp', 'fsdp')), may hold values from 2 to 8
- face_table: int32 [12, 4], replicated, may hold values from 0 to 11
- w_first: float32 [2304, 256], P('fsdp'), may hold values from -0.125 to 0.125
- w_second: float32 [2304, 256], P('fsdp'), may hold values from -0.125 to 0.125
- w_skip: float32 [256, 256], P('fsdp'), may hold values from -0.375 to 0.375
- mom_first: float32 [2304, 256], P('fsdp'), may hold values from -64 to 64
- sq_first: float32 [2304, 256], P('fsdp'), may hold values from 12.16512 to 48.66048
- mom_second: float32 [2304, 256], P('fsdp'), may hold values from -64 to 64
- sq_second: float32 [2304, 256], P('fsdp'), may hold values from 12.16512 to 48.66048
- mom_skip: float32 [256, 256], P('fsdp'), may hold values from -160 to 160
- sq_skip: float32 [256, 256], P('fsdp'), may hold values from 68.56704 to 276.48
Outputs:
- output: bfloat16 [32, 8, 12, 6, 6, 256], P(('dp', 'fsdp'))
- grad_inputs: float32 [32, 8, 12, 6, 6, 256], P(('dp', 'fsdp'))
- new_first: float32 [2304, 256], P('fsdp')
- new_mom_first: float32 [2304, 256], P('fsdp')
- new_sq_first: float32 [2304, 256], P('fsdp')
- new_second: float32 [2304, 256], P('fsdp')
- new_mom_second: float32 [2304, 256], P('fsdp')
- new_sq_second: float32 [2304, 256], P('fsdp')
- new_skip: float32 [256, 256], P('fsdp')
- new_mom_skip: float32 [256, 256], P('fsdp')
- new_sq_skip: float32 [256, 256], P('fsdp')
All inputs are finite; a program needn't handle non-finite values.
Results may differ from a plain program's by a relative error of at most 0.019.
Values may be sent and summed in bfloat16 or wider, within the bound.
No kernel may reach another device: no remote copies, remote signals or barrier semaphores. Data moves between devices by JAX's collectives and lax.ppermute only.
A program may use at most 256 MiB of HBM per device.

v0:
```python
import jax
import jax.numpy as jnp
from jax import lax
from jax.sharding import PartitionSpec as P

C = 256
STEP_COUNT = 10


tap_offsets = [(row_off, col_off) for row_off in range(3) for col_off in range(3)]


def face_hots(face_table, dtype):
    faces = face_table.shape[0]
    labels = jnp.arange(faces, dtype=jnp.int32)
    return [
        (face_table[:, corner_side][:, None] == labels[None, :]).astype(dtype)
        for corner_side in range(4)
    ]


def pad_faces(field, hots):

    def route(matrix, edge, form):
        return jnp.einsum(form, matrix, edge, preferred_element_type=jnp.float32).astype(
            jnp.bfloat16
        )

    north = route(hots[0], field[:, :, -1], "fh,rhwc->rfwc")
    east = route(hots[1], field[:, :, :, 0], "fh,rhwc->rfwc")
    south = route(hots[2], field[:, :, 0], "fh,rhwc->rfwc")
    west = route(hots[3], field[:, :, :, -1], "fh,rhwc->rfwc")
    middle = jnp.concatenate([west[:, :, :, None], field, east[:, :, :, None]], axis=3)
    top_row = jnp.pad(north, ((0, 0), (0, 0), (1, 1), (0, 0)))
    bottom_row = jnp.pad(south, ((0, 0), (0, 0), (1, 1), (0, 0)))
    return jnp.concatenate([top_row[:, :, None], middle, bottom_row[:, :, None]], axis=2)


def unpad_back(spread, hots):
    highest = lax.Precision.HIGHEST
    inner = spread[:, :, 1:-1, 1:-1]
    inner = inner.at[:, :, -1].add(
        jnp.einsum("fh,rfwc->rhwc", hots[0], spread[:, :, 0, 1:-1], precision=highest)
    )
    inner = inner.at[:, :, :, 0].add(
        jnp.einsum("fh,rfwc->rhwc", hots[1], spread[:, :, 1:-1, -1], precision=highest)
    )
    inner = inner.at[:, :, 0].add(
        jnp.einsum("fh,rfwc->rhwc", hots[2], spread[:, :, -1, 1:-1], precision=highest)
    )
    inner = inner.at[:, :, :, -1].add(
        jnp.einsum("fh,rfwc->rhwc", hots[3], spread[:, :, 1:-1, 0], precision=highest)
    )
    return inner


def conv_apply(padded, weight):
    edge_len = padded.shape[2] - 2
    channels = weight.shape[1]
    taps_weight = weight.reshape(9, channels, channels)
    flat_padded = padded.reshape(-1, channels)
    products = jnp.einsum(
        "pc,tcd->ptd", flat_padded, taps_weight, preferred_element_type=jnp.float32
    )
    products = products.reshape(padded.shape[:4] + (9, channels))
    summed = None
    for tap_index, (row_off, col_off) in enumerate(tap_offsets):
        part = products[:, :, row_off : row_off + edge_len, col_off : col_off + edge_len, tap_index]
        summed = part if summed is None else summed + part
    return summed


def conv_back(padded, grad, weight):
    channels = weight.shape[1]
    taps_weight = weight.reshape(9, channels, channels)
    flat_grad = grad.reshape(-1, channels)
    pulled = jnp.einsum("pd,tcd->ptc", flat_grad, taps_weight, preferred_element_type=jnp.float32)
    pulled = pulled.reshape(grad.shape[:4] + (9, channels))
    spread = None
    placed = []
    for tap_index, (row_off, col_off) in enumerate(tap_offsets):
        widths = ((0, 0), (0, 0), (row_off, 2 - row_off), (col_off, 2 - col_off), (0, 0))
        moved = jnp.pad(pulled[:, :, :, :, tap_index], widths)
        spread = moved if spread is None else spread + moved
        placed.append(jnp.pad(grad, widths))
    stacked = jnp.stack(placed, axis=4).reshape(-1, 9, channels)
    flat_padded = padded.reshape(-1, channels)
    weight_grad = jnp.einsum(
        "pc,ptd->tcd", flat_padded, stacked, preferred_element_type=jnp.float32
    )
    return (weight_grad.reshape(9 * channels, channels), spread)


def gelu_tanh(v):
    return jax.nn.gelu(v, approximate=True)


def forward_pass(fields, hots_low, gathered):
    pad_in = pad_faces(fields, hots_low)
    pre_one = conv_apply(pad_in, gathered[0])
    hidden = gelu_tanh(pre_one).astype(jnp.bfloat16)
    pad_hidden = pad_faces(hidden, hots_low)
    pre_two = conv_apply(pad_hidden, gathered[1])
    return (pad_in, pre_one, pad_hidden, pre_two)


def adamw(weight, moment, square, grad, rate):
    moment_new = 0.9 * moment + 0.1 * grad
    square_new = 0.999 * square + 0.001 * grad * grad
    fix_one = 1.0 - 0.9**STEP_COUNT
    fix_two = 1.0 - 0.999**STEP_COUNT
    weight_new = weight - rate * (
        moment_new / fix_one / (jnp.sqrt(square_new / fix_two) + 1e-08) + 0.01 * weight
    )
    return (weight_new, moment_new, square_new)


def per_device(
    inputs,
    cotangent,
    lengths,
    face_table,
    w_first,
    w_second,
    w_skip,
    mom_first,
    sq_first,
    mom_second,
    sq_second,
    mom_skip,
    sq_skip,
):
    fields = inputs[0]
    channels = fields.shape[-1]
    hots_low = face_hots(face_table, jnp.bfloat16)
    hots_full = face_hots(face_table, jnp.float32)
    low_weights = (
        w_first.astype(jnp.bfloat16),
        w_second.astype(jnp.bfloat16),
        w_skip.astype(jnp.bfloat16),
    )
    gathered = (
        lax.all_gather(low_weights[0], "fsdp", axis=0, tiled=True),
        lax.all_gather(low_weights[1], "fsdp", axis=0, tiled=True),
        lax.all_gather(low_weights[2], "fsdp", axis=0, tiled=True),
    )
    saved = forward_pass(fields, hots_low, gathered)
    flat_fields = fields.reshape(-1, channels)
    skipped = jnp.dot(flat_fields, gathered[2], preferred_element_type=jnp.float32).reshape(
        fields.shape
    )
    output = (gelu_tanh(saved[3]) + skipped).astype(jnp.bfloat16)
    gathered = (
        lax.all_gather(low_weights[0], "fsdp", axis=0, tiled=True),
        lax.all_gather(low_weights[1], "fsdp", axis=0, tiled=True),
        lax.all_gather(low_weights[2], "fsdp", axis=0, tiled=True),
    )
    saved = forward_pass(fields, hots_low, gathered)
    pad_in, pre_one, pad_hidden, pre_two = saved
    live = (jnp.arange(fields.shape[0]) < lengths[0]).astype(jnp.bfloat16)
    grad_out = cotangent[0] * live[:, None, None, None, None]
    flat_out = grad_out.reshape(-1, channels)
    dw_skip = lax.dot_general(
        flat_fields, flat_out, (((0,), (0,)), ((), ())), preferred_element_type=jnp.float32
    )
    gelu_pull_two = jax.vjp(gelu_tanh, pre_two)[1]
    grad_two = gelu_pull_two(grad_out.astype(jnp.float32))[0].astype(jnp.bfloat16)
    dw_second, spread_hidden = conv_back(pad_hidden, grad_two, gathered[1])
    grad_hidden = unpad_back(spread_hidden, hots_full)
    gelu_pull_one = jax.vjp(gelu_tanh, pre_one)[1]
    grad_one = gelu_pull_one(grad_hidden)[0].astype(jnp.bfloat16)
    dw_first, spread_in = conv_back(pad_in, grad_one, gathered[0])
    skip_back = lax.dot_general(
        flat_out, gathered[2], (((1,), (1,)), ((), ())), preferred_element_type=jnp.float32
    )
    grad_inputs = unpad_back(spread_in, hots_full) + skip_back.reshape(fields.shape)
    shards = (
        lax.psum_scatter(
            dw_first.astype(jnp.bfloat16), "fsdp", scatter_dimension=0, tiled=True
        ).astype(jnp.float32),
        lax.psum_scatter(
            dw_second.astype(jnp.bfloat16), "fsdp", scatter_dimension=0, tiled=True
        ).astype(jnp.float32),
        lax.psum_scatter(
            dw_skip.astype(jnp.bfloat16), "fsdp", scatter_dimension=0, tiled=True
        ).astype(jnp.float32),
    )
    rate_conv = (9 * C) ** (-0.5)
    rate_skip = C ** (-0.5)
    totals = (
        lax.psum(shards[0].astype(jnp.bfloat16), "dp").astype(jnp.float32),
        lax.psum(shards[1].astype(jnp.bfloat16), "dp").astype(jnp.float32),
        lax.psum(shards[2].astype(jnp.bfloat16), "dp").astype(jnp.float32),
    )
    first_set = adamw(w_first, mom_first, sq_first, totals[0], rate_conv)
    second_set = adamw(w_second, mom_second, sq_second, totals[1], rate_conv)
    skip_set = adamw(w_skip, mom_skip, sq_skip, totals[2], rate_skip)
    return (
        output[None],
        grad_inputs[None],
        first_set[0],
        first_set[1],
        first_set[2],
        second_set[0],
        second_set[1],
        second_set[2],
        skip_set[0],
        skip_set[1],
        skip_set[2],
    )


def solution(mesh):
    placed = (
        P(("dp", "fsdp"), None, None, None, None, None),
        P(("dp", "fsdp"), None, None, None, None, None),
        P(("dp", "fsdp")),
        P(),
        P("fsdp", None),
        P("fsdp", None),
        P("fsdp", None),
        P("fsdp", None),
        P("fsdp", None),
        P("fsdp", None),
        P("fsdp", None),
        P("fsdp", None),
        P("fsdp", None),
    )
    return jax.shard_map(
        per_device,
        mesh=mesh,
        in_specs=placed,
        out_specs=(
            P(("dp", "fsdp"), None, None, None, None, None),
            P(("dp", "fsdp"), None, None, None, None, None),
            P("fsdp", None),
            P("fsdp", None),
            P("fsdp", None),
            P("fsdp", None),
            P("fsdp", None),
            P("fsdp", None),
            P("fsdp", None),
            P("fsdp", None),
            P("fsdp", None),
        ),
        check_vma=False,
    )
```

profile of v0, /device:TPU:0, one launch (start us, length us, event | category | flops | bytes accessed | tf_op | source)
XLA Modules:
  0.0 511.8 jit_solution(13693216425621798046)
XLA Ops:
  7.9 5.0 fusion.84
  15.4 2.5 copy.510
  22.2 2.4 maximum_bitcast_fusion
  24.7 11.1 %reduce-scatter.10.cloned.1.call-done = bf16[64,256]{1,0:T(8,128)(2,1)} async-done(((bf16[256,256]{1,0:T(8,128)(2,1)}), bf16[64,256]{1,0:T(8,128)(2,1)}) %reduce-scatter.10.cloned.1.call-update) | async-done | bytes 32784 | tf_op jit(solution)/shard_map/reduce_scatter | solution.py:184
  35.7 23.7 %psum.23 = bf16[64,256]{1,0:T(8,128)(2,1)S(1)} all-reduce(bf16[64,256]{1,0:T(8,128)(2,1)} %reduce-scatter.10.cloned.1.call-done), channel_id=1, replica_groups=mesh['dp'=8,'fsdp'=4] {'dp'}, use_global_device_ids=true, to_apply=%region_5.6 | all-reduce | flops 16384 | bytes 65536 | tf_op jit(solution)/shard_map/psum | solution.py:193
  60.2 14.7 %all_gather.14 = bf16[256,256]{1,0:T(8,128)(2,1)} all-gather(bf16[64,256]{1,0:T(8,128)(2,1)S(1)} %get-tuple-element.194), channel_id=1, replica_groups=mesh['dp'=8,'fsdp'=4] {'fsdp'}, dimensions={0}, use_global_device_ids=true | all-gather | bytes 163840 | tf_op jit(solution)/shard_map/all_gather | solution.py:145
  74.8 23.7 %fusion.33 = f32[8,12,8,8,9,256]{5,3,4,2,1,0:T(8,128)} fusion(bf16[9,256,256,1,1,1]{2,1,0,5,4,3:T(8,128)(2,1)} %bitcast.404, bf16[8,12,8,8,256,1]{4,1,3,0,2,5:T(8,128)(2,1)} %maximum_bitcast_fusion), kind=kOutput, calls=%fused_computation.102 | convolution fusion | flops 7247757312 | bytes 60948480 | tf_op jit(solution)/shard_map/pc,tcd->ptd/dot_general | solution.py:62
  98.5 17.8 %multiply_convert_fusion = (bf16[8,12,6,6,256]{4,3,2,1,0:T(8,128)(2,1)S(1)}, f32[8,12,6,6,256]{4,3,2,1,0:T(8,128)}) fusion(f32[8,12,8,8,9,256]{5,3,4,2,1,0:T(8,128)} %fusion.33), kind=kLoop, calls=%fused_computation.78 | loop fusion | flops 15040512 | bytes 37158912 | tf_op jit(solution)/shard_map/convert_element_type | solution.py:101
  122.7 22.2 %fusion.115 = f32[8,12,8,8,9,256]{5,3,2,1,0,4:T(8,128)} fusion(bf16[9,256,256,1,1,1]{2,1,5,4,3,0:T(8,128)(2,1)} %bitcast.402, bf16[8,12,1,8,256]{4,3,2,1,0:T(8,128)(2,1)} %copy.301, bf16[8,12,6,1,256]{4,3,2,1,0:T(2,128)(2,1)S(1)} %copy.296, bf16[8,12,6,6,256]{4,3,2,1,0:T(8,128)(2,1)S(1)} %get-tuple-element.164, bf16[8,12,6,1,256]{4,3,2,1,0:T(2,128)(2,1)S(1)} %copy.295, ...), kind=kOutput, calls=%fused_computation.210 | convolution fusion | flops 7263485952 | bytes 60948480 | tf_op jit(solution)/shard_map/pc,tcd->ptd/dot_general | solution.py:62
  145.0 18.3 %fusion.7 = (bf16[8,12,6,6,256]{4,3,2,1,0:T(8,128)(2,1)S(1)}, f32[8,12,6,6,1,256]{5,3,2,1,0,4:T(8,128)}) fusion(bf16[8]{0:T(256)(128)(2,1)S(1)} %copy-done.29, bf16[1,8,12,6,6,256]{5,1,4,3,2,0:T(8,128)(2,1)S(1)} %copy-done.1, f32[8,12,8,8,9,256]{5,3,2,1,0,4:T(8,128)} %fusion.115), kind=kLoop, calls=%fused_computation.19 | loop fusion | flops 26542080 | bytes 38928400 | tf_op jit(solution)/shard_map/convert_element_type | solution.py:167
  163.3 19.7 %fusion.40 = f32[8,12,6,6,9,256]{5,3,2,1,0,4:T(8,128)} fusion(bf16[9,256,256,1,1,1]{2,1,5,4,3,0:T(8,128)(2,1)S(1)} %bitcast.403, f32[8,12,6,6,1,256]{5,3,2,1,0,4:T(8,128)} %get-tuple-element.163, bf16[1,8,12,6,6,256]{5,1,4,3,2,0:T(8,128)(2,1)} %param.30, bf16[8]{0:T(256)(128)(2,1)} %copy-done.28), kind=kOutput, calls=%fused_computation.113 | convolution fusion | flops 4098097152 | bytes 38338576 | tf_op jit(solution)/shard_map/pd,tcd->ptc/dot_general | solution.py:77
  183.0 30.6 %slice_bitcast_fusion.17 = (f32[8,12,6,6,256]{4,3,2,1,0:T(8,128)}, f32[8,12,6,6,256]{4,3,2,1,0:T(8,128)}, f32[8,12,6,6,256]{4,3,2,1,0:T(8,128)}, f32[8,12,6,6,25...) fusion(f32[8,12,6,6,9,256]{5,3,2,1,0,4:T(8,128)} %fusion.40), kind=kLoop, calls=%fused_computation.56 | loop fusion | bytes 63700992 | tf_op jit(solution)/shard_map/squeeze | solution.py:83
  213.5 18.7 %pad_add_fusion.1 = f32[8,12,8,8,256]{4,3,2,1,0:T(8,128)} fusion(f32[8,12,6,6,256]{4,3,2,1,0:T(8,128)} %get-tuple-element.183, f32[8,12,6,6,256]{4,3,2,1,0:T(8,128)} %get-tuple-element.176, f32[8,12,6,6,256]{4,3,2,1,0:T(8,128)} %get-tuple-element.177, f32[8,12,6,6,256]{4,3,2,1,0:T(8,128)} %get-tuple-element.178, f32[8,12,6,6,256]{4,3,2,1,0:T(8,128)} %get-tuple-element.179, ...), kind=kLoop, calls=%fused_computation.7 | loop fusion | flops 12582912 | bytes 38141952 | tf_op jit(solution)/shard_map/add | solution.py:84
  232.2 4.9 fusion.175
  237.2 2.7 slice_bitcast_fusion.26
  239.9 5.3 %slice.563 = f32[8,12,6,6,256]{4,3,2,1,0:T(8,128)} slice(f32[8,12,8,8,256]{4,3,2,1,0:T(8,128)} %pad_add_fusion.1), slice={[0:8], [0:12], [1:7], [1:7], [0:256]} | slice | bytes 7077888 | tf_op jit(solution)/shard_map/slice | solution.py:41
  247.4 2.5 bitcast_dynamic-update-slice_fusion.7
  249.9 2.5 bitcast_dynamic-update-slice_fusion.6
  257.2 2.4 bitcast_dynamic-update-slice_fusion.3
  262.0 2.5 bitcast_dynamic-update-slice_fusion.1
  266.9 13.9 %bitcast_convert_fusion = bf16[9,256,256]{1,2,0:T(8,128)(2,1)} fusion(bf16[8,12,8,8,9,256]{5,3,2,1,0,4:T(8,128)(2,1)} %bitcast_dynamic-update-slice_fusion, bf16[8,12,1,8,256]{4,3,2,1,0:T(8,128)(2,1)S(1)} %copy-done.19, bf16[8,12,6,1,256]{4,3,2,1,0:T(2,128)(2,1)S(1)} %copy-done.16, bf16[8,12,6,6,256]{4,3,2,1,0:T(8,128)(2,1)S(1)} %copy-done.3, ...), kind=kOutput, calls=%fused_computation.111 | convolution fusion | flops 7264075776 | bytes 32636928 | tf_op jit(solution)/shard_map/pc,ptd->tcd/dot_general | solution.py:88
  283.5 2.7 fusion.90
  286.2 3.2 slice_add_fusion.19
  289.4 13.0 %scatter-add.29 = f32[8,12,6,6,256]{4,3,2,1,0:T(8,128)} dynamic-update-slice(f32[8,12,6,6,256]{4,3,2,1,0:T(8,128)} %fusion.90, f32[8,12,6,1,256]{4,3,2,1,0:T(1,128)S(1)} %slice_add_fusion.19, s32[]{:T(128)} %constant.226.clone.1, s32[]{:T(128)} %constant.226.clone.1, s32[]{:T(128)} %constant.226.clone.1, s32[]{:T(128)} %constant.226.clone.1, s32[]{:T(128)} %constant.226.clone.1) | dynamic-update-slice | bytes 1179652 | tf_op jit(solution)/shard_map/scatter-add | solution.py:45
  302.4 2.5 fusion.89
  304.9 3.4 slice_add_fusion.18
  308.3 13.0 %scatter-add.31 = f32[8,12,6,6,256]{4,3,2,1,0:T(8,128)} dynamic-update-slice(f32[8,12,6,6,256]{4,3,2,1,0:T(8,128)} %fusion.89, f32[8,12,6,1,256]{4,3,2,1,0:T(1,128)S(1)} %slice_add_fusion.18, s32[]{:T(128)} %constant.226.clone.1, s32[]{:T(128)} %constant.226.clone.1, s32[]{:T(128)} %constant.226.clone.1, s32[]{:T(128)} %constant.227.clone.1, s32[]{:T(128)} %constant.226.clone.1) | dynamic-update-slice | bytes 1179652 | tf_op jit(solution)/shard_map/scatter-add | solution.py:51
  321.3 5.5 %fusion.16 = bf16[8,12,6,6,256]{4,3,2,1,0:T(8,128)(2,1)S(1)} fusion(f32[8,12,6,6,256]{4,3,2,1,0:T(8,128)} %get-tuple-element.165, f32[8,12,6,6,256]{4,3,2,1,0:T(8,128)} %scatter-add.31), kind=kLoop, calls=%fused_computation.28 | loop fusion | flops 17694720 | bytes 8847360 | tf_op jit(solution)/shard_map/convert_element_type | solution.py:171
  329.1 2.4 bitcast_dynamic-update-slice_fusion.16
  336.3 2.4 bitcast_dynamic-update-slice_fusion.13
  338.7 2.4 bitcast_dynamic-update-slice_fusion.12
  343.6 2.4 bitcast_dynamic-update-slice_fusion.10
  346.0 2.5 bitcast_dynamic-update-slice_fusion.9
  348.5 16.7 %fusion.43 = f32[8,12,6,6,9,256]{5,1,4,3,2,0:T(8,128)} fusion(bf16[9,256,256,1,1,1]{2,1,0,5,4,3:T(8,128)(2,1)S(1)} %bitcast.405, bf16[8,12,6,6,256,1]{4,3,2,1,0,5:T(8,128)(2,1)S(1)} %bitcast.397), kind=kOutput, calls=%fused_computation.116 | convolution fusion | flops 4076863488 | bytes 34799616 | tf_op jit(solution)/shard_map/pd,tcd->ptc/dot_general | solution.py:77
  365.2 31.7 %slice_bitcast_fusion.8 = (f32[8,12,6,6,256]{4,1,3,2,0:T(8,128)}, f32[8,12,6,6,256]{4,1,3,2,0:T(8,128)}, f32[8,12,6,6,256]{4,1,3,2,0:T(8,128)}, f32[8,12,6,6,256...) fusion(f32[8,12,6,6,9,256]{5,1,4,3,2,0:T(8,128)} %fusion.43), kind=kLoop, calls=%fused_computation.47 | loop fusion | bytes 63700992 | tf_op jit(solution)/shard_map/squeeze | solution.py:83
  396.8 15.3 %bitcast_convert_fusion.1 = bf16[9,256,256]{1,2,0:T(8,128)(2,1)} fusion(bf16[8,12,8,8,9,256]{5,3,2,1,0,4:T(8,128)(2,1)} %bitcast_dynamic-update-slice_fusion.9, bf16[8,12,8,8,256,1]{4,1,3,0,2,5:T(8,128)(2,1)} %maximum_bitcast_fusion), kind=kOutput, calls=%fused_computation.112 | convolution fusion | flops 7248347136 | bytes 32636928 | tf_op jit(solution)/shard_map/pc,ptd->tcd/dot_general | solution.py:88
  412.3 4.9 fusion.53
  417.2 3.1 copy.352
  420.3 14.8 %pad_add_fusion = f32[8,12,8,8,256]{4,1,3,2,0:T(8,128)S(1)} fusion(f32[8,12,6,6,256]{4,1,3,2,0:T(8,128)} %get-tuple-element.173, f32[8,12,6,6,256]{4,1,3,2,0:T(8,128)} %get-tuple-element.174, f32[8,12,6,6,256]{4,1,3,2,0:T(8,128)} %get-tuple-element.167, f32[8,12,6,6,256]{4,1,3,2,0:T(8,128)} %get-tuple-element.168, f32[8,12,6,6,256]{4,1,3,2,0:T(8,128)} %get-tuple-element.169, ...), kind=kLoop, calls=%fused_computation | loop fusion | flops 12582912 | bytes 38141952 | tf_op jit(solution)/shard_map/add | solution.py:84
  435.2 2.7 slice.581
  439.2 2.6 fusion.63
  441.8 2.5 fusion.65
  444.4 2.5 fusion.67
  446.9 3.3 add_bitcast_fusion
  450.3 3.8 copy.353
  454.1 45.5 %all-reduce.43.cloned.1.call-done = (bf16[576,256]{1,0:T(8,128)(2,1)}, bf16[576,256]{1,0:T(8,128)(2,1)}) async-done(((bf16[576,256]{1,0:T(8,128)(2,1)}, bf16[576,256]{1,0:T(8,128)(2,1)}), (bf16[576,256]{1,0:T(8,128)(2,1)}, bf16[576,256]{1,0:T(8,128)(2,1)})) %all-reduce.43.cloned.1.call-update) | async-done | bytes 589840 | tf_op jit(solution)/shard_map/psum | solution.py:191
  499.6 2.4 multiply_subtract_fusion.1
  502.1 2.4 multiply_subtract_fusion
  (123 shorter events, 39.1 us)
Async XLA Ops:
  7.2 28.6 %reduce-scatter.10.cloned.1.call-start = ((), (), s32[]{:S(2)}) async-start(), calls=%async_computation.7 | async-start | bytes 163840 | tf_op jit(solution)/shard_map/reduce_scatter | solution.py:184
  7.9 10.1 %copy-start.28 = (bf16[8]{0:T(256)(128)(2,1)}, bf16[8]{0:T(256)(128)(2,1)S(1)}, u32[]{:S(2)}) copy-start(bf16[8]{0:T(256)(128)(2,1)S(1)} %compare_convert_fusion) | copy-start | bytes 52
  7.9 5.9 %copy-start.9 = (f32[576,256]{1,0:T(8,128)S(1)}, f32[576,256]{1,0:T(8,128)}, u32[]{:S(2)}) copy-start(f32[576,256]{1,0:T(8,128)} %param.33) | copy-start | bytes 1769476
  7.9 6.7 %copy-start.11 = (f32[576,256]{1,0:T(8,128)S(1)}, f32[576,256]{1,0:T(8,128)}, u32[]{:S(2)}) copy-start(f32[576,256]{1,0:T(8,128)} %param.34) | copy-start | bytes 1769476
  12.9 5.1 copy-start
  13.7 61.1 %all-gather.3.cloned.1.call-start = ((), (), s32[]{:S(2)}) async-start(), calls=%async_computation.3 | async-start | bytes 1474560 | tf_op jit(solution)/shard_map/all_gather | solution.py:143
  14.5 5.6 %copy-start.30 = (s32[12,4]{0,1:T(4,128)S(1)}, s32[12,4]{0,1:T(4,128)}, u32[]{:S(2)}) copy-start(s32[12,4]{0,1:T(4,128)} %param.32) | copy-start | bytes 580
  14.5 107.4 %all-gather.5.cloned.1.call-start = ((), (), s32[]{:S(2)}) async-start(), calls=%async_computation.4 | async-start | bytes 1474560 | tf_op jit(solution)/shard_map/all_gather | solution.py:144
  15.4 431.5 %reduce-scatter.8.cloned.1.call-start = ((), (), s32[]{:S(2)}) async-start(), calls=%async_computation.6 | async-start | bytes 1474560 | tf_op jit(solution)/shard_map/reduce_scatter | solution.py:181
  22.1 37.4 %copy-start.25 = (f32[64,256]{1,0:T(8,128)S(1)}, f32[64,256]{1,0:T(8,128)}, u32[]{:S(2)}) copy-start(f32[64,256]{1,0:T(8,128)} %param.35) | copy-start | bytes 196612
  22.1 37.4 %copy-start.26 = (f32[64,256]{1,0:T(8,128)S(1)}, f32[64,256]{1,0:T(8,128)}, u32[]{:S(2)}) copy-start(f32[64,256]{1,0:T(8,128)} %param.40) | copy-start | bytes 196612
  22.1 37.4 %copy-start.27 = (f32[64,256]{1,0:T(8,128)S(1)}, f32[64,256]{1,0:T(8,128)}, u32[]{:S(2)}) copy-start(f32[64,256]{1,0:T(8,128)} %param.41) | copy-start | bytes 196612
  116.3 5.7 %copy-start.2 = (bf16[8,12,6,6,256]{4,3,2,1,0:T(8,128)(2,1)}, bf16[8,12,6,6,256]{4,3,2,1,0:T(8,128)(2,1)S(1)}, u32[]{:S(2)}) copy-start(bf16[8,12,6,6,256]{4,3,2,1,0:T(8,128)(2,1)S(1)} %get-tuple-element.164) | copy-start | bytes 5308420
  121.1 0.8 copy-start.13
  121.9 0.8 copy-start.15
  122.7 22.3 %copy-start.1 = (bf16[1,8,12,6,6,256]{5,1,4,3,2,0:T(8,128)(2,1)S(1)}, bf16[1,8,12,6,6,256]{5,1,4,3,2,0:T(8,128)(2,1)}, u32[]{:S(2)}) copy-start(bf16[1,8,12,6,6,256]{5,1,4,3,2,0:T(8,128)(2,1)} %param.30) | copy-start | bytes 5308420
  122.7 22.3 %copy-start.29 = (bf16[8]{0:T(256)(128)(2,1)S(1)}, bf16[8]{0:T(256)(128)(2,1)}, u32[]{:S(2)}) copy-start(bf16[8]{0:T(256)(128)(2,1)} %copy-done.28) | copy-start | bytes 52
  145.0 18.3 %copy-start.5 = (bf16[2304,256]{1,0:T(8,128)(2,1)S(1)}, bf16[2304,256]{1,0:T(8,128)(2,1)}, u32[]{:S(2)}) copy-start(bf16[2304,256]{1,0:T(8,128)(2,1)} %all-gather.5.cloned.1.call-done) | copy-start | bytes 3538948
  262.0 4.9 copy-start.3
  262.0 4.9 copy-start.14
  262.0 4.9 copy-start.16
  262.0 4.9 copy-start.18
  262.0 4.9 copy-start.19
  280.8 1.3 copy-start.8
  280.8 2.0 copy-start.7
  280.9 166.0 %reduce-scatter.6.cloned.1.call-start = ((), (), s32[]{:S(2)}) async-start(), calls=%async_computation.5 | async-start | bytes 1474560 | tf_op jit(solution)/shard_map/reduce_scatter | solution.py:178
  343.6 4.9 copy-start.6
  396.8 15.4 %copy-start.17 = (bf16[1,8,12,6,6,256]{5,1,4,3,2,0:T(8,128)(2,1)S(1)}, bf16[1,8,12,6,6,256]{5,1,4,3,2,0:T(8,128)(2,1)}, u32[]{:S(2)}) copy-start(bf16[1,8,12,6,6,256]{5,1,4,3,2,0:T(8,128)(2,1)} %param.29) | copy-start | bytes 5308420
  396.8 15.4 %copy-start.24 = (bf16[256,256]{1,0:T(8,128)(2,1)S(1)}, bf16[256,256]{1,0:T(8,128)(2,1)}, u32[]{:S(2)}) copy-start(bf16[256,256]{1,0:T(8,128)(2,1)} %all_gather.14) | copy-start | bytes 393220
  412.2 87.4 %all-reduce.43.cloned.1.call-start = ((), (), s32[]{:S(2)}) async-start(), calls=%async_computation.8 | async-start | bytes 1179648 | tf_op jit(solution)/shard_map/psum | solution.py:191
  437.8 9.1 %copy-start.4 = (bf16[8,12,6,6,256]{4,3,2,1,0:T(8,128)(2,1)S(1)}, bf16[8,12,6,6,256]{4,3,2,1,0:T(8,128)(2,1)}, u32[]{:S(2)}) copy-start(bf16[8,12,6,6,256]{4,3,2,1,0:T(8,128)(2,1)} %fusion.39) | copy-start | bytes 5308420
  450.2 49.4 %copy-start.10 = (f32[576,256]{1,0:T(8,128)S(1)}, f32[576,256]{1,0:T(8,128)}, u32[]{:S(2)}) copy-start(f32[576,256]{1,0:T(8,128)} %param.33) | copy-start | bytes 1769476
  450.2 49.4 %copy-start.20 = (f32[576,256]{1,0:T(8,128)S(1)}, f32[576,256]{1,0:T(8,128)}, u32[]{:S(2)}) copy-start(f32[576,256]{1,0:T(8,128)} %param.36) | copy-start | bytes 1769476
  450.2 49.4 %copy-start.21 = (f32[576,256]{1,0:T(8,128)S(1)}, f32[576,256]{1,0:T(8,128)}, u32[]{:S(2)}) copy-start(f32[576,256]{1,0:T(8,128)} %param.37) | copy-start | bytes 1769476
  450.2 51.8 %copy-start.12 = (f32[576,256]{1,0:T(8,128)S(1)}, f32[576,256]{1,0:T(8,128)}, u32[]{:S(2)}) copy-start(f32[576,256]{1,0:T(8,128)} %param.34) | copy-start | bytes 1769476
  450.3 51.8 %copy-start.22 = (f32[576,256]{1,0:T(8,128)S(1)}, f32[576,256]{1,0:T(8,128)}, u32[]{:S(2)}) copy-start(f32[576,256]{1,0:T(8,128)} %param.38) | copy-start | bytes 1769476
  450.3 51.8 %copy-start.23 = (f32[576,256]{1,0:T(8,128)S(1)}, f32[576,256]{1,0:T(8,128)}, u32[]{:S(2)}) copy-start(f32[576,256]{1,0:T(8,128)} %param.39) | copy-start | bytes 1769476
Sparse Core Ops, SparseCore 0:
  13.8 21.8 reduce-scatter.9
  38.0 30.0 all-gather.2
  70.2 29.5 all-gather.4
  281.0 26.5 reduce-scatter.7
  412.3 26.6 reduce-scatter.5
  447.1 52.5 all-reduce.42
where the time goes:
time: 519 us; the launch traced here: 512 us
  local copies, waits for them, and re-layouts  163 us (31%)
  matrix products  139 us (27%)
  other arithmetic  98.6 us (19%)
  waiting for transfers between devices  56.7 us (11%)
  blocking collectives  38.4 us (7%)
  between operations  15.8 us (3%)
    squeeze x2, local copies, waits for them, and re-layouts, conv_back(): moved = jnp.pad(pulled[:, :, :, :, tap_index], widths)  62.2 us
    unnamed x82, local copies, waits for them, and re-layouts  49.7 us
    dot_general x2, matrix products, conv_apply(): jnp.einsum('pc,tcd->ptd', flat_padded, taps_weight, preferred_element_typ...  46 us
    psum x1, waiting for transfers between devices, per_device(): lax.psum(shards[0].astype(jnp.bfloat16), 'dp').astype(jnp.float32)  45.5 us
    dot_general x2, matrix products, conv_back(): jnp.einsum('pd,tcd->ptc', flat_grad, taps_weight, preferred_element_type=...  36.4 us
    add x2, other arithmetic, conv_back(): spread = moved if spread is None else spread + moved  33.5 us
    dot_general x2, matrix products, conv_back(): jnp.einsum('pc,ptd->tcd', flat_padded, stacked, preferred_element_type=jn...  29.2 us
    psum x1, blocking collectives, per_device(): lax.psum(shards[2].astype(jnp.bfloat16), 'dp').astype(jnp.float32)  23.7 us
  transfers between devices with their start and end apart: 6, of which 2 were waited for; matrix products, arithmetic and copies ran while one was open for 45% of the time, Pallas kernels for 0%

commit v1 on v0

v1 whole, which is shorter than its diff:
```python
import functools

import jax
import jax.numpy as jnp
from jax import lax
from jax.experimental import pallas as pl
from jax.experimental.pallas import tpu as pltpu
from jax.sharding import PartitionSpec as P

STEP_COUNT = 10
BF = jnp.bfloat16
F32 = jnp.float32
FS = 6
ROLL = 8
PAIRS = 6
PAIR_ROWS = 2 * ROLL
GELU_K = 0.7978845608028654
GELU_C = 0.044715
VMEM_LIMIT = 56 * 2**20


def spec_any():
    return pl.BlockSpec(memory_space=pl.ANY)


def spec_vmem():
    return pl.BlockSpec(memory_space=pltpu.VMEM)


def spec_smem():
    return pl.BlockSpec(memory_space=pltpu.SMEM)


def gelu_both(v):
    sq = v * v
    t = jnp.tanh(v * (GELU_K + (GELU_K * GELU_C) * sq))
    half = 0.5 + 0.5 * t
    slope = half + (0.5 * v) * (1.0 - t * t) * (GELU_K + (3.0 * GELU_K * GELU_C) * sq)
    return v * half, slope


def window(p_ref, pair, row, rows, col, channels):
    return p_ref[pair, row : row + rows, col : col + FS].reshape(rows * FS * PAIR_ROWS, channels)


def conv_rows(p_ref, w_ref, pair, row, rows):
    c = w_ref.shape[1]
    acc = None
    for a in range(3):
        for b in range(3):
            t = 3 * a + b
            part = jnp.dot(
                window(p_ref, pair, row + a, rows, b, c),
                w_ref[t * c : (t + 1) * c],
                preferred_element_type=F32,
            )
            acc = part if acc is None else acc + part
    return acc


def conv_rows_back(g_ref, w_ref, pair, row, rows):
    c = w_ref.shape[1]
    acc = None
    for a in range(3):
        for b in range(3):
            t = 3 * a + b
            part = lax.dot_general(
                window(g_ref, pair, row + 2 - a, rows, 2 - b, c),
                w_ref[t * c : (t + 1) * c],
                (((1,), (1,)), ((), ())),
                preferred_element_type=F32,
            )
            acc = part if acc is None else acc + part
    return acc


def weight_grad(p_ref, g_ref, dw_ref):
    c = p_ref.shape[-1]
    g = g_ref[:, 1 : FS + 1, 1 : FS + 1].reshape(-1, c)
    for a in range(3):
        for b in range(3):
            t = 3 * a + b
            dw_ref[t * c : (t + 1) * c] = lax.dot_general(
                p_ref[:, a : a + FS, b : b + FS].reshape(-1, c),
                g,
                (((0,), (0,)), ((), ())),
                preferred_element_type=F32,
            ).astype(dw_ref.dtype)


def zero_corners(p_ref):
    zero = jnp.zeros((PAIRS, 1, 1, PAIR_ROWS, p_ref.shape[-1]), p_ref.dtype)
    for i in (0, FS + 1):
        for j in (0, FS + 1):
            p_ref[:, i : i + 1, j : j + 1] = zero


def stash_edges(e_ref, pair, row, rows, v):
    for par in range(2):
        face = 2 * pair + par
        half = v[:, :, par * ROLL : (par + 1) * ROLL]
        if row + rows == FS:
            e_ref[face, 0] = half[rows - 1]
        e_ref[face, 1, row : row + rows] = half[:, 0]
        if row == 0:
            e_ref[face, 2] = half[0]
        e_ref[face, 3, row : row + rows] = half[:, FS - 1]


def fill_halo(e_ref, table_ref, p_ref):
    for pair in range(PAIRS):
        for side in range(4):
            one = e_ref[table_ref[2 * pair, side], side]
            two = e_ref[table_ref[2 * pair + 1, side], side]
            v = jnp.concatenate([one, two], axis=1).astype(p_ref.dtype)
            if side == 0:
                p_ref[pair, 0, 1 : FS + 1] = v
            elif side == 1:
                p_ref[pair, 1 : FS + 1, FS + 1] = v
            elif side == 2:
                p_ref[pair, FS + 1, 1 : FS + 1] = v
            else:
                p_ref[pair, 1 : FS + 1, 0] = v
    zero_corners(p_ref)


def add_edges(e_ref, table_ref, pair, row, rows, v):
    for par in range(2):
        face = 2 * pair + par
        half = v[:, :, par * ROLL : (par + 1) * ROLL]
        if row == 0:
            to = table_ref[face, 0]
            e_ref[to, 0] = e_ref[to, 0] + half[0]
        to = table_ref[face, 1]
        e_ref[to, 1, row : row + rows] = e_ref[to, 1, row : row + rows] + half[:, FS - 1]
        if row + rows == FS:
            to = table_ref[face, 2]
            e_ref[to, 2] = e_ref[to, 2] + half[rows - 1]
        to = table_ref[face, 3]
        e_ref[to, 3, row : row + rows] = e_ref[to, 3, row : row + rows] + half[:, 0]


def fill_halo_back(e_ref, p_ref):
    for pair in range(PAIRS):
        for side in range(4):
            v = jnp.concatenate([e_ref[2 * pair, side], e_ref[2 * pair + 1, side]], axis=1)
            v = v.astype(p_ref.dtype)
            if side == 0:
                p_ref[pair, FS + 1, 1 : FS + 1] = v
            elif side == 1:
                p_ref[pair, 1 : FS + 1, 0] = v
            elif side == 2:
                p_ref[pair, 0, 1 : FS + 1] = v
            else:
                p_ref[pair, 1 : FS + 1, FS + 1] = v
    zero_corners(p_ref)


def to_pairs(ref, row):
    halves = []
    for par in range(2):
        v = ref[0, :, par, row].astype(F32)
        halves.append(jnp.transpose(v, (1, 0, 2)))
    return jnp.concatenate(halves, axis=1)


def from_pairs(ref, row, v):
    for par in range(2):
        half = v[:, par * ROLL : (par + 1) * ROLL]
        ref[0, :, par, row] = jnp.transpose(half, (1, 0, 2)).astype(ref.dtype)


def enter_kernel(lengths_ref, table_ref, x_ref, cot_ref, xp_ref, go_ref, dws_ref, e_ref, acc_ref):
    pair = pl.program_id(0)
    c = x_ref.shape[-1]
    live = (
        lax.broadcasted_iota(jnp.int32, (FS, PAIR_ROWS, c), 1) % ROLL < lengths_ref[0]
    )
    for i in range(FS):
        v = to_pairs(x_ref, i)
        xp_ref[pair, i + 1, 1 : FS + 1] = v.astype(BF)
        for par in range(2):
            face = 2 * pair + par
            half = v[:, par * ROLL : (par + 1) * ROLL]
            if i == FS - 1:
                e_ref[face, 0] = half
            e_ref[face, 1, i] = half[0]
            if i == 0:
                e_ref[face, 2] = half
            e_ref[face, 3, i] = half[FS - 1]
        go_ref[0, i] = jnp.where(live, to_pairs(cot_ref, i), 0.0).astype(BF)
    part = lax.dot_general(
        xp_ref[pair, 1 : FS + 1, 1 : FS + 1].reshape(-1, c),
        go_ref[0].reshape(-1, c),
        (((0,), (0,)), ((), ())),
        preferred_element_type=F32,
    )

    @pl.when(pair == 0)
    def _():
        acc_ref[...] = part

    @pl.when(pair > 0)
    def _():
        acc_ref[...] = acc_ref[...] + part

    @pl.when(pair == PAIRS - 1)
    def _():
        dws_ref[...] = acc_ref[...].astype(dws_ref.dtype)
        fill_halo(e_ref, table_ref, xp_ref)


def enter(lengths, table, x, cot):
    c = x.shape[-1]
    block = pl.BlockSpec((1, ROLL, 2, FS, FS, c), lambda p: (0, 0, p, 0, 0, 0))
    return pl.pallas_call(
        enter_kernel,
        grid=(PAIRS,),
        in_specs=[spec_smem(), spec_smem(), block, block],
        out_specs=[
            spec_vmem(),
            pl.BlockSpec((1, FS, FS, PAIR_ROWS, c), lambda p: (p, 0, 0, 0, 0)),
            spec_vmem(),
        ],
        out_shape=[
            jax.ShapeDtypeStruct((PAIRS, FS + 2, FS + 2, PAIR_ROWS, c), BF),
            jax.ShapeDtypeStruct((PAIRS, FS, FS, PAIR_ROWS, c), BF),
            jax.ShapeDtypeStruct((c, c), BF),
        ],
        scratch_shapes=[
            pltpu.VMEM((2 * PAIRS, 4, FS, ROLL, c), F32),
            pltpu.VMEM((c, c), F32),
        ],
        compiler_params=pltpu.CompilerParams(
            dimension_semantics=("arbitrary",), vmem_limit_bytes=VMEM_LIMIT
        ),
        name="enter",
    )(lengths, table, x, cot)


ROWS = 3


def first_kernel(table_ref, xp_ref, w_ref, hp_ref, slope_ref, e_ref):
    c = w_ref.shape[1]
    for pair in range(PAIRS):
        for row in range(0, FS, ROWS):
            hidden, slope = gelu_both(conv_rows(xp_ref, w_ref, pair, row, ROWS))
            shape = (ROWS, FS, PAIR_ROWS, c)
            low = hidden.astype(BF).reshape(shape)
            hp_ref[pair, row + 1 : row + 1 + ROWS, 1 : FS + 1] = low
            slope_ref[pair, row : row + ROWS] = slope.astype(BF).reshape(shape)
            stash_edges(e_ref, pair, row, ROWS, hidden.reshape(shape))
    fill_halo(e_ref, table_ref, hp_ref)


def first(table, xp, w):
    c = w.shape[1]
    return pl.pallas_call(
        first_kernel,
        in_specs=[spec_smem(), spec_vmem(), spec_vmem()],
        out_specs=[spec_vmem(), spec_vmem()],
        out_shape=[
            jax.ShapeDtypeStruct(xp.shape, BF),
            jax.ShapeDtypeStruct((PAIRS, FS, FS, PAIR_ROWS, c), BF),
        ],
        scratch_shapes=[pltpu.VMEM((2 * PAIRS, 4, FS, ROLL, c), F32)],
        compiler_params=pltpu.CompilerParams(vmem_limit_bytes=VMEM_LIMIT),
        name="first",
    )(table, xp, w)


def second_kernel(table_ref, hp_ref, w_ref, ws_ref, xp_ref, go_ref, out_ref, gp_ref, dw_ref, e_ref):
    c = w_ref.shape[1]
    e_ref[...] = jnp.zeros_like(e_ref)
    for pair in range(PAIRS):
        for row in range(0, FS, ROWS):
            value, slope = gelu_both(conv_rows(hp_ref, w_ref, pair, row, ROWS))
            value = value + jnp.dot(
                window(xp_ref, pair, row + 1, ROWS, 1, c), ws_ref[...], preferred_element_type=F32
            )
            shape = (ROWS, FS, PAIR_ROWS, c)
            value = value.reshape(shape)
            for i in range(ROWS):
                from_pairs(out_ref.at[:, :, 2 * pair : 2 * pair + 2], row + i, value[i])
            grad = go_ref[pair, row : row + ROWS].astype(F32) * slope.reshape(shape)
            low = grad.astype(BF)
            gp_ref[pair, row + 1 : row + 1 + ROWS, 1 : FS + 1] = low
            add_edges(e_ref, table_ref, pair, row, ROWS, low.astype(F32))
    fill_halo_back(e_ref, gp_ref)
    weight_grad(hp_ref, gp_ref, dw_ref)


def second(table, hp, w, ws, xp, go):
    c = w.shape[1]
    return pl.pallas_call(
        second_kernel,
        in_specs=[spec_smem()] + [spec_vmem()] * 5,
        out_specs=[spec_vmem()] * 3,
        out_shape=[
            jax.ShapeDtypeStruct((1, ROLL, 2 * PAIRS, FS, FS, c), BF),
            jax.ShapeDtypeStruct(hp.shape, BF),
            jax.ShapeDtypeStruct(w.shape, BF),
        ],
        scratch_shapes=[pltpu.VMEM((2 * PAIRS, 4, FS, ROLL, c), F32)],
        compiler_params=pltpu.CompilerParams(vmem_limit_bytes=VMEM_LIMIT),
        name="second",
    )(table, hp, w, ws, xp, go)


def hidden_back_kernel(table_ref, gp_ref, w_ref, slope_ref, xp_ref, op_ref, dw_ref, e_ref):
    c = w_ref.shape[1]
    e_ref[...] = jnp.zeros_like(e_ref)
    for pair in range(PAIRS):
        for row in range(0, FS, ROWS):
            shape = (ROWS, FS, PAIR_ROWS, c)
            grad = conv_rows_back(gp_ref, w_ref, pair, row, ROWS).reshape(shape)
            low = (grad * slope_ref[pair, row : row + ROWS].astype(F32)).astype(BF)
            op_ref[pair, row + 1 : row + 1 + ROWS, 1 : FS + 1] = low
            add_edges(e_ref, table_ref, pair, row, ROWS, low.astype(F32))
    fill_halo_back(e_ref, op_ref)
    weight_grad(xp_ref, op_ref, dw_ref)


def hidden_back(table, gp, w, slope, xp):
    c = w.shape[1]
    return pl.pallas_call(
        hidden_back_kernel,
        in_specs=[spec_smem()] + [spec_vmem()] * 4,
        out_specs=[spec_vmem()] * 2,
        out_shape=[
            jax.ShapeDtypeStruct(gp.shape, BF),
            jax.ShapeDtypeStruct(w.shape, BF),
        ],
        scratch_shapes=[pltpu.VMEM((2 * PAIRS, 4, FS, ROLL, c), F32)],
        compiler_params=pltpu.CompilerParams(vmem_limit_bytes=VMEM_LIMIT),
        name="hidden_back",
    )(table, gp, w, slope, xp)


def inputs_back_kernel(gp_ref, w_ref, ws_ref, go_ref, out_ref):
    c = w_ref.shape[1]
    for pair in range(PAIRS):
        for row in range(0, FS, ROWS):
            grad = conv_rows_back(gp_ref, w_ref, pair, row, ROWS)
            grad = grad + lax.dot_general(
                go_ref[pair, row : row + ROWS].reshape(-1, c),
                ws_ref[...],
                (((1,), (1,)), ((), ())),
                preferred_element_type=F32,
            )
            grad = grad.reshape(ROWS, FS, PAIR_ROWS, c)
            for i in range(ROWS):
                from_pairs(out_ref.at[:, :, 2 * pair : 2 * pair + 2], row + i, grad[i])


def inputs_back(gp, w, ws, go):
    c = w.shape[1]
    return pl.pallas_call(
        inputs_back_kernel,
        in_specs=[spec_vmem()] * 4,
        out_specs=spec_vmem(),
        out_shape=jax.ShapeDtypeStruct((1, ROLL, 2 * PAIRS, FS, FS, c), F32),
        compiler_params=pltpu.CompilerParams(vmem_limit_bytes=VMEM_LIMIT),
        name="inputs_back",
    )(gp, w, ws, go)


def adamw(weight, moment, square, grad, rate):
    moment_new = 0.9 * moment + 0.1 * grad
    square_new = 0.999 * square + 0.001 * grad * grad
    fix_one = 1.0 - 0.9**STEP_COUNT
    fix_two = 1.0 - 0.999**STEP_COUNT
    weight_new = weight - rate * (
        moment_new / fix_one / (jnp.sqrt(square_new / fix_two) + 1e-08) + 0.01 * weight
    )
    return (weight_new, moment_new, square_new)


def reduce_rows(grad):
    shard = lax.psum_scatter(grad, "fsdp", scatter_dimension=0, tiled=True)
    return lax.psum(shard, "dp").astype(F32)


def per_device(
    inputs,
    cotangent,
    lengths,
    face_table,
    w_first,
    w_second,
    w_skip,
    mom_first,
    sq_first,
    mom_second,
    sq_second,
    mom_skip,
    sq_skip,
):
    c = inputs.shape[-1]
    gather = functools.partial(lax.all_gather, axis_name="fsdp", axis=0, tiled=True)
    all_first = gather(w_first.astype(BF))
    all_second = gather(w_second.astype(BF))
    all_skip = gather(w_skip.astype(BF))
    xp, go, dw_skip = enter(lengths, face_table, inputs, cotangent)
    hp, slope = first(face_table, xp, all_first)
    output, gp, dw_second = second(face_table, hp, all_second, all_skip, xp, go)
    op, dw_first = hidden_back(face_table, gp, all_second, slope, xp)
    grad_inputs = inputs_back(op, all_first, all_skip, go)
    rate_conv = (9 * c) ** (-0.5)
    rate_skip = c ** (-0.5)
    skip_set = adamw(w_skip, mom_skip, sq_skip, reduce_rows(dw_skip), rate_skip)
    second_set = adamw(w_second, mom_second, sq_second, reduce_rows(dw_second), rate_conv)
    first_set = adamw(w_first, mom_first, sq_first, reduce_rows(dw_first), rate_conv)
    return (output, grad_inputs) + first_set + second_set + skip_set


def solution(mesh):
    fields = P(("dp", "fsdp"), None, None, None, None, None)
    rows = P("fsdp", None)
    return jax.shard_map(
        per_device,
        mesh=mesh,
        in_specs=(fields, fields, P(("dp", "fsdp")), P()) + (rows,) * 9,
        out_specs=(fields, fields) + (rows,) * 9,
        check_vma=False,
    )
```

time: 519 us -> 265 us (0.51); the launches traced: 512 us -> 265 us
  local copies, waits for them, and re-layouts: 163 us -> 16.7 us
  matrix products: 139 us -> 0 us
  other arithmetic: 98.6 us -> 5.6 us
  waiting for transfers between devices: 56.7 us -> 130 us
  Pallas kernels: 0 us -> 58.4 us
    dot_general x25 -> x0, matrix products: 139 us -> none  [the longest x2 46 us: conv_apply(): jnp.einsum('pc,tcd->ptd', flat_padded, taps_weight, preferred_element_typ...]
    reduce_scatter x3, waiting for transfers between devices: 11.1 us -> 78 us  [reduce_rows(): shard = lax.psum_scatter(grad, 'fsdp', scatter_dimension=0, tiled=True)]
    squeeze x5 -> x0, local copies, waits for them, and re-layouts: 65 us -> none  [the longest x2 62.2 us: conv_back(): moved = jnp.pad(pulled[:, :, :, :, tap_index], widths)]
    pallas_call x0 -> x5, Pallas kernels: none -> 58.4 us  [the longest x1 16.1 us: second(): pl.pallas_call(second_kernel, in_specs=[spec_smem()] + [spec_vmem()] * 5,...]
    convert_element_type x6 -> x2, other arithmetic: 43.1 us -> 1.49 us  [the longest x1 0.74 us: per_device(): all_first = gather(w_first.astype(BF))]
    add x4 -> x0, other arithmetic: 40.2 us -> none  [the longest x2 33.5 us: conv_back(): spread = moved if spread is None else spread + moved]
    unnamed x82 -> x27, local copies, waits for them, and re-layouts: 49.7 us -> 16.7 us
    scatter-add x2 -> x0, local copies, waits for them, and re-layouts: 25.9 us -> none  [the longest x1 13 us: unpad_back(): inner.at[:, :, :, 0]]
  transfers between devices with their start and end apart: 6 -> 6, of which waited for: 2 -> 5; matrix products, arithmetic and copies ran while one was open for 45% -> 5% of each run, Pallas kernels for 0% -> 8%
where the time goes in v1:
time: 265 us
  waiting for transfers between devices  130 us (49%)
  Pallas kernels  58.4 us (22%)
  blocking collectives  38.5 us (15%)
  local copies, waits for them, and re-layouts  16.7 us (6%)
  between operations  14.9 us (6%)
  other arithmetic  5.6 us (2%)
    reduce_scatter x3, waiting for transfers between devices, reduce_rows(): shard = lax.psum_scatter(grad, 'fsdp', scatter_dimension=0, tiled=True)  78 us
    psum x1, waiting for transfers between devices, reduce_rows(): return lax.psum(shard, 'dp').astype(F32)  37.3 us
    psum x1, blocking collectives, reduce_rows(): return lax.psum(shard, 'dp').astype(F32)  23.7 us
    unnamed x27, local copies, waits for them, and re-layouts  16.7 us
    pallas_call x1, Pallas kernels, second(): pl.pallas_call(second_kernel, in_specs=[spec_smem()] + [spec_vmem()] * 5,...  16.1 us
    all_gather x1, blocking collectives, per_device(): all_skip = gather(w_skip.astype(BF))  14.8 us
    all_gather x1, waiting for transfers between devices, per_device(): all_second = gather(w_second.astype(BF))  14.5 us
    pallas_call x1, Pallas kernels, hidden_back(): pl.pallas_call(hidden_back_kernel, in_specs=[spec_smem()] + [spec_vmem()]...  13.7 us
  transfers between devices with their start and end apart: 6, of which 5 were waited for; matrix products, arithmetic and copies ran while one was open for 5% of the time, Pallas kernels for 8%

profile of v1, /device:TPU:0, one launch (start us, length us, event | category | flops | bytes accessed | tf_op | source)
XLA Modules:
  0.0 265.1 jit_solution(13567526600133271129)
XLA Ops:
  7.2 0.0 copy-start.3
  7.2 0.0 reduce-scatter.8.cloned.1.call-start
  7.2 1.5 copy.28.table_ref
  9.4 3.4 %copy.25.x_ref = bf16[1,8,12,6,6,256]{5,4,3,2,1,0:T(8,128)(2,1)} copy(bf16[1,8,12,6,6,256]{5,1,4,3,2,0:T(8,128)(2,1)} %param.13) | data formatting | bytes 3538944 | tf_op args[0]
  12.8 0.0 copy-done.3
  12.8 1.9 copy.26.cot_ref
  14.7 0.0 copy-start.1
  14.7 8.3 %enter.1 = (bf16[6,8,8,16,256]{4,3,2,1,0:T(8,128)(2,1)}, bf16[6,6,6,16,256]{4,3,2,1,0:T(8,128)(2,1)}, bf16[256,256]{1,0:T(8,128)(2,1)}) custom-call(s32[1]{0:T(128)S(6)} %copy.34.lengths_ref, s32[12,4]{1,0:T(8,128)} %copy.28.table_ref, bf16[1,8,12,6,6,256]{5,4,3,2,1,0:T(8,128)(2,1)} %copy.25.x_ref, bf16[1,8,12,6,6,256]{5,4,3,2,1,0:T(8,128)(2,1)} %copy.26.cot_ref), custom_call_target="tpu_custom_call" | custom-call | tf_op jit(solution)/shard_map/enter/pallas_call | solution.py:216
  23.0 0.0 copy-start.9
  23.0 0.0 copy-start.10
  23.0 0.0 reduce-scatter.8.cloned.1.call-update
  23.0 0.0 all-gather.3.cloned.1.call-start
  23.1 0.0 copy-done.1
  23.1 0.7 convert_element_type.18
  23.8 0.0 all-gather.3.cloned.1.call-update
  23.9 0.0 all-gather.5.cloned.1.call-start
  23.9 0.0 copy-done.2
  23.9 0.7 convert_element_type.19
  24.7 0.0 all-gather.5.cloned.1.call-update
  24.7 0.0 reduce-scatter.4.cloned.1.call-start
  24.7 20.3 %reduce-scatter.8.cloned.1.call-done = bf16[64,256]{1,0:T(8,128)(2,1)} async-done(((bf16[256,256]{1,0:T(8,128)(2,1)}), bf16[64,256]{1,0:T(8,128)(2,1)}) %reduce-scatter.8.cloned.1.call-update) | async-done | bytes 32784 | tf_op jit(solution)/shard_map/reduce_scatter | solution.py:381
  45.1 23.7 %psum.23 = bf16[64,256]{1,0:T(8,128)(2,1)S(1)} all-reduce(bf16[64,256]{1,0:T(8,128)(2,1)} %reduce-scatter.8.cloned.1.call-done), channel_id=1, replica_groups=mesh['dp'=8,'fsdp'=4] {'dp'}, use_global_device_ids=true, to_apply=%region_5.0 | all-reduce | flops 16384 | bytes 65536 | tf_op jit(solution)/shard_map/psum | solution.py:382
  68.8 0.0 copy-done.8
  68.8 0.0 copy-done.9
  68.8 0.0 copy-done.10
  68.8 0.7 multiply_subtract_fusion.2
  69.5 14.8 %all_gather.11.ws_ref = bf16[256,256]{1,0:T(8,128)(2,1)} all-gather(bf16[64,256]{1,0:T(8,128)(2,1)S(1)} %get-tuple-element.53), channel_id=1, replica_groups=mesh['dp'=8,'fsdp'=4] {'fsdp'}, dimensions={0}, use_global_device_ids=true | all-gather | bytes 163840 | tf_op jit(solution)/shard_map/all_gather | solution.py:404
  84.3 10.4 %first.1 = (bf16[6,8,8,16,256]{4,3,2,1,0:T(8,128)(2,1)}, bf16[6,6,6,16,256]{4,3,2,1,0:T(8,128)(2,1)}) custom-call(s32[12,4]{1,0:T(8,128)} %copy.28.table_ref, bf16[6,8,8,16,256]{4,3,2,1,0:T(8,128)(2,1)} %get-tuple-element.21.xp_ref, bf16[2304,256]{1,0:T(8,128)(2,1)} %all-gather.3.cloned.1.call-done.w_ref), custom_call_target="tpu_custom_call" | custom-call | tf_op jit(solution)/shard_map/first/pallas_call | solution.py:259
  94.7 14.5 %all-gather.5.cloned.1.call-done.w_ref = bf16[2304,256]{1,0:T(8,128)(2,1)} async-done(((bf16[576,256]{1,0:T(8,128)(2,1)}), bf16[2304,256]{1,0:T(8,128)(2,1)}) %all-gather.5.cloned.1.call-update) | async-done | bytes 1179664 | tf_op jit(solution)/shard_map/all_gather | solution.py:403
  109.2 16.1 %second.1 = (bf16[1,8,12,6,6,256]{5,4,3,2,1,0:T(8,128)(2,1)}, bf16[6,8,8,16,256]{4,3,2,1,0:T(8,128)(2,1)}, bf16[2304,256]{1,0:T(8,128)(2,1)}) custom-call(s32[12,4]{1,0:T(8,128)} %copy.28.table_ref, bf16[6,8,8,16,256]{4,3,2,1,0:T(8,128)(2,1)} %get-tuple-element.22.hp_ref, bf16[2304,256]{1,0:T(8,128)(2,1)} %all-gather.5.cloned.1.call-done.w_ref, ...), custom_call_target="tpu_custom_call" | custom-call | tf_op jit(solution)/shard_map/second/pallas_call | solution.py:296
  125.3 13.7 %hidden_back.1 = (bf16[6,8,8,16,256]{4,3,2,1,0:T(8,128)(2,1)}, bf16[2304,256]{1,0:T(8,128)(2,1)}) custom-call(s32[12,4]{1,0:T(8,128)} %copy.28.table_ref, bf16[6,8,8,16,256]{4,3,2,1,0:T(8,128)(2,1)} %get-tuple-element.25.gp_ref, bf16[2304,256]{1,0:T(8,128)(2,1)} %all-gather.5.cloned.1.call-done.w_ref, ...), custom_call_target="tpu_custom_call" | custom-call | tf_op jit(solution)/shard_map/hidden_back/pallas_call | solution.py:327
  139.1 0.0 reduce-scatter.4.cloned.1.call-update
  139.1 0.0 reduce-scatter.6.cloned.1.call-start
  139.1 0.5 reduce-scatter.6.cloned.1.call-update
  139.7 0.3 all-reduce.3.cloned.1.call-start
  140.0 27.5 %reduce-scatter.4.cloned.1.call-done = bf16[576,256]{1,0:T(8,128)(2,1)} async-done(((bf16[2304,256]{1,0:T(8,128)(2,1)}), bf16[576,256]{1,0:T(8,128)(2,1)}) %reduce-scatter.4.cloned.1.call-update) | async-done | bytes 294928 | tf_op jit(solution)/shard_map/reduce_scatter | solution.py:381
  167.5 30.2 %reduce-scatter.6.cloned.1.call-done = bf16[576,256]{1,0:T(8,128)(2,1)} async-done(((bf16[2304,256]{1,0:T(8,128)(2,1)}), bf16[576,256]{1,0:T(8,128)(2,1)}) %reduce-scatter.6.cloned.1.call-update) | async-done | bytes 294928 | tf_op jit(solution)/shard_map/reduce_scatter | solution.py:381
  197.7 0.0 all-reduce.3.cloned.1.call-update
  197.7 0.0 copy-done
  197.7 3.1 %copy.30 = bf16[1,8,12,6,6,256]{5,1,4,3,2,0:T(8,128)(2,1)} copy(bf16[1,8,12,6,6,256]{5,4,3,2,1,0:T(8,128)(2,1)S(1)} %copy-done) | data formatting | bytes 3538944
  200.8 9.9 %inputs_back.1 = f32[1,8,12,6,6,256]{5,4,3,2,1,0:T(8,128)} custom-call(bf16[6,8,8,16,256]{4,3,2,1,0:T(8,128)(2,1)} %get-tuple-element.27.gp_ref, bf16[2304,256]{1,0:T(8,128)(2,1)} %all-gather.3.cloned.1.call-done.w_ref, bf16[256,256]{1,0:T(8,128)(2,1)} %all_gather.11.ws_ref, bf16[6,6,6,16,256]{4,3,2,1,0:T(8,128)(2,1)} %get-tuple-element.23.go_ref), custom_call_target="tpu_custom_call" | custom-call | tf_op jit(solution)/shard_map/inputs_back/pallas_call | solution.py:359
  210.8 6.8 %copy.31 = f32[1,8,12,6,6,256]{5,1,4,3,2,0:T(8,128)} copy(f32[1,8,12,6,6,256]{5,4,3,2,1,0:T(8,128)} %inputs_back.1) | data formatting | bytes 7077888
  217.5 37.3 %all-reduce.3.cloned.1.call-done = (bf16[576,256]{1,0:T(8,128)(2,1)}, bf16[576,256]{1,0:T(8,128)(2,1)}) async-done(((bf16[576,256]{1,0:T(8,128)(2,1)}, bf16[576,256]{1,0:T(8,128)(2,1)}), (bf16[576,256]{1,0:T(8,128)(2,1)}, bf16[576,256]{1,0:T(8,128)(2,1)})) %all-reduce.3.cloned.1.call-update) | async-done | bytes 589840 | tf_op jit(solution)/shard_map/psum | solution.py:382
  254.8 0.0 copy-done.4
  254.8 0.0 copy-done.5
  254.8 0.0 copy-done.6
  254.8 0.0 copy-done.7
  254.8 3.4 %multiply_subtract_fusion = (f32[576,256]{1,0:T(8,128)}, f32[576,256]{1,0:T(8,128)}, f32[576,256]{1,0:T(8,128)}, f32[576,256]{1,0:T(8,128)}, f32[576,256]{1,0:T(8,128)}, /*index=5*/f32[576,256]{1,0:T(8,128)}) fusion(f32[576,256]{1,0:T(8,128)S(1)} %copy-done.2, bf16[576,256]{1,0:T(8,128)(2,1)} %get-tuple-element.43, f32[576,256]{1,0:T(8,128)S(1)} %copy-done.4, ...), kind=kLoop, calls=%fused_computation.8 | loop fusion | flops 4718592 | bytes 7667712 | tf_op jit(solution)/shard_map/sub | solution.py:374
  (8 shorter events, 0.0 us)
Async XLA Ops:
  7.2 5.6 %copy-start.3 = (bf16[1,8,12,6,6,256]{5,1,4,3,2,0:T(8,128)(2,1)S(1)}, bf16[1,8,12,6,6,256]{5,1,4,3,2,0:T(8,128)(2,1)}, u32[]{:S(2)}) copy-start(bf16[1,8,12,6,6,256]{5,1,4,3,2,0:T(8,128)(2,1)} %param.14) | copy-start | bytes 5308420
  7.2 37.9 %reduce-scatter.8.cloned.1.call-start = ((), (), s32[]{:S(2)}) async-start(), calls=%async_computation.7 | async-start | bytes 163840 | tf_op jit(solution)/shard_map/reduce_scatter | solution.py:381
  14.7 8.4 %copy-start.1 = (f32[576,256]{1,0:T(8,128)S(1)}, f32[576,256]{1,0:T(8,128)}, u32[]{:S(2)}) copy-start(f32[576,256]{1,0:T(8,128)} %param.17) | copy-start | bytes 1769476
  14.7 9.3 %copy-start.2 = (f32[576,256]{1,0:T(8,128)S(1)}, f32[576,256]{1,0:T(8,128)}, u32[]{:S(2)}) copy-start(f32[576,256]{1,0:T(8,128)} %param.18) | copy-start | bytes 1769476
  23.0 45.8 %copy-start.8 = (f32[64,256]{1,0:T(8,128)S(1)}, f32[64,256]{1,0:T(8,128)}, u32[]{:S(2)}) copy-start(f32[64,256]{1,0:T(8,128)} %param.19) | copy-start | bytes 196612
  23.0 45.8 %copy-start.9 = (f32[64,256]{1,0:T(8,128)S(1)}, f32[64,256]{1,0:T(8,128)}, u32[]{:S(2)}) copy-start(f32[64,256]{1,0:T(8,128)} %param.24) | copy-start | bytes 196612
  23.0 45.8 %copy-start.10 = (f32[64,256]{1,0:T(8,128)S(1)}, f32[64,256]{1,0:T(8,128)}, u32[]{:S(2)}) copy-start(f32[64,256]{1,0:T(8,128)} %param.25) | copy-start | bytes 196612
  23.0 61.3 %all-gather.3.cloned.1.call-start = ((), (), s32[]{:S(2)}) async-start(), calls=%async_computation.3 | async-start | bytes 1474560 | tf_op jit(solution)/shard_map/all_gather | solution.py:402
  23.9 85.4 %all-gather.5.cloned.1.call-start = ((), (), s32[]{:S(2)}) async-start(), calls=%async_computation.4 | async-start | bytes 1474560 | tf_op jit(solution)/shard_map/all_gather | solution.py:403
  24.7 142.8 %reduce-scatter.4.cloned.1.call-start = ((), (), s32[]{:S(2)}) async-start(), calls=%async_computation.5 | async-start | bytes 1474560 | tf_op jit(solution)/shard_map/reduce_scatter | solution.py:381
  139.1 58.7 %copy-start = (bf16[1,8,12,6,6,256]{5,4,3,2,1,0:T(8,128)(2,1)S(1)}, bf16[1,8,12,6,6,256]{5,4,3,2,1,0:T(8,128)(2,1)}, u32[]{:S(2)}) copy-start(bf16[1,8,12,6,6,256]{5,4,3,2,1,0:T(8,128)(2,1)} %get-tuple-element.31) | copy-start | bytes 5308420
  139.1 58.6 %reduce-scatter.6.cloned.1.call-start = ((), (), s32[]{:S(2)}) async-start(), calls=%async_computation.6 | async-start | bytes 1474560 | tf_op jit(solution)/shard_map/reduce_scatter | solution.py:381
  139.7 115.1 %all-reduce.3.cloned.1.call-start = ((), (), s32[]{:S(2)}) async-start(), calls=%async_computation.8 | async-start | bytes 1179648 | tf_op jit(solution)/shard_map/psum | solution.py:382
  210.7 44.1 %copy-start.4 = (f32[576,256]{1,0:T(8,128)S(1)}, f32[576,256]{1,0:T(8,128)}, u32[]{:S(2)}) copy-start(f32[576,256]{1,0:T(8,128)} %param.22) | copy-start | bytes 1769476
  210.8 44.1 %copy-start.5 = (f32[576,256]{1,0:T(8,128)S(1)}, f32[576,256]{1,0:T(8,128)}, u32[]{:S(2)}) copy-start(f32[576,256]{1,0:T(8,128)} %param.23) | copy-start | bytes 1769476
  210.8 44.1 %copy-start.6 = (f32[576,256]{1,0:T(8,128)S(1)}, f32[576,256]{1,0:T(8,128)}, u32[]{:S(2)}) copy-start(f32[576,256]{1,0:T(8,128)} %param.21) | copy-start | bytes 1769476
  210.8 44.1 %copy-start.7 = (f32[576,256]{1,0:T(8,128)S(1)}, f32[576,256]{1,0:T(8,128)}, u32[]{:S(2)}) copy-start(f32[576,256]{1,0:T(8,128)} %param.20) | copy-start | bytes 1769476
Sparse Core Ops, SparseCore 0:
  23.2 21.8 reduce-scatter.7
  47.3 30.0 all-gather.2
  79.6 29.6 all-gather.4
  139.2 28.2 reduce-scatter.3
  169.8 27.8 reduce-scatter.5
  201.0 53.7 all-reduce.2

commit v2 on v0

v2 whole, which is shorter than its diff:
```python
import jax
import jax.numpy as jnp
from jax import lax
from jax.experimental import pallas as pl
from jax.experimental.pallas import tpu as pltpu
from jax.sharding import Mesh
from jax.sharding import PartitionSpec as P

STEP_COUNT = 10
BF = jnp.bfloat16
F32 = jnp.float32
FS = 6
ROLL = 8
FACES = 12
GELU_K = 0.7978845608028654
GELU_C = 0.044715
VMEM_LIMIT = 40 * 2**20


ANY = pl.BlockSpec(memory_space=pl.ANY)
VMEM = pl.BlockSpec(memory_space=pltpu.VMEM)
SMEM = pl.BlockSpec(memory_space=pltpu.SMEM)


def field(c, dtype=BF):
    return jax.ShapeDtypeStruct((FACES, FS, FS, ROLL, c), dtype)


def padded(c):
    return (FACES, FS + 2, FS + 2, ROLL, c)


def inner(ref):
    return ref.at[:, 1 : FS + 1, 1 : FS + 1]


def params():
    return pltpu.CompilerParams(vmem_limit_bytes=VMEM_LIMIT)


def gelu_both(v):
    sq = v * v
    t = jnp.tanh(v * (GELU_K + (GELU_K * GELU_C) * sq))
    half = 0.5 + 0.5 * t
    slope = half + (0.5 * v) * (1.0 - t * t) * (GELU_K + (3.0 * GELU_K * GELU_C) * sq)
    return v * half, slope


def window(p_ref, face, a, b):
    return p_ref[face, a : a + FS, b : b + FS].reshape(FS * FS * ROLL, p_ref.shape[-1])


def conv(p_ref, w_ref, face):
    c = w_ref.shape[1]
    acc = None
    for a in range(3):
        for b in range(3):
            t = 3 * a + b
            part = jnp.dot(
                window(p_ref, face, a, b), w_ref[t * c : (t + 1) * c], preferred_element_type=F32
            )
            acc = part if acc is None else acc + part
    return acc


def dot_back(v, w):
    return lax.dot_general(v, w, (((1,), (1,)), ((), ())), preferred_element_type=F32)


def conv_back(g_ref, w_ref, face):
    c = w_ref.shape[1]
    acc = None
    for a in range(3):
        for b in range(3):
            t = 3 * a + b
            part = dot_back(window(g_ref, face, 2 - a, 2 - b), w_ref[t * c : (t + 1) * c])
            acc = part if acc is None else acc + part
    return acc


def outer(p, g):
    c = p.shape[-1]
    return lax.dot_general(
        p.reshape(-1, c), g.reshape(-1, c), (((0,), (0,)), ((), ())), preferred_element_type=F32
    )


def zero_corners(p_ref):
    zero = jnp.zeros((FACES, 1, 1, ROLL, p_ref.shape[-1]), p_ref.dtype)
    for i in (0, FS + 1):
        for j in (0, FS + 1):
            p_ref[:, i : i + 1, j : j + 1] = zero


def fill_halo(table_ref, p_ref):
    for face in range(FACES):
        p_ref[face, 0, 1 : FS + 1] = p_ref[table_ref[0, face], FS, 1 : FS + 1]
        p_ref[face, 1 : FS + 1, FS + 1] = p_ref[table_ref[1, face], 1 : FS + 1, 1]
        p_ref[face, FS + 1, 1 : FS + 1] = p_ref[table_ref[2, face], 1, 1 : FS + 1]
        p_ref[face, 1 : FS + 1, 0] = p_ref[table_ref[3, face], 1 : FS + 1, FS]
    zero_corners(p_ref)


def add_edges(e_ref, table_ref, face, v):
    for side, part in enumerate((v[0], v[:, FS - 1], v[FS - 1], v[:, 0])):
        to = table_ref[side, face]
        e_ref[to, side] = e_ref[to, side] + part


def fill_halo_back(e_ref, p_ref):
    for face in range(FACES):
        p_ref[face, FS + 1, 1 : FS + 1] = e_ref[face, 0].astype(p_ref.dtype)
        p_ref[face, 1 : FS + 1, 0] = e_ref[face, 1].astype(p_ref.dtype)
        p_ref[face, 0, 1 : FS + 1] = e_ref[face, 2].astype(p_ref.dtype)
        p_ref[face, 1 : FS + 1, FS + 1] = e_ref[face, 3].astype(p_ref.dtype)
    zero_corners(p_ref)


def edge_sums(c):
    return pltpu.VMEM((FACES, 4, FS, ROLL, c), F32)


class Plan:
    def __init__(self, sizes, channels):
        self.tiles, self.ranks = sizes["tile"], sizes["fsdp"]
        self.c = channels
        self.conv = 9 * channels
        self.piece = self.conv // (self.ranks * 2 * self.tiles)
        self.skip_piece = channels // (self.ranks * 2 * self.tiles)
        self.chunk = 2 * self.piece + self.skip_piece
        self.shard = self.conv // self.ranks
        self.skip_shard = channels // self.ranks


def place_rows(plan, ids_ref, dst_ref, value, first_row, piece, offset):
    core, tile, rank = ids_ref[0], ids_ref[1], ids_ref[2]
    end = first_row + value.shape[0]
    row = first_row
    while row < end:
        number = row // piece
        stop = min(end, (number + 1) * piece)
        to_tile = number % plan.tiles
        to_core = number // plan.tiles % 2
        to_rank = number // (2 * plan.tiles)
        at = offset + row - number * piece
        dst_ref[
            to_core ^ core,
            to_tile ^ tile,
            (to_rank + plan.ranks - rank) % plan.ranks,
            at : at + stop - row,
        ] = value[row - first_row : stop - first_row]
        row = stop


def weight_grad(plan, ids_ref, p_ref, g, dst_ref, offset):
    c = p_ref.shape[-1]
    for a in range(3):
        for b in range(3):
            part = outer(p_ref[:, a : a + FS, b : b + FS], g).astype(BF)
            place_rows(plan, ids_ref, dst_ref, part, (3 * a + b) * c, plan.piece, offset)


def pack_kernel(ids_ref, one_ref, two_ref, skip_ref, low1_ref, half1_ref, low2_ref, low3_ref, half2_ref):
    core = ids_ref[0]
    rows = one_ref.shape[0] // 2
    few = skip_ref.shape[0] // 2
    low1_ref[...] = one_ref[...].astype(BF)
    half1_ref[...] = one_ref[pl.ds(core * rows, rows)].astype(BF)
    low2_ref[...] = two_ref[...].astype(BF)
    low3_ref[...] = skip_ref[...].astype(BF)
    half2_ref[0:rows] = two_ref[pl.ds(core * rows, rows)].astype(BF)
    half2_ref[rows : rows + few] = skip_ref[pl.ds(core * few, few)].astype(BF)


def pack(plan, ids, one, two, skip):
    c, rows, few = plan.c, plan.shard, plan.skip_shard
    shapes = [(rows, c), (rows // 2, c), (rows, c), (few, c), ((rows + few) // 2, c)]
    return pl.pallas_call(
        pack_kernel,
        in_specs=[SMEM] + [VMEM] * 3,
        out_specs=[VMEM] * 5,
        out_shape=[jax.ShapeDtypeStruct(v, BF) for v in shapes],
        compiler_params=params(),
        name="pack",
    )(ids, one, two, skip)


def weight_copies(plan, ids_ref, low_ref, near_refs, far_refs, w_ref, rows, offset, sem):
    core, rank = ids_ref[0], ids_ref[2]
    half = rows // 2
    copies = [pltpu.make_async_copy(low_ref, w_ref.at[pl.ds(rank * rows, rows)], sem.at[0])]
    for d in range(1, plan.ranks):
        start = (rank + plan.ranks - d) % plan.ranks * rows
        for k, refs in enumerate((near_refs, far_refs)):
            side = core if k == 0 else 1 - core
            copies.append(
                pltpu.make_async_copy(
                    refs[d - 1].at[pl.ds(offset, half)],
                    w_ref.at[pl.ds(start + side * half, half)],
                    sem.at[2 * d - 1 + k],
                )
            )
    return copies


def enter_kernel(lengths_ref, table_ref, x_ref, cot_ref, xp_ref, go_ref, dw_ref, sem):
    c = x_ref.shape[-1]
    load = pltpu.make_async_copy(x_ref, inner(xp_ref), sem)
    load.start()
    live = lax.broadcasted_iota(jnp.int32, (FS, FS, ROLL, c), 2) < lengths_ref[0]
    for face in range(FACES):
        go_ref[face] = jnp.where(live, cot_ref[face].astype(F32), 0.0).astype(BF)
    load.wait()
    fill_halo(table_ref, xp_ref)
    dw_ref[...] = outer(xp_ref[:, 1 : FS + 1, 1 : FS + 1], go_ref[...]).astype(dw_ref.dtype)


def enter(lengths, table, x, cot):
    c = x.shape[-1]
    return pl.pallas_call(
        enter_kernel,
        in_specs=[SMEM, SMEM, ANY, VMEM],
        out_specs=[VMEM, VMEM, VMEM],
        out_shape=[
            jax.ShapeDtypeStruct(padded(c), BF),
            field(c),
            jax.ShapeDtypeStruct((c, c), BF),
        ],
        scratch_shapes=[pltpu.SemaphoreType.DMA],
        compiler_params=params(),
        name="enter",
    )(lengths, table, x, cot)


def first(plan, ids, table, xp, low, near, far):
    c = plan.c
    count = plan.ranks - 1

    def kernel(ids_ref, table_ref, xp_ref, low_ref, *refs):
        near_refs, far_refs = refs[:count], refs[count : 2 * count]
        hp_ref, slope_ref, w_out, w_ref, sem, out_sem = refs[2 * count :]
        copies = weight_copies(plan, ids_ref, low_ref, near_refs, far_refs, w_ref, plan.shard, 0, sem)
        for copy in copies:
            copy.start()
        for copy in copies:
            copy.wait()
        keep = pltpu.make_async_copy(w_ref, w_out, out_sem)
        keep.start()
        for face in range(FACES):
            hidden, slope = gelu_both(conv(xp_ref, w_ref, face))
            hp_ref[face, 1 : FS + 1, 1 : FS + 1] = hidden.astype(BF).reshape(FS, FS, ROLL, c)
            slope_ref[face] = slope.astype(BF).reshape(FS, FS, ROLL, c)
        fill_halo(table_ref, hp_ref)
        keep.wait()

    return pl.pallas_call(
        kernel,
        in_specs=[SMEM, SMEM, VMEM] + [ANY] * (1 + 2 * count),
        out_specs=[VMEM, VMEM, ANY],
        out_shape=[
            jax.ShapeDtypeStruct(padded(c), BF),
            field(c),
            jax.ShapeDtypeStruct((plan.conv, c), BF),
        ],
        scratch_shapes=[
            pltpu.VMEM((plan.conv, c), BF),
            pltpu.SemaphoreType.DMA((2 * count + 1,)),
            pltpu.SemaphoreType.DMA,
        ],
        compiler_params=params(),
        name="first",
    )(ids, table, xp, low, *near, *far)


def second(plan, ids, table, hp, slope, xp, go, dws, low, low_skip, near, far):
    c = plan.c
    count = plan.ranks - 1

    def kernel(ids_ref, table_ref, hp_ref, slope_hbm, xp_hbm, go_hbm, dws_ref, low_ref, lows_ref, *refs):
        near_refs, far_refs = refs[:count], refs[count : 2 * count]
        (out_hbm, op_hbm, ws_hbm, keep_hbm, send_hbm) = refs[2 * count : 2 * count + 5]
        (out_ref, op_ref, w_ref, ws_ref, dw_ref, gp_ref, xp_ref, go_ref, slope_ref, e_ref) = refs[
            2 * count + 5 : 2 * count + 15
        ]
        sem, sem_skip, sem_in, sem_out = refs[2 * count + 15 :]
        copies = weight_copies(plan, ids_ref, low_ref, near_refs, far_refs, w_ref, plan.shard, 0, sem)
        copies += weight_copies(
            plan, ids_ref, lows_ref, near_refs, far_refs, ws_ref, plan.skip_shard, plan.shard // 2, sem_skip
        )
        for copy in copies:
            copy.start()
        loads = [
            pltpu.make_async_copy(xp_hbm, xp_ref, sem_in.at[0]),
            pltpu.make_async_copy(go_hbm, go_ref, sem_in.at[1]),
            pltpu.make_async_copy(slope_hbm, slope_ref, sem_in.at[2]),
        ]
        for load in loads:
            load.start()
        e_ref[...] = jnp.zeros_like(e_ref)
        place_rows(plan, ids_ref, dw_ref, dws_ref[...], 0, plan.skip_piece, 2 * plan.piece)
        for copy in copies:
            copy.wait()
        for load in loads:
            load.wait()
        stores = [
            pltpu.make_async_copy(ws_ref, ws_hbm, sem_out.at[0]),
            pltpu.make_async_copy(out_ref, out_hbm, sem_out.at[1]),
            pltpu.make_async_copy(op_ref, op_hbm, sem_out.at[2]),
            pltpu.make_async_copy(dw_ref.at[0], keep_hbm, sem_out.at[3]),
            pltpu.make_async_copy(dw_ref.at[1], send_hbm, sem_out.at[4]),
        ]
        stores[0].start()
        for face in range(FACES):
            value, slope = gelu_both(conv(hp_ref, w_ref, face))
            value = value + jnp.dot(
                xp_ref[face, 1 : FS + 1, 1 : FS + 1].reshape(-1, c),
                ws_ref[...],
                preferred_element_type=F32,
            )
            out_ref[face] = value.astype(BF).reshape(FS, FS, ROLL, c)
            low_grad = (go_ref[face].astype(F32) * slope.reshape(FS, FS, ROLL, c)).astype(BF)
            gp_ref[face, 1 : FS + 1, 1 : FS + 1] = low_grad
            add_edges(e_ref, table_ref, face, low_grad.astype(F32))
        stores[1].start()
        weight_grad(plan, ids_ref, hp_ref, gp_ref[:, 1 : FS + 1, 1 : FS + 1], dw_ref, plan.piece)
        fill_halo_back(e_ref, gp_ref)
        e_ref[...] = jnp.zeros_like(e_ref)
        for face in range(FACES):
            grad = conv_back(gp_ref, w_ref, face).reshape(FS, FS, ROLL, c)
            low_grad = (grad * slope_ref[face].astype(F32)).astype(BF)
            op_ref[face, 1 : FS + 1, 1 : FS + 1] = low_grad
            add_edges(e_ref, table_ref, face, low_grad.astype(F32))
        fill_halo_back(e_ref, op_ref)
        stores[2].start()
        weight_grad(plan, ids_ref, xp_ref, op_ref[:, 1 : FS + 1, 1 : FS + 1], dw_ref, 0)
        stores[3].start()
        stores[4].start()
        for store in stores:
            store.wait()

    sums = (plan.tiles, plan.ranks, plan.chunk, c)
    return pl.pallas_call(
        kernel,
        in_specs=[SMEM, SMEM, VMEM, ANY, ANY, ANY, VMEM] + [ANY] * (2 + 2 * count),
        out_specs=[ANY] * 5,
        out_shape=[
            field(c),
            jax.ShapeDtypeStruct(padded(c), BF),
            jax.ShapeDtypeStruct((c, c), BF),
            jax.ShapeDtypeStruct(sums, BF),
            jax.ShapeDtypeStruct(sums, BF),
        ],
        scratch_shapes=[
            pltpu.VMEM(field(c).shape, BF),
            pltpu.VMEM(padded(c), BF),
            pltpu.VMEM((plan.conv, c), BF),
            pltpu.VMEM((c, c), BF),
            pltpu.VMEM((2,) + sums, BF),
            pltpu.VMEM(padded(c), BF),
            pltpu.VMEM(padded(c), BF),
            pltpu.VMEM(field(c).shape, BF),
            pltpu.VMEM(field(c).shape, BF),
            edge_sums(c),
            pltpu.SemaphoreType.DMA((2 * count + 1,)),
            pltpu.SemaphoreType.DMA((2 * count + 1,)),
            pltpu.SemaphoreType.DMA((3,)),
            pltpu.SemaphoreType.DMA((5,)),
        ],
        compiler_params=params(),
        name="second",
    )(ids, table, hp, slope, xp, go, dws, low, low_skip, *near, *far)


def inputs_back_kernel(gp_ref, w_ref, ws_ref, go_ref, out_hbm, out_ref, sem):
    c = w_ref.shape[1]
    stores = []
    for face in range(FACES):
        grad = conv_back(gp_ref, w_ref, face)
        grad = grad + dot_back(go_ref[face].reshape(-1, c), ws_ref[...])
        out_ref[face] = grad.reshape(FS, FS, ROLL, c)
        stores.append(pltpu.make_async_copy(out_ref.at[face], out_hbm.at[face], sem.at[face]))
        stores[-1].start()
    for store in stores:
        store.wait()


def inputs_back(gp, w, ws, go):
    c = w.shape[1]
    return pl.pallas_call(
        inputs_back_kernel,
        in_specs=[VMEM] * 4,
        out_specs=ANY,
        out_shape=field(c, F32),
        scratch_shapes=[pltpu.VMEM(field(c).shape, F32), pltpu.SemaphoreType.DMA((FACES,))],
        compiler_params=params(),
        name="inputs_back",
    )(gp, w, ws, go)


def adamw(weight, moment, square, grad, rate):
    moment_new = 0.9 * moment + 0.1 * grad
    square_new = 0.999 * square + 0.001 * grad * grad
    fix_one = 1.0 - 0.9**STEP_COUNT
    fix_two = 1.0 - 0.999**STEP_COUNT
    weight_new = weight - rate * (
        moment_new / fix_one / (jnp.sqrt(square_new / fix_two) + 1e-08) + 0.01 * weight
    )
    return (weight_new, moment_new, square_new)


def update(plan, ids, near, far, sets):
    c, tiles = plan.c, plan.tiles

    def kernel(ids_ref, *refs):
        near_refs, far_refs = refs[:tiles], refs[tiles : 2 * tiles]
        state = refs[2 * tiles : 2 * tiles + 9]
        new = refs[2 * tiles + 9 : 2 * tiles + 18]
        g_ref, sum_ref, sem = refs[2 * tiles + 18 :]
        core, tile = ids_ref[0], ids_ref[1]
        copies = []
        for k, group in enumerate((near_refs, far_refs)):
            side = core if k == 0 else 1 - core
            for d in range(tiles):
                copies.append(
                    pltpu.make_async_copy(group[d], g_ref.at[side, tile ^ d], sem.at[k * tiles + d])
                )
        for copy in copies:
            copy.start()
        for copy in copies:
            copy.wait()
        at = 0
        for n in range(3):
            piece = plan.skip_piece if n == 2 else plan.piece
            rows = 2 * tiles * piece
            for side in range(2):
                for t in range(tiles):
                    row = (side * tiles + t) * piece
                    sum_ref[row : row + piece] = g_ref[side, t, at : at + piece].astype(F32)
            at += piece
            rate = (rows * plan.ranks) ** (-0.5)
            done = adamw(*(state[3 * n + k][...] for k in range(3)), sum_ref[0:rows], rate)
            for k in range(3):
                new[3 * n + k][...] = done[k]

    return pl.pallas_call(
        kernel,
        in_specs=[SMEM] + [ANY] * (2 * tiles) + [VMEM] * 9,
        out_specs=[VMEM] * 9,
        out_shape=[jax.ShapeDtypeStruct(v.shape, F32) for v in sets],
        scratch_shapes=[
            pltpu.VMEM((2, tiles, plan.chunk, c), BF),
            pltpu.VMEM((plan.shard, c), F32),
            pltpu.SemaphoreType.DMA((2 * tiles,)),
        ],
        compiler_params=params(),
        name="update",
    )(ids, *near, *far, *sets)


def send(v, axis, size, step):
    if axis == "fsdp":
        pairs = [(i, (i + step) % size) for i in range(size)]
    else:
        pairs = [(i, i ^ step) for i in range(size)]
    return lax.ppermute(v, axis, pairs)


def total(*parts):
    acc = parts[0].astype(F32)
    for part in parts[1:]:
        acc = acc + part.astype(F32)
    return acc.astype(BF)


def make_body(sizes):
    tiles, ranks = sizes["tile"], sizes["fsdp"]

    def to_core(v):
        return send(v, "core", 2, 1)

    def to_tile(v, d):
        return send(v, "tile", tiles, d)

    def to_rank(v, d):
        return send(v, "fsdp", ranks, d)

    def per_device(
        inputs,
        cotangent,
        lengths,
        face_table,
        w_first,
        w_second,
        w_skip,
        mom_first,
        sq_first,
        mom_second,
        sq_second,
        mom_skip,
        sq_skip,
    ):
        plan = Plan(sizes, inputs.shape[-1])
        x = jnp.transpose(inputs[0], (1, 2, 3, 0, 4))
        cot = jnp.transpose(cotangent[0], (1, 2, 3, 0, 4))
        table = face_table.T
        ids = jnp.stack([lax.axis_index(n) for n in ("core", "tile", "fsdp")]).astype(jnp.int32)
        low1, half1, low2, low3, half2 = pack(plan, ids, w_first, w_second, w_skip)
        near1 = [to_rank(half1, d) for d in range(1, ranks)]
        near2 = [to_rank(half2, d) for d in range(1, ranks)]
        x, cot, _ = lax.optimization_barrier((x, cot, half1))
        xp, go, dws = enter(lengths, table, x, cot)
        far1 = [to_core(v) for v in near1]
        hp, slope, w1 = first(plan, ids, table, xp, low1, near1, far1)
        hp, near2 = lax.optimization_barrier((hp, near2))
        far2 = [to_core(v) for v in near2]
        output, op, ws, keep, away = second(
            plan, ids, table, hp, slope, xp, go, dws, low2, low3, near2, far2
        )
        came = to_core(away)
        parts = [total(keep[d], came[d]) for d in range(tiles)]
        op, parts = lax.optimization_barrier((op, parts))
        came = [to_tile(parts[d], d) for d in range(1, tiles)]
        grad_inputs = inputs_back(op, w1, ws, go)
        came, grad_inputs = lax.optimization_barrier((came, grad_inputs))
        parts = [total(parts[0][r], *(v[r] for v in came)) for r in range(ranks)]
        came = [to_rank(parts[d], d) for d in range(1, ranks)]
        mine = total(parts[0], *came)
        near = [mine] + [to_tile(mine, d) for d in range(1, tiles)]
        far = [to_core(v) for v in near]
        news = update(
            plan,
            ids,
            near,
            far,
            (
                w_first,
                mom_first,
                sq_first,
                w_second,
                mom_second,
                sq_second,
                w_skip,
                mom_skip,
                sq_skip,
            ),
        )
        output = jnp.transpose(output, (3, 0, 1, 2, 4))[None]
        grad_inputs = jnp.transpose(grad_inputs, (3, 0, 1, 2, 4))[None]
        return (output, grad_inputs, *news)

    return per_device


def solution(mesh):
    pairs = mesh.shape["dp"] // 2
    ranks = mesh.shape["fsdp"]
    fine = Mesh(mesh.devices.reshape(pairs, 2, ranks), ("tile", "core", "fsdp"))
    sizes = {"tile": pairs, "core": 2, "fsdp": ranks}
    every = ("tile", "core", "fsdp")
    fields = P(every, None, None, None, None, None)
    rows = P("fsdp", None)
    return jax.shard_map(
        make_body(sizes),
        mesh=fine,
        in_specs=(fields, fields, P(every), P()) + (rows,) * 9,
        out_specs=(fields, fields) + (rows,) * 9,
        check_vma=False,
    )
```

time: 519 us -> 117 us (0.23); the launches traced: 512 us -> 116 us
  local copies, waits for them, and re-layouts: 163 us -> 6.65 us
  matrix products: 139 us -> 0 us
  other arithmetic: 98.6 us -> 0.63 us
  Pallas kernels: 0 us -> 46.7 us
  blocking collectives: 38.4 us -> 0 us
  starting transfers between devices: 0.42 us -> 31.1 us
  waiting for transfers between devices: 56.7 us -> 29.6 us
  between operations: 15.8 us -> 1.73 us
    dot_general x25 -> x0, matrix products: 139 us -> none  [the longest x2 46 us: conv_apply(): jnp.einsum('pc,tcd->ptd', flat_padded, taps_weight, preferred_element_typ...]
    squeeze x5 -> x0, local copies, waits for them, and re-layouts: 65 us -> none  [the longest x2 62.2 us: conv_back(): moved = jnp.pad(pulled[:, :, :, :, tap_index], widths)]
    pallas_call x0 -> x6, Pallas kernels: none -> 46.7 us  [the longest x1 26.5 us: second(): pl.pallas_call(kernel, in_specs=[SMEM, SMEM, VMEM, ANY, ANY, ANY, VMEM] +...]
    psum x1 -> x0, waiting for transfers between devices: 45.5 us -> none  [per_device(): lax.psum(shards[0].astype(jnp.bfloat16), 'dp').astype(jnp.float32)]
    unnamed x82 -> x32, local copies, waits for them, and re-layouts: 49.7 us -> 6.65 us
    convert_element_type x6 -> x2, other arithmetic: 43.1 us -> 0.43 us  [total(): return acc.astype(BF)]
    add x4 -> x1, other arithmetic: 40.2 us -> 0.12 us  [total(): acc = acc + part.astype(F32)]
    ppermute x0 -> x26, starting transfers between devices: none -> 31.1 us  [send(): return lax.ppermute(v, axis, pairs)]
  transfers between devices with their start and end apart: 6 -> 26, of which waited for: 2 -> 15; matrix products, arithmetic and copies ran while one was open for 45% -> 0% of each run, Pallas kernels for 0% -> 13%
where the time goes in v2:
time: 117 us; the launch traced here: 116 us
  Pallas kernels  46.7 us (40%)
  starting transfers between devices  31.1 us (27%)
  waiting for transfers between devices  29.6 us (25%)
  local copies, waits for them, and re-layouts  6.65 us (6%)
  between operations  1.73 us (1%)
    ppermute x26, starting transfers between devices, send(): return lax.ppermute(v, axis, pairs)  31.1 us
    ppermute x26, waiting for transfers between devices, send(): return lax.ppermute(v, axis, pairs)  29.6 us
    pallas_call x1, Pallas kernels, second(): pl.pallas_call(kernel, in_specs=[SMEM, SMEM, VMEM, ANY, ANY, ANY, VMEM] +...  26.5 us
    pallas_call x1, Pallas kernels, first(): pl.pallas_call(kernel, in_specs=[SMEM, SMEM, VMEM] + [ANY] * (1 + 2 * cou...  7.92 us
    unnamed x32, local copies, waits for them, and re-layouts  6.65 us
    pallas_call x1, Pallas kernels, inputs_back(): pl.pallas_call(inputs_back_kernel, in_specs=[VMEM] * 4, out_specs=ANY, ou...  5.69 us
    pallas_call x1, Pallas kernels, update(): pl.pallas_call(kernel, in_specs=[SMEM] + [ANY] * (2 * tiles) + [VMEM] * 9...  3.99 us
  transfers between devices with their start and end apart: 26, of which 15 were waited for; matrix products, arithmetic and copies ran while one was open for 0% of the time, Pallas kernels for 13%

profile of v2, /device:TPU:0, one launch (start us, length us, event | category | flops | bytes accessed | tf_op | source)
XLA Modules:
  0.0 116.4 jit_solution(1053831710381633841)
XLA Ops:
  0.6 0.1 pad_add_fusion.ids_ref
  0.7 1.1 copy-done.1
  1.8 1.1 copy-done.3
  2.9 0.8 copy-done.11
  3.7 0.6 pack.1
  4.3 5.1 %collective-permute-start.2 = (bf16[288,256]{1,0:T(8,128)(2,1)S(1)}, bf16[288,256]{1,0:T(8,128)(2,1)S(1)}, u32[]{:S(2)}, u32[]{:S(2)}) collective-permute-start(bf16[288,256]{1,0:T(8,128)(2,1)S(1)} %get-tuple-element.51), channel_id=1, source_target_pairs={{0,3},{1,0},{2,1},{3,2},{4,7},{5,4},{6,5},{7,6},{8,11},{9,8},{10,9... | collective-permute-start | bytes 442376 | tf_op jit(solution)/shard_map/ppermute | solution.py:465
  9.4 1.0 collective-permute-start
  10.5 3.3 %collective-permute-done.2.refs_2_ = bf16[288,256]{1,0:T(8,128)(2,1)S(1)} collective-permute-done((bf16[288,256]{1,0:T(8,128)(2,1)S(1)}, bf16[288,256]{1,0:T(8,128)(2,1)S(1)}, u32[]{:S(2)}, u32[]{:S(2)}) %collective-permute-start.2) | collective-permute-done | bytes 147488 | tf_op jit(solution)/shard_map/ppermute | solution.py:465
  13.7 4.3 %collective-permute-start.8 = (bf16[320,256]{1,0:T(8,128)(2,1)S(1)}, bf16[320,256]{1,0:T(8,128)(2,1)S(1)}, u32[]{:S(2)}, u32[]{:S(2)}) collective-permute-start(bf16[320,256]{1,0:T(8,128)(2,1)S(1)} %get-tuple-element.57), channel_id=1, source_target_pairs={{0,3},{1,0},{2,1},{3,2},{4,7},{5,4},{6,5},{7,6},{8,11},{9,8},{10,9... | collective-permute-start | bytes 491528 | tf_op jit(solution)/shard_map/ppermute | solution.py:465
  18.1 4.6 %collective-permute-done.1.refs_1_ = bf16[288,256]{1,0:T(8,128)(2,1)S(1)} collective-permute-done((bf16[288,256]{1,0:T(8,128)(2,1)S(1)}, bf16[288,256]{1,0:T(8,128)(2,1)S(1)}, u32[]{:S(2)}, u32[]{:S(2)}) %collective-permute-start.1) | collective-permute-done | bytes 147488 | tf_op jit(solution)/shard_map/ppermute | solution.py:465
  22.7 0.5 collective-permute-start.3
  23.8 0.0 copy-start.5
  23.9 1.5 %copy-done.5 = bf16[1,8,12,6,6,256]{5,1,4,3,2,0:T(8,128)(2,1)S(1)} copy-done((bf16[1,8,12,6,6,256]{5,1,4,3,2,0:T(8,128)(2,1)S(1)}, bf16[1,8,12,6,6,256]{5,1,4,3,2,0:T(8,128)(2,1)}, u32[]{:S(2)}) %copy-start.5) | copy-done | bytes 1769496
  25.3 1.5 %copy-done.6 = bf16[1,8,12,6,6,256]{5,1,4,3,2,0:T(8,128)(2,1)S(1)} copy-done((bf16[1,8,12,6,6,256]{5,1,4,3,2,0:T(8,128)(2,1)S(1)}, bf16[1,8,12,6,6,256]{5,1,4,3,2,0:T(8,128)(2,1)}, u32[]{:S(2)}) %copy-start.6) | copy-done | bytes 1769496
  26.8 0.7 copy-done.15
  27.5 2.0 %enter.1 = (bf16[12,8,8,8,256]{4,3,2,1,0:T(8,128)(2,1)S(1)}, bf16[12,6,6,8,256]{4,3,2,1,0:T(8,128)(2,1)S(1)}, bf16[256,256]{1,0:T(8,128)(2,1)S(1)}) custom-call(s32[1]{0:T(128)S(6)} %copy.24.lengths_ref, s32[4,12]{1,0:T(4,128)S(1)} %bitcast.37, bf16[12,6,6,8,256]{4,3,2,1,0:T(8,128)(2,1)S(1)} %bitcast.35, bf16[12,6,6,8,256]{4,3,2,1,0:T(8,128)(2,1)S(1)} %bitcast.36), custom_call_target="tpu_custom_call" | custom-call | tf_op jit(solution)/shard_map/enter/pallas_call | solution.py:220
  29.5 7.9 %first.1 = (bf16[12,8,8,8,256]{4,3,2,1,0:T(8,128)(2,1)S(1)}, bf16[12,6,6,8,256]{4,3,2,1,0:T(8,128)(2,1)S(1)}, bf16[2304,256]{1,0:T(8,128)(2,1)S(1)}) custom-call(s32[3]{0:T(128)S(1)} %pad_add_fusion.ids_ref, s32[4,12]{1,0:T(4,128)S(1)} %bitcast.38, bf16[12,8,8,8,256]{4,3,2,1,0:T(8,128)(2,1)S(1)} %get-tuple-element.54.xp_ref.xp_hbm, ...), custom_call_target="tpu_custom_call" | custom-call | tf_op jit(solution)/shard_map/first/pallas_call | solution.py:256
  37.5 0.2 collective-permute-start.9
  37.6 0.4 collective-permute-start.10
  38.0 0.1 collective-permute-start.11
  38.1 0.8 collective-permute-done.9.refs_3_
  38.9 0.2 collective-permute-done.10.refs_4_
  39.1 0.3 collective-permute-done.11.refs_5_
  39.4 26.5 %second.1 = (bf16[12,6,6,8,256]{4,3,2,1,0:T(8,128)(2,1)}, bf16[12,8,8,8,256]{4,3,2,1,0:T(8,128)(2,1)S(1)}, bf16[256,256]{1,0:T(8,128)(2,1)S(1)}, bf16[4,4,152,25...) custom-call(s32[3]{0:T(128)S(1)} %pad_add_fusion.ids_ref, s32[4,12]{1,0:T(4,128)S(1)} %bitcast.39, ...), custom_call_target="tpu_custom_call" | custom-call | tf_op jit(solution)/shard_map/second/pallas_call | solution.py:342
  65.9 0.3 collective-permute-start.12
  66.2 2.7 %collective-permute-done.12 = bf16[4,4,152,256]{3,2,1,0:T(8,128)(2,1)S(1)} collective-permute-done((bf16[4,4,152,256]{3,2,1,0:T(8,128)(2,1)S(1)}, bf16[4,4,152,256]{3,2,1,0:T(8,128)(2,1)S(1)}, u32[]{:S(2)}, u32[]{:S(2)}) %collective-permute-start.12) | collective-permute-done | bytes 1245216 | tf_op jit(solution)/shard_map/ppermute | solution.py:465
  68.9 0.3 fusion.3
  69.3 1.6 %collective-permute-start.13 = (bf16[4,152,256]{2,1,0:T(8,128)(2,1)S(1)}, bf16[4,152,256]{2,1,0:T(8,128)(2,1)S(1)}, u32[]{:S(2)}, u32[]{:S(2)}) collective-permute-start(bf16[4,152,256]{2,1,0:T(8,128)(2,1)S(1)} %get-tuple-element.71), channel_id=1, source_target_pairs={{0,8},{8,0},{16,24},{24,16},{1,9},{9,1},{17,25},{25,17},{2,10},{10... | collective-permute-start | bytes 933896 | tf_op jit(solution)/shard_map/ppermute | solution.py:465
  70.9 1.5 %collective-permute-start.14 = (bf16[4,152,256]{2,1,0:T(8,128)(2,1)S(1)}, bf16[4,152,256]{2,1,0:T(8,128)(2,1)S(1)}, u32[]{:S(2)}, u32[]{:S(2)}) collective-permute-start(bf16[4,152,256]{2,1,0:T(8,128)(2,1)S(1)} %get-tuple-element.72), channel_id=1, source_target_pairs={{0,16},{8,24},{16,0},{24,8},{1,17},{9,25},{17,1},{25,9},{2,18},{10... | collective-permute-start | bytes 933896 | tf_op jit(solution)/shard_map/ppermute | solution.py:465
  72.4 0.5 collective-permute-start.15
  72.9 5.7 %inputs_back.1 = f32[12,6,6,8,256]{4,3,2,1,0:T(8,128)} custom-call(bf16[12,8,8,8,256]{4,3,2,1,0:T(8,128)(2,1)S(1)} %get-tuple-element.74.gp_ref, bf16[2304,256]{1,0:T(8,128)(2,1)S(1)} %get-tuple-element.75.w_ref, bf16[256,256]{1,0:T(8,128)(2,1)S(1)} %get-tuple-element.76.ws_ref, bf16[12,6,6,8,256]{4,3,2,1,0:T(8,128)(2,1)S(1)} %get-tuple-element.60.go_hbm.go_ref), custom_call_target="tpu_custom_call" | custom-call | tf_op jit(solution)/shard_map/inputs_back/pallas_call | solution.py:389
  78.6 0.9 collective-permute-done.13
  79.5 7.2 %collective-permute-done.14 = bf16[4,152,256]{2,1,0:T(8,128)(2,1)S(1)} collective-permute-done((bf16[4,152,256]{2,1,0:T(8,128)(2,1)S(1)}, bf16[4,152,256]{2,1,0:T(8,128)(2,1)S(1)}, u32[]{:S(2)}, u32[]{:S(2)}) %collective-permute-start.14) | collective-permute-done | bytes 311328 | tf_op jit(solution)/shard_map/ppermute | solution.py:465
  86.7 0.1 fusion.8
  86.9 8.1 %collective-permute-start.16 = (bf16[152,256]{1,0:T(8,128)(2,1)S(1)}, bf16[152,256]{1,0:T(8,128)(2,1)S(1)}, u32[]{:S(2)}, u32[]{:S(2)}) collective-permute-start(bf16[152,256]{1,0:T(8,128)(2,1)S(1)} %get-tuple-element.95), channel_id=1, source_target_pairs={{0,1},{1,2},{2,3},{3,0},{4,5},{5,6},{6,7},{7,4},{8,9},{9,10},{10,1... | collective-permute-start | bytes 233480 | tf_op jit(solution)/shard_map/ppermute | solution.py:465
  95.0 3.9 %collective-permute-start.17 = (bf16[152,256]{1,0:T(8,128)(2,1)S(1)}, bf16[152,256]{1,0:T(8,128)(2,1)S(1)}, u32[]{:S(2)}, u32[]{:S(2)}) collective-permute-start(bf16[152,256]{1,0:T(8,128)(2,1)S(1)} %get-tuple-element.97), channel_id=1, source_target_pairs={{0,2},{1,3},{2,0},{3,1},{4,6},{5,7},{6,4},{7,5},{8,10},{9,11},{10,... | collective-permute-start | bytes 233480 | tf_op jit(solution)/shard_map/ppermute | solution.py:465
  98.9 1.1 collective-permute-done.18
  100.0 3.4 %collective-permute-done.17 = bf16[152,256]{1,0:T(8,128)(2,1)S(1)} collective-permute-done((bf16[152,256]{1,0:T(8,128)(2,1)S(1)}, bf16[152,256]{1,0:T(8,128)(2,1)S(1)}, u32[]{:S(2)}, u32[]{:S(2)}) %collective-permute-start.17) | collective-permute-done | bytes 77856 | tf_op jit(solution)/shard_map/ppermute | solution.py:465
  103.4 0.1 fusion.6.refs_0_
  103.5 1.5 %collective-permute-start.21 = (bf16[152,256]{1,0:T(8,128)(2,1)S(1)}, bf16[152,256]{1,0:T(8,128)(2,1)S(1)}, u32[]{:S(2)}, u32[]{:S(2)}) collective-permute-start(bf16[152,256]{1,0:T(8,128)(2,1)S(1)} %fusion.6.refs_0_), channel_id=1, source_target_pairs={{0,24},{8,16},{16,8},{24,0},{1,25},{9,17},{17,9},{25,1},{2,26},{10... | collective-permute-start | bytes 233480 | tf_op jit(solution)/shard_map/ppermute | solution.py:465
  105.0 1.4 %collective-permute-start.20 = (bf16[152,256]{1,0:T(8,128)(2,1)S(1)}, bf16[152,256]{1,0:T(8,128)(2,1)S(1)}, u32[]{:S(2)}, u32[]{:S(2)}) collective-permute-start(bf16[152,256]{1,0:T(8,128)(2,1)S(1)} %fusion.6.refs_0_), channel_id=1, source_target_pairs={{0,16},{8,24},{16,0},{24,8},{1,17},{9,25},{17,1},{25,9},{2,18},{10... | collective-permute-start | bytes 233480 | tf_op jit(solution)/shard_map/ppermute | solution.py:465
  106.4 0.6 collective-permute-start.19
  107.0 1.8 %collective-permute-done.21.refs_3_ = bf16[152,256]{1,0:T(8,128)(2,1)S(1)} collective-permute-done((bf16[152,256]{1,0:T(8,128)(2,1)S(1)}, bf16[152,256]{1,0:T(8,128)(2,1)S(1)}, u32[]{:S(2)}, u32[]{:S(2)}) %collective-permute-start.21) | collective-permute-done | bytes 77856 | tf_op jit(solution)/shard_map/ppermute | solution.py:465
  108.9 0.8 collective-permute-done.20.refs_2_
  109.7 1.2 %collective-permute-done.19.refs_1_ = bf16[152,256]{1,0:T(8,128)(2,1)S(1)} collective-permute-done((bf16[152,256]{1,0:T(8,128)(2,1)S(1)}, bf16[152,256]{1,0:T(8,128)(2,1)S(1)}, u32[]{:S(2)}, u32[]{:S(2)}) %collective-permute-start.19) | collective-permute-done | bytes 77856 | tf_op jit(solution)/shard_map/ppermute | solution.py:465
  110.9 0.1 collective-permute-done.24.refs_6_
  110.9 1.2 %collective-permute-done.23.refs_5_ = bf16[152,256]{1,0:T(8,128)(2,1)S(1)} collective-permute-done((bf16[152,256]{1,0:T(8,128)(2,1)S(1)}, bf16[152,256]{1,0:T(8,128)(2,1)S(1)}, u32[]{:S(2)}, u32[]{:S(2)}) %collective-permute-start.23) | collective-permute-done | bytes 77856 | tf_op jit(solution)/shard_map/ppermute | solution.py:465
  112.2 4.0 %update.1 = (f32[576,256]{1,0:T(8,128)}, f32[576,256]{1,0:T(8,128)}, f32[576,256]{1,0:T(8,128)}, f32[576,256]{1,0:T(8,128)}, f32[576,256]{1,0:T(8,128)}, /*index...) custom-call(s32[3]{0:T(128)S(1)} %pad_add_fusion.ids_ref, ...), custom_call_target="tpu_custom_call" | custom-call | tf_op jit(solution)/shard_map/update/pallas_call | solution.py:445
  (46 shorter events, 0.1 us)
Async XLA Ops:
  0.7 1.1 copy-start.1
  1.8 1.1 copy-start.3
  2.9 0.8 copy-start.11
  4.3 9.4 %collective-permute-start.2 = (bf16[288,256]{1,0:T(8,128)(2,1)S(1)}, bf16[288,256]{1,0:T(8,128)(2,1)S(1)}, u32[]{:S(2)}, u32[]{:S(2)}) collective-permute-start(bf16[288,256]{1,0:T(8,128)(2,1)S(1)} %get-tuple-element.51), channel_id=1, source_target_pairs={{0,3},{1,0},{2,1},{3,2},{4,7},{5,4},{6,5},{7,6},{8,11},{9,8},{10,9... | collective-permute-start | bytes 442376 | tf_op jit(solution)/shard_map/ppermute | solution.py:465
  9.4 13.2 %collective-permute-start.1 = (bf16[288,256]{1,0:T(8,128)(2,1)S(1)}, bf16[288,256]{1,0:T(8,128)(2,1)S(1)}, u32[]{:S(2)}, u32[]{:S(2)}) collective-permute-start(bf16[288,256]{1,0:T(8,128)(2,1)S(1)} %get-tuple-element.51), channel_id=1, source_target_pairs={{0,2},{1,3},{2,0},{3,1},{4,6},{5,7},{6,4},{7,5},{8,10},{9,11},{10,... | collective-permute-start | bytes 442376 | tf_op jit(solution)/shard_map/ppermute | solution.py:465
  9.4 13.2 %collective-permute-start = (bf16[288,256]{1,0:T(8,128)(2,1)S(1)}, bf16[288,256]{1,0:T(8,128)(2,1)S(1)}, u32[]{:S(2)}, u32[]{:S(2)}) collective-permute-start(bf16[288,256]{1,0:T(8,128)(2,1)S(1)} %get-tuple-element.51), channel_id=1, source_target_pairs={{0,1},{1,2},{2,3},{3,0},{4,5},{5,6},{6,7},{7,4},{8,9},{9,10},{10,1... | collective-permute-start | bytes 442376 | tf_op jit(solution)/shard_map/ppermute | solution.py:465
  13.7 9.0 %collective-permute-start.5 = (bf16[288,256]{1,0:T(8,128)(2,1)S(1)}, bf16[288,256]{1,0:T(8,128)(2,1)S(1)}, u32[]{:S(2)}, u32[]{:S(2)}) collective-permute-start(bf16[288,256]{1,0:T(8,128)(2,1)S(1)} %collective-permute-done.2.refs_2_), channel_id=1, source_target_pairs={{0,4},{4,0},{1,5},{5,1},{2,6},{6,2},{3,7},{7,3},{8,12},{12,8},{9,1... | collective-permute-start | bytes 442376 | tf_op jit(solution)/shard_map/ppermute | solution.py:465
  13.7 23.7 %collective-permute-start.8 = (bf16[320,256]{1,0:T(8,128)(2,1)S(1)}, bf16[320,256]{1,0:T(8,128)(2,1)S(1)}, u32[]{:S(2)}, u32[]{:S(2)}) collective-permute-start(bf16[320,256]{1,0:T(8,128)(2,1)S(1)} %get-tuple-element.57), channel_id=1, source_target_pairs={{0,3},{1,0},{2,1},{3,2},{4,7},{5,4},{6,5},{7,6},{8,11},{9,8},{10,9... | collective-permute-start | bytes 491528 | tf_op jit(solution)/shard_map/ppermute | solution.py:465
  18.1 19.4 %collective-permute-start.7 = (bf16[320,256]{1,0:T(8,128)(2,1)S(1)}, bf16[320,256]{1,0:T(8,128)(2,1)S(1)}, u32[]{:S(2)}, u32[]{:S(2)}) collective-permute-start(bf16[320,256]{1,0:T(8,128)(2,1)S(1)} %get-tuple-element.57), channel_id=1, source_target_pairs={{0,2},{1,3},{2,0},{3,1},{4,6},{5,7},{6,4},{7,5},{8,10},{9,11},{10,... | collective-permute-start | bytes 491528 | tf_op jit(solution)/shard_map/ppermute | solution.py:465
  22.7 14.8 %collective-permute-start.6 = (bf16[320,256]{1,0:T(8,128)(2,1)S(1)}, bf16[320,256]{1,0:T(8,128)(2,1)S(1)}, u32[]{:S(2)}, u32[]{:S(2)}) collective-permute-start(bf16[320,256]{1,0:T(8,128)(2,1)S(1)} %get-tuple-element.57), channel_id=1, source_target_pairs={{0,1},{1,2},{2,3},{3,0},{4,5},{5,6},{6,7},{7,4},{8,9},{9,10},{10,1... | collective-permute-start | bytes 491528 | tf_op jit(solution)/shard_map/ppermute | solution.py:465
  22.7 6.8 %collective-permute-start.4 = (bf16[288,256]{1,0:T(8,128)(2,1)S(1)}, bf16[288,256]{1,0:T(8,128)(2,1)S(1)}, u32[]{:S(2)}, u32[]{:S(2)}) collective-permute-start(bf16[288,256]{1,0:T(8,128)(2,1)S(1)} %collective-permute-done.1.refs_1_), channel_id=1, source_target_pairs={{0,4},{4,0},{1,5},{5,1},{2,6},{6,2},{3,7},{7,3},{8,12},{12,8},{9,1... | collective-permute-start | bytes 442376 | tf_op jit(solution)/shard_map/ppermute | solution.py:465
  22.7 6.8 %collective-permute-start.3 = (bf16[288,256]{1,0:T(8,128)(2,1)S(1)}, bf16[288,256]{1,0:T(8,128)(2,1)S(1)}, u32[]{:S(2)}, u32[]{:S(2)}) collective-permute-start(bf16[288,256]{1,0:T(8,128)(2,1)S(1)} %collective-permute-done.refs_0_), channel_id=1, source_target_pairs={{0,4},{4,0},{1,5},{5,1},{2,6},{6,2},{3,7},{7,3},{8,12},{12,8},{9,1... | collective-permute-start | bytes 442376 | tf_op jit(solution)/shard_map/ppermute | solution.py:465
  23.8 1.5 %copy-start.5 = (bf16[1,8,12,6,6,256]{5,1,4,3,2,0:T(8,128)(2,1)S(1)}, bf16[1,8,12,6,6,256]{5,1,4,3,2,0:T(8,128)(2,1)}, u32[]{:S(2)}) copy-start(bf16[1,8,12,6,6,256]{5,1,4,3,2,0:T(8,128)(2,1)} %param.13) | copy-start | bytes 5308420
  25.3 1.5 %copy-start.6 = (bf16[1,8,12,6,6,256]{5,1,4,3,2,0:T(8,128)(2,1)S(1)}, bf16[1,8,12,6,6,256]{5,1,4,3,2,0:T(8,128)(2,1)}, u32[]{:S(2)}) copy-start(bf16[1,8,12,6,6,256]{5,1,4,3,2,0:T(8,128)(2,1)} %param.14) | copy-start | bytes 5308420
  26.8 0.7 copy-start.15
  29.4 8.0 %copy-start = (bf16[12,8,8,8,256]{4,3,2,1,0:T(8,128)(2,1)}, bf16[12,8,8,8,256]{4,3,2,1,0:T(8,128)(2,1)S(1)}, u32[]{:S(2)}) copy-start(bf16[12,8,8,8,256]{4,3,2,1,0:T(8,128)(2,1)S(1)} %get-tuple-element.54.xp_ref.xp_hbm) | copy-start | bytes 9437188
  37.5 1.5 %collective-permute-start.9 = (bf16[320,256]{1,0:T(8,128)(2,1)S(1)}, bf16[320,256]{1,0:T(8,128)(2,1)S(1)}, u32[]{:S(2)}, u32[]{:S(2)}) collective-permute-start(bf16[320,256]{1,0:T(8,128)(2,1)S(1)} %collective-permute-done.6.refs_0_), channel_id=1, source_target_pairs={{0,4},{4,0},{1,5},{5,1},{2,6},{6,2},{3,7},{7,3},{8,12},{12,8},{9,1... | collective-permute-start | bytes 491528 | tf_op jit(solution)/shard_map/ppermute | solution.py:465
  37.6 1.5 %collective-permute-start.10 = (bf16[320,256]{1,0:T(8,128)(2,1)S(1)}, bf16[320,256]{1,0:T(8,128)(2,1)S(1)}, u32[]{:S(2)}, u32[]{:S(2)}) collective-permute-start(bf16[320,256]{1,0:T(8,128)(2,1)S(1)} %collective-permute-done.7.refs_1_), channel_id=1, source_target_pairs={{0,4},{4,0},{1,5},{5,1},{2,6},{6,2},{3,7},{7,3},{8,12},{12,8},{9,1... | collective-permute-start | bytes 491528 | tf_op jit(solution)/shard_map/ppermute | solution.py:465
  38.0 1.4 %collective-permute-start.11 = (bf16[320,256]{1,0:T(8,128)(2,1)S(1)}, bf16[320,256]{1,0:T(8,128)(2,1)S(1)}, u32[]{:S(2)}, u32[]{:S(2)}) collective-permute-start(bf16[320,256]{1,0:T(8,128)(2,1)S(1)} %collective-permute-done.8.refs_2_), channel_id=1, source_target_pairs={{0,4},{4,0},{1,5},{5,1},{2,6},{6,2},{3,7},{7,3},{8,12},{12,8},{9,1... | collective-permute-start | bytes 491528 | tf_op jit(solution)/shard_map/ppermute | solution.py:465
  65.9 3.0 %collective-permute-start.12 = (bf16[4,4,152,256]{3,2,1,0:T(8,128)(2,1)S(1)}, bf16[4,4,152,256]{3,2,1,0:T(8,128)(2,1)S(1)}, u32[]{:S(2)}, u32[]{:S(2)}) collective-permute-start(bf16[4,4,152,256]{3,2,1,0:T(8,128)(2,1)S(1)} %get-tuple-element.70), channel_id=1, source_target_pairs={{0,4},{4,0},{1,5},{5,1},{2,6},{6,2},{3,7},{7,3},{8,12},{12,8},{9,1... | collective-permute-start | bytes 3735560 | tf_op jit(solution)/shard_map/ppermute | solution.py:465
  69.3 10.3 %collective-permute-start.13 = (bf16[4,152,256]{2,1,0:T(8,128)(2,1)S(1)}, bf16[4,152,256]{2,1,0:T(8,128)(2,1)S(1)}, u32[]{:S(2)}, u32[]{:S(2)}) collective-permute-start(bf16[4,152,256]{2,1,0:T(8,128)(2,1)S(1)} %get-tuple-element.71), channel_id=1, source_target_pairs={{0,8},{8,0},{16,24},{24,16},{1,9},{9,1},{17,25},{25,17},{2,10},{10... | collective-permute-start | bytes 933896 | tf_op jit(solution)/shard_map/ppermute | solution.py:465
  70.9 15.9 %collective-permute-start.14 = (bf16[4,152,256]{2,1,0:T(8,128)(2,1)S(1)}, bf16[4,152,256]{2,1,0:T(8,128)(2,1)S(1)}, u32[]{:S(2)}, u32[]{:S(2)}) collective-permute-start(bf16[4,152,256]{2,1,0:T(8,128)(2,1)S(1)} %get-tuple-element.72), channel_id=1, source_target_pairs={{0,16},{8,24},{16,0},{24,8},{1,17},{9,25},{17,1},{25,9},{2,18},{10... | collective-permute-start | bytes 933896 | tf_op jit(solution)/shard_map/ppermute | solution.py:465
  72.4 14.4 %collective-permute-start.15 = (bf16[4,152,256]{2,1,0:T(8,128)(2,1)S(1)}, bf16[4,152,256]{2,1,0:T(8,128)(2,1)S(1)}, u32[]{:S(2)}, u32[]{:S(2)}) collective-permute-start(bf16[4,152,256]{2,1,0:T(8,128)(2,1)S(1)} %get-tuple-element.73), channel_id=1, source_target_pairs={{0,24},{8,16},{16,8},{24,0},{1,25},{9,17},{17,9},{25,1},{2,26},{10... | collective-permute-start | bytes 933896 | tf_op jit(solution)/shard_map/ppermute | solution.py:465
  72.8 39.3 %copy-start.8 = (f32[576,256]{1,0:T(8,128)S(1)}, f32[576,256]{1,0:T(8,128)}, u32[]{:S(2)}) copy-start(f32[576,256]{1,0:T(8,128)} %refs_10_.1) | copy-start | bytes 1769476
  72.8 39.3 %copy-start.9 = (f32[576,256]{1,0:T(8,128)S(1)}, f32[576,256]{1,0:T(8,128)}, u32[]{:S(2)}) copy-start(f32[576,256]{1,0:T(8,128)} %refs_12_.1) | copy-start | bytes 1769476
  72.8 39.3 %copy-start.10 = (f32[576,256]{1,0:T(8,128)S(1)}, f32[576,256]{1,0:T(8,128)}, u32[]{:S(2)}) copy-start(f32[576,256]{1,0:T(8,128)} %refs_13_.1) | copy-start | bytes 1769476
  72.8 39.3 %copy-start.12 = (f32[64,256]{1,0:T(8,128)S(1)}, f32[64,256]{1,0:T(8,128)}, u32[]{:S(2)}) copy-start(f32[64,256]{1,0:T(8,128)} %refs_14_.1) | copy-start | bytes 196612
  72.8 39.3 %copy-start.13 = (f32[64,256]{1,0:T(8,128)S(1)}, f32[64,256]{1,0:T(8,128)}, u32[]{:S(2)}) copy-start(f32[64,256]{1,0:T(8,128)} %refs_15_.1) | copy-start | bytes 196612
  72.9 39.3 %copy-start.14 = (f32[64,256]{1,0:T(8,128)S(1)}, f32[64,256]{1,0:T(8,128)}, u32[]{:S(2)}) copy-start(f32[64,256]{1,0:T(8,128)} %refs_16_.1) | copy-start | bytes 196612
  78.6 33.6 %copy-start.2 = (f32[576,256]{1,0:T(8,128)S(1)}, f32[576,256]{1,0:T(8,128)}, u32[]{:S(2)}) copy-start(f32[576,256]{1,0:T(8,128)} %refs_8_.1) | copy-start | bytes 1769476
  78.6 33.6 %copy-start.4 = (f32[576,256]{1,0:T(8,128)S(1)}, f32[576,256]{1,0:T(8,128)}, u32[]{:S(2)}) copy-start(f32[576,256]{1,0:T(8,128)} %refs_11_.1) | copy-start | bytes 1769476
  78.6 33.6 %copy-start.7 = (f32[576,256]{1,0:T(8,128)S(1)}, f32[576,256]{1,0:T(8,128)}, u32[]{:S(2)}) copy-start(f32[576,256]{1,0:T(8,128)} %refs_9_.1) | copy-start | bytes 1769476
  86.9 12.1 %collective-permute-start.16 = (bf16[152,256]{1,0:T(8,128)(2,1)S(1)}, bf16[152,256]{1,0:T(8,128)(2,1)S(1)}, u32[]{:S(2)}, u32[]{:S(2)}) collective-permute-start(bf16[152,256]{1,0:T(8,128)(2,1)S(1)} %get-tuple-element.95), channel_id=1, source_target_pairs={{0,1},{1,2},{2,3},{3,0},{4,5},{5,6},{6,7},{7,4},{8,9},{9,10},{10,1... | collective-permute-start | bytes 233480 | tf_op jit(solution)/shard_map/ppermute | solution.py:465
  95.0 5.0 %collective-permute-start.18 = (bf16[152,256]{1,0:T(8,128)(2,1)S(1)}, bf16[152,256]{1,0:T(8,128)(2,1)S(1)}, u32[]{:S(2)}, u32[]{:S(2)}) collective-permute-start(bf16[152,256]{1,0:T(8,128)(2,1)S(1)} %get-tuple-element.96), channel_id=1, source_target_pairs={{0,3},{1,0},{2,1},{3,2},{4,7},{5,4},{6,5},{7,6},{8,11},{9,8},{10,9... | collective-permute-start | bytes 233480 | tf_op jit(solution)/shard_map/ppermute | solution.py:465
  95.0 8.4 %collective-permute-start.17 = (bf16[152,256]{1,0:T(8,128)(2,1)S(1)}, bf16[152,256]{1,0:T(8,128)(2,1)S(1)}, u32[]{:S(2)}, u32[]{:S(2)}) collective-permute-start(bf16[152,256]{1,0:T(8,128)(2,1)S(1)} %get-tuple-element.97), channel_id=1, source_target_pairs={{0,2},{1,3},{2,0},{3,1},{4,6},{5,7},{6,4},{7,5},{8,10},{9,11},{10,... | collective-permute-start | bytes 233480 | tf_op jit(solution)/shard_map/ppermute | solution.py:465
  103.5 5.4 %collective-permute-start.21 = (bf16[152,256]{1,0:T(8,128)(2,1)S(1)}, bf16[152,256]{1,0:T(8,128)(2,1)S(1)}, u32[]{:S(2)}, u32[]{:S(2)}) collective-permute-start(bf16[152,256]{1,0:T(8,128)(2,1)S(1)} %fusion.6.refs_0_), channel_id=1, source_target_pairs={{0,24},{8,16},{16,8},{24,0},{1,25},{9,17},{17,9},{25,1},{2,26},{10... | collective-permute-start | bytes 233480 | tf_op jit(solution)/shard_map/ppermute | solution.py:465
  105.0 4.7 %collective-permute-start.20 = (bf16[152,256]{1,0:T(8,128)(2,1)S(1)}, bf16[152,256]{1,0:T(8,128)(2,1)S(1)}, u32[]{:S(2)}, u32[]{:S(2)}) collective-permute-start(bf16[152,256]{1,0:T(8,128)(2,1)S(1)} %fusion.6.refs_0_), channel_id=1, source_target_pairs={{0,16},{8,24},{16,0},{24,8},{1,17},{9,25},{17,1},{25,9},{2,18},{10... | collective-permute-start | bytes 233480 | tf_op jit(solution)/shard_map/ppermute | solution.py:465
  106.4 4.4 %collective-permute-start.19 = (bf16[152,256]{1,0:T(8,128)(2,1)S(1)}, bf16[152,256]{1,0:T(8,128)(2,1)S(1)}, u32[]{:S(2)}, u32[]{:S(2)}) collective-permute-start(bf16[152,256]{1,0:T(8,128)(2,1)S(1)} %fusion.6.refs_0_), channel_id=1, source_target_pairs={{0,8},{8,0},{16,24},{24,16},{1,9},{9,1},{17,25},{25,17},{2,10},{10... | collective-permute-start | bytes 233480 | tf_op jit(solution)/shard_map/ppermute | solution.py:465
  107.0 3.8 %collective-permute-start.22 = (bf16[152,256]{1,0:T(8,128)(2,1)S(1)}, bf16[152,256]{1,0:T(8,128)(2,1)S(1)}, u32[]{:S(2)}, u32[]{:S(2)}) collective-permute-start(bf16[152,256]{1,0:T(8,128)(2,1)S(1)} %fusion.6.refs_0_), channel_id=1, source_target_pairs={{0,4},{4,0},{1,5},{5,1},{2,6},{6,2},{3,7},{7,3},{8,12},{12,8},{9,1... | collective-permute-start | bytes 233480 | tf_op jit(solution)/shard_map/ppermute | solution.py:465
  108.8 2.0 %collective-permute-start.25 = (bf16[152,256]{1,0:T(8,128)(2,1)S(1)}, bf16[152,256]{1,0:T(8,128)(2,1)S(1)}, u32[]{:S(2)}, u32[]{:S(2)}) collective-permute-start(bf16[152,256]{1,0:T(8,128)(2,1)S(1)} %collective-permute-done.21.refs_3_), channel_id=1, source_target_pairs={{0,4},{4,0},{1,5},{5,1},{2,6},{6,2},{3,7},{7,3},{8,12},{12,8},{9,1... | collective-permute-start | bytes 233480 | tf_op jit(solution)/shard_map/ppermute | solution.py:465
  109.7 1.3 %collective-permute-start.24 = (bf16[152,256]{1,0:T(8,128)(2,1)S(1)}, bf16[152,256]{1,0:T(8,128)(2,1)S(1)}, u32[]{:S(2)}, u32[]{:S(2)}) collective-permute-start(bf16[152,256]{1,0:T(8,128)(2,1)S(1)} %collective-permute-done.20.refs_2_), channel_id=1, source_target_pairs={{0,4},{4,0},{1,5},{5,1},{2,6},{6,2},{3,7},{7,3},{8,12},{12,8},{9,1... | collective-permute-start | bytes 233480 | tf_op jit(solution)/shard_map/ppermute | solution.py:465
  110.8 1.3 %collective-permute-start.23 = (bf16[152,256]{1,0:T(8,128)(2,1)S(1)}, bf16[152,256]{1,0:T(8,128)(2,1)S(1)}, u32[]{:S(2)}, u32[]{:S(2)}) collective-permute-start(bf16[152,256]{1,0:T(8,128)(2,1)S(1)} %collective-permute-done.19.refs_1_), channel_id=1, source_target_pairs={{0,4},{4,0},{1,5},{5,1},{2,6},{6,2},{3,7},{7,3},{8,12},{12,8},{9,1... | collective-permute-start | bytes 233480 | tf_op jit(solution)/shard_map/ppermute | solution.py:465

commit v3 on v2

v3 whole, which is shorter than its diff:
```python
import functools

import jax
import jax.numpy as jnp
from jax import lax
from jax.experimental import pallas as pl
from jax.experimental.pallas import tpu as pltpu
from jax.sharding import Mesh
from jax.sharding import PartitionSpec as P

STEP_COUNT = 10
BF = jnp.bfloat16
F32 = jnp.float32
FS = 6
ROLL = 8
FACES = 12
GELU_K = 0.7978845608028654
GELU_C = 0.044715
VMEM_LIMIT = 26 * 2**20


ANY = pl.BlockSpec(memory_space=pl.ANY)
HBM = pl.BlockSpec(memory_space=pltpu.HBM)
VMEM = pl.BlockSpec(memory_space=pltpu.VMEM)
SMEM = pl.BlockSpec(memory_space=pltpu.SMEM)


def field(c, dtype=BF):
    return jax.ShapeDtypeStruct((FACES, FS, FS, ROLL, c), dtype)


def padded(c):
    return (FACES, FS + 2, FS + 2, ROLL, c)


def inner(ref):
    return ref.at[:, 1 : FS + 1, 1 : FS + 1]


def in_hbm(v):
    return pltpu.with_memory_space_constraint(v, pltpu.HBM)


def params():
    return pltpu.CompilerParams(vmem_limit_bytes=VMEM_LIMIT)


def cost(gflop, mbyte):
    return pl.CostEstimate(flops=int(gflop * 1e9), bytes_accessed=int(mbyte * 1e6), transcendentals=0)


def gelu_both(v):
    a = (GELU_K * GELU_C) * (v * v) + GELU_K
    half = 0.5 * jnp.tanh(v * a) + 0.5
    value = v * half
    return value, half + (value * (1.0 - half)) * (6.0 * a - 4.0 * GELU_K)


def window(p_ref, face, a, b):
    return p_ref[face, a : a + FS, b : b + FS].reshape(FS * FS * ROLL, p_ref.shape[-1])


def conv(p_ref, w_ref, face):
    c = w_ref.shape[1]
    acc = None
    for a in range(3):
        for b in range(3):
            t = 3 * a + b
            part = jnp.dot(
                window(p_ref, face, a, b), w_ref[t * c : (t + 1) * c], preferred_element_type=F32
            )
            acc = part if acc is None else acc + part
    return acc


def dot_back(v, w):
    return lax.dot_general(v, w, (((1,), (1,)), ((), ())), preferred_element_type=F32)


def conv_back(g_ref, w_ref, face):
    c = w_ref.shape[1]
    acc = None
    for a in range(3):
        for b in range(3):
            t = 3 * a + b
            part = dot_back(window(g_ref, face, 2 - a, 2 - b), w_ref[t * c : (t + 1) * c])
            acc = part if acc is None else acc + part
    return acc


def outer(p, g):
    c = p.shape[-1]
    return lax.dot_general(
        p.reshape(-1, c), g.reshape(-1, c), (((0,), (0,)), ((), ())), preferred_element_type=F32
    )


def zero_corners(p_ref):
    zero = jnp.zeros((FACES, 1, 1, ROLL, p_ref.shape[-1]), p_ref.dtype)
    for i in (0, FS + 1):
        for j in (0, FS + 1):
            p_ref[:, i : i + 1, j : j + 1] = zero


def neighbour(ids_ref, side, face):
    return ids_ref[4 + side * FACES + face]


def fill_halo(ids_ref, p_ref):
    for face in range(FACES):
        p_ref[face, 0, 1 : FS + 1] = p_ref[neighbour(ids_ref, 0, face), FS, 1 : FS + 1]
        p_ref[face, 1 : FS + 1, FS + 1] = p_ref[neighbour(ids_ref, 1, face), 1 : FS + 1, 1]
        p_ref[face, FS + 1, 1 : FS + 1] = p_ref[neighbour(ids_ref, 2, face), 1, 1 : FS + 1]
        p_ref[face, 1 : FS + 1, 0] = p_ref[neighbour(ids_ref, 3, face), 1 : FS + 1, FS]
    zero_corners(p_ref)


def add_edges(e_ref, ids_ref, face, v):
    for side, part in enumerate((v[0], v[:, FS - 1], v[FS - 1], v[:, 0])):
        to = neighbour(ids_ref, side, face)
        e_ref[to, side] = e_ref[to, side] + part


def fill_halo_back(e_ref, p_ref):
    for face in range(FACES):
        p_ref[face, FS + 1, 1 : FS + 1] = e_ref[face, 0].astype(p_ref.dtype)
        p_ref[face, 1 : FS + 1, 0] = e_ref[face, 1].astype(p_ref.dtype)
        p_ref[face, 0, 1 : FS + 1] = e_ref[face, 2].astype(p_ref.dtype)
        p_ref[face, 1 : FS + 1, FS + 1] = e_ref[face, 3].astype(p_ref.dtype)
    zero_corners(p_ref)


def edge_sums(c):
    return pltpu.VMEM((FACES, 4, FS, ROLL, c), F32)


class Plan:
    def __init__(self, sizes, channels):
        self.tiles, self.ranks = sizes["tile"], sizes["fsdp"]
        self.c = channels
        self.conv = 9 * channels
        self.shard = self.conv // self.ranks
        self.skip_shard = channels // self.ranks
        self.piece = self.shard // (2 * self.tiles)
        self.skip_piece = self.skip_shard // (2 * self.tiles)
        self.late = self.piece + self.skip_piece
        self.chunk = self.piece + self.late
        self.split = self.piece % 8 == 0 and self.skip_piece % 8 == 0
        if self.split:
            self.sent = self.piece, self.piece, self.skip_piece
        else:
            self.sent = self.shard // 2, self.shard // 2, self.skip_shard // 2


def place_rows(plan, ids_ref, dst_ref, value, first_row, piece, offset):
    core, tile, rank = ids_ref[0], ids_ref[1], ids_ref[2]
    end = first_row + value.shape[0]
    row = first_row
    while row < end:
        number = row // piece
        stop = min(end, (number + 1) * piece)
        to_tile = number % plan.tiles
        to_core = number // plan.tiles % 2
        to_rank = number // (2 * plan.tiles)
        at = offset + row - number * piece
        dst_ref[
            to_core ^ core,
            to_tile ^ tile,
            (to_rank + plan.ranks - rank) % plan.ranks,
            at : at + stop - row,
        ] = value[row - first_row : stop - first_row]
        row = stop


def weight_grad(plan, ids_ref, p_ref, g, dst_ref):
    c = p_ref.shape[-1]
    for a in range(3):
        for b in range(3):
            part = outer(p_ref[:, a : a + FS, b : b + FS], g).astype(BF)
            place_rows(plan, ids_ref, dst_ref, part, (3 * a + b) * c, plan.piece, 0)


def pack(plan, ids, one, two, skip):
    c = plan.c
    sizes = plan.sent

    def kernel(ids_ref, one_hbm, two_hbm, skip_hbm, one_ref, two_ref, rows_ref, sem):
        loads = []
        at = 0
        for k, (hbm, rows) in enumerate(zip((one_hbm, two_hbm, skip_hbm), sizes)):
            start = ids_ref[0] * (hbm.shape[0] // 2)
            if plan.split:
                start = start + ids_ref[1] * rows
            source = hbm.at[pl.ds(pl.multiple_of(start, 8), rows)]
            loads.append(pltpu.make_async_copy(source, rows_ref.at[pl.ds(at, rows)], sem.at[k]))
            at += rows
        for load in loads:
            load.start()
        for load in loads:
            load.wait()
        one_ref[...] = rows_ref[: sizes[0]].astype(BF)
        two_ref[...] = rows_ref[sizes[0] :].astype(BF)

    return pl.pallas_call(
        kernel,
        in_specs=[SMEM, HBM, HBM, HBM],
        out_specs=[VMEM] * 2,
        out_shape=[jax.ShapeDtypeStruct((v, c), BF) for v in (sizes[0], sizes[1] + sizes[2])],
        scratch_shapes=[pltpu.VMEM((sum(sizes), c), F32), pltpu.SemaphoreType.DMA((3,))],
        compiler_params=params(),
        cost_estimate=cost(0, 0.3),
        name="pack",
    )(ids, in_hbm(one), in_hbm(two), in_hbm(skip))


def join_rows(plan, ids_ref, low_ref, pieces, w_ref, rows):
    rank = ids_ref[2]
    w_ref[pl.ds(pl.multiple_of(rank * rows, 8), rows)] = low_ref[...]
    for ref, index, d, row in pieces:
        start = (rank + plan.ranks - d) % plan.ranks * rows + row
        part = ref[index]
        w_ref[pl.ds(pl.multiple_of(start, 8), part.shape[0])] = part


def received(plan, ids_ref, near_refs, far_refs, at, rows, shard):
    core, tile = ids_ref[0], ids_ref[1]
    pieces = []
    for side, group in ((core, near_refs), (1 - core, far_refs)):
        for e, ref in enumerate(group):
            row = side * (shard // 2)
            if plan.split:
                row = row + (tile ^ e) * rows
            pieces += [(ref, (d - 1, pl.ds(at, rows)), d, row) for d in range(1, plan.ranks)]
    return pieces


def enter(plan, ids, x, cot, weights, after):
    c = plan.c

    def kernel(ids_ref, x_hbm, cot_hbm, *refs):
        refs = refs[:3] + refs[3 + len(after) :]
        weights_hbm, xp_ref, go_ref, dw_ref = refs[:3], *refs[3:6]
        low_refs, cot_ref, weight_refs, sem = refs[6:9], refs[9], refs[10:13], refs[13]
        load_x = pltpu.make_async_copy(x_hbm, inner(xp_ref), sem.at[FACES])
        load_x.start()
        loads = []
        for face in range(FACES):
            loads.append(pltpu.make_async_copy(cot_hbm.at[face], cot_ref.at[face], sem.at[face]))
            loads[-1].start()
        low_loads = []
        for k in range(3):
            low_loads.append(
                pltpu.make_async_copy(weights_hbm[k], weight_refs[k], sem.at[FACES + 1 + k])
            )
            low_loads[-1].start()
        live = lax.broadcasted_iota(jnp.int32, (FS, FS, ROLL, c), 2) < ids_ref[3]
        for face in range(FACES):
            loads[face].wait()
            go_ref[face] = jnp.where(live, cot_ref[face].astype(F32), 0.0).astype(BF)
        load_x.wait()
        fill_halo(ids_ref, xp_ref)
        dw_ref[...] = outer(xp_ref[:, 1 : FS + 1, 1 : FS + 1], go_ref[...]).astype(dw_ref.dtype)
        for k in range(3):
            low_loads[k].wait()
            low_refs[k][...] = weight_refs[k][...].astype(BF)

    return pl.pallas_call(
        kernel,
        in_specs=[SMEM] + [HBM] * 5 + [VMEM] * len(after),
        out_specs=[VMEM] * 6,
        out_shape=[
            jax.ShapeDtypeStruct(padded(c), BF),
            field(c),
            jax.ShapeDtypeStruct((c, c), BF),
            *(jax.ShapeDtypeStruct(v.shape, BF) for v in weights),
        ],
        scratch_shapes=[
            pltpu.VMEM(field(c).shape, BF),
            *(pltpu.VMEM(v.shape, F32) for v in weights),
            pltpu.SemaphoreType.DMA((FACES + 4,)),
        ],
        compiler_params=params(),
        cost_estimate=cost(0.6, 9),
        name="enter",
    )(ids, in_hbm(x), in_hbm(cot), *(in_hbm(v) for v in weights), *after)


def first(plan, ids, xp, low, near, far):
    c = plan.c
    count = len(near)

    def kernel(ids_ref, xp_ref, low_ref, *refs):
        near_refs, far_refs = refs[:count], refs[count : 2 * count]
        hp_ref, slope_ref, w_ref = refs[2 * count :]
        pieces = received(plan, ids_ref, near_refs, far_refs, 0, plan.sent[0], plan.shard)
        join_rows(plan, ids_ref, low_ref, pieces, w_ref, plan.shard)
        for face in range(FACES):
            hidden, slope = gelu_both(conv(xp_ref, w_ref, face))
            hp_ref[face, 1 : FS + 1, 1 : FS + 1] = hidden.astype(BF).reshape(FS, FS, ROLL, c)
            slope_ref[face] = slope.astype(BF).reshape(FS, FS, ROLL, c)
        fill_halo(ids_ref, hp_ref)

    return pl.pallas_call(
        kernel,
        in_specs=[SMEM] + [VMEM] * (2 + 2 * count),
        out_specs=[VMEM] * 3,
        out_shape=[
            jax.ShapeDtypeStruct(padded(c), BF),
            field(c),
            jax.ShapeDtypeStruct((plan.conv, c), BF),
        ],
        compiler_params=params(),
        cost_estimate=cost(4.1, 12),
        name="first",
    )(ids, xp, low, *near, *far)


def second(plan, ids, hp, xp, go, dws, low, low_skip, near, far):
    c = plan.c
    count = len(near)

    def kernel(ids_ref, hp_ref, xp_ref, go_ref, dws_ref, low_ref, lows_ref, *refs):
        near_refs, far_refs = refs[:count], refs[count : 2 * count]
        out_hbm, gp_ref, w_ref, ws_ref, keep_ref, send_ref = refs[2 * count : 2 * count + 6]
        out_ref, e_ref, dw_ref, sem_out = refs[2 * count + 6 :]
        pieces = received(plan, ids_ref, near_refs, far_refs, 0, plan.sent[1], plan.shard)
        join_rows(plan, ids_ref, low_ref, pieces, w_ref, plan.shard)
        pieces = received(plan, ids_ref, near_refs, far_refs, *plan.sent[1:], plan.skip_shard)
        join_rows(plan, ids_ref, lows_ref, pieces, ws_ref, plan.skip_shard)
        e_ref[...] = jnp.zeros_like(e_ref)
        place_rows(plan, ids_ref, dw_ref, dws_ref[...], 0, plan.skip_piece, plan.piece)
        for face in range(FACES):
            value, slope = gelu_both(conv(hp_ref, w_ref, face))
            value = value + jnp.dot(
                xp_ref[face, 1 : FS + 1, 1 : FS + 1].reshape(-1, c),
                ws_ref[...],
                preferred_element_type=F32,
            )
            out_ref[face] = value.astype(BF).reshape(FS, FS, ROLL, c)
            low_grad = (go_ref[face].astype(F32) * slope.reshape(FS, FS, ROLL, c)).astype(BF)
            gp_ref[face, 1 : FS + 1, 1 : FS + 1] = low_grad
            add_edges(e_ref, ids_ref, face, low_grad.astype(F32))
        store = pltpu.make_async_copy(out_ref, out_hbm, sem_out)
        store.start()
        weight_grad(plan, ids_ref, hp_ref, gp_ref[:, 1 : FS + 1, 1 : FS + 1], dw_ref)
        keep_ref[...] = dw_ref[0]
        send_ref[...] = dw_ref[1]
        fill_halo_back(e_ref, gp_ref)
        store.wait()

    sums = jax.ShapeDtypeStruct((plan.tiles, plan.ranks, plan.late, c), BF)
    return pl.pallas_call(
        kernel,
        in_specs=[SMEM] + [VMEM] * (6 + 2 * count),
        out_specs=[HBM] + [VMEM] * 5,
        out_shape=[
            field(c),
            jax.ShapeDtypeStruct(padded(c), BF),
            jax.ShapeDtypeStruct((plan.conv, c), BF),
            jax.ShapeDtypeStruct((c, c), BF),
            sums,
            sums,
        ],
        scratch_shapes=[
            pltpu.VMEM(field(c).shape, BF),
            edge_sums(c),
            pltpu.VMEM((2,) + sums.shape, BF),
            pltpu.SemaphoreType.DMA,
        ],
        compiler_params=params(),
        cost_estimate=cost(9, 16),
        name="second",
    )(ids, hp, xp, go, dws, low, low_skip, *near, *far)


def hidden_back_kernel(ids_ref, gp_ref, w_ref, slope_ref, op_ref, e_ref):
    c = w_ref.shape[1]
    e_ref[...] = jnp.zeros_like(e_ref)
    for face in range(FACES):
        grad = conv_back(gp_ref, w_ref, face).reshape(FS, FS, ROLL, c)
        low_grad = (grad * slope_ref[face].astype(F32)).astype(BF)
        op_ref[face, 1 : FS + 1, 1 : FS + 1] = low_grad
        add_edges(e_ref, ids_ref, face, low_grad.astype(F32))
    fill_halo_back(e_ref, op_ref)


def hidden_back(ids, gp, w, slope):
    c = w.shape[1]
    return pl.pallas_call(
        hidden_back_kernel,
        in_specs=[SMEM] + [VMEM] * 3,
        out_specs=VMEM,
        out_shape=jax.ShapeDtypeStruct(padded(c), BF),
        scratch_shapes=[edge_sums(c)],
        compiler_params=params(),
        cost_estimate=cost(4.1, 9),
        name="hidden_back",
    )(ids, gp, w, slope)


def first_grad(plan, ids, xp, op):
    def kernel(ids_ref, xp_ref, op_ref, keep_ref, send_ref, dw_ref):
        weight_grad(plan, ids_ref, xp_ref, op_ref[:, 1 : FS + 1, 1 : FS + 1], dw_ref)
        keep_ref[...] = dw_ref[0]
        send_ref[...] = dw_ref[1]

    sums = jax.ShapeDtypeStruct((plan.tiles, plan.ranks, plan.piece, plan.c), BF)
    return pl.pallas_call(
        kernel,
        in_specs=[SMEM, VMEM, VMEM],
        out_specs=[VMEM] * 2,
        out_shape=[sums, sums],
        scratch_shapes=[pltpu.VMEM((2,) + sums.shape, BF)],
        compiler_params=params(),
        cost_estimate=cost(4.1, 9),
        name="first_grad",
    )(ids, xp, op)


def tile_sums(plan, early, late):
    tiles, ranks, piece = plan.tiles, plan.ranks, plan.piece

    def kernel(*refs):
        for r in range(ranks):
            to = refs[2 * tiles + r]
            for at, group in ((0, refs[:tiles]), (piece, refs[tiles : 2 * tiles])):
                acc = group[0][r].astype(F32)
                for ref in group[1:]:
                    acc = acc + ref[r].astype(F32)
                to[at : at + acc.shape[0]] = acc.astype(BF)

    return pl.pallas_call(
        kernel,
        in_specs=[VMEM] * (2 * tiles),
        out_specs=[VMEM] * ranks,
        out_shape=[jax.ShapeDtypeStruct((plan.chunk, plan.c), BF)] * ranks,
        compiler_params=params(),
        cost_estimate=cost(0, 6),
        name="tile_sums",
    )(*early, *late)


def inputs_back_kernel(gp_ref, w_ref, ws_ref, go_ref, out_hbm, out_ref, sem):
    c = w_ref.shape[1]
    stores = []
    for face in range(FACES):
        grad = conv_back(gp_ref, w_ref, face)
        grad = grad + dot_back(go_ref[face].reshape(-1, c), ws_ref[...])
        out_ref[face] = grad.reshape(FS, FS, ROLL, c)
        stores.append(pltpu.make_async_copy(out_ref.at[face], out_hbm.at[face], sem.at[face]))
        stores[-1].start()
    for store in stores:
        store.wait()


def inputs_back(gp, w, ws, go):
    c = w.shape[1]
    return pl.pallas_call(
        inputs_back_kernel,
        in_specs=[VMEM] * 4,
        out_specs=ANY,
        out_shape=field(c, F32),
        scratch_shapes=[pltpu.VMEM(field(c).shape, F32), pltpu.SemaphoreType.DMA((FACES,))],
        compiler_params=params(),
        cost_estimate=cost(4.6, 10),
        name="inputs_back",
    )(gp, w, ws, go)


def adamw(weight, moment, square, grad, rate):
    moment_new = 0.9 * moment + 0.1 * grad
    square_new = 0.999 * square + 0.001 * grad * grad
    fix_one = 1.0 - 0.9**STEP_COUNT
    fix_two = 1.0 - 0.999**STEP_COUNT
    weight_new = weight - rate * (
        moment_new / fix_one / (jnp.sqrt(square_new / fix_two) + 1e-08) + 0.01 * weight
    )
    return (weight_new, moment_new, square_new)


UPDATE_STEPS = 4


def update(plan, ids, near, far, sets):
    c, tiles = plan.c, plan.tiles

    def kernel(ids_ref, *refs):
        groups, state, new, sum_ref = refs[:2], refs[2:11], refs[11:20], refs[20]
        done_refs, sem = refs[21:30], refs[30]
        core, tile = ids_ref[0], ids_ref[1]
        at = 0
        stores = []
        for n in range(3):
            piece = plan.skip_piece if n == 2 else plan.piece
            rows = 2 * tiles * piece
            for k, group in enumerate(groups):
                side = core if k == 0 else 1 - core
                for d in range(tiles):
                    part = group[d, at : at + piece].astype(F32)
                    if piece % 8:
                        for t in range(2 * tiles):

                            def put(part=part, t=t, piece=piece):
                                sum_ref[t * piece : (t + 1) * piece] = part

                            pl.when(side * tiles + (tile ^ d) == t)(put)
                    else:
                        start = pl.multiple_of((side * tiles + (tile ^ d)) * piece, 8)
                        sum_ref[pl.ds(start, piece)] = part
            at += piece
            rate = (rows * plan.ranks) ** (-0.5)
            step = rows // UPDATE_STEPS if rows % (8 * UPDATE_STEPS) == 0 else rows
            for row in range(0, rows, step):
                old = (state[3 * n + k][row : row + step] for k in range(3))
                done = adamw(*old, sum_ref[row : row + step], rate)
                for k in range(3 * n, 3 * n + 3):
                    done_refs[k][row : row + step] = done[k - 3 * n]
                    source = done_refs[k].at[pl.ds(row, step)]
                    target = new[k].at[pl.ds(row, step)]
                    number = UPDATE_STEPS * k + row // step
                    stores.append(pltpu.make_async_copy(source, target, sem.at[number]))
                    stores[-1].start()
        for store in stores:
            store.wait()

    shapes = [v.shape for v in sets]
    return pl.pallas_call(
        kernel,
        in_specs=[SMEM] + [VMEM] * 11,
        out_specs=[HBM] * 9,
        out_shape=[jax.ShapeDtypeStruct(v, F32) for v in shapes],
        scratch_shapes=[
            pltpu.VMEM((plan.shard, c), F32),
            *(pltpu.VMEM(v, F32) for v in shapes),
            pltpu.SemaphoreType.DMA((9 * UPDATE_STEPS,)),
        ],
        compiler_params=params(),
        cost_estimate=cost(0, 9),
        name="update",
    )(ids, near, far, *sets)


def send(v, axis, size, step):
    if axis == "fsdp":
        pairs = [(i, (i + step) % size) for i in range(size)]
    else:
        pairs = [(i, i ^ step) for i in range(size)]
    return lax.ppermute(v, axis, pairs)


def total(*parts):
    acc = parts[0].astype(F32)
    for part in parts[1:]:
        acc = acc + part.astype(F32)
    return acc.astype(BF)


def make_body(sizes):
    tiles, ranks = sizes["tile"], sizes["fsdp"]

    def to_core(v):
        return send(v, "core", 2, 1)

    def to_tile(v, d):
        return send(v, "tile", tiles, d)

    def to_rank(v, d):
        return send(v, "fsdp", ranks, d)

    def per_device(
        inputs,
        cotangent,
        lengths,
        face_table,
        w_first,
        w_second,
        w_skip,
        mom_first,
        sq_first,
        mom_second,
        sq_second,
        mom_skip,
        sq_skip,
    ):
        plan = Plan(sizes, inputs.shape[-1])
        x = jnp.transpose(inputs[0], (1, 2, 3, 0, 4))
        cot = jnp.transpose(cotangent[0], (1, 2, 3, 0, 4))
        places = jnp.stack([lax.axis_index(n) for n in ("core", "tile", "fsdp")]).astype(jnp.int32)
        weights = w_first, w_second, w_skip
        groups = []
        for sent in pack(plan, places, *weights):
            own = jnp.stack([to_rank(sent, d) for d in range(1, ranks)])
            groups.append([own])
            if plan.split:
                groups[-1] += [to_tile(own, e) for e in range(1, tiles)]
        near1, near2 = groups
        ids = jnp.concatenate([places, lengths, face_table.T.reshape(-1)])
        xp, go, dws, low1, low2, low3 = enter(plan, ids, x, cot, weights, (near1[0], near2[0]))
        xp, near1 = lax.optimization_barrier((xp, near1))
        far1 = [to_core(v) for v in near1]
        hp, slope, w1 = first(plan, ids, xp, low1, near1, far1)
        hp, near2 = lax.optimization_barrier((hp, near2))
        far2 = [to_core(v) for v in near2]
        hp, far2 = lax.optimization_barrier((hp, far2))
        output, gp, w2, ws, keep2, away2 = second(
            plan, ids, hp, xp, go, dws, low2, low3, near2, far2
        )
        came2 = to_core(away2)
        op = hidden_back(ids, gp, w2, slope)
        came2, op = lax.optimization_barrier((came2, op))
        parts2 = [total(keep2[d], came2[d]) for d in range(tiles)]
        op, parts2 = lax.optimization_barrier((op, parts2))
        late = [parts2[0]] + [to_tile(parts2[d], d) for d in range(1, tiles)]
        keep1, away1 = first_grad(plan, ids, xp, op)
        late, away1 = lax.optimization_barrier((late, away1))
        came1 = to_core(away1)
        parts1 = [total(keep1[d], came1[d]) for d in range(tiles)]
        op, parts1 = lax.optimization_barrier((op, parts1))
        early = [parts1[0]] + [to_tile(parts1[d], d) for d in range(1, tiles)]
        grad_inputs = inputs_back(op, w1, ws, go)
        early, late, grad_inputs = lax.optimization_barrier((early, late, grad_inputs))
        parts = tile_sums(plan, early, late)
        came = [to_rank(parts[d], d) for d in range(1, ranks)]
        mine = total(parts[0], *came)
        near = jnp.stack([mine] + [to_tile(mine, d) for d in range(1, tiles)])
        far = to_core(near)
        news = update(
            plan,
            ids,
            near,
            far,
            (
                w_first,
                mom_first,
                sq_first,
                w_second,
                mom_second,
                sq_second,
                w_skip,
                mom_skip,
                sq_skip,
            ),
        )
        output = jnp.transpose(output, (3, 0, 1, 2, 4))[None]
        grad_inputs = jnp.transpose(grad_inputs, (3, 0, 1, 2, 4))[None]
        return (output, grad_inputs, *news)

    return per_device


def solution(mesh):
    pairs = mesh.shape["dp"] // 2
    ranks = mesh.shape["fsdp"]
    fine = Mesh(mesh.devices.reshape(pairs, 2, ranks), ("tile", "core", "fsdp"))
    sizes = {"tile": pairs, "core": 2, "fsdp": ranks}
    every = ("tile", "core", "fsdp")
    fields = P(every, None, None, None, None, None)
    rows = P("fsdp", None)
    return jax.shard_map(
        make_body(sizes),
        mesh=fine,
        in_specs=(fields, fields, P(every), P()) + (rows,) * 9,
        out_specs=(fields, fields) + (rows,) * 9,
        check_vma=False,
    )
```

time: 117 us -> 99.2 us (0.85)
  waiting for transfers between devices: 29.6 us -> 17.8 us
  local copies, waits for them, and re-layouts: 6.65 us -> 0.9 us
  starting transfers between devices: 31.1 us -> 34.3 us
  Pallas kernels: 46.7 us -> 43.8 us
    ppermute x26 -> x35, waiting for transfers between devices: 29.6 us -> 17.8 us  [send(): return lax.ppermute(v, axis, pairs)]
    unnamed x32 -> x18, local copies, waits for them, and re-layouts: 6.65 us -> 0.05 us
    ppermute x26 -> x35, starting transfers between devices: 31.1 us -> 34.3 us  [send(): return lax.ppermute(v, axis, pairs)]
    pallas_call x5 -> x8, Pallas kernels: 41 us -> 38.1 us  [the longest x1 12.8 us: second(): pl.pallas_call(kernel, in_specs=[SMEM] + [VMEM] * (6 + 2 * count), out_sp...]
  transfers between devices with their start and end apart: 26 -> 35, of which waited for: 15 -> 14; matrix products, arithmetic and copies ran while one was open for 0% -> 1% of each run, Pallas kernels for 13% -> 26%
where the time goes in v3:
time: 99.2 us; the launch traced here: 99 us
  Pallas kernels  43.8 us (44%)
  starting transfers between devices  34.3 us (35%)
  waiting for transfers between devices  17.8 us (18%)
  between operations  1.81 us (2%)
    ppermute x35, starting transfers between devices, send(): return lax.ppermute(v, axis, pairs)  34.3 us
    ppermute x35, waiting for transfers between devices, send(): return lax.ppermute(v, axis, pairs)  17.8 us
    pallas_call x1, Pallas kernels, second(): pl.pallas_call(kernel, in_specs=[SMEM] + [VMEM] * (6 + 2 * count), out_sp...  12.8 us
    pallas_call x1, Pallas kernels, first(): pl.pallas_call(kernel, in_specs=[SMEM] + [VMEM] * (2 + 2 * count), out_sp...  6.17 us
    pallas_call x1, Pallas kernels, inputs_back(): pl.pallas_call(inputs_back_kernel, in_specs=[VMEM] * 4, out_specs=ANY, ou...  5.68 us
    pallas_call x1, Pallas kernels, first_grad(): pl.pallas_call(kernel, in_specs=[SMEM, VMEM, VMEM], out_specs=[VMEM] * 2,...  5.4 us
    pallas_call x1, Pallas kernels, hidden_back(): pl.pallas_call(hidden_back_kernel, in_specs=[SMEM] + [VMEM] * 3, out_spec...  5.17 us
    pallas_call x1, Pallas kernels, enter(): pl.pallas_call(kernel, in_specs=[SMEM] + [HBM] * 5 + [VMEM] * len(after),...  3.54 us
  transfers between devices with their start and end apart: 35, of which 14 were waited for; matrix products, arithmetic and copies ran while one was open for 1% of the time, Pallas kernels for 26%

profile of v3, /device:TPU:0, one launch (start us, length us, event | category | flops | bytes accessed | tf_op | source)
XLA Modules:
  0.0 99.0 jit_solution(3757495233158756361)
XLA Ops:
  0.7 1.5 %pack.1 = (bf16[72,256]{1,0:T(8,128)(2,1)S(1)}, bf16[80,256]{1,0:T(8,128)(2,1)S(1)}) custom-call(s32[3]{0:T(128)S(1)} %pad_add_fusion.ids_ref, f32[576,256]{1,0:T(8,128)} %refs_2_.3, f32[576,256]{1,0:T(8,128)} %refs_5_.1, f32[64,256]{1,0:T(8,128)} %refs_8_.1), custom_call_target="tpu_custom_call" | custom-call | bytes 300000 | tf_op jit(solution)/shard_map/pack/pallas_call | solution.py:204
  2.2 5.1 %collective-permute-start.2 = (bf16[72,256]{1,0:T(8,128)(2,1)S(1)}, bf16[72,256]{1,0:T(8,128)(2,1)S(1)}, u32[]{:S(2)}, u32[]{:S(2)}) collective-permute-start(bf16[72,256]{1,0:T(8,128)(2,1)S(1)} %get-tuple-element.84), channel_id=1, source_target_pairs={{0,3},{1,0},{2,1},{3,2},{4,7},{5,4},{6,5},{7,6},{8,11},{9,8},{10,9... | collective-permute-start | bytes 110600 | tf_op jit(solution)/shard_map/ppermute | solution.py:548
  7.3 1.0 %collective-permute-start = (bf16[72,256]{1,0:T(8,128)(2,1)S(1)}, bf16[72,256]{1,0:T(8,128)(2,1)S(1)}, u32[]{:S(2)}, u32[]{:S(2)}) collective-permute-start(bf16[72,256]{1,0:T(8,128)(2,1)S(1)} %get-tuple-element.84), channel_id=1, source_target_pairs={{0,1},{1,2},{2,3},{3,0},{4,5},{5,6},{6,7},{7,4},{8,9},{9,10},{10,1... | collective-permute-start | bytes 110600 | tf_op jit(solution)/shard_map/ppermute | solution.py:548
  8.4 2.8 %collective-permute-start.5 = (bf16[80,256]{1,0:T(8,128)(2,1)S(1)}, bf16[80,256]{1,0:T(8,128)(2,1)S(1)}, u32[]{:S(2)}, u32[]{:S(2)}) collective-permute-start(bf16[80,256]{1,0:T(8,128)(2,1)S(1)} %get-tuple-element.85), channel_id=1, source_target_pairs={{0,3},{1,0},{2,1},{3,2},{4,7},{5,4},{6,5},{7,6},{8,11},{9,8},{10,9... | collective-permute-start | bytes 122888 | tf_op jit(solution)/shard_map/ppermute | solution.py:548
  11.2 1.1 %collective-permute-start.4 = (bf16[80,256]{1,0:T(8,128)(2,1)S(1)}, bf16[80,256]{1,0:T(8,128)(2,1)S(1)}, u32[]{:S(2)}, u32[]{:S(2)}) collective-permute-start(bf16[80,256]{1,0:T(8,128)(2,1)S(1)} %get-tuple-element.85), channel_id=1, source_target_pairs={{0,2},{1,3},{2,0},{3,1},{4,6},{5,7},{6,4},{7,5},{8,10},{9,11},{10,... | collective-permute-start | bytes 122888 | tf_op jit(solution)/shard_map/ppermute | solution.py:548
  12.9 0.8 reshape.57
  13.8 2.5 %collective-permute-start.8 = (bf16[3,72,256]{2,1,0:T(8,128)(2,1)S(1)}, bf16[3,72,256]{2,1,0:T(8,128)(2,1)S(1)}, u32[]{:S(2)}, u32[]{:S(2)}) collective-permute-start(bf16[3,72,256]{2,1,0:T(8,128)(2,1)S(1)} %pad_maximum_fusion.2.refs_3_.refs_0_), channel_id=1, source_target_pairs={{0,24},{8,16},{16,8},{24,0},{1,25},{9,17},{17,9},{25,1},{2,26},{10... | collective-permute-start | bytes 331784 | tf_op jit(solution)/shard_map/ppermute | solution.py:548
  16.4 0.5 collective-permute-start.7
  16.9 0.5 collective-permute-start.6
  17.4 2.2 %collective-permute-done.3 = bf16[80,256]{1,0:T(8,128)(2,1)S(1)} collective-permute-done((bf16[80,256]{1,0:T(8,128)(2,1)S(1)}, bf16[80,256]{1,0:T(8,128)(2,1)S(1)}, u32[]{:S(2)}, u32[]{:S(2)}) %collective-permute-start.3) | collective-permute-done | bytes 40992 | tf_op jit(solution)/shard_map/ppermute | solution.py:548
  19.6 3.5 %enter.1 = (bf16[12,8,8,8,256]{4,3,2,1,0:T(8,128)(2,1)S(1)}, bf16[12,6,6,8,256]{4,3,2,1,0:T(8,128)(2,1)S(1)}, bf16[256,256]{1,0:T(8,128)(2,1)S(1)}, bf16[576,256...) custom-call(s32[52]{0:T(128)S(1)} %concatenate.4.ids_ref, ...), custom_call_target="tpu_custom_call" | custom-call | flops 600000000 | bytes 9000000 | tf_op jit(solution)/shard_map/enter/pallas_call | solution.py:267
  23.3 0.5 collective-permute-start.10
  23.9 0.4 collective-permute-start.12
  24.3 2.5 %collective-permute-start.15 = (bf16[3,80,256]{2,1,0:T(8,128)(2,1)S(1)}, bf16[3,80,256]{2,1,0:T(8,128)(2,1)S(1)}, u32[]{:S(2)}, u32[]{:S(2)}) collective-permute-start(bf16[3,80,256]{2,1,0:T(8,128)(2,1)S(1)} %pad_maximum_fusion.1.refs_4_.refs_0_), channel_id=1, source_target_pairs={{0,24},{8,16},{16,8},{24,0},{1,25},{9,17},{17,9},{25,1},{2,26},{10... | collective-permute-start | bytes 368648 | tf_op jit(solution)/shard_map/ppermute | solution.py:548
  26.7 0.5 collective-permute-start.14
  27.2 0.5 collective-permute-start.13
  27.8 6.2 %first.1 = (bf16[12,8,8,8,256]{4,3,2,1,0:T(8,128)(2,1)S(1)}, bf16[12,6,6,8,256]{4,3,2,1,0:T(8,128)(2,1)S(1)}, bf16[2304,256]{1,0:T(8,128)(2,1)S(1)}) custom-call(s32[52]{0:T(128)S(1)} %concatenate.4.ids_ref, bf16[12,8,8,8,256]{4,3,2,1,0:T(8,128)(2,1)S(1)} %get-tuple-element.87.xp_ref, bf16[576,256]{1,0:T(8,128)(2,1)S(1)} %get-tuple-element.88.low_ref, ...), custom_call_target="tpu_custom_call" | custom-call | flops 4100000000 | bytes 12000000 | tf_op jit(solution)/shard_map/first/pallas_call | solution.py:303
  34.1 0.5 collective-permute-start.17
  34.7 0.4 collective-permute-start.19
  35.1 0.3 collective-permute-done.16.refs_4_
  35.6 0.3 collective-permute-done.18.refs_6_
  36.1 12.8 %second.1 = (bf16[12,6,6,8,256]{4,3,2,1,0:T(8,128)(2,1)}, bf16[12,8,8,8,256]{4,3,2,1,0:T(8,128)(2,1)S(1)}, bf16[2304,256]{1,0:T(8,128)(2,1)S(1)}, bf16[256,256]{...) custom-call(s32[52]{0:T(128)S(1)} %concatenate.4.ids_ref, ...), custom_call_target="tpu_custom_call" | custom-call | flops 8999999488 | bytes 16000000 | tf_op jit(solution)/shard_map/second/pallas_call | solution.py:352
  48.9 0.4 collective-permute-start.20
  49.3 5.2 %hidden_back.1.op_ref.gp_ref = bf16[12,8,8,8,256]{4,3,2,1,0:T(8,128)(2,1)S(1)} custom-call(s32[52]{0:T(128)S(1)} %concatenate.4.ids_ref, bf16[12,8,8,8,256]{4,3,2,1,0:T(8,128)(2,1)S(1)} %get-tuple-element.110.gp_ref, bf16[2304,256]{1,0:T(8,128)(2,1)S(1)} %get-tuple-element.111.w_ref, bf16[12,6,6,8,256]{4,3,2,1,0:T(8,128)(2,1)S(1)} %get-tuple-element.112.slope_ref), custom_call_target="tpu_custom_call" | custom-call | flops 4100000000 | bytes 9000000 | tf_op jit(solution)/shard_map/hidden_back/pallas_call | solution.py:389
  54.7 1.6 %collective-permute-start.21 = (bf16[4,80,256]{2,1,0:T(8,128)(2,1)S(1)}, bf16[4,80,256]{2,1,0:T(8,128)(2,1)S(1)}, u32[]{:S(2)}, u32[]{:S(2)}) collective-permute-start(bf16[4,80,256]{2,1,0:T(8,128)(2,1)S(1)} %get-tuple-element.119), channel_id=1, source_target_pairs={{0,8},{8,0},{16,24},{24,16},{1,9},{9,1},{17,25},{25,17},{2,10},{10... | collective-permute-start | bytes 491528 | tf_op jit(solution)/shard_map/ppermute | solution.py:548
  56.3 1.5 %collective-permute-start.22 = (bf16[4,80,256]{2,1,0:T(8,128)(2,1)S(1)}, bf16[4,80,256]{2,1,0:T(8,128)(2,1)S(1)}, u32[]{:S(2)}, u32[]{:S(2)}) collective-permute-start(bf16[4,80,256]{2,1,0:T(8,128)(2,1)S(1)} %get-tuple-element.120), channel_id=1, source_target_pairs={{0,16},{8,24},{16,0},{24,8},{1,17},{9,25},{17,1},{25,9},{2,18},{10... | collective-permute-start | bytes 491528 | tf_op jit(solution)/shard_map/ppermute | solution.py:548
  57.8 0.5 collective-permute-start.23
  58.3 5.4 %first_grad.1 = (bf16[4,4,72,256]{3,2,1,0:T(8,128)(2,1)S(1)}, bf16[4,4,72,256]{3,2,1,0:T(8,128)(2,1)S(1)}) custom-call(s32[52]{0:T(128)S(1)} %concatenate.4.ids_ref, bf16[12,8,8,8,256]{4,3,2,1,0:T(8,128)(2,1)S(1)} %get-tuple-element.87.xp_ref, bf16[12,8,8,8,256]{4,3,2,1,0:T(8,128)(2,1)S(1)} %hidden_back.1.op_ref.gp_ref), custom_call_target="tpu_custom_call" | custom-call | flops 4100000000 | bytes 9000000 | tf_op jit(solution)/shard_map/first_grad/pallas_call | solution.py:408
  63.7 2.1 %collective-permute-done.22.refs_6_ = bf16[4,80,256]{2,1,0:T(8,128)(2,1)S(1)} collective-permute-done((bf16[4,80,256]{2,1,0:T(8,128)(2,1)S(1)}, bf16[4,80,256]{2,1,0:T(8,128)(2,1)S(1)}, u32[]{:S(2)}, u32[]{:S(2)}) %collective-permute-start.22) | collective-permute-done | bytes 163872 | tf_op jit(solution)/shard_map/ppermute | solution.py:548
  65.8 2.0 %collective-permute-done.24 = bf16[4,4,72,256]{3,2,1,0:T(8,128)(2,1)S(1)} collective-permute-done((bf16[4,4,72,256]{3,2,1,0:T(8,128)(2,1)S(1)}, bf16[4,4,72,256]{3,2,1,0:T(8,128)(2,1)S(1)}, u32[]{:S(2)}, u32[]{:S(2)}) %collective-permute-start.24) | collective-permute-done | bytes 589856 | tf_op jit(solution)/shard_map/ppermute | solution.py:548
  67.9 1.3 %collective-permute-start.25 = (bf16[4,72,256]{2,1,0:T(8,128)(2,1)S(1)}, bf16[4,72,256]{2,1,0:T(8,128)(2,1)S(1)}, u32[]{:S(2)}, u32[]{:S(2)}) collective-permute-start(bf16[4,72,256]{2,1,0:T(8,128)(2,1)S(1)} %get-tuple-element.125), channel_id=1, source_target_pairs={{0,8},{8,0},{16,24},{24,16},{1,9},{9,1},{17,25},{25,17},{2,10},{10... | collective-permute-start | bytes 442376 | tf_op jit(solution)/shard_map/ppermute | solution.py:548
  69.2 0.8 collective-permute-start.26
  70.1 1.4 %collective-permute-start.27 = (bf16[4,72,256]{2,1,0:T(8,128)(2,1)S(1)}, bf16[4,72,256]{2,1,0:T(8,128)(2,1)S(1)}, u32[]{:S(2)}, u32[]{:S(2)}) collective-permute-start(bf16[4,72,256]{2,1,0:T(8,128)(2,1)S(1)} %get-tuple-element.127), channel_id=1, source_target_pairs={{0,24},{8,16},{16,8},{24,0},{1,25},{9,17},{17,9},{25,1},{2,26},{10... | collective-permute-start | bytes 442376 | tf_op jit(solution)/shard_map/ppermute | solution.py:548
  71.5 5.7 %inputs_back.1 = f32[12,6,6,8,256]{4,3,2,1,0:T(8,128)} custom-call(bf16[12,8,8,8,256]{4,3,2,1,0:T(8,128)(2,1)S(1)} %hidden_back.1.op_ref.gp_ref, bf16[2304,256]{1,0:T(8,128)(2,1)S(1)} %get-tuple-element.133.w_ref, bf16[256,256]{1,0:T(8,128)(2,1)S(1)} %get-tuple-element.134.ws_ref, bf16[12,6,6,8,256]{4,3,2,1,0:T(8,128)(2,1)S(1)} %get-tuple-element.100.go_ref), custom_call_target="tpu_custom_call" | custom-call | flops 4600000000 | bytes 10000000 | tf_op jit(solution)/shard_map/inputs_back/pallas_call | solution.py:458
  77.3 0.7 collective-permute-done.27.refs_3_
  78.2 0.2 collective-permute-start.28
  78.4 2.0 %collective-permute-start.29 = (bf16[152,256]{1,0:T(8,128)(2,1)S(1)}, bf16[152,256]{1,0:T(8,128)(2,1)S(1)}, u32[]{:S(2)}, u32[]{:S(2)}) collective-permute-start(bf16[152,256]{1,0:T(8,128)(2,1)S(1)} %get-tuple-element.146), channel_id=1, source_target_pairs={{0,2},{1,3},{2,0},{3,1},{4,6},{5,7},{6,4},{7,5},{8,10},{9,11},{10,... | collective-permute-start | bytes 233480 | tf_op jit(solution)/shard_map/ppermute | solution.py:548
  80.4 1.6 %collective-permute-start.30 = (bf16[152,256]{1,0:T(8,128)(2,1)S(1)}, bf16[152,256]{1,0:T(8,128)(2,1)S(1)}, u32[]{:S(2)}, u32[]{:S(2)}) collective-permute-start(bf16[152,256]{1,0:T(8,128)(2,1)S(1)} %get-tuple-element.147), channel_id=1, source_target_pairs={{0,3},{1,0},{2,1},{3,2},{4,7},{5,4},{6,5},{7,6},{8,11},{9,8},{10,9... | collective-permute-start | bytes 233480 | tf_op jit(solution)/shard_map/ppermute | solution.py:548
  82.0 3.2 %collective-permute-done.28 = bf16[152,256]{1,0:T(8,128)(2,1)S(1)} collective-permute-done((bf16[152,256]{1,0:T(8,128)(2,1)S(1)}, bf16[152,256]{1,0:T(8,128)(2,1)S(1)}, u32[]{:S(2)}, u32[]{:S(2)}) %collective-permute-start.28) | collective-permute-done | bytes 77856 | tf_op jit(solution)/shard_map/ppermute | solution.py:548
  85.3 1.6 %collective-permute-done.29 = bf16[152,256]{1,0:T(8,128)(2,1)S(1)} collective-permute-done((bf16[152,256]{1,0:T(8,128)(2,1)S(1)}, bf16[152,256]{1,0:T(8,128)(2,1)S(1)}, u32[]{:S(2)}, u32[]{:S(2)}) %collective-permute-start.29) | collective-permute-done | bytes 77856 | tf_op jit(solution)/shard_map/ppermute | solution.py:548
  86.9 1.3 %collective-permute-start.33 = (bf16[152,256]{1,0:T(8,128)(2,1)S(1)}, bf16[152,256]{1,0:T(8,128)(2,1)S(1)}, u32[]{:S(2)}, u32[]{:S(2)}) collective-permute-start(bf16[152,256]{1,0:T(8,128)(2,1)S(1)} %add_convert_fusion.8), channel_id=1, source_target_pairs={{0,24},{8,16},{16,8},{24,0},{1,25},{9,17},{17,9},{25,1},{2,26},{10... | collective-permute-start | bytes 233480 | tf_op jit(solution)/shard_map/ppermute | solution.py:548
  88.3 1.1 %collective-permute-start.32 = (bf16[152,256]{1,0:T(8,128)(2,1)S(1)}, bf16[152,256]{1,0:T(8,128)(2,1)S(1)}, u32[]{:S(2)}, u32[]{:S(2)}) collective-permute-start(bf16[152,256]{1,0:T(8,128)(2,1)S(1)} %add_convert_fusion.8), channel_id=1, source_target_pairs={{0,16},{8,24},{16,0},{24,8},{1,17},{9,25},{17,1},{25,9},{2,18},{10... | collective-permute-start | bytes 233480 | tf_op jit(solution)/shard_map/ppermute | solution.py:548
  89.4 1.1 %collective-permute-start.31 = (bf16[152,256]{1,0:T(8,128)(2,1)S(1)}, bf16[152,256]{1,0:T(8,128)(2,1)S(1)}, u32[]{:S(2)}, u32[]{:S(2)}) collective-permute-start(bf16[152,256]{1,0:T(8,128)(2,1)S(1)} %add_convert_fusion.8), channel_id=1, source_target_pairs={{0,8},{8,0},{16,24},{24,16},{1,9},{9,1},{17,25},{25,17},{2,10},{10... | collective-permute-start | bytes 233480 | tf_op jit(solution)/shard_map/ppermute | solution.py:548
  90.5 1.9 %collective-permute-done.33 = bf16[152,256]{1,0:T(8,128)(2,1)S(1)} collective-permute-done((bf16[152,256]{1,0:T(8,128)(2,1)S(1)}, bf16[152,256]{1,0:T(8,128)(2,1)S(1)}, u32[]{:S(2)}, u32[]{:S(2)}) %collective-permute-start.33) | collective-permute-done | bytes 77856 | tf_op jit(solution)/shard_map/ppermute | solution.py:548
  92.4 0.8 collective-permute-done.32
  93.1 0.6 collective-permute-done.31
  93.9 1.6 %collective-permute-done.34.refs_1_ = bf16[4,152,256]{2,1,0:T(8,128)(2,1)S(1)} collective-permute-done((bf16[4,152,256]{2,1,0:T(8,128)(2,1)S(1)}, bf16[4,152,256]{2,1,0:T(8,128)(2,1)S(1)}, u32[]{:S(2)}, u32[]{:S(2)}) %collective-permute-start.34) | collective-permute-done | bytes 311328 | tf_op jit(solution)/shard_map/ppermute | solution.py:548
  95.5 3.3 %update.1 = (f32[576,256]{1,0:T(8,128)}, f32[576,256]{1,0:T(8,128)}, f32[576,256]{1,0:T(8,128)}, f32[576,256]{1,0:T(8,128)}, f32[576,256]{1,0:T(8,128)}, /*index...) custom-call(s32[52]{0:T(128)S(1)} %concatenate.4.ids_ref, ...), custom_call_target="tpu_custom_call" | custom-call | bytes 9000000 | tf_op jit(solution)/shard_map/update/pallas_call | solution.py:527
  (58 shorter events, 1.6 us)
Async XLA Ops:
  2.2 11.6 %collective-permute-start.2 = (bf16[72,256]{1,0:T(8,128)(2,1)S(1)}, bf16[72,256]{1,0:T(8,128)(2,1)S(1)}, u32[]{:S(2)}, u32[]{:S(2)}) collective-permute-start(bf16[72,256]{1,0:T(8,128)(2,1)S(1)} %get-tuple-element.84), channel_id=1, source_target_pairs={{0,3},{1,0},{2,1},{3,2},{4,7},{5,4},{6,5},{7,6},{8,11},{9,8},{10,9... | collective-permute-start | bytes 110600 | tf_op jit(solution)/shard_map/ppermute | solution.py:548
  7.3 6.5 %collective-permute-start.1 = (bf16[72,256]{1,0:T(8,128)(2,1)S(1)}, bf16[72,256]{1,0:T(8,128)(2,1)S(1)}, u32[]{:S(2)}, u32[]{:S(2)}) collective-permute-start(bf16[72,256]{1,0:T(8,128)(2,1)S(1)} %get-tuple-element.84), channel_id=1, source_target_pairs={{0,2},{1,3},{2,0},{3,1},{4,6},{5,7},{6,4},{7,5},{8,10},{9,11},{10,... | collective-permute-start | bytes 110600 | tf_op jit(solution)/shard_map/ppermute | solution.py:548
  7.3 6.5 %collective-permute-start = (bf16[72,256]{1,0:T(8,128)(2,1)S(1)}, bf16[72,256]{1,0:T(8,128)(2,1)S(1)}, u32[]{:S(2)}, u32[]{:S(2)}) collective-permute-start(bf16[72,256]{1,0:T(8,128)(2,1)S(1)} %get-tuple-element.84), channel_id=1, source_target_pairs={{0,1},{1,2},{2,3},{3,0},{4,5},{5,6},{6,7},{7,4},{8,9},{9,10},{10,1... | collective-permute-start | bytes 110600 | tf_op jit(solution)/shard_map/ppermute | solution.py:548
  8.4 8.5 %collective-permute-start.5 = (bf16[80,256]{1,0:T(8,128)(2,1)S(1)}, bf16[80,256]{1,0:T(8,128)(2,1)S(1)}, u32[]{:S(2)}, u32[]{:S(2)}) collective-permute-start(bf16[80,256]{1,0:T(8,128)(2,1)S(1)} %get-tuple-element.85), channel_id=1, source_target_pairs={{0,3},{1,0},{2,1},{3,2},{4,7},{5,4},{6,5},{7,6},{8,11},{9,8},{10,9... | collective-permute-start | bytes 122888 | tf_op jit(solution)/shard_map/ppermute | solution.py:548
  11.2 6.2 %collective-permute-start.4 = (bf16[80,256]{1,0:T(8,128)(2,1)S(1)}, bf16[80,256]{1,0:T(8,128)(2,1)S(1)}, u32[]{:S(2)}, u32[]{:S(2)}) collective-permute-start(bf16[80,256]{1,0:T(8,128)(2,1)S(1)} %get-tuple-element.85), channel_id=1, source_target_pairs={{0,2},{1,3},{2,0},{3,1},{4,6},{5,7},{6,4},{7,5},{8,10},{9,11},{10,... | collective-permute-start | bytes 122888 | tf_op jit(solution)/shard_map/ppermute | solution.py:548
  13.8 5.8 %collective-permute-start.3 = (bf16[80,256]{1,0:T(8,128)(2,1)S(1)}, bf16[80,256]{1,0:T(8,128)(2,1)S(1)}, u32[]{:S(2)}, u32[]{:S(2)}) collective-permute-start(bf16[80,256]{1,0:T(8,128)(2,1)S(1)} %get-tuple-element.85), channel_id=1, source_target_pairs={{0,1},{1,2},{2,3},{3,0},{4,5},{5,6},{6,7},{7,4},{8,9},{9,10},{10,1... | collective-permute-start | bytes 122888 | tf_op jit(solution)/shard_map/ppermute | solution.py:548
  13.8 9.3 %collective-permute-start.8 = (bf16[3,72,256]{2,1,0:T(8,128)(2,1)S(1)}, bf16[3,72,256]{2,1,0:T(8,128)(2,1)S(1)}, u32[]{:S(2)}, u32[]{:S(2)}) collective-permute-start(bf16[3,72,256]{2,1,0:T(8,128)(2,1)S(1)} %pad_maximum_fusion.2.refs_3_.refs_0_), channel_id=1, source_target_pairs={{0,24},{8,16},{16,8},{24,0},{1,25},{9,17},{17,9},{25,1},{2,26},{10... | collective-permute-start | bytes 331784 | tf_op jit(solution)/shard_map/ppermute | solution.py:548
  16.4 6.8 %collective-permute-start.7 = (bf16[3,72,256]{2,1,0:T(8,128)(2,1)S(1)}, bf16[3,72,256]{2,1,0:T(8,128)(2,1)S(1)}, u32[]{:S(2)}, u32[]{:S(2)}) collective-permute-start(bf16[3,72,256]{2,1,0:T(8,128)(2,1)S(1)} %pad_maximum_fusion.2.refs_3_.refs_0_), channel_id=1, source_target_pairs={{0,16},{8,24},{16,0},{24,8},{1,17},{9,25},{17,1},{25,9},{2,18},{10... | collective-permute-start | bytes 331784 | tf_op jit(solution)/shard_map/ppermute | solution.py:548
  16.9 6.3 %collective-permute-start.6 = (bf16[3,72,256]{2,1,0:T(8,128)(2,1)S(1)}, bf16[3,72,256]{2,1,0:T(8,128)(2,1)S(1)}, u32[]{:S(2)}, u32[]{:S(2)}) collective-permute-start(bf16[3,72,256]{2,1,0:T(8,128)(2,1)S(1)} %pad_maximum_fusion.2.refs_3_.refs_0_), channel_id=1, source_target_pairs={{0,8},{8,0},{16,24},{24,16},{1,9},{9,1},{17,25},{25,17},{2,10},{10... | collective-permute-start | bytes 331784 | tf_op jit(solution)/shard_map/ppermute | solution.py:548
  23.2 3.5 %collective-permute-start.9 = (bf16[3,72,256]{2,1,0:T(8,128)(2,1)S(1)}, bf16[3,72,256]{2,1,0:T(8,128)(2,1)S(1)}, u32[]{:S(2)}, u32[]{:S(2)}) collective-permute-start(bf16[3,72,256]{2,1,0:T(8,128)(2,1)S(1)} %pad_maximum_fusion.2.refs_3_.refs_0_), channel_id=1, source_target_pairs={{0,4},{4,0},{1,5},{5,1},{2,6},{6,2},{3,7},{7,3},{8,12},{12,8},{9,1... | collective-permute-start | bytes 331784 | tf_op jit(solution)/shard_map/ppermute | solution.py:548
  23.3 4.0 %collective-permute-start.10 = (bf16[3,72,256]{2,1,0:T(8,128)(2,1)S(1)}, bf16[3,72,256]{2,1,0:T(8,128)(2,1)S(1)}, u32[]{:S(2)}, u32[]{:S(2)}) collective-permute-start(bf16[3,72,256]{2,1,0:T(8,128)(2,1)S(1)} %collective-permute-done.6.refs_1_), channel_id=1, source_target_pairs={{0,4},{4,0},{1,5},{5,1},{2,6},{6,2},{3,7},{7,3},{8,12},{12,8},{9,1... | collective-permute-start | bytes 331784 | tf_op jit(solution)/shard_map/ppermute | solution.py:548
  23.8 4.0 %collective-permute-start.11 = (bf16[3,72,256]{2,1,0:T(8,128)(2,1)S(1)}, bf16[3,72,256]{2,1,0:T(8,128)(2,1)S(1)}, u32[]{:S(2)}, u32[]{:S(2)}) collective-permute-start(bf16[3,72,256]{2,1,0:T(8,128)(2,1)S(1)} %collective-permute-done.7.refs_2_), channel_id=1, source_target_pairs={{0,4},{4,0},{1,5},{5,1},{2,6},{6,2},{3,7},{7,3},{8,12},{12,8},{9,1... | collective-permute-start | bytes 331784 | tf_op jit(solution)/shard_map/ppermute | solution.py:548
  23.9 3.9 %collective-permute-start.12 = (bf16[3,72,256]{2,1,0:T(8,128)(2,1)S(1)}, bf16[3,72,256]{2,1,0:T(8,128)(2,1)S(1)}, u32[]{:S(2)}, u32[]{:S(2)}) collective-permute-start(bf16[3,72,256]{2,1,0:T(8,128)(2,1)S(1)} %collective-permute-done.8.refs_3_), channel_id=1, source_target_pairs={{0,4},{4,0},{1,5},{5,1},{2,6},{6,2},{3,7},{7,3},{8,12},{12,8},{9,1... | collective-permute-start | bytes 331784 | tf_op jit(solution)/shard_map/ppermute | solution.py:548
  24.3 9.7 %collective-permute-start.15 = (bf16[3,80,256]{2,1,0:T(8,128)(2,1)S(1)}, bf16[3,80,256]{2,1,0:T(8,128)(2,1)S(1)}, u32[]{:S(2)}, u32[]{:S(2)}) collective-permute-start(bf16[3,80,256]{2,1,0:T(8,128)(2,1)S(1)} %pad_maximum_fusion.1.refs_4_.refs_0_), channel_id=1, source_target_pairs={{0,24},{8,16},{16,8},{24,0},{1,25},{9,17},{17,9},{25,1},{2,26},{10... | collective-permute-start | bytes 368648 | tf_op jit(solution)/shard_map/ppermute | solution.py:548
  26.7 7.2 %collective-permute-start.14 = (bf16[3,80,256]{2,1,0:T(8,128)(2,1)S(1)}, bf16[3,80,256]{2,1,0:T(8,128)(2,1)S(1)}, u32[]{:S(2)}, u32[]{:S(2)}) collective-permute-start(bf16[3,80,256]{2,1,0:T(8,128)(2,1)S(1)} %pad_maximum_fusion.1.refs_4_.refs_0_), channel_id=1, source_target_pairs={{0,16},{8,24},{16,0},{24,8},{1,17},{9,25},{17,1},{25,9},{2,18},{10... | collective-permute-start | bytes 368648 | tf_op jit(solution)/shard_map/ppermute | solution.py:548
  27.2 6.7 %collective-permute-start.13 = (bf16[3,80,256]{2,1,0:T(8,128)(2,1)S(1)}, bf16[3,80,256]{2,1,0:T(8,128)(2,1)S(1)}, u32[]{:S(2)}, u32[]{:S(2)}) collective-permute-start(bf16[3,80,256]{2,1,0:T(8,128)(2,1)S(1)} %pad_maximum_fusion.1.refs_4_.refs_0_), channel_id=1, source_target_pairs={{0,8},{8,0},{16,24},{24,16},{1,9},{9,1},{17,25},{25,17},{2,10},{10... | collective-permute-start | bytes 368648 | tf_op jit(solution)/shard_map/ppermute | solution.py:548
  34.0 1.4 %collective-permute-start.16 = (bf16[3,80,256]{2,1,0:T(8,128)(2,1)S(1)}, bf16[3,80,256]{2,1,0:T(8,128)(2,1)S(1)}, u32[]{:S(2)}, u32[]{:S(2)}) collective-permute-start(bf16[3,80,256]{2,1,0:T(8,128)(2,1)S(1)} %pad_maximum_fusion.1.refs_4_.refs_0_), channel_id=1, source_target_pairs={{0,4},{4,0},{1,5},{5,1},{2,6},{6,2},{3,7},{7,3},{8,12},{12,8},{9,1... | collective-permute-start | bytes 368648 | tf_op jit(solution)/shard_map/ppermute | solution.py:548
  34.1 1.5 %collective-permute-start.17 = (bf16[3,80,256]{2,1,0:T(8,128)(2,1)S(1)}, bf16[3,80,256]{2,1,0:T(8,128)(2,1)S(1)}, u32[]{:S(2)}, u32[]{:S(2)}) collective-permute-start(bf16[3,80,256]{2,1,0:T(8,128)(2,1)S(1)} %collective-permute-done.13.refs_1_), channel_id=1, source_target_pairs={{0,4},{4,0},{1,5},{5,1},{2,6},{6,2},{3,7},{7,3},{8,12},{12,8},{9,1... | collective-permute-start | bytes 368648 | tf_op jit(solution)/shard_map/ppermute | solution.py:548
  34.6 1.3 %collective-permute-start.18 = (bf16[3,80,256]{2,1,0:T(8,128)(2,1)S(1)}, bf16[3,80,256]{2,1,0:T(8,128)(2,1)S(1)}, u32[]{:S(2)}, u32[]{:S(2)}) collective-permute-start(bf16[3,80,256]{2,1,0:T(8,128)(2,1)S(1)} %collective-permute-done.14.refs_2_), channel_id=1, source_target_pairs={{0,4},{4,0},{1,5},{5,1},{2,6},{6,2},{3,7},{7,3},{8,12},{12,8},{9,1... | collective-permute-start | bytes 368648 | tf_op jit(solution)/shard_map/ppermute | solution.py:548
  34.7 1.4 %collective-permute-start.19 = (bf16[3,80,256]{2,1,0:T(8,128)(2,1)S(1)}, bf16[3,80,256]{2,1,0:T(8,128)(2,1)S(1)}, u32[]{:S(2)}, u32[]{:S(2)}) collective-permute-start(bf16[3,80,256]{2,1,0:T(8,128)(2,1)S(1)} %collective-permute-done.15.refs_3_), channel_id=1, source_target_pairs={{0,4},{4,0},{1,5},{5,1},{2,6},{6,2},{3,7},{7,3},{8,12},{12,8},{9,1... | collective-permute-start | bytes 368648 | tf_op jit(solution)/shard_map/ppermute | solution.py:548
  48.9 5.6 %collective-permute-start.20 = (bf16[4,4,80,256]{3,2,1,0:T(8,128)(2,1)S(1)}, bf16[4,4,80,256]{3,2,1,0:T(8,128)(2,1)S(1)}, u32[]{:S(2)}, u32[]{:S(2)}) collective-permute-start(bf16[4,4,80,256]{3,2,1,0:T(8,128)(2,1)S(1)} %get-tuple-element.109), channel_id=1, source_target_pairs={{0,4},{4,0},{1,5},{5,1},{2,6},{6,2},{3,7},{7,3},{8,12},{12,8},{9,1... | collective-permute-start | bytes 1966088 | tf_op jit(solution)/shard_map/ppermute | solution.py:548
  54.7 9.0 %collective-permute-start.21 = (bf16[4,80,256]{2,1,0:T(8,128)(2,1)S(1)}, bf16[4,80,256]{2,1,0:T(8,128)(2,1)S(1)}, u32[]{:S(2)}, u32[]{:S(2)}) collective-permute-start(bf16[4,80,256]{2,1,0:T(8,128)(2,1)S(1)} %get-tuple-element.119), channel_id=1, source_target_pairs={{0,8},{8,0},{16,24},{24,16},{1,9},{9,1},{17,25},{25,17},{2,10},{10... | collective-permute-start | bytes 491528 | tf_op jit(solution)/shard_map/ppermute | solution.py:548
  56.3 9.5 %collective-permute-start.22 = (bf16[4,80,256]{2,1,0:T(8,128)(2,1)S(1)}, bf16[4,80,256]{2,1,0:T(8,128)(2,1)S(1)}, u32[]{:S(2)}, u32[]{:S(2)}) collective-permute-start(bf16[4,80,256]{2,1,0:T(8,128)(2,1)S(1)} %get-tuple-element.120), channel_id=1, source_target_pairs={{0,16},{8,24},{16,0},{24,8},{1,17},{9,25},{17,1},{25,9},{2,18},{10... | collective-permute-start | bytes 491528 | tf_op jit(solution)/shard_map/ppermute | solution.py:548
  57.8 8.0 %collective-permute-start.23 = (bf16[4,80,256]{2,1,0:T(8,128)(2,1)S(1)}, bf16[4,80,256]{2,1,0:T(8,128)(2,1)S(1)}, u32[]{:S(2)}, u32[]{:S(2)}) collective-permute-start(bf16[4,80,256]{2,1,0:T(8,128)(2,1)S(1)} %get-tuple-element.121), channel_id=1, source_target_pairs={{0,24},{8,16},{16,8},{24,0},{1,25},{9,17},{17,9},{25,1},{2,26},{10... | collective-permute-start | bytes 491528 | tf_op jit(solution)/shard_map/ppermute | solution.py:548
  65.8 2.0 %collective-permute-start.24 = (bf16[4,4,72,256]{3,2,1,0:T(8,128)(2,1)S(1)}, bf16[4,4,72,256]{3,2,1,0:T(8,128)(2,1)S(1)}, u32[]{:S(2)}, u32[]{:S(2)}) collective-permute-start(bf16[4,4,72,256]{3,2,1,0:T(8,128)(2,1)S(1)} %get-tuple-element.123), channel_id=1, source_target_pairs={{0,4},{4,0},{1,5},{5,1},{2,6},{6,2},{3,7},{7,3},{8,12},{12,8},{9,1... | collective-permute-start | bytes 1769480 | tf_op jit(solution)/shard_map/ppermute | solution.py:548
  67.9 9.3 %collective-permute-start.25 = (bf16[4,72,256]{2,1,0:T(8,128)(2,1)S(1)}, bf16[4,72,256]{2,1,0:T(8,128)(2,1)S(1)}, u32[]{:S(2)}, u32[]{:S(2)}) collective-permute-start(bf16[4,72,256]{2,1,0:T(8,128)(2,1)S(1)} %get-tuple-element.125), channel_id=1, source_target_pairs={{0,8},{8,0},{16,24},{24,16},{1,9},{9,1},{17,25},{25,17},{2,10},{10... | collective-permute-start | bytes 442376 | tf_op jit(solution)/shard_map/ppermute | solution.py:548
  69.2 8.0 %collective-permute-start.26 = (bf16[4,72,256]{2,1,0:T(8,128)(2,1)S(1)}, bf16[4,72,256]{2,1,0:T(8,128)(2,1)S(1)}, u32[]{:S(2)}, u32[]{:S(2)}) collective-permute-start(bf16[4,72,256]{2,1,0:T(8,128)(2,1)S(1)} %get-tuple-element.126), channel_id=1, source_target_pairs={{0,16},{8,24},{16,0},{24,8},{1,17},{9,25},{17,1},{25,9},{2,18},{10... | collective-permute-start | bytes 442376 | tf_op jit(solution)/shard_map/ppermute | solution.py:548
  70.1 7.9 %collective-permute-start.27 = (bf16[4,72,256]{2,1,0:T(8,128)(2,1)S(1)}, bf16[4,72,256]{2,1,0:T(8,128)(2,1)S(1)}, u32[]{:S(2)}, u32[]{:S(2)}) collective-permute-start(bf16[4,72,256]{2,1,0:T(8,128)(2,1)S(1)} %get-tuple-element.127), channel_id=1, source_target_pairs={{0,24},{8,16},{16,8},{24,0},{1,25},{9,17},{17,9},{25,1},{2,26},{10... | collective-permute-start | bytes 442376 | tf_op jit(solution)/shard_map/ppermute | solution.py:548
  71.5 24.0 %copy-start.4 = (f32[576,256]{1,0:T(8,128)S(1)}, f32[576,256]{1,0:T(8,128)}, u32[]{:S(2)}) copy-start(f32[576,256]{1,0:T(8,128)} %refs_4_.1) | copy-start | bytes 1769476
  71.5 24.0 %copy-start.5 = (f32[576,256]{1,0:T(8,128)S(1)}, f32[576,256]{1,0:T(8,128)}, u32[]{:S(2)}) copy-start(f32[576,256]{1,0:T(8,128)} %refs_6_.1) | copy-start | bytes 1769476
  71.5 24.0 %copy-start.6 = (f32[576,256]{1,0:T(8,128)S(1)}, f32[576,256]{1,0:T(8,128)}, u32[]{:S(2)}) copy-start(f32[576,256]{1,0:T(8,128)} %refs_7_.1) | copy-start | bytes 1769476
  77.2 18.3 %copy-start = (f32[576,256]{1,0:T(8,128)S(1)}, f32[576,256]{1,0:T(8,128)}, u32[]{:S(2)}) copy-start(f32[576,256]{1,0:T(8,128)} %refs_2_.3) | copy-start | bytes 1769476
  77.2 18.3 %copy-start.1 = (f32[576,256]{1,0:T(8,128)S(1)}, f32[576,256]{1,0:T(8,128)}, u32[]{:S(2)}) copy-start(f32[576,256]{1,0:T(8,128)} %refs_5_.1) | copy-start | bytes 1769476
  77.2 18.3 %copy-start.2 = (f32[64,256]{1,0:T(8,128)S(1)}, f32[64,256]{1,0:T(8,128)}, u32[]{:S(2)}) copy-start(f32[64,256]{1,0:T(8,128)} %refs_8_.1) | copy-start | bytes 196612
  77.2 18.3 %copy-start.3 = (f32[576,256]{1,0:T(8,128)S(1)}, f32[576,256]{1,0:T(8,128)}, u32[]{:S(2)}) copy-start(f32[576,256]{1,0:T(8,128)} %refs_3_.1) | copy-start | bytes 1769476
  77.2 18.3 %copy-start.7 = (f32[64,256]{1,0:T(8,128)S(1)}, f32[64,256]{1,0:T(8,128)}, u32[]{:S(2)}) copy-start(f32[64,256]{1,0:T(8,128)} %refs_9_.1) | copy-start | bytes 196612
  77.2 18.3 %copy-start.8 = (f32[64,256]{1,0:T(8,128)S(1)}, f32[64,256]{1,0:T(8,128)}, u32[]{:S(2)}) copy-start(f32[64,256]{1,0:T(8,128)} %refs_10_.1) | copy-start | bytes 196612
  78.2 7.1 %collective-permute-start.28 = (bf16[152,256]{1,0:T(8,128)(2,1)S(1)}, bf16[152,256]{1,0:T(8,128)(2,1)S(1)}, u32[]{:S(2)}, u32[]{:S(2)}) collective-permute-start(bf16[152,256]{1,0:T(8,128)(2,1)S(1)} %get-tuple-element.145), channel_id=1, source_target_pairs={{0,1},{1,2},{2,3},{3,0},{4,5},{5,6},{6,7},{7,4},{8,9},{9,10},{10,1... | collective-permute-start | bytes 233480 | tf_op jit(solution)/shard_map/ppermute | solution.py:548
  78.4 8.5 %collective-permute-start.29 = (bf16[152,256]{1,0:T(8,128)(2,1)S(1)}, bf16[152,256]{1,0:T(8,128)(2,1)S(1)}, u32[]{:S(2)}, u32[]{:S(2)}) collective-permute-start(bf16[152,256]{1,0:T(8,128)(2,1)S(1)} %get-tuple-element.146), channel_id=1, source_target_pairs={{0,2},{1,3},{2,0},{3,1},{4,6},{5,7},{6,4},{7,5},{8,10},{9,11},{10,... | collective-permute-start | bytes 233480 | tf_op jit(solution)/shard_map/ppermute | solution.py:548
  80.4 6.5 %collective-permute-start.30 = (bf16[152,256]{1,0:T(8,128)(2,1)S(1)}, bf16[152,256]{1,0:T(8,128)(2,1)S(1)}, u32[]{:S(2)}, u32[]{:S(2)}) collective-permute-start(bf16[152,256]{1,0:T(8,128)(2,1)S(1)} %get-tuple-element.147), channel_id=1, source_target_pairs={{0,3},{1,0},{2,1},{3,2},{4,7},{5,4},{6,5},{7,6},{8,11},{9,8},{10,9... | collective-permute-start | bytes 233480 | tf_op jit(solution)/shard_map/ppermute | solution.py:548
  86.9 5.4 %collective-permute-start.33 = (bf16[152,256]{1,0:T(8,128)(2,1)S(1)}, bf16[152,256]{1,0:T(8,128)(2,1)S(1)}, u32[]{:S(2)}, u32[]{:S(2)}) collective-permute-start(bf16[152,256]{1,0:T(8,128)(2,1)S(1)} %add_convert_fusion.8), channel_id=1, source_target_pairs={{0,24},{8,16},{16,8},{24,0},{1,25},{9,17},{17,9},{25,1},{2,26},{10... | collective-permute-start | bytes 233480 | tf_op jit(solution)/shard_map/ppermute | solution.py:548
  88.3 4.9 %collective-permute-start.32 = (bf16[152,256]{1,0:T(8,128)(2,1)S(1)}, bf16[152,256]{1,0:T(8,128)(2,1)S(1)}, u32[]{:S(2)}, u32[]{:S(2)}) collective-permute-start(bf16[152,256]{1,0:T(8,128)(2,1)S(1)} %add_convert_fusion.8), channel_id=1, source_target_pairs={{0,16},{8,24},{16,0},{24,8},{1,17},{9,25},{17,1},{25,9},{2,18},{10... | collective-permute-start | bytes 233480 | tf_op jit(solution)/shard_map/ppermute | solution.py:548
  89.4 4.4 %collective-permute-start.31 = (bf16[152,256]{1,0:T(8,128)(2,1)S(1)}, bf16[152,256]{1,0:T(8,128)(2,1)S(1)}, u32[]{:S(2)}, u32[]{:S(2)}) collective-permute-start(bf16[152,256]{1,0:T(8,128)(2,1)S(1)} %add_convert_fusion.8), channel_id=1, source_target_pairs={{0,8},{8,0},{16,24},{24,16},{1,9},{9,1},{17,25},{25,17},{2,10},{10... | collective-permute-start | bytes 233480 | tf_op jit(solution)/shard_map/ppermute | solution.py:548
  93.8 1.7 %collective-permute-start.34 = (bf16[4,152,256]{2,1,0:T(8,128)(2,1)S(1)}, bf16[4,152,256]{2,1,0:T(8,128)(2,1)S(1)}, u32[]{:S(2)}, u32[]{:S(2)}) collective-permute-start(bf16[4,152,256]{2,1,0:T(8,128)(2,1)S(1)} %pad_maximum_fusion.refs_0_), channel_id=1, source_target_pairs={{0,4},{4,0},{1,5},{5,1},{2,6},{6,2},{3,7},{7,3},{8,12},{12,8},{9,1... | collective-permute-start | bytes 933896 | tf_op jit(solution)/shard_map/ppermute | solution.py:548

commit v4 on v3

--- a/solution.py
+++ b/solution.py
@@ -16,7 +16,8 @@
 FACES = 12
 GELU_K = 0.7978845608028654
 GELU_C = 0.044715
-VMEM_LIMIT = 26 * 2**20
+VMEM_LIMIT = 30 * 2**20
+GROUP = 2
 
 
 ANY = pl.BlockSpec(memory_space=pl.ANY)
@@ -56,36 +57,61 @@
     return value, half + (value * (1.0 - half)) * (6.0 * a - 4.0 * GELU_K)
 
 
-def window(p_ref, face, a, b):
-    return p_ref[face, a : a + FS, b : b + FS].reshape(FS * FS * ROLL, p_ref.shape[-1])
-
-
-def conv(p_ref, w_ref, face):
+def pair_shape(c):
+    return (4, FS // 2, FACES, FS + 2, ROLL, c)
+
+
+def grad_pairs(c):
+    return (4, FS // 2, FACES, FS, ROLL, c)
+
+
+def pair_rows(p_ref, v_ref, face, count):
+    for t in range(FS // 2):
+        d0, d1, d2, d3 = (p_ref[face : face + count, 2 * t + q] for q in range(4))
+        v_ref[0, t, face : face + count] = d0 - d2
+        v_ref[1, t, face : face + count] = d1 + d2
+        v_ref[2, t, face : face + count] = d2 - d1
+        v_ref[3, t, face : face + count] = d1 - d3
+
+
+def pair_weights(w_ref, u_ref):
     c = w_ref.shape[1]
-    acc = None
-    for a in range(3):
-        for b in range(3):
-            t = 3 * a + b
-            part = jnp.dot(
-                window(p_ref, face, a, b), w_ref[t * c : (t + 1) * c], preferred_element_type=F32
-            )
-            acc = part if acc is None else acc + part
-    return acc
+    for b in range(3):
+        g0, g1, g2 = (w_ref[(3 * a + b) * c : (3 * a + b + 1) * c].astype(F32) for a in range(3))
+        outside, middle = 0.5 * (g0 + g2), 0.5 * g1
+        u_ref[0, b] = (outside + middle).astype(BF)
+        u_ref[1, b] = (outside - middle).astype(BF)
 
 
 def dot_back(v, w):
     return lax.dot_general(v, w, (((1,), (1,)), ((), ())), preferred_element_type=F32)
 
 
-def conv_back(g_ref, w_ref, face):
+def conv(v_ref, w_ref, u_ref, face, count, back=False):
     c = w_ref.shape[1]
-    acc = None
-    for a in range(3):
+    products = []
+    for k in range(4):
+        acc = None
         for b in range(3):
-            t = 3 * a + b
-            part = dot_back(window(g_ref, face, 2 - a, 2 - b), w_ref[t * c : (t + 1) * c])
+            v = v_ref[k, :, face : face + count, b : b + FS].reshape(-1, c)
+            col = 2 - b if back else b
+            if k in (0, 3):
+                t = 3 * (2 if (k == 3) != back else 0) + col
+                g = w_ref[t * c : (t + 1) * c]
+            else:
+                g = u_ref[k - 1, col]
+            part = dot_back(v, g) if back else jnp.dot(v, g, preferred_element_type=F32)
             acc = part if acc is None else acc + part
-    return acc
+        products.append(acc.reshape(FS // 2, count, FS, ROLL, c))
+    m0, m1, m2, m3 = products
+    even, odd = m0 + m1 + m2, m1 - m2 - m3
+    return [(odd if i % 2 else even)[i // 2] for i in range(FS)]
+
+
+def by_rows(ref, face, count, first_row, first_col):
+    cols = slice(first_col, first_col + FS)
+    rows = [ref[face : face + count, first_row + i, cols] for i in range(FS)]
+    return jnp.stack(rows).reshape(-1, ref.shape[-1])
 
 
 def outer(p, g):
@@ -115,10 +141,12 @@
     zero_corners(p_ref)
 
 
-def add_edges(e_ref, ids_ref, face, v):
-    for side, part in enumerate((v[0], v[:, FS - 1], v[FS - 1], v[:, 0])):
+def add_edges(e_ref, ids_ref, face, p_ref):
+    rows = cols = slice(1, FS + 1)
+    edges = (p_ref[face, 1, cols], p_ref[face, rows, FS], p_ref[face, FS, cols], p_ref[face, rows, 1])
+    for side, part in enumerate(edges):
         to = neighbour(ids_ref, side, face)
-        e_ref[to, side] = e_ref[to, side] + part
+        e_ref[to, side] = e_ref[to, side] + part.astype(F32)
 
 
 def fill_halo_back(e_ref, p_ref):
@@ -172,19 +200,28 @@
         row = stop
 
 
-def weight_grad(plan, ids_ref, p_ref, g, dst_ref):
-    c = p_ref.shape[-1]
-    for a in range(3):
-        for b in range(3):
-            part = outer(p_ref[:, a : a + FS, b : b + FS], g).astype(BF)
-            place_rows(plan, ids_ref, dst_ref, part, (3 * a + b) * c, plan.piece, 0)
+def weight_grad(plan, ids_ref, v_ref, g_ref, z_ref, dst_ref):
+    c = plan.c
+    halves = range(FS // 2)
+    cols = slice(1, FS + 1)
+    for t in halves:
+        y0, y1 = g_ref[:, 2 * t + 1, cols], g_ref[:, 2 * t + 2, cols]
+        z_ref[0, t] = y0
+        z_ref[1, t] = (y0 + y1) * 0.5
+        z_ref[2, t] = (y0 - y1) * 0.5
+        z_ref[3, t] = y1
+    for b in range(3):
+        m0, m1, m2, m3 = (outer(v_ref[k, :, :, b : b + FS], z_ref[k]) for k in range(4))
+        both = m1 + m2
+        for a, part in enumerate((m0 + both, m1 - m2, both - m3)):
+            place_rows(plan, ids_ref, dst_ref, part.astype(BF), (3 * a + b) * c, plan.piece, 0)
 
 
 def pack(plan, ids, one, two, skip):
     c = plan.c
     sizes = plan.sent
 
-    def kernel(ids_ref, one_hbm, two_hbm, skip_hbm, one_ref, two_ref, rows_ref, sem):
+    def kernel(ids_ref, one_hbm, two_hbm, skip_hbm, sent_ref, rows_ref, sem):
         loads = []
         at = 0
         for k, (hbm, rows) in enumerate(zip((one_hbm, two_hbm, skip_hbm), sizes)):
@@ -198,14 +235,13 @@
             load.start()
         for load in loads:
             load.wait()
-        one_ref[...] = rows_ref[: sizes[0]].astype(BF)
-        two_ref[...] = rows_ref[sizes[0] :].astype(BF)
+        sent_ref[...] = rows_ref[...].astype(BF)
 
     return pl.pallas_call(
         kernel,
         in_specs=[SMEM, HBM, HBM, HBM],
-        out_specs=[VMEM] * 2,
-        out_shape=[jax.ShapeDtypeStruct((v, c), BF) for v in (sizes[0], sizes[1] + sizes[2])],
+        out_specs=VMEM,
+        out_shape=jax.ShapeDtypeStruct((sum(sizes), c), BF),
         scratch_shapes=[pltpu.VMEM((sum(sizes), c), F32), pltpu.SemaphoreType.DMA((3,))],
         compiler_params=params(),
         cost_estimate=cost(0, 0.3),
@@ -280,7 +316,7 @@
             pltpu.SemaphoreType.DMA((FACES + 4,)),
         ],
         compiler_params=params(),
-        cost_estimate=cost(0.6, 9),
+        cost_estimate=cost(0, 0),
         name="enter",
     )(ids, in_hbm(x), in_hbm(cot), *(in_hbm(v) for v in weights), *after)
 
@@ -291,24 +327,30 @@
 
     def kernel(ids_ref, xp_ref, low_ref, *refs):
         near_refs, far_refs = refs[:count], refs[count : 2 * count]
-        hp_ref, slope_ref, w_ref = refs[2 * count :]
+        hp_ref, slope_ref, w_ref, u_ref, v_ref = refs[2 * count :]
         pieces = received(plan, ids_ref, near_refs, far_refs, 0, plan.sent[0], plan.shard)
         join_rows(plan, ids_ref, low_ref, pieces, w_ref, plan.shard)
-        for face in range(FACES):
-            hidden, slope = gelu_both(conv(xp_ref, w_ref, face))
-            hp_ref[face, 1 : FS + 1, 1 : FS + 1] = hidden.astype(BF).reshape(FS, FS, ROLL, c)
-            slope_ref[face] = slope.astype(BF).reshape(FS, FS, ROLL, c)
+        pair_weights(w_ref, u_ref)
+        for face in range(0, FACES, GROUP):
+            faces = slice(face, face + GROUP)
+            pair_rows(xp_ref, v_ref, face, GROUP)
+            for i, pre in enumerate(conv(v_ref, w_ref, u_ref, face, GROUP)):
+                hidden, slope = gelu_both(pre)
+                hp_ref[faces, i + 1, 1 : FS + 1] = hidden.astype(BF)
+                slope_ref[faces, i] = slope.astype(BF)
         fill_halo(ids_ref, hp_ref)
 
     return pl.pallas_call(
         kernel,
         in_specs=[SMEM] + [VMEM] * (2 + 2 * count),
-        out_specs=[VMEM] * 3,
+        out_specs=[VMEM] * 4,
         out_shape=[
             jax.ShapeDtypeStruct(padded(c), BF),
             field(c),
             jax.ShapeDtypeStruct((plan.conv, c), BF),
+            jax.ShapeDtypeStruct((2, 3, c, c), BF),
         ],
+        scratch_shapes=[pltpu.VMEM(pair_shape(c), BF)],
         compiler_params=params(),
         cost_estimate=cost(4.1, 12),
         name="first",
@@ -321,28 +363,32 @@
 
     def kernel(ids_ref, hp_ref, xp_ref, go_ref, dws_ref, low_ref, lows_ref, *refs):
         near_refs, far_refs = refs[:count], refs[count : 2 * count]
-        out_hbm, gp_ref, w_ref, ws_ref, keep_ref, send_ref = refs[2 * count : 2 * count + 6]
-        out_ref, e_ref, dw_ref, sem_out = refs[2 * count + 6 :]
-        pieces = received(plan, ids_ref, near_refs, far_refs, 0, plan.sent[1], plan.shard)
+        out_hbm, gp_ref, w_ref, u_ref, ws_ref, keep_ref, send_ref = refs[2 * count : 2 * count + 7]
+        out_ref, e_ref, dw_ref, v_ref, z_ref, sem_out = refs[2 * count + 7 :]
+        pieces = received(plan, ids_ref, near_refs, far_refs, plan.sent[0], plan.sent[1], plan.shard)
         join_rows(plan, ids_ref, low_ref, pieces, w_ref, plan.shard)
-        pieces = received(plan, ids_ref, near_refs, far_refs, *plan.sent[1:], plan.skip_shard)
+        at = plan.sent[0] + plan.sent[1]
+        pieces = received(plan, ids_ref, near_refs, far_refs, at, plan.sent[2], plan.skip_shard)
         join_rows(plan, ids_ref, lows_ref, pieces, ws_ref, plan.skip_shard)
         e_ref[...] = jnp.zeros_like(e_ref)
         place_rows(plan, ids_ref, dw_ref, dws_ref[...], 0, plan.skip_piece, plan.piece)
-        for face in range(FACES):
-            value, slope = gelu_both(conv(hp_ref, w_ref, face))
-            value = value + jnp.dot(
-                xp_ref[face, 1 : FS + 1, 1 : FS + 1].reshape(-1, c),
-                ws_ref[...],
-                preferred_element_type=F32,
-            )
-            out_ref[face] = value.astype(BF).reshape(FS, FS, ROLL, c)
-            low_grad = (go_ref[face].astype(F32) * slope.reshape(FS, FS, ROLL, c)).astype(BF)
-            gp_ref[face, 1 : FS + 1, 1 : FS + 1] = low_grad
-            add_edges(e_ref, ids_ref, face, low_grad.astype(F32))
+        pair_weights(w_ref, u_ref)
+        for face in range(0, FACES, GROUP):
+            faces = slice(face, face + GROUP)
+            pair_rows(hp_ref, v_ref, face, GROUP)
+            skip = jnp.dot(
+                by_rows(xp_ref, face, GROUP, 1, 1), ws_ref[...], preferred_element_type=F32
+            ).reshape(FS, GROUP, FS, ROLL, c)
+            for i, pre in enumerate(conv(v_ref, w_ref, u_ref, face, GROUP)):
+                value, slope = gelu_both(pre)
+                out_ref[faces, i] = (value + skip[i]).astype(BF)
+                low_grad = (go_ref[faces, i].astype(F32) * slope).astype(BF)
+                gp_ref[faces, i + 1, 1 : FS + 1] = low_grad
+            for one in range(face, face + GROUP):
+                add_edges(e_ref, ids_ref, one, gp_ref)
         store = pltpu.make_async_copy(out_ref, out_hbm, sem_out)
         store.start()
-        weight_grad(plan, ids_ref, hp_ref, gp_ref[:, 1 : FS + 1, 1 : FS + 1], dw_ref)
+        weight_grad(plan, ids_ref, v_ref, gp_ref, z_ref, dw_ref)
         keep_ref[...] = dw_ref[0]
         send_ref[...] = dw_ref[1]
         fill_halo_back(e_ref, gp_ref)
@@ -352,11 +398,12 @@
     return pl.pallas_call(
         kernel,
         in_specs=[SMEM] + [VMEM] * (6 + 2 * count),
-        out_specs=[HBM] + [VMEM] * 5,
+        out_specs=[HBM] + [VMEM] * 6,
         out_shape=[
             field(c),
             jax.ShapeDtypeStruct(padded(c), BF),
             jax.ShapeDtypeStruct((plan.conv, c), BF),
+            jax.ShapeDtypeStruct((2, 3, c, c), BF),
             jax.ShapeDtypeStruct((c, c), BF),
             sums,
             sums,
@@ -365,6 +412,8 @@
             pltpu.VMEM(field(c).shape, BF),
             edge_sums(c),
             pltpu.VMEM((2,) + sums.shape, BF),
+            pltpu.VMEM(pair_shape(c), BF),
+            pltpu.VMEM(grad_pairs(c), BF),
             pltpu.SemaphoreType.DMA,
         ],
         compiler_params=params(),
@@ -373,48 +422,42 @@
     )(ids, hp, xp, go, dws, low, low_skip, *near, *far)
 
 
-def hidden_back_kernel(ids_ref, gp_ref, w_ref, slope_ref, op_ref, e_ref):
-    c = w_ref.shape[1]
-    e_ref[...] = jnp.zeros_like(e_ref)
-    for face in range(FACES):
-        grad = conv_back(gp_ref, w_ref, face).reshape(FS, FS, ROLL, c)
-        low_grad = (grad * slope_ref[face].astype(F32)).astype(BF)
-        op_ref[face, 1 : FS + 1, 1 : FS + 1] = low_grad
-        add_edges(e_ref, ids_ref, face, low_grad.astype(F32))
-    fill_halo_back(e_ref, op_ref)
-
-
-def hidden_back(ids, gp, w, slope):
-    c = w.shape[1]
-    return pl.pallas_call(
-        hidden_back_kernel,
-        in_specs=[SMEM] + [VMEM] * 3,
-        out_specs=VMEM,
-        out_shape=jax.ShapeDtypeStruct(padded(c), BF),
-        scratch_shapes=[edge_sums(c)],
-        compiler_params=params(),
-        cost_estimate=cost(4.1, 9),
-        name="hidden_back",
-    )(ids, gp, w, slope)
-
-
-def first_grad(plan, ids, xp, op):
-    def kernel(ids_ref, xp_ref, op_ref, keep_ref, send_ref, dw_ref):
-        weight_grad(plan, ids_ref, xp_ref, op_ref[:, 1 : FS + 1, 1 : FS + 1], dw_ref)
+def hidden_back(plan, ids, gp, w, u, slope, xp, after):
+    c = plan.c
+
+    def kernel(ids_ref, gp_ref, w_ref, u_ref, slope_ref, xp_ref, _, op_ref, keep_ref, send_ref, *refs):
+        e_ref, v_ref, z_ref, dw_ref = refs
+        e_ref[...] = jnp.zeros_like(e_ref)
+        for face in range(0, FACES, GROUP):
+            faces = slice(face, face + GROUP)
+            pair_rows(gp_ref, v_ref, face, GROUP)
+            for i, grad in enumerate(conv(v_ref, w_ref, u_ref, face, GROUP, back=True)):
+                low_grad = (grad * slope_ref[faces, i].astype(F32)).astype(BF)
+                op_ref[faces, i + 1, 1 : FS + 1] = low_grad
+            for one in range(face, face + GROUP):
+                add_edges(e_ref, ids_ref, one, op_ref)
+        pair_rows(xp_ref, v_ref, 0, FACES)
+        weight_grad(plan, ids_ref, v_ref, op_ref, z_ref, dw_ref)
+        fill_halo_back(e_ref, op_ref)
         keep_ref[...] = dw_ref[0]
         send_ref[...] = dw_ref[1]
 
-    sums = jax.ShapeDtypeStruct((plan.tiles, plan.ranks, plan.piece, plan.c), BF)
+    sums = (plan.tiles, plan.ranks, plan.piece, c)
     return pl.pallas_call(
         kernel,
-        in_specs=[SMEM, VMEM, VMEM],
-        out_specs=[VMEM] * 2,
-        out_shape=[sums, sums],
-        scratch_shapes=[pltpu.VMEM((2,) + sums.shape, BF)],
+        in_specs=[SMEM] + [VMEM] * 6,
+        out_specs=[VMEM] * 3,
+        out_shape=[jax.ShapeDtypeStruct(v, BF) for v in (padded(c), sums, sums)],
+        scratch_shapes=[
+            edge_sums(c),
+            pltpu.VMEM(pair_shape(c), BF),
+            pltpu.VMEM(grad_pairs(c), BF),
+            pltpu.VMEM((2,) + sums, BF),
+        ],
         compiler_params=params(),
-        cost_estimate=cost(4.1, 9),
-        name="first_grad",
-    )(ids, xp, op)
+        cost_estimate=cost(0, 0),
+        name="hidden_back",
+    )(ids, gp, w, u, slope, xp, after)
 
 
 def tile_sums(plan, early, late):
@@ -440,31 +483,40 @@
     )(*early, *late)
 
 
-def inputs_back_kernel(gp_ref, w_ref, ws_ref, go_ref, out_hbm, out_ref, sem):
+def inputs_back_kernel(gp_ref, w_ref, u_ref, ws_ref, go_ref, out_hbm, out_ref, v_ref, sem):
     c = w_ref.shape[1]
     stores = []
-    for face in range(FACES):
-        grad = conv_back(gp_ref, w_ref, face)
-        grad = grad + dot_back(go_ref[face].reshape(-1, c), ws_ref[...])
-        out_ref[face] = grad.reshape(FS, FS, ROLL, c)
-        stores.append(pltpu.make_async_copy(out_ref.at[face], out_hbm.at[face], sem.at[face]))
-        stores[-1].start()
+    for face in range(0, FACES, GROUP):
+        faces = slice(face, face + GROUP)
+        pair_rows(gp_ref, v_ref, face, GROUP)
+        skip = dot_back(by_rows(go_ref, face, GROUP, 0, 0), ws_ref[...])
+        skip = skip.reshape(FS, GROUP, FS, ROLL, c)
+        for i, grad in enumerate(conv(v_ref, w_ref, u_ref, face, GROUP, back=True)):
+            out_ref[faces, i] = grad + skip[i]
+        part = pl.ds(face, GROUP)
+        copy = pltpu.make_async_copy(out_ref.at[part], out_hbm.at[part], sem.at[face // GROUP])
+        copy.start()
+        stores.append(copy)
     for store in stores:
         store.wait()
 
 
-def inputs_back(gp, w, ws, go):
+def inputs_back(gp, w, u, ws, go):
     c = w.shape[1]
     return pl.pallas_call(
         inputs_back_kernel,
-        in_specs=[VMEM] * 4,
-        out_specs=ANY,
+        in_specs=[VMEM] * 5,
+        out_specs=HBM,
         out_shape=field(c, F32),
-        scratch_shapes=[pltpu.VMEM(field(c).shape, F32), pltpu.SemaphoreType.DMA((FACES,))],
+        scratch_shapes=[
+            pltpu.VMEM(field(c).shape, F32),
+            pltpu.VMEM(pair_shape(c), BF),
+            pltpu.SemaphoreType.DMA((FACES // GROUP,)),
+        ],
         compiler_params=params(),
-        cost_estimate=cost(4.6, 10),
+        cost_estimate=cost(0, 0),
         name="inputs_back",
-    )(gp, w, ws, go)
+    )(gp, w, u, ws, go)
 
 
 def adamw(weight, moment, square, grad, rate):
@@ -587,37 +639,28 @@
         cot = jnp.transpose(cotangent[0], (1, 2, 3, 0, 4))
         places = jnp.stack([lax.axis_index(n) for n in ("core", "tile", "fsdp")]).astype(jnp.int32)
         weights = w_first, w_second, w_skip
-        groups = []
-        for sent in pack(plan, places, *weights):
-            own = jnp.stack([to_rank(sent, d) for d in range(1, ranks)])
-            groups.append([own])
-            if plan.split:
-                groups[-1] += [to_tile(own, e) for e in range(1, tiles)]
-        near1, near2 = groups
+        sent = pack(plan, places, *weights)
+        near = [jnp.stack([to_rank(sent, d) for d in range(1, ranks)])]
+        if plan.split:
+            near += [to_tile(near[0], e) for e in range(1, tiles)]
         ids = jnp.concatenate([places, lengths, face_table.T.reshape(-1)])
-        xp, go, dws, low1, low2, low3 = enter(plan, ids, x, cot, weights, (near1[0], near2[0]))
-        xp, near1 = lax.optimization_barrier((xp, near1))
-        far1 = [to_core(v) for v in near1]
-        hp, slope, w1 = first(plan, ids, xp, low1, near1, far1)
-        hp, near2 = lax.optimization_barrier((hp, near2))
-        far2 = [to_core(v) for v in near2]
-        hp, far2 = lax.optimization_barrier((hp, far2))
-        output, gp, w2, ws, keep2, away2 = second(
-            plan, ids, hp, xp, go, dws, low2, low3, near2, far2
+        xp, go, dws, low1, low2, low3 = enter(plan, ids, x, cot, weights, near[:1])
+        xp, near = lax.optimization_barrier((xp, near))
+        far = [to_core(v) for v in near]
+        hp, slope, w1, u1 = first(plan, ids, xp, low1, near, far)
+        output, gp, w2, u2, ws, keep2, away2 = second(
+            plan, ids, hp, xp, go, dws, low2, low3, near, far
         )
         came2 = to_core(away2)
-        op = hidden_back(ids, gp, w2, slope)
-        came2, op = lax.optimization_barrier((came2, op))
         parts2 = [total(keep2[d], came2[d]) for d in range(tiles)]
-        op, parts2 = lax.optimization_barrier((op, parts2))
+        op, keep1, away1 = hidden_back(plan, ids, gp, w2, u2, slope, xp, parts2[0])
         late = [parts2[0]] + [to_tile(parts2[d], d) for d in range(1, tiles)]
-        keep1, away1 = first_grad(plan, ids, xp, op)
         late, away1 = lax.optimization_barrier((late, away1))
         came1 = to_core(away1)
         parts1 = [total(keep1[d], came1[d]) for d in range(tiles)]
         op, parts1 = lax.optimization_barrier((op, parts1))
         early = [parts1[0]] + [to_tile(parts1[d], d) for d in range(1, tiles)]
-        grad_inputs = inputs_back(op, w1, ws, go)
+        grad_inputs = inputs_back(op, w1, u1, ws, go)
         early, late, grad_inputs = lax.optimization_barrier((early, late, grad_inputs))
         parts = tile_sums(plan, early, late)
         came = [to_rank(parts[d], d) for d in range(1, ranks)]

time: 99.2 us -> 93.5 us (0.943)
  waiting for transfers between devices: 17.8 us -> 28.1 us
  starting transfers between devices: 34.3 us -> 25.9 us
  Pallas kernels: 43.8 us -> 36.8 us
    ppermute x35 -> x25, waiting for transfers between devices: 17.8 us -> 28.1 us  [send(): return lax.ppermute(v, axis, pairs)]
    ppermute x35 -> x25, starting transfers between devices: 34.3 us -> 25.9 us  [send(): return lax.ppermute(v, axis, pairs)]
    pallas_call x4 -> x3, Pallas kernels: 17.8 us -> 13.6 us  [the longest x1 7.41 us: hidden_back(): pl.pallas_call(kernel, in_specs=[SMEM] + [VMEM] * 6, out_specs=[VMEM] * 3...]
    pallas_call x1, Pallas kernels: 12.8 us -> 10.9 us  [second(): pl.pallas_call(kernel, in_specs=[SMEM] + [VMEM] * (6 + 2 * count), out_sp...]
  transfers between devices with their start and end apart: 35 -> 25, of which waited for: 14 -> 18; matrix products, arithmetic and copies ran while one was open for 1% -> 0% of each run, Pallas kernels for 26% -> 17%
where the time goes in v4:
time: 93.5 us; the launch traced here: 93.3 us
  Pallas kernels  36.8 us (39%)
  waiting for transfers between devices  28.1 us (30%)
  starting transfers between devices  25.9 us (28%)
  between operations  1.75 us (2%)
    ppermute x25, waiting for transfers between devices, send(): return lax.ppermute(v, axis, pairs)  28.1 us
    ppermute x25, starting transfers between devices, send(): return lax.ppermute(v, axis, pairs)  25.9 us
    pallas_call x1, Pallas kernels, second(): pl.pallas_call(kernel, in_specs=[SMEM] + [VMEM] * (6 + 2 * count), out_sp...  10.9 us
    pallas_call x1, Pallas kernels, hidden_back(): pl.pallas_call(kernel, in_specs=[SMEM] + [VMEM] * 6, out_specs=[VMEM] * 3...  7.41 us
    pallas_call x1, Pallas kernels, first(): pl.pallas_call(kernel, in_specs=[SMEM] + [VMEM] * (2 + 2 * count), out_sp...  5.34 us
    pallas_call x1, Pallas kernels, inputs_back(): pl.pallas_call(inputs_back_kernel, in_specs=[VMEM] * 5, out_specs=HBM, ou...  4.66 us
    pallas_call x1, Pallas kernels, enter(): pl.pallas_call(kernel, in_specs=[SMEM] + [HBM] * 5 + [VMEM] * len(after),...  3.54 us
    pallas_call x1, Pallas kernels, update(): pl.pallas_call(kernel, in_specs=[SMEM] + [VMEM] * 11, out_specs=[HBM] * 9...  3.32 us
  transfers between devices with their start and end apart: 25, of which 18 were waited for; matrix products, arithmetic and copies ran while one was open for 0% of the time, Pallas kernels for 17%

profile of v4, /device:TPU:0, one launch (start us, length us, event | category | flops | bytes accessed | tf_op | source)
XLA Modules:
  0.0 93.3 jit_solution(3179287488086406948)
XLA Ops:
  0.7 1.5 %pack.1 = bf16[152,256]{1,0:T(8,128)(2,1)S(1)} custom-call(s32[3]{0:T(128)S(1)} %pad_add_fusion.ids_ref, f32[576,256]{1,0:T(8,128)} %refs_2_.3, f32[576,256]{1,0:T(8,128)} %refs_5_.1, f32[64,256]{1,0:T(8,128)} %refs_8_.1), custom_call_target="tpu_custom_call" | custom-call | bytes 300000 | tf_op jit(solution)/shard_map/pack/pallas_call | solution.py:240
  2.2 5.1 %collective-permute-start.2 = (bf16[152,256]{1,0:T(8,128)(2,1)S(1)}, bf16[152,256]{1,0:T(8,128)(2,1)S(1)}, u32[]{:S(2)}, u32[]{:S(2)}) collective-permute-start(bf16[152,256]{1,0:T(8,128)(2,1)S(1)} %pack.1), channel_id=1, source_target_pairs={{0,3},{1,0},{2,1},{3,2},{4,7},{5,4},{6,5},{7,6},{8,11},{9,8},{10,9... | collective-permute-start | bytes 233480 | tf_op jit(solution)/shard_map/ppermute | solution.py:600
  7.4 1.0 %collective-permute-start = (bf16[152,256]{1,0:T(8,128)(2,1)S(1)}, bf16[152,256]{1,0:T(8,128)(2,1)S(1)}, u32[]{:S(2)}, u32[]{:S(2)}) collective-permute-start(bf16[152,256]{1,0:T(8,128)(2,1)S(1)} %pack.1), channel_id=1, source_target_pairs={{0,1},{1,2},{2,3},{3,0},{4,5},{5,6},{6,7},{7,4},{8,9},{9,10},{10,1... | collective-permute-start | bytes 233480 | tf_op jit(solution)/shard_map/ppermute | solution.py:600
  8.4 1.7 %collective-permute-done.2 = bf16[152,256]{1,0:T(8,128)(2,1)S(1)} collective-permute-done((bf16[152,256]{1,0:T(8,128)(2,1)S(1)}, bf16[152,256]{1,0:T(8,128)(2,1)S(1)}, u32[]{:S(2)}, u32[]{:S(2)}) %collective-permute-start.2) | collective-permute-done | bytes 77856 | tf_op jit(solution)/shard_map/ppermute | solution.py:600
  10.1 4.5 %collective-permute-done.1 = bf16[152,256]{1,0:T(8,128)(2,1)S(1)} collective-permute-done((bf16[152,256]{1,0:T(8,128)(2,1)S(1)}, bf16[152,256]{1,0:T(8,128)(2,1)S(1)}, u32[]{:S(2)}, u32[]{:S(2)}) %collective-permute-start.1) | collective-permute-done | bytes 77856 | tf_op jit(solution)/shard_map/ppermute | solution.py:600
  14.6 2.5 %collective-permute-start.5 = (bf16[3,152,256]{2,1,0:T(8,128)(2,1)S(1)}, bf16[3,152,256]{2,1,0:T(8,128)(2,1)S(1)}, u32[]{:S(2)}, u32[]{:S(2)}) collective-permute-start(bf16[3,152,256]{2,1,0:T(8,128)(2,1)S(1)} %pad_maximum_fusion.1.refs_3_.refs_0_), channel_id=1, source_target_pairs={{0,24},{8,16},{16,8},{24,0},{1,25},{9,17},{17,9},{25,1},{2,26},{10... | collective-permute-start | bytes 700424 | tf_op jit(solution)/shard_map/ppermute | solution.py:600
  17.1 0.5 collective-permute-start.4
  17.6 0.5 collective-permute-start.3
  18.9 0.1 concatenate.4.ids_ref
  19.0 3.5 %enter.1 = (bf16[12,8,8,8,256]{4,3,2,1,0:T(8,128)(2,1)S(1)}, bf16[12,6,6,8,256]{4,3,2,1,0:T(8,128)(2,1)S(1)}, bf16[256,256]{1,0:T(8,128)(2,1)S(1)}, bf16[576,256...) custom-call(s32[52]{0:T(128)S(1)} %concatenate.4.ids_ref, ...), custom_call_target="tpu_custom_call" | custom-call | tf_op jit(solution)/shard_map/enter/pallas_call | solution.py:303
  22.5 1.7 %collective-permute-done.5.refs_3_ = bf16[3,152,256]{2,1,0:T(8,128)(2,1)S(1)} collective-permute-done((bf16[3,152,256]{2,1,0:T(8,128)(2,1)S(1)}, bf16[3,152,256]{2,1,0:T(8,128)(2,1)S(1)}, u32[]{:S(2)}, u32[]{:S(2)}) %collective-permute-start.5) | collective-permute-done | bytes 233504 | tf_op jit(solution)/shard_map/ppermute | solution.py:600
  24.2 3.8 %collective-permute-done.4.refs_2_ = bf16[3,152,256]{2,1,0:T(8,128)(2,1)S(1)} collective-permute-done((bf16[3,152,256]{2,1,0:T(8,128)(2,1)S(1)}, bf16[3,152,256]{2,1,0:T(8,128)(2,1)S(1)}, u32[]{:S(2)}, u32[]{:S(2)}) %collective-permute-start.4) | collective-permute-done | bytes 233504 | tf_op jit(solution)/shard_map/ppermute | solution.py:600
  28.0 0.1 collective-permute-done.3.refs_1_
  28.1 0.5 collective-permute-start.7
  28.6 0.5 collective-permute-start.9
  29.1 0.5 collective-permute-done.6.refs_4_
  29.6 0.3 collective-permute-done.7.refs_5_
  29.9 0.3 collective-permute-done.8.refs_6_
  30.2 0.3 collective-permute-done.9.refs_7_
  30.6 5.3 %first.1 = (bf16[12,8,8,8,256]{4,3,2,1,0:T(8,128)(2,1)S(1)}, bf16[12,6,6,8,256]{4,3,2,1,0:T(8,128)(2,1)S(1)}, bf16[2304,256]{1,0:T(8,128)(2,1)S(1)}, bf16[2,3,256,256]{3,2,1,0:T(8,128)(2,1)S(1)}) custom-call(s32[52]{0:T(128)S(1)} %concatenate.4.ids_ref, bf16[12,8,8,8,256]{4,3,2,1,0:T(8,128)(2,1)S(1)} %get-tuple-element.69.xp_ref, ...), custom_call_target="tpu_custom_call" | custom-call | flops 4100000000 | bytes 12000000 | tf_op jit(solution)/shard_map/first/pallas_call | solution.py:343
  35.9 10.9 %second.1 = (bf16[12,6,6,8,256]{4,3,2,1,0:T(8,128)(2,1)}, bf16[12,8,8,8,256]{4,3,2,1,0:T(8,128)(2,1)S(1)}, bf16[2304,256]{1,0:T(8,128)(2,1)S(1)}, bf16[2,3,256,2...) custom-call(s32[52]{0:T(128)S(1)} %concatenate.4.ids_ref, ...), custom_call_target="tpu_custom_call" | custom-call | flops 8999999488 | bytes 16000000 | tf_op jit(solution)/shard_map/second/pallas_call | solution.py:398
  46.8 0.2 collective-permute-start.10
  47.1 1.9 %collective-permute-done.10 = bf16[4,4,80,256]{3,2,1,0:T(8,128)(2,1)S(1)} collective-permute-done((bf16[4,4,80,256]{3,2,1,0:T(8,128)(2,1)S(1)}, bf16[4,4,80,256]{3,2,1,0:T(8,128)(2,1)S(1)}, u32[]{:S(2)}, u32[]{:S(2)}) %collective-permute-start.10) | collective-permute-done | bytes 655392 | tf_op jit(solution)/shard_map/ppermute | solution.py:600
  49.0 0.2 fusion.3
  49.1 1.7 %collective-permute-start.13 = (bf16[4,80,256]{2,1,0:T(8,128)(2,1)S(1)}, bf16[4,80,256]{2,1,0:T(8,128)(2,1)S(1)}, u32[]{:S(2)}, u32[]{:S(2)}) collective-permute-start(bf16[4,80,256]{2,1,0:T(8,128)(2,1)S(1)} %get-tuple-element.125), channel_id=1, source_target_pairs={{0,24},{8,16},{16,8},{24,0},{1,25},{9,17},{17,9},{25,1},{2,26},{10... | collective-permute-start | bytes 491528 | tf_op jit(solution)/shard_map/ppermute | solution.py:600
  50.9 1.3 %collective-permute-start.12 = (bf16[4,80,256]{2,1,0:T(8,128)(2,1)S(1)}, bf16[4,80,256]{2,1,0:T(8,128)(2,1)S(1)}, u32[]{:S(2)}, u32[]{:S(2)}) collective-permute-start(bf16[4,80,256]{2,1,0:T(8,128)(2,1)S(1)} %get-tuple-element.126), channel_id=1, source_target_pairs={{0,16},{8,24},{16,0},{24,8},{1,17},{9,25},{17,1},{25,9},{2,18},{10... | collective-permute-start | bytes 491528 | tf_op jit(solution)/shard_map/ppermute | solution.py:600
  52.2 0.5 collective-permute-start.11
  52.7 7.4 %hidden_back.1 = (bf16[12,8,8,8,256]{4,3,2,1,0:T(8,128)(2,1)S(1)}, bf16[4,4,72,256]{3,2,1,0:T(8,128)(2,1)S(1)}, bf16[4,4,72,256]{3,2,1,0:T(8,128)(2,1)S(1)}) custom-call(s32[52]{0:T(128)S(1)} %concatenate.4.ids_ref, bf16[12,8,8,8,256]{4,3,2,1,0:T(8,128)(2,1)S(1)} %get-tuple-element.81.gp_ref, bf16[2304,256]{1,0:T(8,128)(2,1)S(1)} %get-tuple-element.82.w_ref, ...), custom_call_target="tpu_custom_call" | custom-call | tf_op jit(solution)/shard_map/hidden_back/pallas_call | solution.py:446
  60.2 2.0 %collective-permute-done.14 = bf16[4,4,72,256]{3,2,1,0:T(8,128)(2,1)S(1)} collective-permute-done((bf16[4,4,72,256]{3,2,1,0:T(8,128)(2,1)S(1)}, bf16[4,4,72,256]{3,2,1,0:T(8,128)(2,1)S(1)}, u32[]{:S(2)}, u32[]{:S(2)}) %collective-permute-start.14) | collective-permute-done | bytes 589856 | tf_op jit(solution)/shard_map/ppermute | solution.py:600
  62.2 0.2 fusion.7
  62.4 1.6 %collective-permute-start.15 = (bf16[4,72,256]{2,1,0:T(8,128)(2,1)S(1)}, bf16[4,72,256]{2,1,0:T(8,128)(2,1)S(1)}, u32[]{:S(2)}, u32[]{:S(2)}) collective-permute-start(bf16[4,72,256]{2,1,0:T(8,128)(2,1)S(1)} %get-tuple-element.92), channel_id=1, source_target_pairs={{0,8},{8,0},{16,24},{24,16},{1,9},{9,1},{17,25},{25,17},{2,10},{10... | collective-permute-start | bytes 442376 | tf_op jit(solution)/shard_map/ppermute | solution.py:600
  63.9 0.7 collective-permute-start.16
  64.7 1.3 %collective-permute-start.17 = (bf16[4,72,256]{2,1,0:T(8,128)(2,1)S(1)}, bf16[4,72,256]{2,1,0:T(8,128)(2,1)S(1)}, u32[]{:S(2)}, u32[]{:S(2)}) collective-permute-start(bf16[4,72,256]{2,1,0:T(8,128)(2,1)S(1)} %get-tuple-element.94), channel_id=1, source_target_pairs={{0,24},{8,16},{16,8},{24,0},{1,25},{9,17},{17,9},{25,1},{2,26},{10... | collective-permute-start | bytes 442376 | tf_op jit(solution)/shard_map/ppermute | solution.py:600
  65.9 4.7 %inputs_back.1 = f32[12,6,6,8,256]{4,3,2,1,0:T(8,128)} custom-call(bf16[12,8,8,8,256]{4,3,2,1,0:T(8,128)(2,1)S(1)} %get-tuple-element.99.gp_ref, bf16[2304,256]{1,0:T(8,128)(2,1)S(1)} %get-tuple-element.100.w_ref, bf16[2,3,256,256]{3,2,1,0:T(8,128)(2,1)S(1)} %get-tuple-element.101.u_ref, bf16[256,256]{1,0:T(8,128)(2,1)S(1)} %get-tuple-element.102.ws_ref, ...), custom_call_target="tpu_custom_call" | custom-call | tf_op jit(solution)/shard_map/inputs_back/pallas_call | solution.py:506
  70.7 2.0 %collective-permute-done.16.refs_2_ = bf16[4,72,256]{2,1,0:T(8,128)(2,1)S(1)} collective-permute-done((bf16[4,72,256]{2,1,0:T(8,128)(2,1)S(1)}, bf16[4,72,256]{2,1,0:T(8,128)(2,1)S(1)}, u32[]{:S(2)}, u32[]{:S(2)}) %collective-permute-start.16) | collective-permute-done | bytes 147488 | tf_op jit(solution)/shard_map/ppermute | solution.py:600
  72.7 0.2 tile_sums.1
  72.9 1.2 %collective-permute-start.19 = (bf16[152,256]{1,0:T(8,128)(2,1)S(1)}, bf16[152,256]{1,0:T(8,128)(2,1)S(1)}, u32[]{:S(2)}, u32[]{:S(2)}) collective-permute-start(bf16[152,256]{1,0:T(8,128)(2,1)S(1)} %get-tuple-element.114), channel_id=1, source_target_pairs={{0,2},{1,3},{2,0},{3,1},{4,6},{5,7},{6,4},{7,5},{8,10},{9,11},{10,... | collective-permute-start | bytes 233480 | tf_op jit(solution)/shard_map/ppermute | solution.py:600
  74.2 2.8 %collective-permute-start.20 = (bf16[152,256]{1,0:T(8,128)(2,1)S(1)}, bf16[152,256]{1,0:T(8,128)(2,1)S(1)}, u32[]{:S(2)}, u32[]{:S(2)}) collective-permute-start(bf16[152,256]{1,0:T(8,128)(2,1)S(1)} %get-tuple-element.115), channel_id=1, source_target_pairs={{0,3},{1,0},{2,1},{3,2},{4,7},{5,4},{6,5},{7,6},{8,11},{9,8},{10,9... | collective-permute-start | bytes 233480 | tf_op jit(solution)/shard_map/ppermute | solution.py:600
  77.0 2.7 %collective-permute-done.18 = bf16[152,256]{1,0:T(8,128)(2,1)S(1)} collective-permute-done((bf16[152,256]{1,0:T(8,128)(2,1)S(1)}, bf16[152,256]{1,0:T(8,128)(2,1)S(1)}, u32[]{:S(2)}, u32[]{:S(2)}) %collective-permute-start.18) | collective-permute-done | bytes 77856 | tf_op jit(solution)/shard_map/ppermute | solution.py:600
  79.7 1.6 %collective-permute-done.19 = bf16[152,256]{1,0:T(8,128)(2,1)S(1)} collective-permute-done((bf16[152,256]{1,0:T(8,128)(2,1)S(1)}, bf16[152,256]{1,0:T(8,128)(2,1)S(1)}, u32[]{:S(2)}, u32[]{:S(2)}) %collective-permute-start.19) | collective-permute-done | bytes 77856 | tf_op jit(solution)/shard_map/ppermute | solution.py:600
  81.4 1.6 %collective-permute-start.23 = (bf16[152,256]{1,0:T(8,128)(2,1)S(1)}, bf16[152,256]{1,0:T(8,128)(2,1)S(1)}, u32[]{:S(2)}, u32[]{:S(2)}) collective-permute-start(bf16[152,256]{1,0:T(8,128)(2,1)S(1)} %add_convert_fusion.8), channel_id=1, source_target_pairs={{0,24},{8,16},{16,8},{24,0},{1,25},{9,17},{17,9},{25,1},{2,26},{10... | collective-permute-start | bytes 233480 | tf_op jit(solution)/shard_map/ppermute | solution.py:600
  82.9 0.7 collective-permute-start.22
  83.6 1.3 %collective-permute-start.21 = (bf16[152,256]{1,0:T(8,128)(2,1)S(1)}, bf16[152,256]{1,0:T(8,128)(2,1)S(1)}, u32[]{:S(2)}, u32[]{:S(2)}) collective-permute-start(bf16[152,256]{1,0:T(8,128)(2,1)S(1)} %add_convert_fusion.8), channel_id=1, source_target_pairs={{0,8},{8,0},{16,24},{24,16},{1,9},{9,1},{17,25},{25,17},{2,10},{10... | collective-permute-start | bytes 233480 | tf_op jit(solution)/shard_map/ppermute | solution.py:600
  84.9 1.8 %collective-permute-done.23 = bf16[152,256]{1,0:T(8,128)(2,1)S(1)} collective-permute-done((bf16[152,256]{1,0:T(8,128)(2,1)S(1)}, bf16[152,256]{1,0:T(8,128)(2,1)S(1)}, u32[]{:S(2)}, u32[]{:S(2)}) %collective-permute-start.23) | collective-permute-done | bytes 77856 | tf_op jit(solution)/shard_map/ppermute | solution.py:600
  86.7 0.8 collective-permute-done.22
  87.5 0.5 collective-permute-done.21
  88.2 1.6 %collective-permute-done.24.refs_1_ = bf16[4,152,256]{2,1,0:T(8,128)(2,1)S(1)} collective-permute-done((bf16[4,152,256]{2,1,0:T(8,128)(2,1)S(1)}, bf16[4,152,256]{2,1,0:T(8,128)(2,1)S(1)}, u32[]{:S(2)}, u32[]{:S(2)}) %collective-permute-start.24) | collective-permute-done | bytes 311328 | tf_op jit(solution)/shard_map/ppermute | solution.py:600
  89.8 3.3 %update.1 = (f32[576,256]{1,0:T(8,128)}, f32[576,256]{1,0:T(8,128)}, f32[576,256]{1,0:T(8,128)}, f32[576,256]{1,0:T(8,128)}, f32[576,256]{1,0:T(8,128)}, /*index...) custom-call(s32[52]{0:T(128)S(1)} %concatenate.4.ids_ref, ...), custom_call_target="tpu_custom_call" | custom-call | bytes 9000000 | tf_op jit(solution)/shard_map/update/pallas_call | solution.py:579
  (38 shorter events, 0.6 us)
Async XLA Ops:
  0.6 18.2 %copy-start.9 = (s32[12,4]{0,1:T(4,128)S(1)}, s32[12,4]{0,1:T(4,128)}, u32[]{:S(2)}) copy-start(s32[12,4]{0,1:T(4,128)} %param.16) | copy-start | bytes 580
  2.2 7.9 %collective-permute-start.2 = (bf16[152,256]{1,0:T(8,128)(2,1)S(1)}, bf16[152,256]{1,0:T(8,128)(2,1)S(1)}, u32[]{:S(2)}, u32[]{:S(2)}) collective-permute-start(bf16[152,256]{1,0:T(8,128)(2,1)S(1)} %pack.1), channel_id=1, source_target_pairs={{0,3},{1,0},{2,1},{3,2},{4,7},{5,4},{6,5},{7,6},{8,11},{9,8},{10,9... | collective-permute-start | bytes 233480 | tf_op jit(solution)/shard_map/ppermute | solution.py:600
  7.3 7.2 %collective-permute-start.1 = (bf16[152,256]{1,0:T(8,128)(2,1)S(1)}, bf16[152,256]{1,0:T(8,128)(2,1)S(1)}, u32[]{:S(2)}, u32[]{:S(2)}) collective-permute-start(bf16[152,256]{1,0:T(8,128)(2,1)S(1)} %pack.1), channel_id=1, source_target_pairs={{0,2},{1,3},{2,0},{3,1},{4,6},{5,7},{6,4},{7,5},{8,10},{9,11},{10,... | collective-permute-start | bytes 233480 | tf_op jit(solution)/shard_map/ppermute | solution.py:600
  7.4 7.2 %collective-permute-start = (bf16[152,256]{1,0:T(8,128)(2,1)S(1)}, bf16[152,256]{1,0:T(8,128)(2,1)S(1)}, u32[]{:S(2)}, u32[]{:S(2)}) collective-permute-start(bf16[152,256]{1,0:T(8,128)(2,1)S(1)} %pack.1), channel_id=1, source_target_pairs={{0,1},{1,2},{2,3},{3,0},{4,5},{5,6},{6,7},{7,4},{8,9},{9,10},{10,1... | collective-permute-start | bytes 233480 | tf_op jit(solution)/shard_map/ppermute | solution.py:600
  14.6 9.6 %collective-permute-start.5 = (bf16[3,152,256]{2,1,0:T(8,128)(2,1)S(1)}, bf16[3,152,256]{2,1,0:T(8,128)(2,1)S(1)}, u32[]{:S(2)}, u32[]{:S(2)}) collective-permute-start(bf16[3,152,256]{2,1,0:T(8,128)(2,1)S(1)} %pad_maximum_fusion.1.refs_3_.refs_0_), channel_id=1, source_target_pairs={{0,24},{8,16},{16,8},{24,0},{1,25},{9,17},{17,9},{25,1},{2,26},{10... | collective-permute-start | bytes 700424 | tf_op jit(solution)/shard_map/ppermute | solution.py:600
  17.1 10.9 %collective-permute-start.4 = (bf16[3,152,256]{2,1,0:T(8,128)(2,1)S(1)}, bf16[3,152,256]{2,1,0:T(8,128)(2,1)S(1)}, u32[]{:S(2)}, u32[]{:S(2)}) collective-permute-start(bf16[3,152,256]{2,1,0:T(8,128)(2,1)S(1)} %pad_maximum_fusion.1.refs_3_.refs_0_), channel_id=1, source_target_pairs={{0,16},{8,24},{16,0},{24,8},{1,17},{9,25},{17,1},{25,9},{2,18},{10... | collective-permute-start | bytes 700424 | tf_op jit(solution)/shard_map/ppermute | solution.py:600
  17.6 10.5 %collective-permute-start.3 = (bf16[3,152,256]{2,1,0:T(8,128)(2,1)S(1)}, bf16[3,152,256]{2,1,0:T(8,128)(2,1)S(1)}, u32[]{:S(2)}, u32[]{:S(2)}) collective-permute-start(bf16[3,152,256]{2,1,0:T(8,128)(2,1)S(1)} %pad_maximum_fusion.1.refs_3_.refs_0_), channel_id=1, source_target_pairs={{0,8},{8,0},{16,24},{24,16},{1,9},{9,1},{17,25},{25,17},{2,10},{10... | collective-permute-start | bytes 700424 | tf_op jit(solution)/shard_map/ppermute | solution.py:600
  28.1 1.5 %collective-permute-start.6 = (bf16[3,152,256]{2,1,0:T(8,128)(2,1)S(1)}, bf16[3,152,256]{2,1,0:T(8,128)(2,1)S(1)}, u32[]{:S(2)}, u32[]{:S(2)}) collective-permute-start(bf16[3,152,256]{2,1,0:T(8,128)(2,1)S(1)} %pad_maximum_fusion.1.refs_3_.refs_0_), channel_id=1, source_target_pairs={{0,4},{4,0},{1,5},{5,1},{2,6},{6,2},{3,7},{7,3},{8,12},{12,8},{9,1... | collective-permute-start | bytes 700424 | tf_op jit(solution)/shard_map/ppermute | solution.py:600
  28.1 1.8 %collective-permute-start.7 = (bf16[3,152,256]{2,1,0:T(8,128)(2,1)S(1)}, bf16[3,152,256]{2,1,0:T(8,128)(2,1)S(1)}, u32[]{:S(2)}, u32[]{:S(2)}) collective-permute-start(bf16[3,152,256]{2,1,0:T(8,128)(2,1)S(1)} %collective-permute-done.3.refs_1_), channel_id=1, source_target_pairs={{0,4},{4,0},{1,5},{5,1},{2,6},{6,2},{3,7},{7,3},{8,12},{12,8},{9,1... | collective-permute-start | bytes 700424 | tf_op jit(solution)/shard_map/ppermute | solution.py:600
  28.6 1.7 %collective-permute-start.8 = (bf16[3,152,256]{2,1,0:T(8,128)(2,1)S(1)}, bf16[3,152,256]{2,1,0:T(8,128)(2,1)S(1)}, u32[]{:S(2)}, u32[]{:S(2)}) collective-permute-start(bf16[3,152,256]{2,1,0:T(8,128)(2,1)S(1)} %collective-permute-done.4.refs_2_), channel_id=1, source_target_pairs={{0,4},{4,0},{1,5},{5,1},{2,6},{6,2},{3,7},{7,3},{8,12},{12,8},{9,1... | collective-permute-start | bytes 700424 | tf_op jit(solution)/shard_map/ppermute | solution.py:600
  28.6 2.0 %collective-permute-start.9 = (bf16[3,152,256]{2,1,0:T(8,128)(2,1)S(1)}, bf16[3,152,256]{2,1,0:T(8,128)(2,1)S(1)}, u32[]{:S(2)}, u32[]{:S(2)}) collective-permute-start(bf16[3,152,256]{2,1,0:T(8,128)(2,1)S(1)} %collective-permute-done.5.refs_3_), channel_id=1, source_target_pairs={{0,4},{4,0},{1,5},{5,1},{2,6},{6,2},{3,7},{7,3},{8,12},{12,8},{9,1... | collective-permute-start | bytes 700424 | tf_op jit(solution)/shard_map/ppermute | solution.py:600
  46.8 2.2 %collective-permute-start.10 = (bf16[4,4,80,256]{3,2,1,0:T(8,128)(2,1)S(1)}, bf16[4,4,80,256]{3,2,1,0:T(8,128)(2,1)S(1)}, u32[]{:S(2)}, u32[]{:S(2)}) collective-permute-start(bf16[4,4,80,256]{3,2,1,0:T(8,128)(2,1)S(1)} %get-tuple-element.86), channel_id=1, source_target_pairs={{0,4},{4,0},{1,5},{5,1},{2,6},{6,2},{3,7},{7,3},{8,12},{12,8},{9,1... | collective-permute-start | bytes 1966088 | tf_op jit(solution)/shard_map/ppermute | solution.py:600
  49.1 11.0 %collective-permute-start.13 = (bf16[4,80,256]{2,1,0:T(8,128)(2,1)S(1)}, bf16[4,80,256]{2,1,0:T(8,128)(2,1)S(1)}, u32[]{:S(2)}, u32[]{:S(2)}) collective-permute-start(bf16[4,80,256]{2,1,0:T(8,128)(2,1)S(1)} %get-tuple-element.125), channel_id=1, source_target_pairs={{0,24},{8,16},{16,8},{24,0},{1,25},{9,17},{17,9},{25,1},{2,26},{10... | collective-permute-start | bytes 491528 | tf_op jit(solution)/shard_map/ppermute | solution.py:600
  50.9 9.3 %collective-permute-start.12 = (bf16[4,80,256]{2,1,0:T(8,128)(2,1)S(1)}, bf16[4,80,256]{2,1,0:T(8,128)(2,1)S(1)}, u32[]{:S(2)}, u32[]{:S(2)}) collective-permute-start(bf16[4,80,256]{2,1,0:T(8,128)(2,1)S(1)} %get-tuple-element.126), channel_id=1, source_target_pairs={{0,16},{8,24},{16,0},{24,8},{1,17},{9,25},{17,1},{25,9},{2,18},{10... | collective-permute-start | bytes 491528 | tf_op jit(solution)/shard_map/ppermute | solution.py:600
  52.2 8.0 %collective-permute-start.11 = (bf16[4,80,256]{2,1,0:T(8,128)(2,1)S(1)}, bf16[4,80,256]{2,1,0:T(8,128)(2,1)S(1)}, u32[]{:S(2)}, u32[]{:S(2)}) collective-permute-start(bf16[4,80,256]{2,1,0:T(8,128)(2,1)S(1)} %get-tuple-element.127), channel_id=1, source_target_pairs={{0,8},{8,0},{16,24},{24,16},{1,9},{9,1},{17,25},{25,17},{2,10},{10... | collective-permute-start | bytes 491528 | tf_op jit(solution)/shard_map/ppermute | solution.py:600
  60.1 2.1 %collective-permute-start.14 = (bf16[4,4,72,256]{3,2,1,0:T(8,128)(2,1)S(1)}, bf16[4,4,72,256]{3,2,1,0:T(8,128)(2,1)S(1)}, u32[]{:S(2)}, u32[]{:S(2)}) collective-permute-start(bf16[4,4,72,256]{3,2,1,0:T(8,128)(2,1)S(1)} %get-tuple-element.90), channel_id=1, source_target_pairs={{0,4},{4,0},{1,5},{5,1},{2,6},{6,2},{3,7},{7,3},{8,12},{12,8},{9,1... | collective-permute-start | bytes 1769480 | tf_op jit(solution)/shard_map/ppermute | solution.py:600
  62.4 8.3 %collective-permute-start.15 = (bf16[4,72,256]{2,1,0:T(8,128)(2,1)S(1)}, bf16[4,72,256]{2,1,0:T(8,128)(2,1)S(1)}, u32[]{:S(2)}, u32[]{:S(2)}) collective-permute-start(bf16[4,72,256]{2,1,0:T(8,128)(2,1)S(1)} %get-tuple-element.92), channel_id=1, source_target_pairs={{0,8},{8,0},{16,24},{24,16},{1,9},{9,1},{17,25},{25,17},{2,10},{10... | collective-permute-start | bytes 442376 | tf_op jit(solution)/shard_map/ppermute | solution.py:600
  63.9 8.8 %collective-permute-start.16 = (bf16[4,72,256]{2,1,0:T(8,128)(2,1)S(1)}, bf16[4,72,256]{2,1,0:T(8,128)(2,1)S(1)}, u32[]{:S(2)}, u32[]{:S(2)}) collective-permute-start(bf16[4,72,256]{2,1,0:T(8,128)(2,1)S(1)} %get-tuple-element.93), channel_id=1, source_target_pairs={{0,16},{8,24},{16,0},{24,8},{1,17},{9,25},{17,1},{25,9},{2,18},{10... | collective-permute-start | bytes 442376 | tf_op jit(solution)/shard_map/ppermute | solution.py:600
  64.7 8.0 %collective-permute-start.17 = (bf16[4,72,256]{2,1,0:T(8,128)(2,1)S(1)}, bf16[4,72,256]{2,1,0:T(8,128)(2,1)S(1)}, u32[]{:S(2)}, u32[]{:S(2)}) collective-permute-start(bf16[4,72,256]{2,1,0:T(8,128)(2,1)S(1)} %get-tuple-element.94), channel_id=1, source_target_pairs={{0,24},{8,16},{16,8},{24,0},{1,25},{9,17},{17,9},{25,1},{2,26},{10... | collective-permute-start | bytes 442376 | tf_op jit(solution)/shard_map/ppermute | solution.py:600
  65.9 23.8 %copy-start.4 = (f32[576,256]{1,0:T(8,128)S(1)}, f32[576,256]{1,0:T(8,128)}, u32[]{:S(2)}) copy-start(f32[576,256]{1,0:T(8,128)} %refs_4_.1) | copy-start | bytes 1769476
  65.9 23.8 %copy-start.5 = (f32[576,256]{1,0:T(8,128)S(1)}, f32[576,256]{1,0:T(8,128)}, u32[]{:S(2)}) copy-start(f32[576,256]{1,0:T(8,128)} %refs_6_.1) | copy-start | bytes 1769476
  65.9 23.8 %copy-start.6 = (f32[576,256]{1,0:T(8,128)S(1)}, f32[576,256]{1,0:T(8,128)}, u32[]{:S(2)}) copy-start(f32[576,256]{1,0:T(8,128)} %refs_7_.1) | copy-start | bytes 1769476
  70.6 19.2 %copy-start = (f32[576,256]{1,0:T(8,128)S(1)}, f32[576,256]{1,0:T(8,128)}, u32[]{:S(2)}) copy-start(f32[576,256]{1,0:T(8,128)} %refs_2_.3) | copy-start | bytes 1769476
  70.6 19.2 %copy-start.1 = (f32[576,256]{1,0:T(8,128)S(1)}, f32[576,256]{1,0:T(8,128)}, u32[]{:S(2)}) copy-start(f32[576,256]{1,0:T(8,128)} %refs_5_.1) | copy-start | bytes 1769476
  70.6 19.2 %copy-start.2 = (f32[64,256]{1,0:T(8,128)S(1)}, f32[64,256]{1,0:T(8,128)}, u32[]{:S(2)}) copy-start(f32[64,256]{1,0:T(8,128)} %refs_8_.1) | copy-start | bytes 196612
  70.6 19.2 %copy-start.3 = (f32[576,256]{1,0:T(8,128)S(1)}, f32[576,256]{1,0:T(8,128)}, u32[]{:S(2)}) copy-start(f32[576,256]{1,0:T(8,128)} %refs_3_.1) | copy-start | bytes 1769476
  70.7 19.1 %copy-start.7 = (f32[64,256]{1,0:T(8,128)S(1)}, f32[64,256]{1,0:T(8,128)}, u32[]{:S(2)}) copy-start(f32[64,256]{1,0:T(8,128)} %refs_9_.1) | copy-start | bytes 196612
  70.7 19.1 %copy-start.8 = (f32[64,256]{1,0:T(8,128)S(1)}, f32[64,256]{1,0:T(8,128)}, u32[]{:S(2)}) copy-start(f32[64,256]{1,0:T(8,128)} %refs_10_.1) | copy-start | bytes 196612
  72.9 6.8 %collective-permute-start.18 = (bf16[152,256]{1,0:T(8,128)(2,1)S(1)}, bf16[152,256]{1,0:T(8,128)(2,1)S(1)}, u32[]{:S(2)}, u32[]{:S(2)}) collective-permute-start(bf16[152,256]{1,0:T(8,128)(2,1)S(1)} %get-tuple-element.113), channel_id=1, source_target_pairs={{0,1},{1,2},{2,3},{3,0},{4,5},{5,6},{6,7},{7,4},{8,9},{9,10},{10,1... | collective-permute-start | bytes 233480 | tf_op jit(solution)/shard_map/ppermute | solution.py:600
  72.9 8.4 %collective-permute-start.19 = (bf16[152,256]{1,0:T(8,128)(2,1)S(1)}, bf16[152,256]{1,0:T(8,128)(2,1)S(1)}, u32[]{:S(2)}, u32[]{:S(2)}) collective-permute-start(bf16[152,256]{1,0:T(8,128)(2,1)S(1)} %get-tuple-element.114), channel_id=1, source_target_pairs={{0,2},{1,3},{2,0},{3,1},{4,6},{5,7},{6,4},{7,5},{8,10},{9,11},{10,... | collective-permute-start | bytes 233480 | tf_op jit(solution)/shard_map/ppermute | solution.py:600
  74.2 7.1 %collective-permute-start.20 = (bf16[152,256]{1,0:T(8,128)(2,1)S(1)}, bf16[152,256]{1,0:T(8,128)(2,1)S(1)}, u32[]{:S(2)}, u32[]{:S(2)}) collective-permute-start(bf16[152,256]{1,0:T(8,128)(2,1)S(1)} %get-tuple-element.115), channel_id=1, source_target_pairs={{0,3},{1,0},{2,1},{3,2},{4,7},{5,4},{6,5},{7,6},{8,11},{9,8},{10,9... | collective-permute-start | bytes 233480 | tf_op jit(solution)/shard_map/ppermute | solution.py:600
  81.4 5.4 %collective-permute-start.23 = (bf16[152,256]{1,0:T(8,128)(2,1)S(1)}, bf16[152,256]{1,0:T(8,128)(2,1)S(1)}, u32[]{:S(2)}, u32[]{:S(2)}) collective-permute-start(bf16[152,256]{1,0:T(8,128)(2,1)S(1)} %add_convert_fusion.8), channel_id=1, source_target_pairs={{0,24},{8,16},{16,8},{24,0},{1,25},{9,17},{17,9},{25,1},{2,26},{10... | collective-permute-start | bytes 233480 | tf_op jit(solution)/shard_map/ppermute | solution.py:600
  82.9 4.6 %collective-permute-start.22 = (bf16[152,256]{1,0:T(8,128)(2,1)S(1)}, bf16[152,256]{1,0:T(8,128)(2,1)S(1)}, u32[]{:S(2)}, u32[]{:S(2)}) collective-permute-start(bf16[152,256]{1,0:T(8,128)(2,1)S(1)} %add_convert_fusion.8), channel_id=1, source_target_pairs={{0,16},{8,24},{16,0},{24,8},{1,17},{9,25},{17,1},{25,9},{2,18},{10... | collective-permute-start | bytes 233480 | tf_op jit(solution)/shard_map/ppermute | solution.py:600
  83.6 4.4 %collective-permute-start.21 = (bf16[152,256]{1,0:T(8,128)(2,1)S(1)}, bf16[152,256]{1,0:T(8,128)(2,1)S(1)}, u32[]{:S(2)}, u32[]{:S(2)}) collective-permute-start(bf16[152,256]{1,0:T(8,128)(2,1)S(1)} %add_convert_fusion.8), channel_id=1, source_target_pairs={{0,8},{8,0},{16,24},{24,16},{1,9},{9,1},{17,25},{25,17},{2,10},{10... | collective-permute-start | bytes 233480 | tf_op jit(solution)/shard_map/ppermute | solution.py:600
  88.1 1.7 %collective-permute-start.24 = (bf16[4,152,256]{2,1,0:T(8,128)(2,1)S(1)}, bf16[4,152,256]{2,1,0:T(8,128)(2,1)S(1)}, u32[]{:S(2)}, u32[]{:S(2)}) collective-permute-start(bf16[4,152,256]{2,1,0:T(8,128)(2,1)S(1)} %pad_maximum_fusion.refs_0_), channel_id=1, source_target_pairs={{0,4},{4,0},{1,5},{5,1},{2,6},{6,2},{3,7},{7,3},{8,12},{12,8},{9,1... | collective-permute-start | bytes 933896 | tf_op jit(solution)/shard_map/ppermute | solution.py:600

commit v5 on v4

--- a/solution.py
+++ b/solution.py
@@ -174,10 +174,17 @@
         self.late = self.piece + self.skip_piece
         self.chunk = self.piece + self.late
         self.split = self.piece % 8 == 0 and self.skip_piece % 8 == 0
+        self.halves = self.shard // 2, self.shard // 2, self.skip_shard // 2
+        self.sent = self.halves
+        self.direct = ()
         if self.split:
             self.sent = self.piece, self.piece, self.skip_piece
-        else:
-            self.sent = self.shard // 2, self.shard // 2, self.skip_shard // 2
+            self.direct = tuple(d for d in (1, 2) if d < self.ranks - 1)
+        self.start = {}
+        rows = 0
+        for d in range(1, self.ranks):
+            self.start[d] = rows
+            rows += self.sent[0] if d in self.direct else sum(self.sent)
 
 
 def place_rows(plan, ids_ref, dst_ref, value, first_row, piece, offset):
@@ -194,7 +201,7 @@
         dst_ref[
             to_core ^ core,
             to_tile ^ tile,
-            (to_rank + plan.ranks - rank) % plan.ranks,
+            to_rank ^ rank,
             at : at + stop - row,
         ] = value[row - first_row : stop - first_row]
         row = stop
@@ -217,56 +224,93 @@
             place_rows(plan, ids_ref, dst_ref, part.astype(BF), (3 * a + b) * c, plan.piece, 0)
 
 
-def pack(plan, ids, one, two, skip):
+def pack(plan, ids, weights, rows, shared, parts):
     c = plan.c
-    sizes = plan.sent
-
-    def kernel(ids_ref, one_hbm, two_hbm, skip_hbm, sent_ref, rows_ref, sem):
+    count = len(weights)
+
+    def kernel(ids_ref, *refs):
+        rows_ref, sem = refs[count + len(parts) :]
         loads = []
         at = 0
-        for k, (hbm, rows) in enumerate(zip((one_hbm, two_hbm, skip_hbm), sizes)):
+        for k in range(count):
+            hbm = refs[k]
             start = ids_ref[0] * (hbm.shape[0] // 2)
-            if plan.split:
-                start = start + ids_ref[1] * rows
-            source = hbm.at[pl.ds(pl.multiple_of(start, 8), rows)]
-            loads.append(pltpu.make_async_copy(source, rows_ref.at[pl.ds(at, rows)], sem.at[k]))
-            at += rows
+            if shared:
+                start = start + ids_ref[1] * rows[k]
+            source = hbm.at[pl.ds(pl.multiple_of(start, 8), rows[k])]
+            loads.append(pltpu.make_async_copy(source, rows_ref.at[pl.ds(at, rows[k])], sem.at[k]))
+            at += rows[k]
         for load in loads:
             load.start()
         for load in loads:
             load.wait()
-        sent_ref[...] = rows_ref[...].astype(BF)
+        for k, part in enumerate(parts):
+            refs[count + k][...] = rows_ref[0:part].astype(BF)
 
     return pl.pallas_call(
         kernel,
-        in_specs=[SMEM, HBM, HBM, HBM],
+        in_specs=[SMEM] + [HBM] * count,
+        out_specs=[VMEM] * len(parts),
+        out_shape=[jax.ShapeDtypeStruct((v, c), BF) for v in parts],
+        scratch_shapes=[pltpu.VMEM((sum(rows), c), F32), pltpu.SemaphoreType.DMA((count,))],
+        compiler_params=params(),
+        cost_estimate=cost(0, 0),
+        name="pack",
+    )(ids, *(in_hbm(v) for v in weights))
+
+
+def below(arrays):
+    rows = [v.shape[0] for v in arrays]
+
+    def kernel(*refs):
+        at = 0
+        for ref, count in zip(refs, rows):
+            refs[-1][at : at + count] = ref[...]
+            at += count
+
+    return pl.pallas_call(
+        kernel,
+        in_specs=[VMEM] * len(rows),
         out_specs=VMEM,
-        out_shape=jax.ShapeDtypeStruct((sum(sizes), c), BF),
-        scratch_shapes=[pltpu.VMEM((sum(sizes), c), F32), pltpu.SemaphoreType.DMA((3,))],
-        compiler_params=params(),
-        cost_estimate=cost(0, 0.3),
-        name="pack",
-    )(ids, in_hbm(one), in_hbm(two), in_hbm(skip))
+        out_shape=jax.ShapeDtypeStruct((sum(rows), arrays[0].shape[1]), BF),
+        compiler_params=params(),
+        cost_estimate=cost(0, 0),
+        name="below",
+    )(*arrays)
 
 
 def join_rows(plan, ids_ref, low_ref, pieces, w_ref, rows):
     rank = ids_ref[2]
     w_ref[pl.ds(pl.multiple_of(rank * rows, 8), rows)] = low_ref[...]
     for ref, index, d, row in pieces:
-        start = (rank + plan.ranks - d) % plan.ranks * rows + row
+        start = (rank ^ d) * rows + row
         part = ref[index]
         w_ref[pl.ds(pl.multiple_of(start, 8), part.shape[0])] = part
 
 
-def received(plan, ids_ref, near_refs, far_refs, at, rows, shard):
+def received(plan, ids_ref, near_refs, far_refs, weight):
     core, tile = ids_ref[0], ids_ref[1]
+    rows = plan.sent[weight]
     pieces = []
     for side, group in ((core, near_refs), (1 - core, far_refs)):
         for e, ref in enumerate(group):
-            row = side * (shard // 2)
+            row = side * plan.halves[weight]
             if plan.split:
                 row = row + (tile ^ e) * rows
-            pieces += [(ref, (d - 1, pl.ds(at, rows)), d, row) for d in range(1, plan.ranks)]
+            for d in range(1, plan.ranks):
+                if weight == 0 or d not in plan.direct:
+                    at = plan.start[d] + sum(plan.sent[:weight])
+                    pieces.append((ref, pl.ds(at, rows), d, row))
+    return pieces
+
+
+def received_directly(plan, ids_ref, near_refs, far_refs, at, weight):
+    core = ids_ref[0]
+    rows = plan.halves[weight]
+    pieces = []
+    for side, group in ((core, near_refs), (1 - core, far_refs)):
+        for ref, d in zip(group, plan.direct):
+            pieces.append((ref, pl.ds(at, rows), d, side * rows))
     return pieces
 
 
@@ -328,7 +372,7 @@
     def kernel(ids_ref, xp_ref, low_ref, *refs):
         near_refs, far_refs = refs[:count], refs[count : 2 * count]
         hp_ref, slope_ref, w_ref, u_ref, v_ref = refs[2 * count :]
-        pieces = received(plan, ids_ref, near_refs, far_refs, 0, plan.sent[0], plan.shard)
+        pieces = received(plan, ids_ref, near_refs, far_refs, 0)
         join_rows(plan, ids_ref, low_ref, pieces, w_ref, plan.shard)
         pair_weights(w_ref, u_ref)
         for face in range(0, FACES, GROUP):
@@ -352,23 +396,28 @@
         ],
         scratch_shapes=[pltpu.VMEM(pair_shape(c), BF)],
         compiler_params=params(),
-        cost_estimate=cost(4.1, 12),
+        cost_estimate=cost(0, 0),
         name="first",
     )(ids, xp, low, *near, *far)
 
 
-def second(plan, ids, hp, xp, go, dws, low, low_skip, near, far):
+def second(plan, ids, hp, xp, go, dws, low, low_skip, near, far, near_half, far_half):
     c = plan.c
     count = len(near)
+    halves = len(near_half)
 
     def kernel(ids_ref, hp_ref, xp_ref, go_ref, dws_ref, low_ref, lows_ref, *refs):
-        near_refs, far_refs = refs[:count], refs[count : 2 * count]
-        out_hbm, gp_ref, w_ref, u_ref, ws_ref, keep_ref, send_ref = refs[2 * count : 2 * count + 7]
-        out_ref, e_ref, dw_ref, v_ref, z_ref, sem_out = refs[2 * count + 7 :]
-        pieces = received(plan, ids_ref, near_refs, far_refs, plan.sent[0], plan.sent[1], plan.shard)
+        groups = refs[:count], refs[count : 2 * count]
+        refs = refs[2 * count :]
+        direct = refs[:halves], refs[halves : 2 * halves]
+        refs = refs[2 * halves :]
+        out_hbm, gp_ref, w_ref, u_ref, ws_ref, keep_ref, send_ref = refs[:7]
+        out_ref, e_ref, dw_ref, v_ref, z_ref, sem_out = refs[7:]
+        pieces = received(plan, ids_ref, *groups, 1)
+        pieces += received_directly(plan, ids_ref, *direct, 0, 1)
         join_rows(plan, ids_ref, low_ref, pieces, w_ref, plan.shard)
-        at = plan.sent[0] + plan.sent[1]
-        pieces = received(plan, ids_ref, near_refs, far_refs, at, plan.sent[2], plan.skip_shard)
+        pieces = received(plan, ids_ref, *groups, 2)
+        pieces += received_directly(plan, ids_ref, *direct, plan.halves[1], 2)
         join_rows(plan, ids_ref, lows_ref, pieces, ws_ref, plan.skip_shard)
         e_ref[...] = jnp.zeros_like(e_ref)
         place_rows(plan, ids_ref, dw_ref, dws_ref[...], 0, plan.skip_piece, plan.piece)
@@ -397,7 +446,7 @@
     sums = jax.ShapeDtypeStruct((plan.tiles, plan.ranks, plan.late, c), BF)
     return pl.pallas_call(
         kernel,
-        in_specs=[SMEM] + [VMEM] * (6 + 2 * count),
+        in_specs=[SMEM] + [VMEM] * (6 + 2 * count + 2 * halves),
         out_specs=[HBM] + [VMEM] * 6,
         out_shape=[
             field(c),
@@ -419,7 +468,7 @@
         compiler_params=params(),
         cost_estimate=cost(9, 16),
         name="second",
-    )(ids, hp, xp, go, dws, low, low_skip, *near, *far)
+    )(ids, hp, xp, go, dws, low, low_skip, *near, *far, *near_half, *far_half)
 
 
 def hidden_back(plan, ids, gp, w, u, slope, xp, after):
@@ -593,11 +642,7 @@
 
 
 def send(v, axis, size, step):
-    if axis == "fsdp":
-        pairs = [(i, (i + step) % size) for i in range(size)]
-    else:
-        pairs = [(i, i ^ step) for i in range(size)]
-    return lax.ppermute(v, axis, pairs)
+    return lax.ppermute(v, axis, [(i, i ^ step) for i in range(size)])
 
 
 def total(*parts):
@@ -639,17 +684,25 @@
         cot = jnp.transpose(cotangent[0], (1, 2, 3, 0, 4))
         places = jnp.stack([lax.axis_index(n) for n in ("core", "tile", "fsdp")]).astype(jnp.int32)
         weights = w_first, w_second, w_skip
-        sent = pack(plan, places, *weights)
-        near = [jnp.stack([to_rank(sent, d) for d in range(1, ranks)])]
+        parts = (plan.sent[0], sum(plan.sent))
+        some, sent = pack(plan, places, weights, plan.sent, plan.split, parts)
+        near = [to_rank(some if d in plan.direct else sent, d) for d in range(1, ranks)]
+        near = [below(near)]
+        near_half, after = [], near[:]
         if plan.split:
             near += [to_tile(near[0], e) for e in range(1, tiles)]
+            (half,) = pack(plan, places, weights[1:], plan.halves[1:], False, (sum(plan.halves[1:]),))
+            near_half = [to_rank(half, d) for d in plan.direct]
+            after.append(half)
         ids = jnp.concatenate([places, lengths, face_table.T.reshape(-1)])
-        xp, go, dws, low1, low2, low3 = enter(plan, ids, x, cot, weights, near[:1])
-        xp, near = lax.optimization_barrier((xp, near))
+        xp, go, dws, low1, low2, low3 = enter(plan, ids, x, cot, weights, after)
+        xp, near, near_half = lax.optimization_barrier((xp, near, near_half))
         far = [to_core(v) for v in near]
+        far_half = [to_core(v) for v in near_half]
         hp, slope, w1, u1 = first(plan, ids, xp, low1, near, far)
+        hp, far_half = lax.optimization_barrier((hp, far_half))
         output, gp, w2, u2, ws, keep2, away2 = second(
-            plan, ids, hp, xp, go, dws, low2, low3, near, far
+            plan, ids, hp, xp, go, dws, low2, low3, near, far, near_half, far_half
         )
         came2 = to_core(away2)
         parts2 = [total(keep2[d], came2[d]) for d in range(tiles)]

time: 93.5 us -> 88.5 us (0.947)
  waiting for transfers between devices: 28.1 us -> 17.2 us
  starting transfers between devices: 25.9 us -> 30.3 us
  Pallas kernels: 36.8 us -> 38.3 us
    ppermute x25 -> x29, waiting for transfers between devices: 28.1 us -> 17.2 us  [send(): return lax.ppermute(v, axis, [(i, i ^ step) for i in range(size)])]
    ppermute x25 -> x29, starting transfers between devices: 25.9 us -> 30.3 us  [send(): return lax.ppermute(v, axis, [(i, i ^ step) for i in range(size)])]
    pallas_call x2 -> x4, Pallas kernels: 12.4 us -> 13.9 us  [the longest x1 10.9 us: second(): pl.pallas_call(kernel, in_specs=[SMEM] + [VMEM] * (6 + 2 * count + 2 * ha...]
  transfers between devices with their start and end apart: 25 -> 29, of which waited for: 18 -> 13; matrix products, arithmetic and copies ran while one was open for 0% -> 0% of each run, Pallas kernels for 17% -> 25%
where the time goes in v5:
time: 88.5 us; the launch traced here: 88.3 us
  Pallas kernels  38.3 us (43%)
  starting transfers between devices  30.3 us (34%)
  waiting for transfers between devices  17.2 us (19%)
  between operations  1.79 us (2%)
    ppermute x29, starting transfers between devices, send(): return lax.ppermute(v, axis, [(i, i ^ step) for i in range(size)])  30.3 us
    ppermute x29, waiting for transfers between devices, send(): return lax.ppermute(v, axis, [(i, i ^ step) for i in range(size)])  17.2 us
    pallas_call x1, Pallas kernels, second(): pl.pallas_call(kernel, in_specs=[SMEM] + [VMEM] * (6 + 2 * count + 2 * ha...  10.9 us
    pallas_call x1, Pallas kernels, hidden_back(): pl.pallas_call(kernel, in_specs=[SMEM] + [VMEM] * 6, out_specs=[VMEM] * 3...  7.4 us
    pallas_call x1, Pallas kernels, first(): pl.pallas_call(kernel, in_specs=[SMEM] + [VMEM] * (2 + 2 * count), out_sp...  5.34 us
    pallas_call x1, Pallas kernels, inputs_back(): pl.pallas_call(inputs_back_kernel, in_specs=[VMEM] * 5, out_specs=HBM, ou...  4.66 us
    pallas_call x1, Pallas kernels, enter(): pl.pallas_call(kernel, in_specs=[SMEM] + [HBM] * 5 + [VMEM] * len(after),...  3.54 us
    pallas_call x1, Pallas kernels, update(): pl.pallas_call(kernel, in_specs=[SMEM] + [VMEM] * 11, out_specs=[HBM] * 9...  3.32 us
  transfers between devices with their start and end apart: 29, of which 13 were waited for; matrix products, arithmetic and copies ran while one was open for 0% of the time, Pallas kernels for 25%

profile of v5, /device:TPU:0, one launch (start us, length us, event | category | flops | bytes accessed | tf_op | source)
XLA Modules:
  0.0 88.3 jit_solution(10827822807186195403)
XLA Ops:
  0.7 1.5 %pack.2 = (bf16[72,256]{1,0:T(8,128)(2,1)S(1)}, bf16[152,256]{1,0:T(8,128)(2,1)S(1)}) custom-call(s32[3]{0:T(128)S(1)} %pad_add_fusion.ids_ref, f32[576,256]{1,0:T(8,128)} %refs_2_.5, f32[576,256]{1,0:T(8,128)} %refs_5_.1, f32[64,256]{1,0:T(8,128)} %refs_8_.1), custom_call_target="tpu_custom_call" | custom-call | tf_op jit(solution)/shard_map/pack/pallas_call | solution.py:250
  2.2 5.1 %collective-permute-start.2 = (bf16[152,256]{1,0:T(8,128)(2,1)S(1)}, bf16[152,256]{1,0:T(8,128)(2,1)S(1)}, u32[]{:S(2)}, u32[]{:S(2)}) collective-permute-start(bf16[152,256]{1,0:T(8,128)(2,1)S(1)} %get-tuple-element.76), channel_id=1, source_target_pairs={{0,3},{1,2},{2,1},{3,0},{4,7},{5,6},{6,5},{7,4},{8,11},{9,10},{10,... | collective-permute-start | bytes 233480 | tf_op jit(solution)/shard_map/ppermute | solution.py:645
  7.4 0.6 collective-permute-start
  8.0 1.5 %pack.3.refs_4_ = bf16[320,256]{1,0:T(8,128)(2,1)S(1)} custom-call(s32[3]{0:T(128)S(1)} %pad_add_fusion.ids_ref, f32[576,256]{1,0:T(8,128)} %refs_5_.1, f32[64,256]{1,0:T(8,128)} %refs_8_.1), custom_call_target="tpu_custom_call" | custom-call | tf_op jit(solution)/shard_map/pack/pallas_call | solution.py:250
  9.6 2.4 %collective-permute-start.7 = (bf16[320,256]{1,0:T(8,128)(2,1)S(1)}, bf16[320,256]{1,0:T(8,128)(2,1)S(1)}, u32[]{:S(2)}, u32[]{:S(2)}) collective-permute-start(bf16[320,256]{1,0:T(8,128)(2,1)S(1)} %pack.3.refs_4_), channel_id=1, source_target_pairs={{0,2},{1,3},{2,0},{3,1},{4,6},{5,7},{6,4},{7,5},{8,10},{9,11},{10,... | collective-permute-start | bytes 491528 | tf_op jit(solution)/shard_map/ppermute | solution.py:645
  11.9 2.0 %collective-permute-start.6 = (bf16[320,256]{1,0:T(8,128)(2,1)S(1)}, bf16[320,256]{1,0:T(8,128)(2,1)S(1)}, u32[]{:S(2)}, u32[]{:S(2)}) collective-permute-start(bf16[320,256]{1,0:T(8,128)(2,1)S(1)} %pack.3.refs_4_), channel_id=1, source_target_pairs={{0,1},{1,0},{2,3},{3,2},{4,5},{5,4},{6,7},{7,6},{8,9},{9,8},{10,11... | collective-permute-start | bytes 491528 | tf_op jit(solution)/shard_map/ppermute | solution.py:645
  14.0 2.5 %collective-permute-start.5 = (bf16[296,256]{1,0:T(8,128)(2,1)S(1)}, bf16[296,256]{1,0:T(8,128)(2,1)S(1)}, u32[]{:S(2)}, u32[]{:S(2)}) collective-permute-start(bf16[296,256]{1,0:T(8,128)(2,1)S(1)} %below.1.refs_3_.refs_0_), channel_id=1, source_target_pairs={{0,24},{8,16},{16,8},{24,0},{1,25},{9,17},{17,9},{25,1},{2,26},{10... | collective-permute-start | bytes 454664 | tf_op jit(solution)/shard_map/ppermute | solution.py:645
  16.5 0.5 collective-permute-start.4
  17.0 0.5 collective-permute-start.3
  18.3 0.1 concatenate.4.ids_ref
  18.3 3.5 %enter.1 = (bf16[12,8,8,8,256]{4,3,2,1,0:T(8,128)(2,1)S(1)}, bf16[12,6,6,8,256]{4,3,2,1,0:T(8,128)(2,1)S(1)}, bf16[256,256]{1,0:T(8,128)(2,1)S(1)}, bf16[576,256...) custom-call(s32[52]{0:T(128)S(1)} %concatenate.4.ids_ref, ...), custom_call_target="tpu_custom_call" | custom-call | tf_op jit(solution)/shard_map/enter/pallas_call | solution.py:347
  21.9 0.6 collective-permute-done.4.refs_2_
  22.6 0.5 collective-permute-start.12
  23.1 0.5 collective-permute-start.9
  23.6 0.4 collective-permute-done.8.refs_4_
  23.9 0.2 collective-permute-start.11
  24.1 0.6 collective-permute-done.9.refs_5_
  24.7 0.3 collective-permute-done.10.refs_6_
  25.0 0.4 collective-permute-done.11.refs_7_
  25.3 5.3 %first.1 = (bf16[12,8,8,8,256]{4,3,2,1,0:T(8,128)(2,1)S(1)}, bf16[12,6,6,8,256]{4,3,2,1,0:T(8,128)(2,1)S(1)}, bf16[2304,256]{1,0:T(8,128)(2,1)S(1)}, bf16[2,3,256,256]{3,2,1,0:T(8,128)(2,1)S(1)}) custom-call(s32[52]{0:T(128)S(1)} %concatenate.4.ids_ref, bf16[12,8,8,8,256]{4,3,2,1,0:T(8,128)(2,1)S(1)} %get-tuple-element.78.xp_ref, ...), custom_call_target="tpu_custom_call" | custom-call | tf_op jit(solution)/shard_map/first/pallas_call | solution.py:387
  30.7 10.9 %second.1 = (bf16[12,6,6,8,256]{4,3,2,1,0:T(8,128)(2,1)}, bf16[12,8,8,8,256]{4,3,2,1,0:T(8,128)(2,1)S(1)}, bf16[2304,256]{1,0:T(8,128)(2,1)S(1)}, bf16[2,3,256,2...) custom-call(s32[52]{0:T(128)S(1)} %concatenate.4.ids_ref, ...), custom_call_target="tpu_custom_call" | custom-call | flops 8999999488 | bytes 16000000 | tf_op jit(solution)/shard_map/second/pallas_call | solution.py:447
  41.5 0.2 collective-permute-start.14
  41.8 1.9 %collective-permute-done.14 = bf16[4,4,80,256]{3,2,1,0:T(8,128)(2,1)S(1)} collective-permute-done((bf16[4,4,80,256]{3,2,1,0:T(8,128)(2,1)S(1)}, bf16[4,4,80,256]{3,2,1,0:T(8,128)(2,1)S(1)}, u32[]{:S(2)}, u32[]{:S(2)}) %collective-permute-start.14) | collective-permute-done | bytes 655392 | tf_op jit(solution)/shard_map/ppermute | solution.py:645
  43.7 0.2 fusion.3
  43.9 2.0 %collective-permute-start.17 = (bf16[4,80,256]{2,1,0:T(8,128)(2,1)S(1)}, bf16[4,80,256]{2,1,0:T(8,128)(2,1)S(1)}, u32[]{:S(2)}, u32[]{:S(2)}) collective-permute-start(bf16[4,80,256]{2,1,0:T(8,128)(2,1)S(1)} %get-tuple-element.139), channel_id=1, source_target_pairs={{0,24},{8,16},{16,8},{24,0},{1,25},{9,17},{17,9},{25,1},{2,26},{10... | collective-permute-start | bytes 491528 | tf_op jit(solution)/shard_map/ppermute | solution.py:645
  45.9 1.0 %collective-permute-start.16 = (bf16[4,80,256]{2,1,0:T(8,128)(2,1)S(1)}, bf16[4,80,256]{2,1,0:T(8,128)(2,1)S(1)}, u32[]{:S(2)}, u32[]{:S(2)}) collective-permute-start(bf16[4,80,256]{2,1,0:T(8,128)(2,1)S(1)} %get-tuple-element.140), channel_id=1, source_target_pairs={{0,16},{8,24},{16,0},{24,8},{1,17},{9,25},{17,1},{25,9},{2,18},{10... | collective-permute-start | bytes 491528 | tf_op jit(solution)/shard_map/ppermute | solution.py:645
  46.9 0.5 collective-permute-start.15
  47.4 7.4 %hidden_back.1 = (bf16[12,8,8,8,256]{4,3,2,1,0:T(8,128)(2,1)S(1)}, bf16[4,4,72,256]{3,2,1,0:T(8,128)(2,1)S(1)}, bf16[4,4,72,256]{3,2,1,0:T(8,128)(2,1)S(1)}) custom-call(s32[52]{0:T(128)S(1)} %concatenate.4.ids_ref, bf16[12,8,8,8,256]{4,3,2,1,0:T(8,128)(2,1)S(1)} %get-tuple-element.95.gp_ref, bf16[2304,256]{1,0:T(8,128)(2,1)S(1)} %get-tuple-element.96.w_ref, ...), custom_call_target="tpu_custom_call" | custom-call | tf_op jit(solution)/shard_map/hidden_back/pallas_call | solution.py:495
  55.0 2.0 %collective-permute-done.18 = bf16[4,4,72,256]{3,2,1,0:T(8,128)(2,1)S(1)} collective-permute-done((bf16[4,4,72,256]{3,2,1,0:T(8,128)(2,1)S(1)}, bf16[4,4,72,256]{3,2,1,0:T(8,128)(2,1)S(1)}, u32[]{:S(2)}, u32[]{:S(2)}) %collective-permute-start.18) | collective-permute-done | bytes 589856 | tf_op jit(solution)/shard_map/ppermute | solution.py:645
  57.0 0.2 fusion.7
  57.1 1.6 %collective-permute-start.19 = (bf16[4,72,256]{2,1,0:T(8,128)(2,1)S(1)}, bf16[4,72,256]{2,1,0:T(8,128)(2,1)S(1)}, u32[]{:S(2)}, u32[]{:S(2)}) collective-permute-start(bf16[4,72,256]{2,1,0:T(8,128)(2,1)S(1)} %get-tuple-element.106), channel_id=1, source_target_pairs={{0,8},{8,0},{16,24},{24,16},{1,9},{9,1},{17,25},{25,17},{2,10},{10... | collective-permute-start | bytes 442376 | tf_op jit(solution)/shard_map/ppermute | solution.py:645
  58.7 1.0 %collective-permute-start.20 = (bf16[4,72,256]{2,1,0:T(8,128)(2,1)S(1)}, bf16[4,72,256]{2,1,0:T(8,128)(2,1)S(1)}, u32[]{:S(2)}, u32[]{:S(2)}) collective-permute-start(bf16[4,72,256]{2,1,0:T(8,128)(2,1)S(1)} %get-tuple-element.107), channel_id=1, source_target_pairs={{0,16},{8,24},{16,0},{24,8},{1,17},{9,25},{17,1},{25,9},{2,18},{10... | collective-permute-start | bytes 442376 | tf_op jit(solution)/shard_map/ppermute | solution.py:645
  59.6 1.0 %collective-permute-start.21 = (bf16[4,72,256]{2,1,0:T(8,128)(2,1)S(1)}, bf16[4,72,256]{2,1,0:T(8,128)(2,1)S(1)}, u32[]{:S(2)}, u32[]{:S(2)}) collective-permute-start(bf16[4,72,256]{2,1,0:T(8,128)(2,1)S(1)} %get-tuple-element.108), channel_id=1, source_target_pairs={{0,24},{8,16},{16,8},{24,0},{1,25},{9,17},{17,9},{25,1},{2,26},{10... | collective-permute-start | bytes 442376 | tf_op jit(solution)/shard_map/ppermute | solution.py:645
  60.7 4.7 %inputs_back.1 = f32[12,6,6,8,256]{4,3,2,1,0:T(8,128)} custom-call(bf16[12,8,8,8,256]{4,3,2,1,0:T(8,128)(2,1)S(1)} %get-tuple-element.113.gp_ref, bf16[2304,256]{1,0:T(8,128)(2,1)S(1)} %get-tuple-element.114.w_ref, bf16[2,3,256,256]{3,2,1,0:T(8,128)(2,1)S(1)} %get-tuple-element.115.u_ref, bf16[256,256]{1,0:T(8,128)(2,1)S(1)} %get-tuple-element.116.ws_ref, ...), custom_call_target="tpu_custom_call" | custom-call | tf_op jit(solution)/shard_map/inputs_back/pallas_call | solution.py:555
  65.4 2.0 %collective-permute-done.20.refs_2_ = bf16[4,72,256]{2,1,0:T(8,128)(2,1)S(1)} collective-permute-done((bf16[4,72,256]{2,1,0:T(8,128)(2,1)S(1)}, bf16[4,72,256]{2,1,0:T(8,128)(2,1)S(1)}, u32[]{:S(2)}, u32[]{:S(2)}) %collective-permute-start.20) | collective-permute-done | bytes 147488 | tf_op jit(solution)/shard_map/ppermute | solution.py:645
  67.4 0.2 tile_sums.1
  67.6 0.4 collective-permute-start.22
  68.0 1.1 %collective-permute-start.23 = (bf16[152,256]{1,0:T(8,128)(2,1)S(1)}, bf16[152,256]{1,0:T(8,128)(2,1)S(1)}, u32[]{:S(2)}, u32[]{:S(2)}) collective-permute-start(bf16[152,256]{1,0:T(8,128)(2,1)S(1)} %get-tuple-element.128), channel_id=1, source_target_pairs={{0,2},{1,3},{2,0},{3,1},{4,6},{5,7},{6,4},{7,5},{8,10},{9,11},{10,... | collective-permute-start | bytes 233480 | tf_op jit(solution)/shard_map/ppermute | solution.py:645
  69.1 3.0 %collective-permute-start.24 = (bf16[152,256]{1,0:T(8,128)(2,1)S(1)}, bf16[152,256]{1,0:T(8,128)(2,1)S(1)}, u32[]{:S(2)}, u32[]{:S(2)}) collective-permute-start(bf16[152,256]{1,0:T(8,128)(2,1)S(1)} %get-tuple-element.129), channel_id=1, source_target_pairs={{0,3},{1,2},{2,1},{3,0},{4,7},{5,6},{6,5},{7,4},{8,11},{9,10},{10,... | collective-permute-start | bytes 233480 | tf_op jit(solution)/shard_map/ppermute | solution.py:645
  72.1 4.0 %collective-permute-done.23 = bf16[152,256]{1,0:T(8,128)(2,1)S(1)} collective-permute-done((bf16[152,256]{1,0:T(8,128)(2,1)S(1)}, bf16[152,256]{1,0:T(8,128)(2,1)S(1)}, u32[]{:S(2)}, u32[]{:S(2)}) %collective-permute-start.23) | collective-permute-done | bytes 77856 | tf_op jit(solution)/shard_map/ppermute | solution.py:645
  76.1 1.6 %collective-permute-start.27 = (bf16[152,256]{1,0:T(8,128)(2,1)S(1)}, bf16[152,256]{1,0:T(8,128)(2,1)S(1)}, u32[]{:S(2)}, u32[]{:S(2)}) collective-permute-start(bf16[152,256]{1,0:T(8,128)(2,1)S(1)} %add_convert_fusion.8), channel_id=1, source_target_pairs={{0,24},{8,16},{16,8},{24,0},{1,25},{9,17},{17,9},{25,1},{2,26},{10... | collective-permute-start | bytes 233480 | tf_op jit(solution)/shard_map/ppermute | solution.py:645
  77.7 0.9 %collective-permute-start.26 = (bf16[152,256]{1,0:T(8,128)(2,1)S(1)}, bf16[152,256]{1,0:T(8,128)(2,1)S(1)}, u32[]{:S(2)}, u32[]{:S(2)}) collective-permute-start(bf16[152,256]{1,0:T(8,128)(2,1)S(1)} %add_convert_fusion.8), channel_id=1, source_target_pairs={{0,16},{8,24},{16,0},{24,8},{1,17},{9,25},{17,1},{25,9},{2,18},{10... | collective-permute-start | bytes 233480 | tf_op jit(solution)/shard_map/ppermute | solution.py:645
  78.7 1.0 %collective-permute-start.25 = (bf16[152,256]{1,0:T(8,128)(2,1)S(1)}, bf16[152,256]{1,0:T(8,128)(2,1)S(1)}, u32[]{:S(2)}, u32[]{:S(2)}) collective-permute-start(bf16[152,256]{1,0:T(8,128)(2,1)S(1)} %add_convert_fusion.8), channel_id=1, source_target_pairs={{0,8},{8,0},{16,24},{24,16},{1,9},{9,1},{17,25},{25,17},{2,10},{10... | collective-permute-start | bytes 233480 | tf_op jit(solution)/shard_map/ppermute | solution.py:645
  79.7 1.8 %collective-permute-done.27 = bf16[152,256]{1,0:T(8,128)(2,1)S(1)} collective-permute-done((bf16[152,256]{1,0:T(8,128)(2,1)S(1)}, bf16[152,256]{1,0:T(8,128)(2,1)S(1)}, u32[]{:S(2)}, u32[]{:S(2)}) %collective-permute-start.27) | collective-permute-done | bytes 77856 | tf_op jit(solution)/shard_map/ppermute | solution.py:645
  81.5 0.8 collective-permute-done.26
  82.3 0.7 collective-permute-done.25
  83.2 1.6 %collective-permute-done.28.refs_1_ = bf16[4,152,256]{2,1,0:T(8,128)(2,1)S(1)} collective-permute-done((bf16[4,152,256]{2,1,0:T(8,128)(2,1)S(1)}, bf16[4,152,256]{2,1,0:T(8,128)(2,1)S(1)}, u32[]{:S(2)}, u32[]{:S(2)}) %collective-permute-start.28) | collective-permute-done | bytes 311328 | tf_op jit(solution)/shard_map/ppermute | solution.py:645
  84.8 3.3 %update.1 = (f32[576,256]{1,0:T(8,128)}, f32[576,256]{1,0:T(8,128)}, f32[576,256]{1,0:T(8,128)}, f32[576,256]{1,0:T(8,128)}, f32[576,256]{1,0:T(8,128)}, /*index...) custom-call(s32[52]{0:T(128)S(1)} %concatenate.4.ids_ref, ...), custom_call_target="tpu_custom_call" | custom-call | bytes 9000000 | tf_op jit(solution)/shard_map/update/pallas_call | solution.py:628
  (47 shorter events, 0.5 us)
Async XLA Ops:
  0.6 17.5 %copy-start.9 = (s32[12,4]{0,1:T(4,128)S(1)}, s32[12,4]{0,1:T(4,128)}, u32[]{:S(2)}) copy-start(s32[12,4]{0,1:T(4,128)} %param.16) | copy-start | bytes 580
  2.2 11.7 %collective-permute-start.2 = (bf16[152,256]{1,0:T(8,128)(2,1)S(1)}, bf16[152,256]{1,0:T(8,128)(2,1)S(1)}, u32[]{:S(2)}, u32[]{:S(2)}) collective-permute-start(bf16[152,256]{1,0:T(8,128)(2,1)S(1)} %get-tuple-element.76), channel_id=1, source_target_pairs={{0,3},{1,2},{2,1},{3,0},{4,7},{5,6},{6,5},{7,4},{8,11},{9,10},{10,... | collective-permute-start | bytes 233480 | tf_op jit(solution)/shard_map/ppermute | solution.py:645
  7.4 6.6 %collective-permute-start.1 = (bf16[72,256]{1,0:T(8,128)(2,1)S(1)}, bf16[72,256]{1,0:T(8,128)(2,1)S(1)}, u32[]{:S(2)}, u32[]{:S(2)}) collective-permute-start(bf16[72,256]{1,0:T(8,128)(2,1)S(1)} %get-tuple-element.75), channel_id=1, source_target_pairs={{0,2},{1,3},{2,0},{3,1},{4,6},{5,7},{6,4},{7,5},{8,10},{9,11},{10,... | collective-permute-start | bytes 110600 | tf_op jit(solution)/shard_map/ppermute | solution.py:645
  7.4 6.6 %collective-permute-start = (bf16[72,256]{1,0:T(8,128)(2,1)S(1)}, bf16[72,256]{1,0:T(8,128)(2,1)S(1)}, u32[]{:S(2)}, u32[]{:S(2)}) collective-permute-start(bf16[72,256]{1,0:T(8,128)(2,1)S(1)} %get-tuple-element.75), channel_id=1, source_target_pairs={{0,1},{1,0},{2,3},{3,2},{4,5},{5,4},{6,7},{7,6},{8,9},{9,8},{10,11... | collective-permute-start | bytes 110600 | tf_op jit(solution)/shard_map/ppermute | solution.py:645
  9.6 12.3 %collective-permute-start.7 = (bf16[320,256]{1,0:T(8,128)(2,1)S(1)}, bf16[320,256]{1,0:T(8,128)(2,1)S(1)}, u32[]{:S(2)}, u32[]{:S(2)}) collective-permute-start(bf16[320,256]{1,0:T(8,128)(2,1)S(1)} %pack.3.refs_4_), channel_id=1, source_target_pairs={{0,2},{1,3},{2,0},{3,1},{4,6},{5,7},{6,4},{7,5},{8,10},{9,11},{10,... | collective-permute-start | bytes 491528 | tf_op jit(solution)/shard_map/ppermute | solution.py:645
  11.9 10.0 %collective-permute-start.6 = (bf16[320,256]{1,0:T(8,128)(2,1)S(1)}, bf16[320,256]{1,0:T(8,128)(2,1)S(1)}, u32[]{:S(2)}, u32[]{:S(2)}) collective-permute-start(bf16[320,256]{1,0:T(8,128)(2,1)S(1)} %pack.3.refs_4_), channel_id=1, source_target_pairs={{0,1},{1,0},{2,3},{3,2},{4,5},{5,4},{6,7},{7,6},{8,9},{9,8},{10,11... | collective-permute-start | bytes 491528 | tf_op jit(solution)/shard_map/ppermute | solution.py:645
  14.0 8.0 %collective-permute-start.5 = (bf16[296,256]{1,0:T(8,128)(2,1)S(1)}, bf16[296,256]{1,0:T(8,128)(2,1)S(1)}, u32[]{:S(2)}, u32[]{:S(2)}) collective-permute-start(bf16[296,256]{1,0:T(8,128)(2,1)S(1)} %below.1.refs_3_.refs_0_), channel_id=1, source_target_pairs={{0,24},{8,16},{16,8},{24,0},{1,25},{9,17},{17,9},{25,1},{2,26},{10... | collective-permute-start | bytes 454664 | tf_op jit(solution)/shard_map/ppermute | solution.py:645
  16.5 6.0 %collective-permute-start.4 = (bf16[296,256]{1,0:T(8,128)(2,1)S(1)}, bf16[296,256]{1,0:T(8,128)(2,1)S(1)}, u32[]{:S(2)}, u32[]{:S(2)}) collective-permute-start(bf16[296,256]{1,0:T(8,128)(2,1)S(1)} %below.1.refs_3_.refs_0_), channel_id=1, source_target_pairs={{0,16},{8,24},{16,0},{24,8},{1,17},{9,25},{17,1},{25,9},{2,18},{10... | collective-permute-start | bytes 454664 | tf_op jit(solution)/shard_map/ppermute | solution.py:645
  17.0 5.6 %collective-permute-start.3 = (bf16[296,256]{1,0:T(8,128)(2,1)S(1)}, bf16[296,256]{1,0:T(8,128)(2,1)S(1)}, u32[]{:S(2)}, u32[]{:S(2)}) collective-permute-start(bf16[296,256]{1,0:T(8,128)(2,1)S(1)} %below.1.refs_3_.refs_0_), channel_id=1, source_target_pairs={{0,8},{8,0},{16,24},{24,16},{1,9},{9,1},{17,25},{25,17},{2,10},{10... | collective-permute-start | bytes 454664 | tf_op jit(solution)/shard_map/ppermute | solution.py:645
  22.6 1.4 %collective-permute-start.8 = (bf16[296,256]{1,0:T(8,128)(2,1)S(1)}, bf16[296,256]{1,0:T(8,128)(2,1)S(1)}, u32[]{:S(2)}, u32[]{:S(2)}) collective-permute-start(bf16[296,256]{1,0:T(8,128)(2,1)S(1)} %below.1.refs_3_.refs_0_), channel_id=1, source_target_pairs={{0,4},{4,0},{1,5},{5,1},{2,6},{6,2},{3,7},{7,3},{8,12},{12,8},{9,1... | collective-permute-start | bytes 454664 | tf_op jit(solution)/shard_map/ppermute | solution.py:645
  22.6 8.1 %collective-permute-start.12 = (bf16[320,256]{1,0:T(8,128)(2,1)S(1)}, bf16[320,256]{1,0:T(8,128)(2,1)S(1)}, u32[]{:S(2)}, u32[]{:S(2)}) collective-permute-start(bf16[320,256]{1,0:T(8,128)(2,1)S(1)} %collective-permute-done.6.refs_8_), channel_id=1, source_target_pairs={{0,4},{4,0},{1,5},{5,1},{2,6},{6,2},{3,7},{7,3},{8,12},{12,8},{9,1... | collective-permute-start | bytes 491528 | tf_op jit(solution)/shard_map/ppermute | solution.py:645
  23.1 7.6 %collective-permute-start.13 = (bf16[320,256]{1,0:T(8,128)(2,1)S(1)}, bf16[320,256]{1,0:T(8,128)(2,1)S(1)}, u32[]{:S(2)}, u32[]{:S(2)}) collective-permute-start(bf16[320,256]{1,0:T(8,128)(2,1)S(1)} %collective-permute-done.7.refs_9_), channel_id=1, source_target_pairs={{0,4},{4,0},{1,5},{5,1},{2,6},{6,2},{3,7},{7,3},{8,12},{12,8},{9,1... | collective-permute-start | bytes 491528 | tf_op jit(solution)/shard_map/ppermute | solution.py:645
  23.1 1.6 %collective-permute-start.9 = (bf16[296,256]{1,0:T(8,128)(2,1)S(1)}, bf16[296,256]{1,0:T(8,128)(2,1)S(1)}, u32[]{:S(2)}, u32[]{:S(2)}) collective-permute-start(bf16[296,256]{1,0:T(8,128)(2,1)S(1)} %collective-permute-done.3.refs_1_), channel_id=1, source_target_pairs={{0,4},{4,0},{1,5},{5,1},{2,6},{6,2},{3,7},{7,3},{8,12},{12,8},{9,1... | collective-permute-start | bytes 454664 | tf_op jit(solution)/shard_map/ppermute | solution.py:645
  23.6 1.4 %collective-permute-start.10 = (bf16[296,256]{1,0:T(8,128)(2,1)S(1)}, bf16[296,256]{1,0:T(8,128)(2,1)S(1)}, u32[]{:S(2)}, u32[]{:S(2)}) collective-permute-start(bf16[296,256]{1,0:T(8,128)(2,1)S(1)} %collective-permute-done.4.refs_2_), channel_id=1, source_target_pairs={{0,4},{4,0},{1,5},{5,1},{2,6},{6,2},{3,7},{7,3},{8,12},{12,8},{9,1... | collective-permute-start | bytes 454664 | tf_op jit(solution)/shard_map/ppermute | solution.py:645
  23.9 1.4 %collective-permute-start.11 = (bf16[296,256]{1,0:T(8,128)(2,1)S(1)}, bf16[296,256]{1,0:T(8,128)(2,1)S(1)}, u32[]{:S(2)}, u32[]{:S(2)}) collective-permute-start(bf16[296,256]{1,0:T(8,128)(2,1)S(1)} %collective-permute-done.5.refs_3_), channel_id=1, source_target_pairs={{0,4},{4,0},{1,5},{5,1},{2,6},{6,2},{3,7},{7,3},{8,12},{12,8},{9,1... | collective-permute-start | bytes 454664 | tf_op jit(solution)/shard_map/ppermute | solution.py:645
  41.5 2.2 %collective-permute-start.14 = (bf16[4,4,80,256]{3,2,1,0:T(8,128)(2,1)S(1)}, bf16[4,4,80,256]{3,2,1,0:T(8,128)(2,1)S(1)}, u32[]{:S(2)}, u32[]{:S(2)}) collective-permute-start(bf16[4,4,80,256]{3,2,1,0:T(8,128)(2,1)S(1)} %get-tuple-element.100), channel_id=1, source_target_pairs={{0,4},{4,0},{1,5},{5,1},{2,6},{6,2},{3,7},{7,3},{8,12},{12,8},{9,1... | collective-permute-start | bytes 1966088 | tf_op jit(solution)/shard_map/ppermute | solution.py:645
  43.9 11.0 %collective-permute-start.17 = (bf16[4,80,256]{2,1,0:T(8,128)(2,1)S(1)}, bf16[4,80,256]{2,1,0:T(8,128)(2,1)S(1)}, u32[]{:S(2)}, u32[]{:S(2)}) collective-permute-start(bf16[4,80,256]{2,1,0:T(8,128)(2,1)S(1)} %get-tuple-element.139), channel_id=1, source_target_pairs={{0,24},{8,16},{16,8},{24,0},{1,25},{9,17},{17,9},{25,1},{2,26},{10... | collective-permute-start | bytes 491528 | tf_op jit(solution)/shard_map/ppermute | solution.py:645
  45.9 9.0 %collective-permute-start.16 = (bf16[4,80,256]{2,1,0:T(8,128)(2,1)S(1)}, bf16[4,80,256]{2,1,0:T(8,128)(2,1)S(1)}, u32[]{:S(2)}, u32[]{:S(2)}) collective-permute-start(bf16[4,80,256]{2,1,0:T(8,128)(2,1)S(1)} %get-tuple-element.140), channel_id=1, source_target_pairs={{0,16},{8,24},{16,0},{24,8},{1,17},{9,25},{17,1},{25,9},{2,18},{10... | collective-permute-start | bytes 491528 | tf_op jit(solution)/shard_map/ppermute | solution.py:645
  46.9 8.0 %collective-permute-start.15 = (bf16[4,80,256]{2,1,0:T(8,128)(2,1)S(1)}, bf16[4,80,256]{2,1,0:T(8,128)(2,1)S(1)}, u32[]{:S(2)}, u32[]{:S(2)}) collective-permute-start(bf16[4,80,256]{2,1,0:T(8,128)(2,1)S(1)} %get-tuple-element.141), channel_id=1, source_target_pairs={{0,8},{8,0},{16,24},{24,16},{1,9},{9,1},{17,25},{25,17},{2,10},{10... | collective-permute-start | bytes 491528 | tf_op jit(solution)/shard_map/ppermute | solution.py:645
  54.9 2.1 %collective-permute-start.18 = (bf16[4,4,72,256]{3,2,1,0:T(8,128)(2,1)S(1)}, bf16[4,4,72,256]{3,2,1,0:T(8,128)(2,1)S(1)}, u32[]{:S(2)}, u32[]{:S(2)}) collective-permute-start(bf16[4,4,72,256]{3,2,1,0:T(8,128)(2,1)S(1)} %get-tuple-element.104), channel_id=1, source_target_pairs={{0,4},{4,0},{1,5},{5,1},{2,6},{6,2},{3,7},{7,3},{8,12},{12,8},{9,1... | collective-permute-start | bytes 1769480 | tf_op jit(solution)/shard_map/ppermute | solution.py:645
  57.1 8.3 %collective-permute-start.19 = (bf16[4,72,256]{2,1,0:T(8,128)(2,1)S(1)}, bf16[4,72,256]{2,1,0:T(8,128)(2,1)S(1)}, u32[]{:S(2)}, u32[]{:S(2)}) collective-permute-start(bf16[4,72,256]{2,1,0:T(8,128)(2,1)S(1)} %get-tuple-element.106), channel_id=1, source_target_pairs={{0,8},{8,0},{16,24},{24,16},{1,9},{9,1},{17,25},{25,17},{2,10},{10... | collective-permute-start | bytes 442376 | tf_op jit(solution)/shard_map/ppermute | solution.py:645
  58.7 8.8 %collective-permute-start.20 = (bf16[4,72,256]{2,1,0:T(8,128)(2,1)S(1)}, bf16[4,72,256]{2,1,0:T(8,128)(2,1)S(1)}, u32[]{:S(2)}, u32[]{:S(2)}) collective-permute-start(bf16[4,72,256]{2,1,0:T(8,128)(2,1)S(1)} %get-tuple-element.107), channel_id=1, source_target_pairs={{0,16},{8,24},{16,0},{24,8},{1,17},{9,25},{17,1},{25,9},{2,18},{10... | collective-permute-start | bytes 442376 | tf_op jit(solution)/shard_map/ppermute | solution.py:645
  59.6 7.8 %collective-permute-start.21 = (bf16[4,72,256]{2,1,0:T(8,128)(2,1)S(1)}, bf16[4,72,256]{2,1,0:T(8,128)(2,1)S(1)}, u32[]{:S(2)}, u32[]{:S(2)}) collective-permute-start(bf16[4,72,256]{2,1,0:T(8,128)(2,1)S(1)} %get-tuple-element.108), channel_id=1, source_target_pairs={{0,24},{8,16},{16,8},{24,0},{1,25},{9,17},{17,9},{25,1},{2,26},{10... | collective-permute-start | bytes 442376 | tf_op jit(solution)/shard_map/ppermute | solution.py:645
  60.7 24.1 %copy-start.4 = (f32[576,256]{1,0:T(8,128)S(1)}, f32[576,256]{1,0:T(8,128)}, u32[]{:S(2)}) copy-start(f32[576,256]{1,0:T(8,128)} %refs_4_.1) | copy-start | bytes 1769476
  60.7 24.1 %copy-start.5 = (f32[576,256]{1,0:T(8,128)S(1)}, f32[576,256]{1,0:T(8,128)}, u32[]{:S(2)}) copy-start(f32[576,256]{1,0:T(8,128)} %refs_6_.1) | copy-start | bytes 1769476
  60.7 24.1 %copy-start.6 = (f32[576,256]{1,0:T(8,128)S(1)}, f32[576,256]{1,0:T(8,128)}, u32[]{:S(2)}) copy-start(f32[576,256]{1,0:T(8,128)} %refs_7_.1) | copy-start | bytes 1769476
  65.3 19.4 %copy-start = (f32[576,256]{1,0:T(8,128)S(1)}, f32[576,256]{1,0:T(8,128)}, u32[]{:S(2)}) copy-start(f32[576,256]{1,0:T(8,128)} %refs_5_.1) | copy-start | bytes 1769476
  65.3 19.4 %copy-start.1 = (f32[576,256]{1,0:T(8,128)S(1)}, f32[576,256]{1,0:T(8,128)}, u32[]{:S(2)}) copy-start(f32[576,256]{1,0:T(8,128)} %refs_2_.5) | copy-start | bytes 1769476
  65.4 19.4 %copy-start.2 = (f32[64,256]{1,0:T(8,128)S(1)}, f32[64,256]{1,0:T(8,128)}, u32[]{:S(2)}) copy-start(f32[64,256]{1,0:T(8,128)} %refs_8_.1) | copy-start | bytes 196612
  65.4 19.4 %copy-start.3 = (f32[576,256]{1,0:T(8,128)S(1)}, f32[576,256]{1,0:T(8,128)}, u32[]{:S(2)}) copy-start(f32[576,256]{1,0:T(8,128)} %refs_3_.1) | copy-start | bytes 1769476
  65.4 19.4 %copy-start.7 = (f32[64,256]{1,0:T(8,128)S(1)}, f32[64,256]{1,0:T(8,128)}, u32[]{:S(2)}) copy-start(f32[64,256]{1,0:T(8,128)} %refs_9_.1) | copy-start | bytes 196612
  65.4 19.4 %copy-start.8 = (f32[64,256]{1,0:T(8,128)S(1)}, f32[64,256]{1,0:T(8,128)}, u32[]{:S(2)}) copy-start(f32[64,256]{1,0:T(8,128)} %refs_10_.1) | copy-start | bytes 196612
  67.6 4.5 %collective-permute-start.22 = (bf16[152,256]{1,0:T(8,128)(2,1)S(1)}, bf16[152,256]{1,0:T(8,128)(2,1)S(1)}, u32[]{:S(2)}, u32[]{:S(2)}) collective-permute-start(bf16[152,256]{1,0:T(8,128)(2,1)S(1)} %get-tuple-element.127), channel_id=1, source_target_pairs={{0,1},{1,0},{2,3},{3,2},{4,5},{5,4},{6,7},{7,6},{8,9},{9,8},{10,11... | collective-permute-start | bytes 233480 | tf_op jit(solution)/shard_map/ppermute | solution.py:645
  68.0 8.1 %collective-permute-start.23 = (bf16[152,256]{1,0:T(8,128)(2,1)S(1)}, bf16[152,256]{1,0:T(8,128)(2,1)S(1)}, u32[]{:S(2)}, u32[]{:S(2)}) collective-permute-start(bf16[152,256]{1,0:T(8,128)(2,1)S(1)} %get-tuple-element.128), channel_id=1, source_target_pairs={{0,2},{1,3},{2,0},{3,1},{4,6},{5,7},{6,4},{7,5},{8,10},{9,11},{10,... | collective-permute-start | bytes 233480 | tf_op jit(solution)/shard_map/ppermute | solution.py:645
  69.1 7.0 %collective-permute-start.24 = (bf16[152,256]{1,0:T(8,128)(2,1)S(1)}, bf16[152,256]{1,0:T(8,128)(2,1)S(1)}, u32[]{:S(2)}, u32[]{:S(2)}) collective-permute-start(bf16[152,256]{1,0:T(8,128)(2,1)S(1)} %get-tuple-element.129), channel_id=1, source_target_pairs={{0,3},{1,2},{2,1},{3,0},{4,7},{5,6},{6,5},{7,4},{8,11},{9,10},{10,... | collective-permute-start | bytes 233480 | tf_op jit(solution)/shard_map/ppermute | solution.py:645
  76.1 5.4 %collective-permute-start.27 = (bf16[152,256]{1,0:T(8,128)(2,1)S(1)}, bf16[152,256]{1,0:T(8,128)(2,1)S(1)}, u32[]{:S(2)}, u32[]{:S(2)}) collective-permute-start(bf16[152,256]{1,0:T(8,128)(2,1)S(1)} %add_convert_fusion.8), channel_id=1, source_target_pairs={{0,24},{8,16},{16,8},{24,0},{1,25},{9,17},{17,9},{25,1},{2,26},{10... | collective-permute-start | bytes 233480 | tf_op jit(solution)/shard_map/ppermute | solution.py:645
  77.7 4.6 %collective-permute-start.26 = (bf16[152,256]{1,0:T(8,128)(2,1)S(1)}, bf16[152,256]{1,0:T(8,128)(2,1)S(1)}, u32[]{:S(2)}, u32[]{:S(2)}) collective-permute-start(bf16[152,256]{1,0:T(8,128)(2,1)S(1)} %add_convert_fusion.8), channel_id=1, source_target_pairs={{0,16},{8,24},{16,0},{24,8},{1,17},{9,25},{17,1},{25,9},{2,18},{10... | collective-permute-start | bytes 233480 | tf_op jit(solution)/shard_map/ppermute | solution.py:645
  78.7 4.4 %collective-permute-start.25 = (bf16[152,256]{1,0:T(8,128)(2,1)S(1)}, bf16[152,256]{1,0:T(8,128)(2,1)S(1)}, u32[]{:S(2)}, u32[]{:S(2)}) collective-permute-start(bf16[152,256]{1,0:T(8,128)(2,1)S(1)} %add_convert_fusion.8), channel_id=1, source_target_pairs={{0,8},{8,0},{16,24},{24,16},{1,9},{9,1},{17,25},{25,17},{2,10},{10... | collective-permute-start | bytes 233480 | tf_op jit(solution)/shard_map/ppermute | solution.py:645
  83.1 1.7 %collective-permute-start.28 = (bf16[4,152,256]{2,1,0:T(8,128)(2,1)S(1)}, bf16[4,152,256]{2,1,0:T(8,128)(2,1)S(1)}, u32[]{:S(2)}, u32[]{:S(2)}) collective-permute-start(bf16[4,152,256]{2,1,0:T(8,128)(2,1)S(1)} %pad_maximum_fusion.refs_0_), channel_id=1, source_target_pairs={{0,4},{4,0},{1,5},{5,1},{2,6},{6,2},{3,7},{7,3},{8,12},{12,8},{9,1... | collective-permute-start | bytes 933896 | tf_op jit(solution)/shard_map/ppermute | solution.py:645

commit v6 on v5

--- a/solution.py
+++ b/solution.py
@@ -509,27 +509,58 @@
     )(ids, gp, w, u, slope, xp, after)
 
 
-def tile_sums(plan, early, late):
-    tiles, ranks, piece = plan.tiles, plan.ranks, plan.piece
+def add_up(parts):
+    acc = parts[0].astype(F32)
+    for part in parts[1:]:
+        acc = acc + part.astype(F32)
+    return acc.astype(BF)
+
+
+def tile_sums(plan, parts, below_last=None, after=()):
+    tiles, ranks = plan.tiles, plan.ranks
+    rows = parts[0].shape[1]
+    extra = [] if below_last is None else [below_last]
+    shapes = [rows] * (ranks - 1) + [rows + sum(v.shape[0] for v in extra)]
+    inputs = [*parts, *extra, *after]
 
     def kernel(*refs):
+        results = refs[len(inputs) :]
         for r in range(ranks):
-            to = refs[2 * tiles + r]
-            for at, group in ((0, refs[:tiles]), (piece, refs[tiles : 2 * tiles])):
-                acc = group[0][r].astype(F32)
-                for ref in group[1:]:
-                    acc = acc + ref[r].astype(F32)
-                to[at : at + acc.shape[0]] = acc.astype(BF)
-
-    return pl.pallas_call(
-        kernel,
-        in_specs=[VMEM] * (2 * tiles),
+            results[r][0:rows] = add_up([ref[r] for ref in refs[:tiles]])
+        if extra:
+            results[-1][rows:] = refs[tiles][...]
+
+    return pl.pallas_call(
+        kernel,
+        in_specs=[VMEM] * len(inputs),
         out_specs=[VMEM] * ranks,
-        out_shape=[jax.ShapeDtypeStruct((plan.chunk, plan.c), BF)] * ranks,
-        compiler_params=params(),
-        cost_estimate=cost(0, 6),
+        out_shape=[jax.ShapeDtypeStruct((v, plan.c), BF) for v in shapes],
+        compiler_params=params(),
+        cost_estimate=cost(0, 0),
         name="tile_sums",
-    )(*early, *late)
+    )(*inputs)
+
+
+def rank_sums(plan, early, late, last):
+    piece = plan.piece
+    count = len(early)
+    inputs = [*early, *late, last]
+
+    def kernel(*refs):
+        rows_ref = refs[len(inputs) - 1]
+        to = refs[-1]
+        to[0:piece] = add_up([ref[...] for ref in refs[:count]] + [rows_ref[0:piece]])
+        to[piece:] = add_up([ref[...] for ref in refs[count:-2]] + [rows_ref[piece:]])
+
+    return pl.pallas_call(
+        kernel,
+        in_specs=[VMEM] * len(inputs),
+        out_specs=VMEM,
+        out_shape=jax.ShapeDtypeStruct((plan.chunk, plan.c), BF),
+        compiler_params=params(),
+        cost_estimate=cost(0, 0),
+        name="rank_sums",
+    )(*inputs)
 
 
 def inputs_back_kernel(gp_ref, w_ref, u_ref, ws_ref, go_ref, out_hbm, out_ref, v_ref, sem):
@@ -582,44 +613,42 @@
 UPDATE_STEPS = 4
 
 
-def update(plan, ids, near, far, sets):
+def update(plan, ids, grads, sets, far, old=()):
     c, tiles = plan.c, plan.tiles
 
-    def kernel(ids_ref, *refs):
-        groups, state, new, sum_ref = refs[:2], refs[2:11], refs[11:20], refs[20]
-        done_refs, sem = refs[21:30], refs[30]
+    def kernel(ids_ref, grads_ref, *refs):
+        state = refs[:9]
+        new, done_refs = refs[9 + len(old) : 18 + len(old)], refs[18 + len(old) : 27 + len(old)]
+        sum_ref, sem = refs[27 + len(old) :]
         core, tile = ids_ref[0], ids_ref[1]
+        side = 1 - core if far else core
         at = 0
         stores = []
         for n in range(3):
             piece = plan.skip_piece if n == 2 else plan.piece
-            rows = 2 * tiles * piece
-            for k, group in enumerate(groups):
-                side = core if k == 0 else 1 - core
-                for d in range(tiles):
-                    part = group[d, at : at + piece].astype(F32)
-                    if piece % 8:
-                        for t in range(2 * tiles):
-
-                            def put(part=part, t=t, piece=piece):
-                                sum_ref[t * piece : (t + 1) * piece] = part
-
-                            pl.when(side * tiles + (tile ^ d) == t)(put)
-                    else:
-                        start = pl.multiple_of((side * tiles + (tile ^ d)) * piece, 8)
-                        sum_ref[pl.ds(start, piece)] = part
+            rows = tiles * piece
+            for d in range(tiles):
+                part = grads_ref[d, at : at + piece].astype(F32)
+                if piece % 8:
+                    for t in range(tiles):
+
+                        def put(part=part, t=t, piece=piece):
+                            sum_ref[t * piece : (t + 1) * piece] = part
+
+                        pl.when(tile ^ d == t)(put)
+                else:
+                    sum_ref[pl.ds(pl.multiple_of((tile ^ d) * piece, 8), piece)] = part
             at += piece
-            rate = (rows * plan.ranks) ** (-0.5)
+            rate = (2 * rows * plan.ranks) ** (-0.5)
             step = rows // UPDATE_STEPS if rows % (8 * UPDATE_STEPS) == 0 else rows
             for row in range(0, rows, step):
-                old = (state[3 * n + k][row : row + step] for k in range(3))
-                done = adamw(*old, sum_ref[row : row + step], rate)
+                here = pl.ds(pl.multiple_of(side * rows + row, 8), step)
+                done = adamw(*(state[3 * n + k][here] for k in range(3)), sum_ref[row : row + step], rate)
                 for k in range(3 * n, 3 * n + 3):
                     done_refs[k][row : row + step] = done[k - 3 * n]
                     source = done_refs[k].at[pl.ds(row, step)]
-                    target = new[k].at[pl.ds(row, step)]
                     number = UPDATE_STEPS * k + row // step
-                    stores.append(pltpu.make_async_copy(source, target, sem.at[number]))
+                    stores.append(pltpu.make_async_copy(source, new[k].at[here], sem.at[number]))
                     stores[-1].start()
         for store in stores:
             store.wait()
@@ -627,18 +656,19 @@
     shapes = [v.shape for v in sets]
     return pl.pallas_call(
         kernel,
-        in_specs=[SMEM] + [VMEM] * 11,
+        in_specs=[SMEM] + [VMEM] * 10 + [HBM] * len(old),
         out_specs=[HBM] * 9,
         out_shape=[jax.ShapeDtypeStruct(v, F32) for v in shapes],
         scratch_shapes=[
-            pltpu.VMEM((plan.shard, c), F32),
-            *(pltpu.VMEM(v, F32) for v in shapes),
+            *(pltpu.VMEM((v[0] // 2, c), F32) for v in shapes),
+            pltpu.VMEM((plan.shard // 2, c), F32),
             pltpu.SemaphoreType.DMA((9 * UPDATE_STEPS,)),
         ],
-        compiler_params=params(),
-        cost_estimate=cost(0, 9),
+        input_output_aliases={11 + k: k for k in range(len(old))},
+        compiler_params=params(),
+        cost_estimate=cost(2, 9),
         name="update",
-    )(ids, near, far, *sets)
+    )(ids, grads, *sets, *old)
 
 
 def send(v, axis, size, step):
@@ -710,33 +740,32 @@
         late = [parts2[0]] + [to_tile(parts2[d], d) for d in range(1, tiles)]
         late, away1 = lax.optimization_barrier((late, away1))
         came1 = to_core(away1)
+        late = tile_sums(plan, late)
         parts1 = [total(keep1[d], came1[d]) for d in range(tiles)]
-        op, parts1 = lax.optimization_barrier((op, parts1))
+        op, parts1, late = lax.optimization_barrier((op, parts1, late))
         early = [parts1[0]] + [to_tile(parts1[d], d) for d in range(1, tiles)]
+        late, late_last = late[:-1], late[-1]
+        late = [late[0]] + [to_rank(v, d) for d, v in enumerate(late) if d]
         grad_inputs = inputs_back(op, w1, u1, ws, go)
         early, late, grad_inputs = lax.optimization_barrier((early, late, grad_inputs))
-        parts = tile_sums(plan, early, late)
-        came = [to_rank(parts[d], d) for d in range(1, ranks)]
-        mine = total(parts[0], *came)
+        early = tile_sums(plan, early, late_last, late[1:])
+        early = [early[0]] + [to_rank(v, d) for d, v in enumerate(early) if d]
+        mine = rank_sums(plan, early[:-1], late, early[-1])
         near = jnp.stack([mine] + [to_tile(mine, d) for d in range(1, tiles)])
         far = to_core(near)
-        news = update(
-            plan,
-            ids,
-            near,
-            far,
-            (
-                w_first,
-                mom_first,
-                sq_first,
-                w_second,
-                mom_second,
-                sq_second,
-                w_skip,
-                mom_skip,
-                sq_skip,
-            ),
+        sets = (
+            w_first,
+            mom_first,
+            sq_first,
+            w_second,
+            mom_second,
+            sq_second,
+            w_skip,
+            mom_skip,
+            sq_skip,
         )
+        news = update(plan, ids, near, sets, False)
+        news = update(plan, ids, far, sets, True, news)
         output = jnp.transpose(output, (3, 0, 1, 2, 4))[None]
         grad_inputs = jnp.transpose(grad_inputs, (3, 0, 1, 2, 4))[None]
         return (output, grad_inputs, *news)

time: 88.5 us -> 87.4 us (0.988)
  waiting for transfers between devices: 17.2 us -> 13.4 us
  starting transfers between devices: 30.3 us -> 31.8 us
  Pallas kernels: 38.3 us -> 39.5 us
    ppermute x29 -> x31, waiting for transfers between devices: 17.2 us -> 13.4 us  [send(): return lax.ppermute(v, axis, [(i, i ^ step) for i in range(size)])]
    ppermute x29 -> x31, starting transfers between devices: 30.3 us -> 31.8 us  [send(): return lax.ppermute(v, axis, [(i, i ^ step) for i in range(size)])]
    pallas_call x2 -> x5, Pallas kernels: 3.48 us -> 4.68 us  [the longest x2 4.47 us: update(): pl.pallas_call(kernel, in_specs=[SMEM] + [VMEM] * 10 + [HBM] * len(old),...]
  transfers between devices with their start and end apart: 29 -> 31, of which waited for: 13 -> 13; matrix products, arithmetic and copies ran while one was open for 0% -> 0% of each run, Pallas kernels for 25% -> 28%
where the time goes in v6:
time: 87.4 us; the launch traced here: 87.2 us
  Pallas kernels  39.5 us (45%)
  starting transfers between devices  31.8 us (36%)
  waiting for transfers between devices  13.4 us (15%)
  between operations  1.85 us (2%)
    ppermute x31, starting transfers between devices, send(): return lax.ppermute(v, axis, [(i, i ^ step) for i in range(size)])  31.8 us
    ppermute x31, waiting for transfers between devices, send(): return lax.ppermute(v, axis, [(i, i ^ step) for i in range(size)])  13.4 us
    pallas_call x1, Pallas kernels, second(): pl.pallas_call(kernel, in_specs=[SMEM] + [VMEM] * (6 + 2 * count + 2 * ha...  10.8 us
    pallas_call x1, Pallas kernels, hidden_back(): pl.pallas_call(kernel, in_specs=[SMEM] + [VMEM] * 6, out_specs=[VMEM] * 3...  7.41 us
    pallas_call x1, Pallas kernels, first(): pl.pallas_call(kernel, in_specs=[SMEM] + [VMEM] * (2 + 2 * count), out_sp...  5.34 us
    pallas_call x1, Pallas kernels, inputs_back(): pl.pallas_call(inputs_back_kernel, in_specs=[VMEM] * 5, out_specs=HBM, ou...  4.66 us
    pallas_call x2, Pallas kernels, update(): pl.pallas_call(kernel, in_specs=[SMEM] + [VMEM] * 10 + [HBM] * len(old),...  4.47 us
    pallas_call x1, Pallas kernels, enter(): pl.pallas_call(kernel, in_specs=[SMEM] + [HBM] * 5 + [VMEM] * len(after),...  3.54 us
  transfers between devices with their start and end apart: 31, of which 13 were waited for; matrix products, arithmetic and copies ran while one was open for 0% of the time, Pallas kernels for 28%

profile of v6, /device:TPU:0, one launch (start us, length us, event | category | flops | bytes accessed | tf_op | source)
XLA Modules:
  0.0 87.2 jit_solution(5405822405220213756)
XLA Ops:
  0.7 1.5 %pack.2 = (bf16[72,256]{1,0:T(8,128)(2,1)S(1)}, bf16[152,256]{1,0:T(8,128)(2,1)S(1)}) custom-call(s32[3]{0:T(128)S(1)} %pad_add_fusion.ids_ref, f32[576,256]{1,0:T(8,128)} %refs_0_.9, f32[576,256]{1,0:T(8,128)} %refs_3_.3, f32[64,256]{1,0:T(8,128)} %refs_6_.3), custom_call_target="tpu_custom_call" | custom-call | tf_op jit(solution)/shard_map/pack/pallas_call | solution.py:250
  2.2 5.1 %collective-permute-start.2 = (bf16[152,256]{1,0:T(8,128)(2,1)S(1)}, bf16[152,256]{1,0:T(8,128)(2,1)S(1)}, u32[]{:S(2)}, u32[]{:S(2)}) collective-permute-start(bf16[152,256]{1,0:T(8,128)(2,1)S(1)} %get-tuple-element.92), channel_id=1, source_target_pairs={{0,3},{1,2},{2,1},{3,0},{4,7},{5,6},{6,5},{7,4},{8,11},{9,10},{10,... | collective-permute-start | bytes 233480 | tf_op jit(solution)/shard_map/ppermute | solution.py:675
  7.4 0.6 collective-permute-start
  8.0 1.5 %pack.3.refs_4_ = bf16[320,256]{1,0:T(8,128)(2,1)S(1)} custom-call(s32[3]{0:T(128)S(1)} %pad_add_fusion.ids_ref, f32[576,256]{1,0:T(8,128)} %refs_3_.3, f32[64,256]{1,0:T(8,128)} %refs_6_.3), custom_call_target="tpu_custom_call" | custom-call | tf_op jit(solution)/shard_map/pack/pallas_call | solution.py:250
  9.6 2.4 %collective-permute-start.7 = (bf16[320,256]{1,0:T(8,128)(2,1)S(1)}, bf16[320,256]{1,0:T(8,128)(2,1)S(1)}, u32[]{:S(2)}, u32[]{:S(2)}) collective-permute-start(bf16[320,256]{1,0:T(8,128)(2,1)S(1)} %pack.3.refs_4_), channel_id=1, source_target_pairs={{0,2},{1,3},{2,0},{3,1},{4,6},{5,7},{6,4},{7,5},{8,10},{9,11},{10,... | collective-permute-start | bytes 491528 | tf_op jit(solution)/shard_map/ppermute | solution.py:675
  11.9 2.0 %collective-permute-start.6 = (bf16[320,256]{1,0:T(8,128)(2,1)S(1)}, bf16[320,256]{1,0:T(8,128)(2,1)S(1)}, u32[]{:S(2)}, u32[]{:S(2)}) collective-permute-start(bf16[320,256]{1,0:T(8,128)(2,1)S(1)} %pack.3.refs_4_), channel_id=1, source_target_pairs={{0,1},{1,0},{2,3},{3,2},{4,5},{5,4},{6,7},{7,6},{8,9},{9,8},{10,11... | collective-permute-start | bytes 491528 | tf_op jit(solution)/shard_map/ppermute | solution.py:675
  14.0 2.5 %collective-permute-start.5 = (bf16[296,256]{1,0:T(8,128)(2,1)S(1)}, bf16[296,256]{1,0:T(8,128)(2,1)S(1)}, u32[]{:S(2)}, u32[]{:S(2)}) collective-permute-start(bf16[296,256]{1,0:T(8,128)(2,1)S(1)} %below.1.refs_3_.refs_0_), channel_id=1, source_target_pairs={{0,24},{8,16},{16,8},{24,0},{1,25},{9,17},{17,9},{25,1},{2,26},{10... | collective-permute-start | bytes 454664 | tf_op jit(solution)/shard_map/ppermute | solution.py:675
  16.5 0.5 collective-permute-start.4
  17.0 0.5 collective-permute-start.3
  18.3 3.5 %enter.1 = (bf16[12,8,8,8,256]{4,3,2,1,0:T(8,128)(2,1)S(1)}, bf16[12,6,6,8,256]{4,3,2,1,0:T(8,128)(2,1)S(1)}, bf16[256,256]{1,0:T(8,128)(2,1)S(1)}, bf16[576,256...) custom-call(s32[52]{0:T(128)S(1)} %concatenate.4.ids_ref, ...), custom_call_target="tpu_custom_call" | custom-call | tf_op jit(solution)/shard_map/enter/pallas_call | solution.py:347
  21.9 0.6 collective-permute-done.4.refs_2_
  22.6 0.5 collective-permute-start.12
  23.1 0.5 collective-permute-start.9
  23.6 0.4 collective-permute-done.8.refs_4_
  23.9 0.2 collective-permute-start.11
  24.1 0.6 collective-permute-done.9.refs_5_
  24.7 0.3 collective-permute-done.10.refs_6_
  25.0 0.4 collective-permute-done.11.refs_7_
  25.3 5.3 %first.1 = (bf16[12,8,8,8,256]{4,3,2,1,0:T(8,128)(2,1)S(1)}, bf16[12,6,6,8,256]{4,3,2,1,0:T(8,128)(2,1)S(1)}, bf16[2304,256]{1,0:T(8,128)(2,1)S(1)}, bf16[2,3,256,256]{3,2,1,0:T(8,128)(2,1)S(1)}) custom-call(s32[52]{0:T(128)S(1)} %concatenate.4.ids_ref, bf16[12,8,8,8,256]{4,3,2,1,0:T(8,128)(2,1)S(1)} %get-tuple-element.94.xp_ref, ...), custom_call_target="tpu_custom_call" | custom-call | tf_op jit(solution)/shard_map/first/pallas_call | solution.py:387
  30.7 10.8 %second.1 = (bf16[12,6,6,8,256]{4,3,2,1,0:T(8,128)(2,1)}, bf16[12,8,8,8,256]{4,3,2,1,0:T(8,128)(2,1)S(1)}, bf16[2304,256]{1,0:T(8,128)(2,1)S(1)}, bf16[2,3,256,2...) custom-call(s32[52]{0:T(128)S(1)} %concatenate.4.ids_ref, ...), custom_call_target="tpu_custom_call" | custom-call | flops 8999999488 | bytes 16000000 | tf_op jit(solution)/shard_map/second/pallas_call | solution.py:447
  41.5 0.2 collective-permute-start.14
  41.8 1.9 %collective-permute-done.14 = bf16[4,4,80,256]{3,2,1,0:T(8,128)(2,1)S(1)} collective-permute-done((bf16[4,4,80,256]{3,2,1,0:T(8,128)(2,1)S(1)}, bf16[4,4,80,256]{3,2,1,0:T(8,128)(2,1)S(1)}, u32[]{:S(2)}, u32[]{:S(2)}) %collective-permute-start.14) | collective-permute-done | bytes 655392 | tf_op jit(solution)/shard_map/ppermute | solution.py:675
  43.7 0.2 fusion.3
  43.9 2.0 %collective-permute-start.17 = (bf16[4,80,256]{2,1,0:T(8,128)(2,1)S(1)}, bf16[4,80,256]{2,1,0:T(8,128)(2,1)S(1)}, u32[]{:S(2)}, u32[]{:S(2)}) collective-permute-start(bf16[4,80,256]{2,1,0:T(8,128)(2,1)S(1)} %get-tuple-element.171), channel_id=1, source_target_pairs={{0,24},{8,16},{16,8},{24,0},{1,25},{9,17},{17,9},{25,1},{2,26},{10... | collective-permute-start | bytes 491528 | tf_op jit(solution)/shard_map/ppermute | solution.py:675
  45.8 1.0 %collective-permute-start.16 = (bf16[4,80,256]{2,1,0:T(8,128)(2,1)S(1)}, bf16[4,80,256]{2,1,0:T(8,128)(2,1)S(1)}, u32[]{:S(2)}, u32[]{:S(2)}) collective-permute-start(bf16[4,80,256]{2,1,0:T(8,128)(2,1)S(1)} %get-tuple-element.172), channel_id=1, source_target_pairs={{0,16},{8,24},{16,0},{24,8},{1,17},{9,25},{17,1},{25,9},{2,18},{10... | collective-permute-start | bytes 491528 | tf_op jit(solution)/shard_map/ppermute | solution.py:675
  46.9 0.5 collective-permute-start.15
  47.4 7.4 %hidden_back.1 = (bf16[12,8,8,8,256]{4,3,2,1,0:T(8,128)(2,1)S(1)}, bf16[4,4,72,256]{3,2,1,0:T(8,128)(2,1)S(1)}, bf16[4,4,72,256]{3,2,1,0:T(8,128)(2,1)S(1)}) custom-call(s32[52]{0:T(128)S(1)} %concatenate.4.ids_ref, bf16[12,8,8,8,256]{4,3,2,1,0:T(8,128)(2,1)S(1)} %get-tuple-element.111.gp_ref, bf16[2304,256]{1,0:T(8,128)(2,1)S(1)} %get-tuple-element.112.w_ref, ...), custom_call_target="tpu_custom_call" | custom-call | tf_op jit(solution)/shard_map/hidden_back/pallas_call | solution.py:495
  55.0 1.9 %collective-permute-done.18 = bf16[4,4,72,256]{3,2,1,0:T(8,128)(2,1)S(1)} collective-permute-done((bf16[4,4,72,256]{3,2,1,0:T(8,128)(2,1)S(1)}, bf16[4,4,72,256]{3,2,1,0:T(8,128)(2,1)S(1)}, u32[]{:S(2)}, u32[]{:S(2)}) %collective-permute-start.18) | collective-permute-done | bytes 589856 | tf_op jit(solution)/shard_map/ppermute | solution.py:675
  56.9 0.2 fusion.7
  57.1 1.6 %collective-permute-start.19 = (bf16[4,72,256]{2,1,0:T(8,128)(2,1)S(1)}, bf16[4,72,256]{2,1,0:T(8,128)(2,1)S(1)}, u32[]{:S(2)}, u32[]{:S(2)}) collective-permute-start(bf16[4,72,256]{2,1,0:T(8,128)(2,1)S(1)} %get-tuple-element.130), channel_id=1, source_target_pairs={{0,8},{8,0},{16,24},{24,16},{1,9},{9,1},{17,25},{25,17},{2,10},{10... | collective-permute-start | bytes 442376 | tf_op jit(solution)/shard_map/ppermute | solution.py:675
  58.7 1.0 %collective-permute-start.20 = (bf16[4,72,256]{2,1,0:T(8,128)(2,1)S(1)}, bf16[4,72,256]{2,1,0:T(8,128)(2,1)S(1)}, u32[]{:S(2)}, u32[]{:S(2)}) collective-permute-start(bf16[4,72,256]{2,1,0:T(8,128)(2,1)S(1)} %get-tuple-element.131), channel_id=1, source_target_pairs={{0,16},{8,24},{16,0},{24,8},{1,17},{9,25},{17,1},{25,9},{2,18},{10... | collective-permute-start | bytes 442376 | tf_op jit(solution)/shard_map/ppermute | solution.py:675
  59.6 1.0 %collective-permute-start.21 = (bf16[4,72,256]{2,1,0:T(8,128)(2,1)S(1)}, bf16[4,72,256]{2,1,0:T(8,128)(2,1)S(1)}, u32[]{:S(2)}, u32[]{:S(2)}) collective-permute-start(bf16[4,72,256]{2,1,0:T(8,128)(2,1)S(1)} %get-tuple-element.132), channel_id=1, source_target_pairs={{0,24},{8,16},{16,8},{24,0},{1,25},{9,17},{17,9},{25,1},{2,26},{10... | collective-permute-start | bytes 442376 | tf_op jit(solution)/shard_map/ppermute | solution.py:675
  60.7 0.2 collective-permute-start.22
  60.9 1.2 %collective-permute-start.23 = (bf16[80,256]{1,0:T(8,128)(2,1)S(1)}, bf16[80,256]{1,0:T(8,128)(2,1)S(1)}, u32[]{:S(2)}, u32[]{:S(2)}) collective-permute-start(bf16[80,256]{1,0:T(8,128)(2,1)S(1)} %get-tuple-element.135), channel_id=1, source_target_pairs={{0,2},{1,3},{2,0},{3,1},{4,6},{5,7},{6,4},{7,5},{8,10},{9,11},{10,... | collective-permute-start | bytes 122888 | tf_op jit(solution)/shard_map/ppermute | solution.py:675
  62.2 4.7 %inputs_back.1 = f32[12,6,6,8,256]{4,3,2,1,0:T(8,128)} custom-call(bf16[12,8,8,8,256]{4,3,2,1,0:T(8,128)(2,1)S(1)} %get-tuple-element.136.gp_ref, bf16[2304,256]{1,0:T(8,128)(2,1)S(1)} %get-tuple-element.137.w_ref, bf16[2,3,256,256]{3,2,1,0:T(8,128)(2,1)S(1)} %get-tuple-element.138.u_ref, bf16[256,256]{1,0:T(8,128)(2,1)S(1)} %get-tuple-element.139.ws_ref, ...), custom_call_target="tpu_custom_call" | custom-call | tf_op jit(solution)/shard_map/inputs_back/pallas_call | solution.py:586
  66.9 0.6 collective-permute-done.20.refs_2_
  67.5 2.5 %collective-permute-start.26 = (bf16[152,256]{1,0:T(8,128)(2,1)S(1)}, bf16[152,256]{1,0:T(8,128)(2,1)S(1)}, u32[]{:S(2)}, u32[]{:S(2)}) collective-permute-start(bf16[152,256]{1,0:T(8,128)(2,1)S(1)} %get-tuple-element.152), channel_id=1, source_target_pairs={{0,3},{1,2},{2,1},{3,0},{4,7},{5,6},{6,5},{7,4},{8,11},{9,10},{10,... | collective-permute-start | bytes 233480 | tf_op jit(solution)/shard_map/ppermute | solution.py:675
  70.0 2.0 %collective-permute-start.25 = (bf16[72,256]{1,0:T(8,128)(2,1)S(1)}, bf16[72,256]{1,0:T(8,128)(2,1)S(1)}, u32[]{:S(2)}, u32[]{:S(2)}) collective-permute-start(bf16[72,256]{1,0:T(8,128)(2,1)S(1)} %get-tuple-element.150), channel_id=1, source_target_pairs={{0,2},{1,3},{2,0},{3,1},{4,6},{5,7},{6,4},{7,5},{8,10},{9,11},{10,... | collective-permute-start | bytes 110600 | tf_op jit(solution)/shard_map/ppermute | solution.py:675
  72.0 2.5 %collective-permute-done.24.refs_1_ = bf16[72,256]{1,0:T(8,128)(2,1)S(1)} collective-permute-done((bf16[72,256]{1,0:T(8,128)(2,1)S(1)}, bf16[72,256]{1,0:T(8,128)(2,1)S(1)}, u32[]{:S(2)}, u32[]{:S(2)}) %collective-permute-start.24) | collective-permute-done | bytes 36896 | tf_op jit(solution)/shard_map/ppermute | solution.py:675
  74.4 0.4 collective-permute-done.25.refs_2_
  74.9 2.0 %collective-permute-start.29 = (bf16[152,256]{1,0:T(8,128)(2,1)S(1)}, bf16[152,256]{1,0:T(8,128)(2,1)S(1)}, u32[]{:S(2)}, u32[]{:S(2)}) collective-permute-start(bf16[152,256]{1,0:T(8,128)(2,1)S(1)} %rank_sums.1), channel_id=1, source_target_pairs={{0,24},{8,16},{16,8},{24,0},{1,25},{9,17},{17,9},{25,1},{2,26},{10... | collective-permute-start | bytes 233480 | tf_op jit(solution)/shard_map/ppermute | solution.py:675
  76.9 1.0 %collective-permute-start.28 = (bf16[152,256]{1,0:T(8,128)(2,1)S(1)}, bf16[152,256]{1,0:T(8,128)(2,1)S(1)}, u32[]{:S(2)}, u32[]{:S(2)}) collective-permute-start(bf16[152,256]{1,0:T(8,128)(2,1)S(1)} %rank_sums.1), channel_id=1, source_target_pairs={{0,16},{8,24},{16,0},{24,8},{1,17},{9,25},{17,1},{25,9},{2,18},{10... | collective-permute-start | bytes 233480 | tf_op jit(solution)/shard_map/ppermute | solution.py:675
  77.9 0.5 collective-permute-start.27
  78.5 2.5 %collective-permute-done.29 = bf16[152,256]{1,0:T(8,128)(2,1)S(1)} collective-permute-done((bf16[152,256]{1,0:T(8,128)(2,1)S(1)}, bf16[152,256]{1,0:T(8,128)(2,1)S(1)}, u32[]{:S(2)}, u32[]{:S(2)}) %collective-permute-start.29) | collective-permute-done | bytes 77856 | tf_op jit(solution)/shard_map/ppermute | solution.py:675
  81.0 0.6 collective-permute-done.28
  81.6 0.7 collective-permute-done.27
  82.5 2.2 %update.2 = (f32[576,256]{1,0:T(8,128)}, f32[576,256]{1,0:T(8,128)}, f32[576,256]{1,0:T(8,128)}, f32[576,256]{1,0:T(8,128)}, f32[576,256]{1,0:T(8,128)}, /*index...) custom-call(s32[52]{0:T(128)S(1)} %concatenate.4.ids_ref, ...), custom_call_target="tpu_custom_call" | custom-call | flops 2000000000 | bytes 9000000 | tf_op jit(solution)/shard_map/update/pallas_call | solution.py:657
  84.8 2.2 %update.3 = (f32[576,256]{1,0:T(8,128)}, f32[576,256]{1,0:T(8,128)}, f32[576,256]{1,0:T(8,128)}, f32[576,256]{1,0:T(8,128)}, f32[576,256]{1,0:T(8,128)}, /*index...) custom-call(s32[52]{0:T(128)S(1)} %concatenate.4.ids_ref, ...), custom_call_target="tpu_custom_call", output_to_operand_aliasing={{0}: (11, {}), {1}: (12, {}), {2}: (13, {}), {3}: (14, {}),... | custom-call | flops 2000000000 | bytes 9000000 | tf_op jit(solution)/shard_map/update/pallas_call | solution.py:657
  (53 shorter events, 0.8 us)
Async XLA Ops:
  0.6 17.5 %copy-start.9 = (s32[12,4]{0,1:T(4,128)S(1)}, s32[12,4]{0,1:T(4,128)}, u32[]{:S(2)}) copy-start(s32[12,4]{0,1:T(4,128)} %param.16) | copy-start | bytes 580
  2.2 11.7 %collective-permute-start.2 = (bf16[152,256]{1,0:T(8,128)(2,1)S(1)}, bf16[152,256]{1,0:T(8,128)(2,1)S(1)}, u32[]{:S(2)}, u32[]{:S(2)}) collective-permute-start(bf16[152,256]{1,0:T(8,128)(2,1)S(1)} %get-tuple-element.92), channel_id=1, source_target_pairs={{0,3},{1,2},{2,1},{3,0},{4,7},{5,6},{6,5},{7,4},{8,11},{9,10},{10,... | collective-permute-start | bytes 233480 | tf_op jit(solution)/shard_map/ppermute | solution.py:675
  7.4 6.6 %collective-permute-start.1 = (bf16[72,256]{1,0:T(8,128)(2,1)S(1)}, bf16[72,256]{1,0:T(8,128)(2,1)S(1)}, u32[]{:S(2)}, u32[]{:S(2)}) collective-permute-start(bf16[72,256]{1,0:T(8,128)(2,1)S(1)} %get-tuple-element.91), channel_id=1, source_target_pairs={{0,2},{1,3},{2,0},{3,1},{4,6},{5,7},{6,4},{7,5},{8,10},{9,11},{10,... | collective-permute-start | bytes 110600 | tf_op jit(solution)/shard_map/ppermute | solution.py:675
  7.4 6.6 %collective-permute-start = (bf16[72,256]{1,0:T(8,128)(2,1)S(1)}, bf16[72,256]{1,0:T(8,128)(2,1)S(1)}, u32[]{:S(2)}, u32[]{:S(2)}) collective-permute-start(bf16[72,256]{1,0:T(8,128)(2,1)S(1)} %get-tuple-element.91), channel_id=1, source_target_pairs={{0,1},{1,0},{2,3},{3,2},{4,5},{5,4},{6,7},{7,6},{8,9},{9,8},{10,11... | collective-permute-start | bytes 110600 | tf_op jit(solution)/shard_map/ppermute | solution.py:675
  9.6 12.3 %collective-permute-start.7 = (bf16[320,256]{1,0:T(8,128)(2,1)S(1)}, bf16[320,256]{1,0:T(8,128)(2,1)S(1)}, u32[]{:S(2)}, u32[]{:S(2)}) collective-permute-start(bf16[320,256]{1,0:T(8,128)(2,1)S(1)} %pack.3.refs_4_), channel_id=1, source_target_pairs={{0,2},{1,3},{2,0},{3,1},{4,6},{5,7},{6,4},{7,5},{8,10},{9,11},{10,... | collective-permute-start | bytes 491528 | tf_op jit(solution)/shard_map/ppermute | solution.py:675
  11.9 10.0 %collective-permute-start.6 = (bf16[320,256]{1,0:T(8,128)(2,1)S(1)}, bf16[320,256]{1,0:T(8,128)(2,1)S(1)}, u32[]{:S(2)}, u32[]{:S(2)}) collective-permute-start(bf16[320,256]{1,0:T(8,128)(2,1)S(1)} %pack.3.refs_4_), channel_id=1, source_target_pairs={{0,1},{1,0},{2,3},{3,2},{4,5},{5,4},{6,7},{7,6},{8,9},{9,8},{10,11... | collective-permute-start | bytes 491528 | tf_op jit(solution)/shard_map/ppermute | solution.py:675
  14.0 8.0 %collective-permute-start.5 = (bf16[296,256]{1,0:T(8,128)(2,1)S(1)}, bf16[296,256]{1,0:T(8,128)(2,1)S(1)}, u32[]{:S(2)}, u32[]{:S(2)}) collective-permute-start(bf16[296,256]{1,0:T(8,128)(2,1)S(1)} %below.1.refs_3_.refs_0_), channel_id=1, source_target_pairs={{0,24},{8,16},{16,8},{24,0},{1,25},{9,17},{17,9},{25,1},{2,26},{10... | collective-permute-start | bytes 454664 | tf_op jit(solution)/shard_map/ppermute | solution.py:675
  16.5 6.0 %collective-permute-start.4 = (bf16[296,256]{1,0:T(8,128)(2,1)S(1)}, bf16[296,256]{1,0:T(8,128)(2,1)S(1)}, u32[]{:S(2)}, u32[]{:S(2)}) collective-permute-start(bf16[296,256]{1,0:T(8,128)(2,1)S(1)} %below.1.refs_3_.refs_0_), channel_id=1, source_target_pairs={{0,16},{8,24},{16,0},{24,8},{1,17},{9,25},{17,1},{25,9},{2,18},{10... | collective-permute-start | bytes 454664 | tf_op jit(solution)/shard_map/ppermute | solution.py:675
  17.0 5.6 %collective-permute-start.3 = (bf16[296,256]{1,0:T(8,128)(2,1)S(1)}, bf16[296,256]{1,0:T(8,128)(2,1)S(1)}, u32[]{:S(2)}, u32[]{:S(2)}) collective-permute-start(bf16[296,256]{1,0:T(8,128)(2,1)S(1)} %below.1.refs_3_.refs_0_), channel_id=1, source_target_pairs={{0,8},{8,0},{16,24},{24,16},{1,9},{9,1},{17,25},{25,17},{2,10},{10... | collective-permute-start | bytes 454664 | tf_op jit(solution)/shard_map/ppermute | solution.py:675
  22.6 1.4 %collective-permute-start.8 = (bf16[296,256]{1,0:T(8,128)(2,1)S(1)}, bf16[296,256]{1,0:T(8,128)(2,1)S(1)}, u32[]{:S(2)}, u32[]{:S(2)}) collective-permute-start(bf16[296,256]{1,0:T(8,128)(2,1)S(1)} %below.1.refs_3_.refs_0_), channel_id=1, source_target_pairs={{0,4},{4,0},{1,5},{5,1},{2,6},{6,2},{3,7},{7,3},{8,12},{12,8},{9,1... | collective-permute-start | bytes 454664 | tf_op jit(solution)/shard_map/ppermute | solution.py:675
  22.6 8.1 %collective-permute-start.12 = (bf16[320,256]{1,0:T(8,128)(2,1)S(1)}, bf16[320,256]{1,0:T(8,128)(2,1)S(1)}, u32[]{:S(2)}, u32[]{:S(2)}) collective-permute-start(bf16[320,256]{1,0:T(8,128)(2,1)S(1)} %collective-permute-done.6.refs_8_), channel_id=1, source_target_pairs={{0,4},{4,0},{1,5},{5,1},{2,6},{6,2},{3,7},{7,3},{8,12},{12,8},{9,1... | collective-permute-start | bytes 491528 | tf_op jit(solution)/shard_map/ppermute | solution.py:675
  23.1 7.6 %collective-permute-start.13 = (bf16[320,256]{1,0:T(8,128)(2,1)S(1)}, bf16[320,256]{1,0:T(8,128)(2,1)S(1)}, u32[]{:S(2)}, u32[]{:S(2)}) collective-permute-start(bf16[320,256]{1,0:T(8,128)(2,1)S(1)} %collective-permute-done.7.refs_9_), channel_id=1, source_target_pairs={{0,4},{4,0},{1,5},{5,1},{2,6},{6,2},{3,7},{7,3},{8,12},{12,8},{9,1... | collective-permute-start | bytes 491528 | tf_op jit(solution)/shard_map/ppermute | solution.py:675
  23.1 1.6 %collective-permute-start.9 = (bf16[296,256]{1,0:T(8,128)(2,1)S(1)}, bf16[296,256]{1,0:T(8,128)(2,1)S(1)}, u32[]{:S(2)}, u32[]{:S(2)}) collective-permute-start(bf16[296,256]{1,0:T(8,128)(2,1)S(1)} %collective-permute-done.3.refs_1_), channel_id=1, source_target_pairs={{0,4},{4,0},{1,5},{5,1},{2,6},{6,2},{3,7},{7,3},{8,12},{12,8},{9,1... | collective-permute-start | bytes 454664 | tf_op jit(solution)/shard_map/ppermute | solution.py:675
  23.6 1.4 %collective-permute-start.10 = (bf16[296,256]{1,0:T(8,128)(2,1)S(1)}, bf16[296,256]{1,0:T(8,128)(2,1)S(1)}, u32[]{:S(2)}, u32[]{:S(2)}) collective-permute-start(bf16[296,256]{1,0:T(8,128)(2,1)S(1)} %collective-permute-done.4.refs_2_), channel_id=1, source_target_pairs={{0,4},{4,0},{1,5},{5,1},{2,6},{6,2},{3,7},{7,3},{8,12},{12,8},{9,1... | collective-permute-start | bytes 454664 | tf_op jit(solution)/shard_map/ppermute | solution.py:675
  23.9 1.4 %collective-permute-start.11 = (bf16[296,256]{1,0:T(8,128)(2,1)S(1)}, bf16[296,256]{1,0:T(8,128)(2,1)S(1)}, u32[]{:S(2)}, u32[]{:S(2)}) collective-permute-start(bf16[296,256]{1,0:T(8,128)(2,1)S(1)} %collective-permute-done.5.refs_3_), channel_id=1, source_target_pairs={{0,4},{4,0},{1,5},{5,1},{2,6},{6,2},{3,7},{7,3},{8,12},{12,8},{9,1... | collective-permute-start | bytes 454664 | tf_op jit(solution)/shard_map/ppermute | solution.py:675
  41.5 2.2 %collective-permute-start.14 = (bf16[4,4,80,256]{3,2,1,0:T(8,128)(2,1)S(1)}, bf16[4,4,80,256]{3,2,1,0:T(8,128)(2,1)S(1)}, u32[]{:S(2)}, u32[]{:S(2)}) collective-permute-start(bf16[4,4,80,256]{3,2,1,0:T(8,128)(2,1)S(1)} %get-tuple-element.116), channel_id=1, source_target_pairs={{0,4},{4,0},{1,5},{5,1},{2,6},{6,2},{3,7},{7,3},{8,12},{12,8},{9,1... | collective-permute-start | bytes 1966088 | tf_op jit(solution)/shard_map/ppermute | solution.py:675
  43.9 11.0 %collective-permute-start.17 = (bf16[4,80,256]{2,1,0:T(8,128)(2,1)S(1)}, bf16[4,80,256]{2,1,0:T(8,128)(2,1)S(1)}, u32[]{:S(2)}, u32[]{:S(2)}) collective-permute-start(bf16[4,80,256]{2,1,0:T(8,128)(2,1)S(1)} %get-tuple-element.171), channel_id=1, source_target_pairs={{0,24},{8,16},{16,8},{24,0},{1,25},{9,17},{17,9},{25,1},{2,26},{10... | collective-permute-start | bytes 491528 | tf_op jit(solution)/shard_map/ppermute | solution.py:675
  45.8 9.0 %collective-permute-start.16 = (bf16[4,80,256]{2,1,0:T(8,128)(2,1)S(1)}, bf16[4,80,256]{2,1,0:T(8,128)(2,1)S(1)}, u32[]{:S(2)}, u32[]{:S(2)}) collective-permute-start(bf16[4,80,256]{2,1,0:T(8,128)(2,1)S(1)} %get-tuple-element.172), channel_id=1, source_target_pairs={{0,16},{8,24},{16,0},{24,8},{1,17},{9,25},{17,1},{25,9},{2,18},{10... | collective-permute-start | bytes 491528 | tf_op jit(solution)/shard_map/ppermute | solution.py:675
  46.9 8.0 %collective-permute-start.15 = (bf16[4,80,256]{2,1,0:T(8,128)(2,1)S(1)}, bf16[4,80,256]{2,1,0:T(8,128)(2,1)S(1)}, u32[]{:S(2)}, u32[]{:S(2)}) collective-permute-start(bf16[4,80,256]{2,1,0:T(8,128)(2,1)S(1)} %get-tuple-element.173), channel_id=1, source_target_pairs={{0,8},{8,0},{16,24},{24,16},{1,9},{9,1},{17,25},{25,17},{2,10},{10... | collective-permute-start | bytes 491528 | tf_op jit(solution)/shard_map/ppermute | solution.py:675
  54.9 2.1 %collective-permute-start.18 = (bf16[4,4,72,256]{3,2,1,0:T(8,128)(2,1)S(1)}, bf16[4,4,72,256]{3,2,1,0:T(8,128)(2,1)S(1)}, u32[]{:S(2)}, u32[]{:S(2)}) collective-permute-start(bf16[4,4,72,256]{3,2,1,0:T(8,128)(2,1)S(1)} %get-tuple-element.120), channel_id=1, source_target_pairs={{0,4},{4,0},{1,5},{5,1},{2,6},{6,2},{3,7},{7,3},{8,12},{12,8},{9,1... | collective-permute-start | bytes 1769480 | tf_op jit(solution)/shard_map/ppermute | solution.py:675
  57.1 9.8 %collective-permute-start.19 = (bf16[4,72,256]{2,1,0:T(8,128)(2,1)S(1)}, bf16[4,72,256]{2,1,0:T(8,128)(2,1)S(1)}, u32[]{:S(2)}, u32[]{:S(2)}) collective-permute-start(bf16[4,72,256]{2,1,0:T(8,128)(2,1)S(1)} %get-tuple-element.130), channel_id=1, source_target_pairs={{0,8},{8,0},{16,24},{24,16},{1,9},{9,1},{17,25},{25,17},{2,10},{10... | collective-permute-start | bytes 442376 | tf_op jit(solution)/shard_map/ppermute | solution.py:675
  58.7 8.8 %collective-permute-start.20 = (bf16[4,72,256]{2,1,0:T(8,128)(2,1)S(1)}, bf16[4,72,256]{2,1,0:T(8,128)(2,1)S(1)}, u32[]{:S(2)}, u32[]{:S(2)}) collective-permute-start(bf16[4,72,256]{2,1,0:T(8,128)(2,1)S(1)} %get-tuple-element.131), channel_id=1, source_target_pairs={{0,16},{8,24},{16,0},{24,8},{1,17},{9,25},{17,1},{25,9},{2,18},{10... | collective-permute-start | bytes 442376 | tf_op jit(solution)/shard_map/ppermute | solution.py:675
  59.6 7.8 %collective-permute-start.21 = (bf16[4,72,256]{2,1,0:T(8,128)(2,1)S(1)}, bf16[4,72,256]{2,1,0:T(8,128)(2,1)S(1)}, u32[]{:S(2)}, u32[]{:S(2)}) collective-permute-start(bf16[4,72,256]{2,1,0:T(8,128)(2,1)S(1)} %get-tuple-element.132), channel_id=1, source_target_pairs={{0,24},{8,16},{16,8},{24,0},{1,25},{9,17},{17,9},{25,1},{2,26},{10... | collective-permute-start | bytes 442376 | tf_op jit(solution)/shard_map/ppermute | solution.py:675
  60.7 6.2 %collective-permute-start.22 = (bf16[80,256]{1,0:T(8,128)(2,1)S(1)}, bf16[80,256]{1,0:T(8,128)(2,1)S(1)}, u32[]{:S(2)}, u32[]{:S(2)}) collective-permute-start(bf16[80,256]{1,0:T(8,128)(2,1)S(1)} %get-tuple-element.134), channel_id=1, source_target_pairs={{0,1},{1,0},{2,3},{3,2},{4,5},{5,4},{6,7},{7,6},{8,9},{9,8},{10,11... | collective-permute-start | bytes 122888 | tf_op jit(solution)/shard_map/ppermute | solution.py:675
  60.9 5.9 %collective-permute-start.23 = (bf16[80,256]{1,0:T(8,128)(2,1)S(1)}, bf16[80,256]{1,0:T(8,128)(2,1)S(1)}, u32[]{:S(2)}, u32[]{:S(2)}) collective-permute-start(bf16[80,256]{1,0:T(8,128)(2,1)S(1)} %get-tuple-element.135), channel_id=1, source_target_pairs={{0,2},{1,3},{2,0},{3,1},{4,6},{5,7},{6,4},{7,5},{8,10},{9,11},{10,... | collective-permute-start | bytes 122888 | tf_op jit(solution)/shard_map/ppermute | solution.py:675
  62.1 20.3 %copy-start = (f32[576,256]{1,0:T(8,128)S(1)}, f32[576,256]{1,0:T(8,128)}, u32[]{:S(2)}) copy-start(f32[576,256]{1,0:T(8,128)} %refs_3_.3) | copy-start | bytes 1769476
  62.1 20.4 %copy-start.1 = (f32[576,256]{1,0:T(8,128)S(1)}, f32[576,256]{1,0:T(8,128)}, u32[]{:S(2)}) copy-start(f32[576,256]{1,0:T(8,128)} %refs_0_.9) | copy-start | bytes 1769476
  62.1 20.4 %copy-start.2 = (f32[64,256]{1,0:T(8,128)S(1)}, f32[64,256]{1,0:T(8,128)}, u32[]{:S(2)}) copy-start(f32[64,256]{1,0:T(8,128)} %refs_6_.3) | copy-start | bytes 196612
  62.1 20.4 %copy-start.3 = (f32[576,256]{1,0:T(8,128)S(1)}, f32[576,256]{1,0:T(8,128)}, u32[]{:S(2)}) copy-start(f32[576,256]{1,0:T(8,128)} %refs_1_.9) | copy-start | bytes 1769476
  62.1 20.4 %copy-start.4 = (f32[576,256]{1,0:T(8,128)S(1)}, f32[576,256]{1,0:T(8,128)}, u32[]{:S(2)}) copy-start(f32[576,256]{1,0:T(8,128)} %refs_2_.7) | copy-start | bytes 1769476
  62.1 20.4 %copy-start.5 = (f32[576,256]{1,0:T(8,128)S(1)}, f32[576,256]{1,0:T(8,128)}, u32[]{:S(2)}) copy-start(f32[576,256]{1,0:T(8,128)} %refs_4_.3) | copy-start | bytes 1769476
  62.1 20.4 %copy-start.6 = (f32[576,256]{1,0:T(8,128)S(1)}, f32[576,256]{1,0:T(8,128)}, u32[]{:S(2)}) copy-start(f32[576,256]{1,0:T(8,128)} %refs_5_.3) | copy-start | bytes 1769476
  62.1 20.4 %copy-start.7 = (f32[64,256]{1,0:T(8,128)S(1)}, f32[64,256]{1,0:T(8,128)}, u32[]{:S(2)}) copy-start(f32[64,256]{1,0:T(8,128)} %refs_7_.3) | copy-start | bytes 196612
  62.2 20.4 %copy-start.8 = (f32[64,256]{1,0:T(8,128)S(1)}, f32[64,256]{1,0:T(8,128)}, u32[]{:S(2)}) copy-start(f32[64,256]{1,0:T(8,128)} %refs_8_.3) | copy-start | bytes 196612
  67.5 7.3 %collective-permute-start.26 = (bf16[152,256]{1,0:T(8,128)(2,1)S(1)}, bf16[152,256]{1,0:T(8,128)(2,1)S(1)}, u32[]{:S(2)}, u32[]{:S(2)}) collective-permute-start(bf16[152,256]{1,0:T(8,128)(2,1)S(1)} %get-tuple-element.152), channel_id=1, source_target_pairs={{0,3},{1,2},{2,1},{3,0},{4,7},{5,6},{6,5},{7,4},{8,11},{9,10},{10,... | collective-permute-start | bytes 233480 | tf_op jit(solution)/shard_map/ppermute | solution.py:675
  70.0 4.4 %collective-permute-start.24 = (bf16[72,256]{1,0:T(8,128)(2,1)S(1)}, bf16[72,256]{1,0:T(8,128)(2,1)S(1)}, u32[]{:S(2)}, u32[]{:S(2)}) collective-permute-start(bf16[72,256]{1,0:T(8,128)(2,1)S(1)} %get-tuple-element.149), channel_id=1, source_target_pairs={{0,1},{1,0},{2,3},{3,2},{4,5},{5,4},{6,7},{7,6},{8,9},{9,8},{10,11... | collective-permute-start | bytes 110600 | tf_op jit(solution)/shard_map/ppermute | solution.py:675
  70.0 4.9 %collective-permute-start.25 = (bf16[72,256]{1,0:T(8,128)(2,1)S(1)}, bf16[72,256]{1,0:T(8,128)(2,1)S(1)}, u32[]{:S(2)}, u32[]{:S(2)}) collective-permute-start(bf16[72,256]{1,0:T(8,128)(2,1)S(1)} %get-tuple-element.150), channel_id=1, source_target_pairs={{0,2},{1,3},{2,0},{3,1},{4,6},{5,7},{6,4},{7,5},{8,10},{9,11},{10,... | collective-permute-start | bytes 110600 | tf_op jit(solution)/shard_map/ppermute | solution.py:675
  74.9 6.1 %collective-permute-start.29 = (bf16[152,256]{1,0:T(8,128)(2,1)S(1)}, bf16[152,256]{1,0:T(8,128)(2,1)S(1)}, u32[]{:S(2)}, u32[]{:S(2)}) collective-permute-start(bf16[152,256]{1,0:T(8,128)(2,1)S(1)} %rank_sums.1), channel_id=1, source_target_pairs={{0,24},{8,16},{16,8},{24,0},{1,25},{9,17},{17,9},{25,1},{2,26},{10... | collective-permute-start | bytes 233480 | tf_op jit(solution)/shard_map/ppermute | solution.py:675
  76.9 4.7 %collective-permute-start.28 = (bf16[152,256]{1,0:T(8,128)(2,1)S(1)}, bf16[152,256]{1,0:T(8,128)(2,1)S(1)}, u32[]{:S(2)}, u32[]{:S(2)}) collective-permute-start(bf16[152,256]{1,0:T(8,128)(2,1)S(1)} %rank_sums.1), channel_id=1, source_target_pairs={{0,16},{8,24},{16,0},{24,8},{1,17},{9,25},{17,1},{25,9},{2,18},{10... | collective-permute-start | bytes 233480 | tf_op jit(solution)/shard_map/ppermute | solution.py:675
  77.9 4.4 %collective-permute-start.27 = (bf16[152,256]{1,0:T(8,128)(2,1)S(1)}, bf16[152,256]{1,0:T(8,128)(2,1)S(1)}, u32[]{:S(2)}, u32[]{:S(2)}) collective-permute-start(bf16[152,256]{1,0:T(8,128)(2,1)S(1)} %rank_sums.1), channel_id=1, source_target_pairs={{0,8},{8,0},{16,24},{24,16},{1,9},{9,1},{17,25},{25,17},{2,10},{10... | collective-permute-start | bytes 233480 | tf_op jit(solution)/shard_map/ppermute | solution.py:675
  82.4 2.4 %collective-permute-start.30 = (bf16[4,152,256]{2,1,0:T(8,128)(2,1)S(1)}, bf16[4,152,256]{2,1,0:T(8,128)(2,1)S(1)}, u32[]{:S(2)}, u32[]{:S(2)}) collective-permute-start(bf16[4,152,256]{2,1,0:T(8,128)(2,1)S(1)} %pad_maximum_fusion.grads_ref), channel_id=1, source_target_pairs={{0,4},{4,0},{1,5},{5,1},{2,6},{6,2},{3,7},{7,3},{8,12},{12,8},{9,1... | collective-permute-start | bytes 933896 | tf_op jit(solution)/shard_map/ppermute | solution.py:675

commit v7 on v6

--- a/solution.py
+++ b/solution.py
@@ -146,7 +146,7 @@
     edges = (p_ref[face, 1, cols], p_ref[face, rows, FS], p_ref[face, FS, cols], p_ref[face, rows, 1])
     for side, part in enumerate(edges):
         to = neighbour(ids_ref, side, face)
-        e_ref[to, side] = e_ref[to, side] + part.astype(F32)
+        e_ref[to, side] = e_ref[to, side] + part
 
 
 def fill_halo_back(e_ref, p_ref):
@@ -159,7 +159,7 @@
 
 
 def edge_sums(c):
-    return pltpu.VMEM((FACES, 4, FS, ROLL, c), F32)
+    return pltpu.VMEM((FACES, 4, FS, ROLL, c), BF)
 
 
 class Plan:

time: 87.4 us -> 87 us (level)
  no operation moved by 1% of the time
where the time goes in v7:
time: 87 us; the launch traced here: 86.8 us
  Pallas kernels  39.1 us (45%)
  starting transfers between devices  31.8 us (37%)
  waiting for transfers between devices  13.4 us (15%)
  between operations  1.85 us (2%)
    ppermute x31, starting transfers between devices, send(): return lax.ppermute(v, axis, [(i, i ^ step) for i in range(size)])  31.8 us
    ppermute x31, waiting for transfers between devices, send(): return lax.ppermute(v, axis, [(i, i ^ step) for i in range(size)])  13.4 us
    pallas_call x1, Pallas kernels, second(): pl.pallas_call(kernel, in_specs=[SMEM] + [VMEM] * (6 + 2 * count + 2 * ha...  10.6 us
    pallas_call x1, Pallas kernels, hidden_back(): pl.pallas_call(kernel, in_specs=[SMEM] + [VMEM] * 6, out_specs=[VMEM] * 3...  7.25 us
    pallas_call x1, Pallas kernels, first(): pl.pallas_call(kernel, in_specs=[SMEM] + [VMEM] * (2 + 2 * count), out_sp...  5.34 us
    pallas_call x1, Pallas kernels, inputs_back(): pl.pallas_call(inputs_back_kernel, in_specs=[VMEM] * 5, out_specs=HBM, ou...  4.66 us
    pallas_call x2, Pallas kernels, update(): pl.pallas_call(kernel, in_specs=[SMEM] + [VMEM] * 10 + [HBM] * len(old),...  4.47 us
    pallas_call x1, Pallas kernels, enter(): pl.pallas_call(kernel, in_specs=[SMEM] + [HBM] * 5 + [VMEM] * len(after),...  3.54 us
  transfers between devices with their start and end apart: 31, of which 13 were waited for; matrix products, arithmetic and copies ran while one was open for 0% of the time, Pallas kernels for 28%

profile of v7, /device:TPU:0, one launch (start us, length us, event | category | flops | bytes accessed | tf_op | source)
XLA Modules:
  0.0 86.8 jit_solution(12936270464284034704)
XLA Ops:
  0.7 1.5 %pack.2 = (bf16[72,256]{1,0:T(8,128)(2,1)S(1)}, bf16[152,256]{1,0:T(8,128)(2,1)S(1)}) custom-call(s32[3]{0:T(128)S(1)} %pad_add_fusion.ids_ref, f32[576,256]{1,0:T(8,128)} %refs_0_.9, f32[576,256]{1,0:T(8,128)} %refs_3_.3, f32[64,256]{1,0:T(8,128)} %refs_6_.3), custom_call_target="tpu_custom_call" | custom-call | tf_op jit(solution)/shard_map/pack/pallas_call | solution.py:250
  2.2 5.1 %collective-permute-start.2 = (bf16[152,256]{1,0:T(8,128)(2,1)S(1)}, bf16[152,256]{1,0:T(8,128)(2,1)S(1)}, u32[]{:S(2)}, u32[]{:S(2)}) collective-permute-start(bf16[152,256]{1,0:T(8,128)(2,1)S(1)} %get-tuple-element.92), channel_id=1, source_target_pairs={{0,3},{1,2},{2,1},{3,0},{4,7},{5,6},{6,5},{7,4},{8,11},{9,10},{10,... | collective-permute-start | bytes 233480 | tf_op jit(solution)/shard_map/ppermute | solution.py:675
  7.4 0.6 collective-permute-start
  8.0 1.5 %pack.3.refs_4_ = bf16[320,256]{1,0:T(8,128)(2,1)S(1)} custom-call(s32[3]{0:T(128)S(1)} %pad_add_fusion.ids_ref, f32[576,256]{1,0:T(8,128)} %refs_3_.3, f32[64,256]{1,0:T(8,128)} %refs_6_.3), custom_call_target="tpu_custom_call" | custom-call | tf_op jit(solution)/shard_map/pack/pallas_call | solution.py:250
  9.6 2.4 %collective-permute-start.7 = (bf16[320,256]{1,0:T(8,128)(2,1)S(1)}, bf16[320,256]{1,0:T(8,128)(2,1)S(1)}, u32[]{:S(2)}, u32[]{:S(2)}) collective-permute-start(bf16[320,256]{1,0:T(8,128)(2,1)S(1)} %pack.3.refs_4_), channel_id=1, source_target_pairs={{0,2},{1,3},{2,0},{3,1},{4,6},{5,7},{6,4},{7,5},{8,10},{9,11},{10,... | collective-permute-start | bytes 491528 | tf_op jit(solution)/shard_map/ppermute | solution.py:675
  11.9 2.0 %collective-permute-start.6 = (bf16[320,256]{1,0:T(8,128)(2,1)S(1)}, bf16[320,256]{1,0:T(8,128)(2,1)S(1)}, u32[]{:S(2)}, u32[]{:S(2)}) collective-permute-start(bf16[320,256]{1,0:T(8,128)(2,1)S(1)} %pack.3.refs_4_), channel_id=1, source_target_pairs={{0,1},{1,0},{2,3},{3,2},{4,5},{5,4},{6,7},{7,6},{8,9},{9,8},{10,11... | collective-permute-start | bytes 491528 | tf_op jit(solution)/shard_map/ppermute | solution.py:675
  14.0 2.5 %collective-permute-start.5 = (bf16[296,256]{1,0:T(8,128)(2,1)S(1)}, bf16[296,256]{1,0:T(8,128)(2,1)S(1)}, u32[]{:S(2)}, u32[]{:S(2)}) collective-permute-start(bf16[296,256]{1,0:T(8,128)(2,1)S(1)} %below.1.refs_3_.refs_0_), channel_id=1, source_target_pairs={{0,24},{8,16},{16,8},{24,0},{1,25},{9,17},{17,9},{25,1},{2,26},{10... | collective-permute-start | bytes 454664 | tf_op jit(solution)/shard_map/ppermute | solution.py:675
  16.5 0.5 collective-permute-start.4
  17.0 0.5 collective-permute-start.3
  18.3 3.5 %enter.1 = (bf16[12,8,8,8,256]{4,3,2,1,0:T(8,128)(2,1)S(1)}, bf16[12,6,6,8,256]{4,3,2,1,0:T(8,128)(2,1)S(1)}, bf16[256,256]{1,0:T(8,128)(2,1)S(1)}, bf16[576,256...) custom-call(s32[52]{0:T(128)S(1)} %concatenate.4.ids_ref, ...), custom_call_target="tpu_custom_call" | custom-call | tf_op jit(solution)/shard_map/enter/pallas_call | solution.py:347
  21.9 0.6 collective-permute-done.4.refs_2_
  22.6 0.5 collective-permute-start.12
  23.1 0.5 collective-permute-start.9
  23.6 0.4 collective-permute-done.8.refs_4_
  23.9 0.2 collective-permute-start.11
  24.1 0.6 collective-permute-done.9.refs_5_
  24.7 0.3 collective-permute-done.10.refs_6_
  25.0 0.4 collective-permute-done.11.refs_7_
  25.3 5.3 %first.1 = (bf16[12,8,8,8,256]{4,3,2,1,0:T(8,128)(2,1)S(1)}, bf16[12,6,6,8,256]{4,3,2,1,0:T(8,128)(2,1)S(1)}, bf16[2304,256]{1,0:T(8,128)(2,1)S(1)}, bf16[2,3,256,256]{3,2,1,0:T(8,128)(2,1)S(1)}) custom-call(s32[52]{0:T(128)S(1)} %concatenate.4.ids_ref, bf16[12,8,8,8,256]{4,3,2,1,0:T(8,128)(2,1)S(1)} %get-tuple-element.94.xp_ref, ...), custom_call_target="tpu_custom_call" | custom-call | tf_op jit(solution)/shard_map/first/pallas_call | solution.py:387
  30.7 10.6 %second.1 = (bf16[12,6,6,8,256]{4,3,2,1,0:T(8,128)(2,1)}, bf16[12,8,8,8,256]{4,3,2,1,0:T(8,128)(2,1)S(1)}, bf16[2304,256]{1,0:T(8,128)(2,1)S(1)}, bf16[2,3,256,2...) custom-call(s32[52]{0:T(128)S(1)} %concatenate.4.ids_ref, ...), custom_call_target="tpu_custom_call" | custom-call | flops 8999999488 | bytes 16000000 | tf_op jit(solution)/shard_map/second/pallas_call | solution.py:447
  41.3 0.2 collective-permute-start.14
  41.5 1.9 %collective-permute-done.14 = bf16[4,4,80,256]{3,2,1,0:T(8,128)(2,1)S(1)} collective-permute-done((bf16[4,4,80,256]{3,2,1,0:T(8,128)(2,1)S(1)}, bf16[4,4,80,256]{3,2,1,0:T(8,128)(2,1)S(1)}, u32[]{:S(2)}, u32[]{:S(2)}) %collective-permute-start.14) | collective-permute-done | bytes 655392 | tf_op jit(solution)/shard_map/ppermute | solution.py:675
  43.5 0.2 fusion.3
  43.7 2.0 %collective-permute-start.17 = (bf16[4,80,256]{2,1,0:T(8,128)(2,1)S(1)}, bf16[4,80,256]{2,1,0:T(8,128)(2,1)S(1)}, u32[]{:S(2)}, u32[]{:S(2)}) collective-permute-start(bf16[4,80,256]{2,1,0:T(8,128)(2,1)S(1)} %get-tuple-element.171), channel_id=1, source_target_pairs={{0,24},{8,16},{16,8},{24,0},{1,25},{9,17},{17,9},{25,1},{2,26},{10... | collective-permute-start | bytes 491528 | tf_op jit(solution)/shard_map/ppermute | solution.py:675
  45.6 1.0 %collective-permute-start.16 = (bf16[4,80,256]{2,1,0:T(8,128)(2,1)S(1)}, bf16[4,80,256]{2,1,0:T(8,128)(2,1)S(1)}, u32[]{:S(2)}, u32[]{:S(2)}) collective-permute-start(bf16[4,80,256]{2,1,0:T(8,128)(2,1)S(1)} %get-tuple-element.172), channel_id=1, source_target_pairs={{0,16},{8,24},{16,0},{24,8},{1,17},{9,25},{17,1},{25,9},{2,18},{10... | collective-permute-start | bytes 491528 | tf_op jit(solution)/shard_map/ppermute | solution.py:675
  46.7 0.5 collective-permute-start.15
  47.2 7.2 %hidden_back.1 = (bf16[12,8,8,8,256]{4,3,2,1,0:T(8,128)(2,1)S(1)}, bf16[4,4,72,256]{3,2,1,0:T(8,128)(2,1)S(1)}, bf16[4,4,72,256]{3,2,1,0:T(8,128)(2,1)S(1)}) custom-call(s32[52]{0:T(128)S(1)} %concatenate.4.ids_ref, bf16[12,8,8,8,256]{4,3,2,1,0:T(8,128)(2,1)S(1)} %get-tuple-element.111.gp_ref, bf16[2304,256]{1,0:T(8,128)(2,1)S(1)} %get-tuple-element.112.w_ref, ...), custom_call_target="tpu_custom_call" | custom-call | tf_op jit(solution)/shard_map/hidden_back/pallas_call | solution.py:495
  54.7 1.9 %collective-permute-done.18 = bf16[4,4,72,256]{3,2,1,0:T(8,128)(2,1)S(1)} collective-permute-done((bf16[4,4,72,256]{3,2,1,0:T(8,128)(2,1)S(1)}, bf16[4,4,72,256]{3,2,1,0:T(8,128)(2,1)S(1)}, u32[]{:S(2)}, u32[]{:S(2)}) %collective-permute-start.18) | collective-permute-done | bytes 589856 | tf_op jit(solution)/shard_map/ppermute | solution.py:675
  56.6 0.2 fusion.7
  56.7 1.6 %collective-permute-start.19 = (bf16[4,72,256]{2,1,0:T(8,128)(2,1)S(1)}, bf16[4,72,256]{2,1,0:T(8,128)(2,1)S(1)}, u32[]{:S(2)}, u32[]{:S(2)}) collective-permute-start(bf16[4,72,256]{2,1,0:T(8,128)(2,1)S(1)} %get-tuple-element.130), channel_id=1, source_target_pairs={{0,8},{8,0},{16,24},{24,16},{1,9},{9,1},{17,25},{25,17},{2,10},{10... | collective-permute-start | bytes 442376 | tf_op jit(solution)/shard_map/ppermute | solution.py:675
  58.3 1.0 %collective-permute-start.20 = (bf16[4,72,256]{2,1,0:T(8,128)(2,1)S(1)}, bf16[4,72,256]{2,1,0:T(8,128)(2,1)S(1)}, u32[]{:S(2)}, u32[]{:S(2)}) collective-permute-start(bf16[4,72,256]{2,1,0:T(8,128)(2,1)S(1)} %get-tuple-element.131), channel_id=1, source_target_pairs={{0,16},{8,24},{16,0},{24,8},{1,17},{9,25},{17,1},{25,9},{2,18},{10... | collective-permute-start | bytes 442376 | tf_op jit(solution)/shard_map/ppermute | solution.py:675
  59.3 1.0 %collective-permute-start.21 = (bf16[4,72,256]{2,1,0:T(8,128)(2,1)S(1)}, bf16[4,72,256]{2,1,0:T(8,128)(2,1)S(1)}, u32[]{:S(2)}, u32[]{:S(2)}) collective-permute-start(bf16[4,72,256]{2,1,0:T(8,128)(2,1)S(1)} %get-tuple-element.132), channel_id=1, source_target_pairs={{0,24},{8,16},{16,8},{24,0},{1,25},{9,17},{17,9},{25,1},{2,26},{10... | collective-permute-start | bytes 442376 | tf_op jit(solution)/shard_map/ppermute | solution.py:675
  60.3 0.2 collective-permute-start.22
  60.5 1.2 %collective-permute-start.23 = (bf16[80,256]{1,0:T(8,128)(2,1)S(1)}, bf16[80,256]{1,0:T(8,128)(2,1)S(1)}, u32[]{:S(2)}, u32[]{:S(2)}) collective-permute-start(bf16[80,256]{1,0:T(8,128)(2,1)S(1)} %get-tuple-element.135), channel_id=1, source_target_pairs={{0,2},{1,3},{2,0},{3,1},{4,6},{5,7},{6,4},{7,5},{8,10},{9,11},{10,... | collective-permute-start | bytes 122888 | tf_op jit(solution)/shard_map/ppermute | solution.py:675
  61.8 4.7 %inputs_back.1 = f32[12,6,6,8,256]{4,3,2,1,0:T(8,128)} custom-call(bf16[12,8,8,8,256]{4,3,2,1,0:T(8,128)(2,1)S(1)} %get-tuple-element.136.gp_ref, bf16[2304,256]{1,0:T(8,128)(2,1)S(1)} %get-tuple-element.137.w_ref, bf16[2,3,256,256]{3,2,1,0:T(8,128)(2,1)S(1)} %get-tuple-element.138.u_ref, bf16[256,256]{1,0:T(8,128)(2,1)S(1)} %get-tuple-element.139.ws_ref, ...), custom_call_target="tpu_custom_call" | custom-call | tf_op jit(solution)/shard_map/inputs_back/pallas_call | solution.py:586
  66.5 0.6 collective-permute-done.20.refs_2_
  67.1 2.5 %collective-permute-start.26 = (bf16[152,256]{1,0:T(8,128)(2,1)S(1)}, bf16[152,256]{1,0:T(8,128)(2,1)S(1)}, u32[]{:S(2)}, u32[]{:S(2)}) collective-permute-start(bf16[152,256]{1,0:T(8,128)(2,1)S(1)} %get-tuple-element.152), channel_id=1, source_target_pairs={{0,3},{1,2},{2,1},{3,0},{4,7},{5,6},{6,5},{7,4},{8,11},{9,10},{10,... | collective-permute-start | bytes 233480 | tf_op jit(solution)/shard_map/ppermute | solution.py:675
  69.6 2.0 %collective-permute-start.25 = (bf16[72,256]{1,0:T(8,128)(2,1)S(1)}, bf16[72,256]{1,0:T(8,128)(2,1)S(1)}, u32[]{:S(2)}, u32[]{:S(2)}) collective-permute-start(bf16[72,256]{1,0:T(8,128)(2,1)S(1)} %get-tuple-element.150), channel_id=1, source_target_pairs={{0,2},{1,3},{2,0},{3,1},{4,6},{5,7},{6,4},{7,5},{8,10},{9,11},{10,... | collective-permute-start | bytes 110600 | tf_op jit(solution)/shard_map/ppermute | solution.py:675
  71.6 2.5 %collective-permute-done.24.refs_1_ = bf16[72,256]{1,0:T(8,128)(2,1)S(1)} collective-permute-done((bf16[72,256]{1,0:T(8,128)(2,1)S(1)}, bf16[72,256]{1,0:T(8,128)(2,1)S(1)}, u32[]{:S(2)}, u32[]{:S(2)}) %collective-permute-start.24) | collective-permute-done | bytes 36896 | tf_op jit(solution)/shard_map/ppermute | solution.py:675
  74.0 0.4 collective-permute-done.25.refs_2_
  74.5 2.0 %collective-permute-start.29 = (bf16[152,256]{1,0:T(8,128)(2,1)S(1)}, bf16[152,256]{1,0:T(8,128)(2,1)S(1)}, u32[]{:S(2)}, u32[]{:S(2)}) collective-permute-start(bf16[152,256]{1,0:T(8,128)(2,1)S(1)} %rank_sums.1), channel_id=1, source_target_pairs={{0,24},{8,16},{16,8},{24,0},{1,25},{9,17},{17,9},{25,1},{2,26},{10... | collective-permute-start | bytes 233480 | tf_op jit(solution)/shard_map/ppermute | solution.py:675
  76.5 1.0 %collective-permute-start.28 = (bf16[152,256]{1,0:T(8,128)(2,1)S(1)}, bf16[152,256]{1,0:T(8,128)(2,1)S(1)}, u32[]{:S(2)}, u32[]{:S(2)}) collective-permute-start(bf16[152,256]{1,0:T(8,128)(2,1)S(1)} %rank_sums.1), channel_id=1, source_target_pairs={{0,16},{8,24},{16,0},{24,8},{1,17},{9,25},{17,1},{25,9},{2,18},{10... | collective-permute-start | bytes 233480 | tf_op jit(solution)/shard_map/ppermute | solution.py:675
  77.5 0.5 collective-permute-start.27
  78.1 2.5 %collective-permute-done.29 = bf16[152,256]{1,0:T(8,128)(2,1)S(1)} collective-permute-done((bf16[152,256]{1,0:T(8,128)(2,1)S(1)}, bf16[152,256]{1,0:T(8,128)(2,1)S(1)}, u32[]{:S(2)}, u32[]{:S(2)}) %collective-permute-start.29) | collective-permute-done | bytes 77856 | tf_op jit(solution)/shard_map/ppermute | solution.py:675
  80.6 0.6 collective-permute-done.28
  81.2 0.7 collective-permute-done.27
  82.1 2.2 %update.2 = (f32[576,256]{1,0:T(8,128)}, f32[576,256]{1,0:T(8,128)}, f32[576,256]{1,0:T(8,128)}, f32[576,256]{1,0:T(8,128)}, f32[576,256]{1,0:T(8,128)}, /*index...) custom-call(s32[52]{0:T(128)S(1)} %concatenate.4.ids_ref, ...), custom_call_target="tpu_custom_call" | custom-call | flops 2000000000 | bytes 9000000 | tf_op jit(solution)/shard_map/update/pallas_call | solution.py:657
  84.4 2.2 %update.3 = (f32[576,256]{1,0:T(8,128)}, f32[576,256]{1,0:T(8,128)}, f32[576,256]{1,0:T(8,128)}, f32[576,256]{1,0:T(8,128)}, f32[576,256]{1,0:T(8,128)}, /*index...) custom-call(s32[52]{0:T(128)S(1)} %concatenate.4.ids_ref, ...), custom_call_target="tpu_custom_call", output_to_operand_aliasing={{0}: (11, {}), {1}: (12, {}), {2}: (13, {}), {3}: (14, {}),... | custom-call | flops 2000000000 | bytes 9000000 | tf_op jit(solution)/shard_map/update/pallas_call | solution.py:657
  (53 shorter events, 0.8 us)
Async XLA Ops:
  0.6 17.5 %copy-start.9 = (s32[12,4]{0,1:T(4,128)S(1)}, s32[12,4]{0,1:T(4,128)}, u32[]{:S(2)}) copy-start(s32[12,4]{0,1:T(4,128)} %param.16) | copy-start | bytes 580
  2.2 11.7 %collective-permute-start.2 = (bf16[152,256]{1,0:T(8,128)(2,1)S(1)}, bf16[152,256]{1,0:T(8,128)(2,1)S(1)}, u32[]{:S(2)}, u32[]{:S(2)}) collective-permute-start(bf16[152,256]{1,0:T(8,128)(2,1)S(1)} %get-tuple-element.92), channel_id=1, source_target_pairs={{0,3},{1,2},{2,1},{3,0},{4,7},{5,6},{6,5},{7,4},{8,11},{9,10},{10,... | collective-permute-start | bytes 233480 | tf_op jit(solution)/shard_map/ppermute | solution.py:675
  7.4 6.6 %collective-permute-start.1 = (bf16[72,256]{1,0:T(8,128)(2,1)S(1)}, bf16[72,256]{1,0:T(8,128)(2,1)S(1)}, u32[]{:S(2)}, u32[]{:S(2)}) collective-permute-start(bf16[72,256]{1,0:T(8,128)(2,1)S(1)} %get-tuple-element.91), channel_id=1, source_target_pairs={{0,2},{1,3},{2,0},{3,1},{4,6},{5,7},{6,4},{7,5},{8,10},{9,11},{10,... | collective-permute-start | bytes 110600 | tf_op jit(solution)/shard_map/ppermute | solution.py:675
  7.4 6.6 %collective-permute-start = (bf16[72,256]{1,0:T(8,128)(2,1)S(1)}, bf16[72,256]{1,0:T(8,128)(2,1)S(1)}, u32[]{:S(2)}, u32[]{:S(2)}) collective-permute-start(bf16[72,256]{1,0:T(8,128)(2,1)S(1)} %get-tuple-element.91), channel_id=1, source_target_pairs={{0,1},{1,0},{2,3},{3,2},{4,5},{5,4},{6,7},{7,6},{8,9},{9,8},{10,11... | collective-permute-start | bytes 110600 | tf_op jit(solution)/shard_map/ppermute | solution.py:675
  9.6 12.3 %collective-permute-start.7 = (bf16[320,256]{1,0:T(8,128)(2,1)S(1)}, bf16[320,256]{1,0:T(8,128)(2,1)S(1)}, u32[]{:S(2)}, u32[]{:S(2)}) collective-permute-start(bf16[320,256]{1,0:T(8,128)(2,1)S(1)} %pack.3.refs_4_), channel_id=1, source_target_pairs={{0,2},{1,3},{2,0},{3,1},{4,6},{5,7},{6,4},{7,5},{8,10},{9,11},{10,... | collective-permute-start | bytes 491528 | tf_op jit(solution)/shard_map/ppermute | solution.py:675
  11.9 10.0 %collective-permute-start.6 = (bf16[320,256]{1,0:T(8,128)(2,1)S(1)}, bf16[320,256]{1,0:T(8,128)(2,1)S(1)}, u32[]{:S(2)}, u32[]{:S(2)}) collective-permute-start(bf16[320,256]{1,0:T(8,128)(2,1)S(1)} %pack.3.refs_4_), channel_id=1, source_target_pairs={{0,1},{1,0},{2,3},{3,2},{4,5},{5,4},{6,7},{7,6},{8,9},{9,8},{10,11... | collective-permute-start | bytes 491528 | tf_op jit(solution)/shard_map/ppermute | solution.py:675
  14.0 8.0 %collective-permute-start.5 = (bf16[296,256]{1,0:T(8,128)(2,1)S(1)}, bf16[296,256]{1,0:T(8,128)(2,1)S(1)}, u32[]{:S(2)}, u32[]{:S(2)}) collective-permute-start(bf16[296,256]{1,0:T(8,128)(2,1)S(1)} %below.1.refs_3_.refs_0_), channel_id=1, source_target_pairs={{0,24},{8,16},{16,8},{24,0},{1,25},{9,17},{17,9},{25,1},{2,26},{10... | collective-permute-start | bytes 454664 | tf_op jit(solution)/shard_map/ppermute | solution.py:675
  16.5 6.0 %collective-permute-start.4 = (bf16[296,256]{1,0:T(8,128)(2,1)S(1)}, bf16[296,256]{1,0:T(8,128)(2,1)S(1)}, u32[]{:S(2)}, u32[]{:S(2)}) collective-permute-start(bf16[296,256]{1,0:T(8,128)(2,1)S(1)} %below.1.refs_3_.refs_0_), channel_id=1, source_target_pairs={{0,16},{8,24},{16,0},{24,8},{1,17},{9,25},{17,1},{25,9},{2,18},{10... | collective-permute-start | bytes 454664 | tf_op jit(solution)/shard_map/ppermute | solution.py:675
  17.0 5.6 %collective-permute-start.3 = (bf16[296,256]{1,0:T(8,128)(2,1)S(1)}, bf16[296,256]{1,0:T(8,128)(2,1)S(1)}, u32[]{:S(2)}, u32[]{:S(2)}) collective-permute-start(bf16[296,256]{1,0:T(8,128)(2,1)S(1)} %below.1.refs_3_.refs_0_), channel_id=1, source_target_pairs={{0,8},{8,0},{16,24},{24,16},{1,9},{9,1},{17,25},{25,17},{2,10},{10... | collective-permute-start | bytes 454664 | tf_op jit(solution)/shard_map/ppermute | solution.py:675
  22.6 1.4 %collective-permute-start.8 = (bf16[296,256]{1,0:T(8,128)(2,1)S(1)}, bf16[296,256]{1,0:T(8,128)(2,1)S(1)}, u32[]{:S(2)}, u32[]{:S(2)}) collective-permute-start(bf16[296,256]{1,0:T(8,128)(2,1)S(1)} %below.1.refs_3_.refs_0_), channel_id=1, source_target_pairs={{0,4},{4,0},{1,5},{5,1},{2,6},{6,2},{3,7},{7,3},{8,12},{12,8},{9,1... | collective-permute-start | bytes 454664 | tf_op jit(solution)/shard_map/ppermute | solution.py:675
  22.6 8.1 %collective-permute-start.12 = (bf16[320,256]{1,0:T(8,128)(2,1)S(1)}, bf16[320,256]{1,0:T(8,128)(2,1)S(1)}, u32[]{:S(2)}, u32[]{:S(2)}) collective-permute-start(bf16[320,256]{1,0:T(8,128)(2,1)S(1)} %collective-permute-done.6.refs_8_), channel_id=1, source_target_pairs={{0,4},{4,0},{1,5},{5,1},{2,6},{6,2},{3,7},{7,3},{8,12},{12,8},{9,1... | collective-permute-start | bytes 491528 | tf_op jit(solution)/shard_map/ppermute | solution.py:675
  23.1 7.6 %collective-permute-start.13 = (bf16[320,256]{1,0:T(8,128)(2,1)S(1)}, bf16[320,256]{1,0:T(8,128)(2,1)S(1)}, u32[]{:S(2)}, u32[]{:S(2)}) collective-permute-start(bf16[320,256]{1,0:T(8,128)(2,1)S(1)} %collective-permute-done.7.refs_9_), channel_id=1, source_target_pairs={{0,4},{4,0},{1,5},{5,1},{2,6},{6,2},{3,7},{7,3},{8,12},{12,8},{9,1... | collective-permute-start | bytes 491528 | tf_op jit(solution)/shard_map/ppermute | solution.py:675
  23.1 1.6 %collective-permute-start.9 = (bf16[296,256]{1,0:T(8,128)(2,1)S(1)}, bf16[296,256]{1,0:T(8,128)(2,1)S(1)}, u32[]{:S(2)}, u32[]{:S(2)}) collective-permute-start(bf16[296,256]{1,0:T(8,128)(2,1)S(1)} %collective-permute-done.3.refs_1_), channel_id=1, source_target_pairs={{0,4},{4,0},{1,5},{5,1},{2,6},{6,2},{3,7},{7,3},{8,12},{12,8},{9,1... | collective-permute-start | bytes 454664 | tf_op jit(solution)/shard_map/ppermute | solution.py:675
  23.6 1.4 %collective-permute-start.10 = (bf16[296,256]{1,0:T(8,128)(2,1)S(1)}, bf16[296,256]{1,0:T(8,128)(2,1)S(1)}, u32[]{:S(2)}, u32[]{:S(2)}) collective-permute-start(bf16[296,256]{1,0:T(8,128)(2,1)S(1)} %collective-permute-done.4.refs_2_), channel_id=1, source_target_pairs={{0,4},{4,0},{1,5},{5,1},{2,6},{6,2},{3,7},{7,3},{8,12},{12,8},{9,1... | collective-permute-start | bytes 454664 | tf_op jit(solution)/shard_map/ppermute | solution.py:675
  23.9 1.4 %collective-permute-start.11 = (bf16[296,256]{1,0:T(8,128)(2,1)S(1)}, bf16[296,256]{1,0:T(8,128)(2,1)S(1)}, u32[]{:S(2)}, u32[]{:S(2)}) collective-permute-start(bf16[296,256]{1,0:T(8,128)(2,1)S(1)} %collective-permute-done.5.refs_3_), channel_id=1, source_target_pairs={{0,4},{4,0},{1,5},{5,1},{2,6},{6,2},{3,7},{7,3},{8,12},{12,8},{9,1... | collective-permute-start | bytes 454664 | tf_op jit(solution)/shard_map/ppermute | solution.py:675
  41.3 2.2 %collective-permute-start.14 = (bf16[4,4,80,256]{3,2,1,0:T(8,128)(2,1)S(1)}, bf16[4,4,80,256]{3,2,1,0:T(8,128)(2,1)S(1)}, u32[]{:S(2)}, u32[]{:S(2)}) collective-permute-start(bf16[4,4,80,256]{3,2,1,0:T(8,128)(2,1)S(1)} %get-tuple-element.116), channel_id=1, source_target_pairs={{0,4},{4,0},{1,5},{5,1},{2,6},{6,2},{3,7},{7,3},{8,12},{12,8},{9,1... | collective-permute-start | bytes 1966088 | tf_op jit(solution)/shard_map/ppermute | solution.py:675
  43.7 10.8 %collective-permute-start.17 = (bf16[4,80,256]{2,1,0:T(8,128)(2,1)S(1)}, bf16[4,80,256]{2,1,0:T(8,128)(2,1)S(1)}, u32[]{:S(2)}, u32[]{:S(2)}) collective-permute-start(bf16[4,80,256]{2,1,0:T(8,128)(2,1)S(1)} %get-tuple-element.171), channel_id=1, source_target_pairs={{0,24},{8,16},{16,8},{24,0},{1,25},{9,17},{17,9},{25,1},{2,26},{10... | collective-permute-start | bytes 491528 | tf_op jit(solution)/shard_map/ppermute | solution.py:675
  45.6 8.9 %collective-permute-start.16 = (bf16[4,80,256]{2,1,0:T(8,128)(2,1)S(1)}, bf16[4,80,256]{2,1,0:T(8,128)(2,1)S(1)}, u32[]{:S(2)}, u32[]{:S(2)}) collective-permute-start(bf16[4,80,256]{2,1,0:T(8,128)(2,1)S(1)} %get-tuple-element.172), channel_id=1, source_target_pairs={{0,16},{8,24},{16,0},{24,8},{1,17},{9,25},{17,1},{25,9},{2,18},{10... | collective-permute-start | bytes 491528 | tf_op jit(solution)/shard_map/ppermute | solution.py:675
  46.7 7.8 %collective-permute-start.15 = (bf16[4,80,256]{2,1,0:T(8,128)(2,1)S(1)}, bf16[4,80,256]{2,1,0:T(8,128)(2,1)S(1)}, u32[]{:S(2)}, u32[]{:S(2)}) collective-permute-start(bf16[4,80,256]{2,1,0:T(8,128)(2,1)S(1)} %get-tuple-element.173), channel_id=1, source_target_pairs={{0,8},{8,0},{16,24},{24,16},{1,9},{9,1},{17,25},{25,17},{2,10},{10... | collective-permute-start | bytes 491528 | tf_op jit(solution)/shard_map/ppermute | solution.py:675
  54.5 2.1 %collective-permute-start.18 = (bf16[4,4,72,256]{3,2,1,0:T(8,128)(2,1)S(1)}, bf16[4,4,72,256]{3,2,1,0:T(8,128)(2,1)S(1)}, u32[]{:S(2)}, u32[]{:S(2)}) collective-permute-start(bf16[4,4,72,256]{3,2,1,0:T(8,128)(2,1)S(1)} %get-tuple-element.120), channel_id=1, source_target_pairs={{0,4},{4,0},{1,5},{5,1},{2,6},{6,2},{3,7},{7,3},{8,12},{12,8},{9,1... | collective-permute-start | bytes 1769480 | tf_op jit(solution)/shard_map/ppermute | solution.py:675
  56.7 9.8 %collective-permute-start.19 = (bf16[4,72,256]{2,1,0:T(8,128)(2,1)S(1)}, bf16[4,72,256]{2,1,0:T(8,128)(2,1)S(1)}, u32[]{:S(2)}, u32[]{:S(2)}) collective-permute-start(bf16[4,72,256]{2,1,0:T(8,128)(2,1)S(1)} %get-tuple-element.130), channel_id=1, source_target_pairs={{0,8},{8,0},{16,24},{24,16},{1,9},{9,1},{17,25},{25,17},{2,10},{10... | collective-permute-start | bytes 442376 | tf_op jit(solution)/shard_map/ppermute | solution.py:675
  58.3 8.8 %collective-permute-start.20 = (bf16[4,72,256]{2,1,0:T(8,128)(2,1)S(1)}, bf16[4,72,256]{2,1,0:T(8,128)(2,1)S(1)}, u32[]{:S(2)}, u32[]{:S(2)}) collective-permute-start(bf16[4,72,256]{2,1,0:T(8,128)(2,1)S(1)} %get-tuple-element.131), channel_id=1, source_target_pairs={{0,16},{8,24},{16,0},{24,8},{1,17},{9,25},{17,1},{25,9},{2,18},{10... | collective-permute-start | bytes 442376 | tf_op jit(solution)/shard_map/ppermute | solution.py:675
  59.3 7.8 %collective-permute-start.21 = (bf16[4,72,256]{2,1,0:T(8,128)(2,1)S(1)}, bf16[4,72,256]{2,1,0:T(8,128)(2,1)S(1)}, u32[]{:S(2)}, u32[]{:S(2)}) collective-permute-start(bf16[4,72,256]{2,1,0:T(8,128)(2,1)S(1)} %get-tuple-element.132), channel_id=1, source_target_pairs={{0,24},{8,16},{16,8},{24,0},{1,25},{9,17},{17,9},{25,1},{2,26},{10... | collective-permute-start | bytes 442376 | tf_op jit(solution)/shard_map/ppermute | solution.py:675
  60.3 6.2 %collective-permute-start.22 = (bf16[80,256]{1,0:T(8,128)(2,1)S(1)}, bf16[80,256]{1,0:T(8,128)(2,1)S(1)}, u32[]{:S(2)}, u32[]{:S(2)}) collective-permute-start(bf16[80,256]{1,0:T(8,128)(2,1)S(1)} %get-tuple-element.134), channel_id=1, source_target_pairs={{0,1},{1,0},{2,3},{3,2},{4,5},{5,4},{6,7},{7,6},{8,9},{9,8},{10,11... | collective-permute-start | bytes 122888 | tf_op jit(solution)/shard_map/ppermute | solution.py:675
  60.5 5.9 %collective-permute-start.23 = (bf16[80,256]{1,0:T(8,128)(2,1)S(1)}, bf16[80,256]{1,0:T(8,128)(2,1)S(1)}, u32[]{:S(2)}, u32[]{:S(2)}) collective-permute-start(bf16[80,256]{1,0:T(8,128)(2,1)S(1)} %get-tuple-element.135), channel_id=1, source_target_pairs={{0,2},{1,3},{2,0},{3,1},{4,6},{5,7},{6,4},{7,5},{8,10},{9,11},{10,... | collective-permute-start | bytes 122888 | tf_op jit(solution)/shard_map/ppermute | solution.py:675
  61.7 20.3 %copy-start = (f32[576,256]{1,0:T(8,128)S(1)}, f32[576,256]{1,0:T(8,128)}, u32[]{:S(2)}) copy-start(f32[576,256]{1,0:T(8,128)} %refs_3_.3) | copy-start | bytes 1769476
  61.7 20.4 %copy-start.1 = (f32[576,256]{1,0:T(8,128)S(1)}, f32[576,256]{1,0:T(8,128)}, u32[]{:S(2)}) copy-start(f32[576,256]{1,0:T(8,128)} %refs_0_.9) | copy-start | bytes 1769476
  61.7 20.4 %copy-start.2 = (f32[64,256]{1,0:T(8,128)S(1)}, f32[64,256]{1,0:T(8,128)}, u32[]{:S(2)}) copy-start(f32[64,256]{1,0:T(8,128)} %refs_6_.3) | copy-start | bytes 196612
  61.7 20.4 %copy-start.3 = (f32[576,256]{1,0:T(8,128)S(1)}, f32[576,256]{1,0:T(8,128)}, u32[]{:S(2)}) copy-start(f32[576,256]{1,0:T(8,128)} %refs_1_.9) | copy-start | bytes 1769476
  61.7 20.4 %copy-start.4 = (f32[576,256]{1,0:T(8,128)S(1)}, f32[576,256]{1,0:T(8,128)}, u32[]{:S(2)}) copy-start(f32[576,256]{1,0:T(8,128)} %refs_2_.7) | copy-start | bytes 1769476
  61.7 20.4 %copy-start.5 = (f32[576,256]{1,0:T(8,128)S(1)}, f32[576,256]{1,0:T(8,128)}, u32[]{:S(2)}) copy-start(f32[576,256]{1,0:T(8,128)} %refs_4_.3) | copy-start | bytes 1769476
  61.8 20.4 %copy-start.6 = (f32[576,256]{1,0:T(8,128)S(1)}, f32[576,256]{1,0:T(8,128)}, u32[]{:S(2)}) copy-start(f32[576,256]{1,0:T(8,128)} %refs_5_.3) | copy-start | bytes 1769476
  61.8 20.4 %copy-start.7 = (f32[64,256]{1,0:T(8,128)S(1)}, f32[64,256]{1,0:T(8,128)}, u32[]{:S(2)}) copy-start(f32[64,256]{1,0:T(8,128)} %refs_7_.3) | copy-start | bytes 196612
  61.8 20.4 %copy-start.8 = (f32[64,256]{1,0:T(8,128)S(1)}, f32[64,256]{1,0:T(8,128)}, u32[]{:S(2)}) copy-start(f32[64,256]{1,0:T(8,128)} %refs_8_.3) | copy-start | bytes 196612
  67.1 7.3 %collective-permute-start.26 = (bf16[152,256]{1,0:T(8,128)(2,1)S(1)}, bf16[152,256]{1,0:T(8,128)(2,1)S(1)}, u32[]{:S(2)}, u32[]{:S(2)}) collective-permute-start(bf16[152,256]{1,0:T(8,128)(2,1)S(1)} %get-tuple-element.152), channel_id=1, source_target_pairs={{0,3},{1,2},{2,1},{3,0},{4,7},{5,6},{6,5},{7,4},{8,11},{9,10},{10,... | collective-permute-start | bytes 233480 | tf_op jit(solution)/shard_map/ppermute | solution.py:675
  69.6 4.4 %collective-permute-start.24 = (bf16[72,256]{1,0:T(8,128)(2,1)S(1)}, bf16[72,256]{1,0:T(8,128)(2,1)S(1)}, u32[]{:S(2)}, u32[]{:S(2)}) collective-permute-start(bf16[72,256]{1,0:T(8,128)(2,1)S(1)} %get-tuple-element.149), channel_id=1, source_target_pairs={{0,1},{1,0},{2,3},{3,2},{4,5},{5,4},{6,7},{7,6},{8,9},{9,8},{10,11... | collective-permute-start | bytes 110600 | tf_op jit(solution)/shard_map/ppermute | solution.py:675
  69.6 4.9 %collective-permute-start.25 = (bf16[72,256]{1,0:T(8,128)(2,1)S(1)}, bf16[72,256]{1,0:T(8,128)(2,1)S(1)}, u32[]{:S(2)}, u32[]{:S(2)}) collective-permute-start(bf16[72,256]{1,0:T(8,128)(2,1)S(1)} %get-tuple-element.150), channel_id=1, source_target_pairs={{0,2},{1,3},{2,0},{3,1},{4,6},{5,7},{6,4},{7,5},{8,10},{9,11},{10,... | collective-permute-start | bytes 110600 | tf_op jit(solution)/shard_map/ppermute | solution.py:675
  74.5 6.1 %collective-permute-start.29 = (bf16[152,256]{1,0:T(8,128)(2,1)S(1)}, bf16[152,256]{1,0:T(8,128)(2,1)S(1)}, u32[]{:S(2)}, u32[]{:S(2)}) collective-permute-start(bf16[152,256]{1,0:T(8,128)(2,1)S(1)} %rank_sums.1), channel_id=1, source_target_pairs={{0,24},{8,16},{16,8},{24,0},{1,25},{9,17},{17,9},{25,1},{2,26},{10... | collective-permute-start | bytes 233480 | tf_op jit(solution)/shard_map/ppermute | solution.py:675
  76.5 4.7 %collective-permute-start.28 = (bf16[152,256]{1,0:T(8,128)(2,1)S(1)}, bf16[152,256]{1,0:T(8,128)(2,1)S(1)}, u32[]{:S(2)}, u32[]{:S(2)}) collective-permute-start(bf16[152,256]{1,0:T(8,128)(2,1)S(1)} %rank_sums.1), channel_id=1, source_target_pairs={{0,16},{8,24},{16,0},{24,8},{1,17},{9,25},{17,1},{25,9},{2,18},{10... | collective-permute-start | bytes 233480 | tf_op jit(solution)/shard_map/ppermute | solution.py:675
  77.5 4.4 %collective-permute-start.27 = (bf16[152,256]{1,0:T(8,128)(2,1)S(1)}, bf16[152,256]{1,0:T(8,128)(2,1)S(1)}, u32[]{:S(2)}, u32[]{:S(2)}) collective-permute-start(bf16[152,256]{1,0:T(8,128)(2,1)S(1)} %rank_sums.1), channel_id=1, source_target_pairs={{0,8},{8,0},{16,24},{24,16},{1,9},{9,1},{17,25},{25,17},{2,10},{10... | collective-permute-start | bytes 233480 | tf_op jit(solution)/shard_map/ppermute | solution.py:675
  82.0 2.4 %collective-permute-start.30 = (bf16[4,152,256]{2,1,0:T(8,128)(2,1)S(1)}, bf16[4,152,256]{2,1,0:T(8,128)(2,1)S(1)}, u32[]{:S(2)}, u32[]{:S(2)}) collective-permute-start(bf16[4,152,256]{2,1,0:T(8,128)(2,1)S(1)} %pad_maximum_fusion.grads_ref), channel_id=1, source_target_pairs={{0,4},{4,0},{1,5},{5,1},{2,6},{6,2},{3,7},{7,3},{8,12},{12,8},{9,1... | collective-permute-start | bytes 933896 | tf_op jit(solution)/shard_map/ppermute | solution.py:675

commit v8 on v7

--- a/solution.py
+++ b/solution.py
@@ -213,12 +213,12 @@
     cols = slice(1, FS + 1)
     for t in halves:
         y0, y1 = g_ref[:, 2 * t + 1, cols], g_ref[:, 2 * t + 2, cols]
-        z_ref[0, t] = y0
         z_ref[1, t] = (y0 + y1) * 0.5
         z_ref[2, t] = (y0 - y1) * 0.5
-        z_ref[3, t] = y1
     for b in range(3):
-        m0, m1, m2, m3 = (outer(v_ref[k, :, :, b : b + FS], z_ref[k]) for k in range(4))
+        y0, y1 = (jnp.stack([g_ref[:, 2 * t + q, cols] for t in halves]) for q in (1, 2))
+        sides = (y0, z_ref[1], z_ref[2], y1)
+        m0, m1, m2, m3 = (outer(v_ref[k, :, :, b : b + FS], sides[k]) for k in range(4))
         both = m1 + m2
         for a, part in enumerate((m0 + both, m1 - m2, both - m3)):
             place_rows(plan, ids_ref, dst_ref, part.astype(BF), (3 * a + b) * c, plan.piece, 0)

time: 87 us -> 87 us (level)
  no operation moved by 1% of the time
where the time goes in v8:
time: 87 us; the launch traced here: 86.8 us
  Pallas kernels  39.1 us (45%)
  starting transfers between devices  31.8 us (37%)
  waiting for transfers between devices  13.4 us (15%)
  between operations  1.85 us (2%)
    ppermute x31, starting transfers between devices, send(): return lax.ppermute(v, axis, [(i, i ^ step) for i in range(size)])  31.8 us
    ppermute x31, waiting for transfers between devices, send(): return lax.ppermute(v, axis, [(i, i ^ step) for i in range(size)])  13.4 us
    pallas_call x1, Pallas kernels, second(): pl.pallas_call(kernel, in_specs=[SMEM] + [VMEM] * (6 + 2 * count + 2 * ha...  10.7 us
    pallas_call x1, Pallas kernels, hidden_back(): pl.pallas_call(kernel, in_specs=[SMEM] + [VMEM] * 6, out_specs=[VMEM] * 3...  7.18 us
    pallas_call x1, Pallas kernels, first(): pl.pallas_call(kernel, in_specs=[SMEM] + [VMEM] * (2 + 2 * count), out_sp...  5.34 us
    pallas_call x1, Pallas kernels, inputs_back(): pl.pallas_call(inputs_back_kernel, in_specs=[VMEM] * 5, out_specs=HBM, ou...  4.67 us
    pallas_call x2, Pallas kernels, update(): pl.pallas_call(kernel, in_specs=[SMEM] + [VMEM] * 10 + [HBM] * len(old),...  4.47 us
    pallas_call x1, Pallas kernels, enter(): pl.pallas_call(kernel, in_specs=[SMEM] + [HBM] * 5 + [VMEM] * len(after),...  3.54 us
  transfers between devices with their start and end apart: 31, of which 13 were waited for; matrix products, arithmetic and copies ran while one was open for 0% of the time, Pallas kernels for 28%

profile of v8, /device:TPU:0, one launch (start us, length us, event | category | flops | bytes accessed | tf_op | source)
XLA Modules:
  0.0 86.8 jit_solution(9643146732856678664)
XLA Ops:
  0.7 1.5 %pack.2 = (bf16[72,256]{1,0:T(8,128)(2,1)S(1)}, bf16[152,256]{1,0:T(8,128)(2,1)S(1)}) custom-call(s32[3]{0:T(128)S(1)} %pad_add_fusion.ids_ref, f32[576,256]{1,0:T(8,128)} %refs_0_.9, f32[576,256]{1,0:T(8,128)} %refs_3_.3, f32[64,256]{1,0:T(8,128)} %refs_6_.3), custom_call_target="tpu_custom_call" | custom-call | tf_op jit(solution)/shard_map/pack/pallas_call | solution.py:250
  2.2 5.1 %collective-permute-start.2 = (bf16[152,256]{1,0:T(8,128)(2,1)S(1)}, bf16[152,256]{1,0:T(8,128)(2,1)S(1)}, u32[]{:S(2)}, u32[]{:S(2)}) collective-permute-start(bf16[152,256]{1,0:T(8,128)(2,1)S(1)} %get-tuple-element.92), channel_id=1, source_target_pairs={{0,3},{1,2},{2,1},{3,0},{4,7},{5,6},{6,5},{7,4},{8,11},{9,10},{10,... | collective-permute-start | bytes 233480 | tf_op jit(solution)/shard_map/ppermute | solution.py:675
  7.4 0.6 collective-permute-start
  8.0 1.5 %pack.3.refs_4_ = bf16[320,256]{1,0:T(8,128)(2,1)S(1)} custom-call(s32[3]{0:T(128)S(1)} %pad_add_fusion.ids_ref, f32[576,256]{1,0:T(8,128)} %refs_3_.3, f32[64,256]{1,0:T(8,128)} %refs_6_.3), custom_call_target="tpu_custom_call" | custom-call | tf_op jit(solution)/shard_map/pack/pallas_call | solution.py:250
  9.6 2.4 %collective-permute-start.7 = (bf16[320,256]{1,0:T(8,128)(2,1)S(1)}, bf16[320,256]{1,0:T(8,128)(2,1)S(1)}, u32[]{:S(2)}, u32[]{:S(2)}) collective-permute-start(bf16[320,256]{1,0:T(8,128)(2,1)S(1)} %pack.3.refs_4_), channel_id=1, source_target_pairs={{0,2},{1,3},{2,0},{3,1},{4,6},{5,7},{6,4},{7,5},{8,10},{9,11},{10,... | collective-permute-start | bytes 491528 | tf_op jit(solution)/shard_map/ppermute | solution.py:675
  11.9 2.0 %collective-permute-start.6 = (bf16[320,256]{1,0:T(8,128)(2,1)S(1)}, bf16[320,256]{1,0:T(8,128)(2,1)S(1)}, u32[]{:S(2)}, u32[]{:S(2)}) collective-permute-start(bf16[320,256]{1,0:T(8,128)(2,1)S(1)} %pack.3.refs_4_), channel_id=1, source_target_pairs={{0,1},{1,0},{2,3},{3,2},{4,5},{5,4},{6,7},{7,6},{8,9},{9,8},{10,11... | collective-permute-start | bytes 491528 | tf_op jit(solution)/shard_map/ppermute | solution.py:675
  14.0 2.5 %collective-permute-start.5 = (bf16[296,256]{1,0:T(8,128)(2,1)S(1)}, bf16[296,256]{1,0:T(8,128)(2,1)S(1)}, u32[]{:S(2)}, u32[]{:S(2)}) collective-permute-start(bf16[296,256]{1,0:T(8,128)(2,1)S(1)} %below.1.refs_3_.refs_0_), channel_id=1, source_target_pairs={{0,24},{8,16},{16,8},{24,0},{1,25},{9,17},{17,9},{25,1},{2,26},{10... | collective-permute-start | bytes 454664 | tf_op jit(solution)/shard_map/ppermute | solution.py:675
  16.5 0.5 collective-permute-start.4
  17.0 0.5 collective-permute-start.3
  18.3 3.5 %enter.1 = (bf16[12,8,8,8,256]{4,3,2,1,0:T(8,128)(2,1)S(1)}, bf16[12,6,6,8,256]{4,3,2,1,0:T(8,128)(2,1)S(1)}, bf16[256,256]{1,0:T(8,128)(2,1)S(1)}, bf16[576,256...) custom-call(s32[52]{0:T(128)S(1)} %concatenate.4.ids_ref, ...), custom_call_target="tpu_custom_call" | custom-call | tf_op jit(solution)/shard_map/enter/pallas_call | solution.py:347
  21.9 0.6 collective-permute-done.4.refs_2_
  22.6 0.5 collective-permute-start.12
  23.1 0.5 collective-permute-start.9
  23.6 0.4 collective-permute-done.8.refs_4_
  23.9 0.2 collective-permute-start.11
  24.1 0.6 collective-permute-done.9.refs_5_
  24.7 0.3 collective-permute-done.10.refs_6_
  25.0 0.4 collective-permute-done.11.refs_7_
  25.3 5.3 %first.1 = (bf16[12,8,8,8,256]{4,3,2,1,0:T(8,128)(2,1)S(1)}, bf16[12,6,6,8,256]{4,3,2,1,0:T(8,128)(2,1)S(1)}, bf16[2304,256]{1,0:T(8,128)(2,1)S(1)}, bf16[2,3,256,256]{3,2,1,0:T(8,128)(2,1)S(1)}) custom-call(s32[52]{0:T(128)S(1)} %concatenate.4.ids_ref, bf16[12,8,8,8,256]{4,3,2,1,0:T(8,128)(2,1)S(1)} %get-tuple-element.94.xp_ref, ...), custom_call_target="tpu_custom_call" | custom-call | tf_op jit(solution)/shard_map/first/pallas_call | solution.py:387
  30.7 10.7 %second.1 = (bf16[12,6,6,8,256]{4,3,2,1,0:T(8,128)(2,1)}, bf16[12,8,8,8,256]{4,3,2,1,0:T(8,128)(2,1)S(1)}, bf16[2304,256]{1,0:T(8,128)(2,1)S(1)}, bf16[2,3,256,2...) custom-call(s32[52]{0:T(128)S(1)} %concatenate.4.ids_ref, ...), custom_call_target="tpu_custom_call" | custom-call | flops 8999999488 | bytes 16000000 | tf_op jit(solution)/shard_map/second/pallas_call | solution.py:447
  41.3 0.2 collective-permute-start.14
  41.6 1.9 %collective-permute-done.14 = bf16[4,4,80,256]{3,2,1,0:T(8,128)(2,1)S(1)} collective-permute-done((bf16[4,4,80,256]{3,2,1,0:T(8,128)(2,1)S(1)}, bf16[4,4,80,256]{3,2,1,0:T(8,128)(2,1)S(1)}, u32[]{:S(2)}, u32[]{:S(2)}) %collective-permute-start.14) | collective-permute-done | bytes 655392 | tf_op jit(solution)/shard_map/ppermute | solution.py:675
  43.5 0.2 fusion.3
  43.7 2.0 %collective-permute-start.17 = (bf16[4,80,256]{2,1,0:T(8,128)(2,1)S(1)}, bf16[4,80,256]{2,1,0:T(8,128)(2,1)S(1)}, u32[]{:S(2)}, u32[]{:S(2)}) collective-permute-start(bf16[4,80,256]{2,1,0:T(8,128)(2,1)S(1)} %get-tuple-element.171), channel_id=1, source_target_pairs={{0,24},{8,16},{16,8},{24,0},{1,25},{9,17},{17,9},{25,1},{2,26},{10... | collective-permute-start | bytes 491528 | tf_op jit(solution)/shard_map/ppermute | solution.py:675
  45.6 1.0 %collective-permute-start.16 = (bf16[4,80,256]{2,1,0:T(8,128)(2,1)S(1)}, bf16[4,80,256]{2,1,0:T(8,128)(2,1)S(1)}, u32[]{:S(2)}, u32[]{:S(2)}) collective-permute-start(bf16[4,80,256]{2,1,0:T(8,128)(2,1)S(1)} %get-tuple-element.172), channel_id=1, source_target_pairs={{0,16},{8,24},{16,0},{24,8},{1,17},{9,25},{17,1},{25,9},{2,18},{10... | collective-permute-start | bytes 491528 | tf_op jit(solution)/shard_map/ppermute | solution.py:675
  46.7 0.5 collective-permute-start.15
  47.2 7.2 %hidden_back.1 = (bf16[12,8,8,8,256]{4,3,2,1,0:T(8,128)(2,1)S(1)}, bf16[4,4,72,256]{3,2,1,0:T(8,128)(2,1)S(1)}, bf16[4,4,72,256]{3,2,1,0:T(8,128)(2,1)S(1)}) custom-call(s32[52]{0:T(128)S(1)} %concatenate.4.ids_ref, bf16[12,8,8,8,256]{4,3,2,1,0:T(8,128)(2,1)S(1)} %get-tuple-element.111.gp_ref, bf16[2304,256]{1,0:T(8,128)(2,1)S(1)} %get-tuple-element.112.w_ref, ...), custom_call_target="tpu_custom_call" | custom-call | tf_op jit(solution)/shard_map/hidden_back/pallas_call | solution.py:495
  54.6 1.9 %collective-permute-done.18 = bf16[4,4,72,256]{3,2,1,0:T(8,128)(2,1)S(1)} collective-permute-done((bf16[4,4,72,256]{3,2,1,0:T(8,128)(2,1)S(1)}, bf16[4,4,72,256]{3,2,1,0:T(8,128)(2,1)S(1)}, u32[]{:S(2)}, u32[]{:S(2)}) %collective-permute-start.18) | collective-permute-done | bytes 589856 | tf_op jit(solution)/shard_map/ppermute | solution.py:675
  56.5 0.2 fusion.7
  56.7 1.6 %collective-permute-start.19 = (bf16[4,72,256]{2,1,0:T(8,128)(2,1)S(1)}, bf16[4,72,256]{2,1,0:T(8,128)(2,1)S(1)}, u32[]{:S(2)}, u32[]{:S(2)}) collective-permute-start(bf16[4,72,256]{2,1,0:T(8,128)(2,1)S(1)} %get-tuple-element.130), channel_id=1, source_target_pairs={{0,8},{8,0},{16,24},{24,16},{1,9},{9,1},{17,25},{25,17},{2,10},{10... | collective-permute-start | bytes 442376 | tf_op jit(solution)/shard_map/ppermute | solution.py:675
  58.2 1.0 %collective-permute-start.20 = (bf16[4,72,256]{2,1,0:T(8,128)(2,1)S(1)}, bf16[4,72,256]{2,1,0:T(8,128)(2,1)S(1)}, u32[]{:S(2)}, u32[]{:S(2)}) collective-permute-start(bf16[4,72,256]{2,1,0:T(8,128)(2,1)S(1)} %get-tuple-element.131), channel_id=1, source_target_pairs={{0,16},{8,24},{16,0},{24,8},{1,17},{9,25},{17,1},{25,9},{2,18},{10... | collective-permute-start | bytes 442376 | tf_op jit(solution)/shard_map/ppermute | solution.py:675
  59.2 1.0 %collective-permute-start.21 = (bf16[4,72,256]{2,1,0:T(8,128)(2,1)S(1)}, bf16[4,72,256]{2,1,0:T(8,128)(2,1)S(1)}, u32[]{:S(2)}, u32[]{:S(2)}) collective-permute-start(bf16[4,72,256]{2,1,0:T(8,128)(2,1)S(1)} %get-tuple-element.132), channel_id=1, source_target_pairs={{0,24},{8,16},{16,8},{24,0},{1,25},{9,17},{17,9},{25,1},{2,26},{10... | collective-permute-start | bytes 442376 | tf_op jit(solution)/shard_map/ppermute | solution.py:675
  60.2 0.2 collective-permute-start.22
  60.5 1.2 %collective-permute-start.23 = (bf16[80,256]{1,0:T(8,128)(2,1)S(1)}, bf16[80,256]{1,0:T(8,128)(2,1)S(1)}, u32[]{:S(2)}, u32[]{:S(2)}) collective-permute-start(bf16[80,256]{1,0:T(8,128)(2,1)S(1)} %get-tuple-element.135), channel_id=1, source_target_pairs={{0,2},{1,3},{2,0},{3,1},{4,6},{5,7},{6,4},{7,5},{8,10},{9,11},{10,... | collective-permute-start | bytes 122888 | tf_op jit(solution)/shard_map/ppermute | solution.py:675
  61.7 4.7 %inputs_back.1 = f32[12,6,6,8,256]{4,3,2,1,0:T(8,128)} custom-call(bf16[12,8,8,8,256]{4,3,2,1,0:T(8,128)(2,1)S(1)} %get-tuple-element.136.gp_ref, bf16[2304,256]{1,0:T(8,128)(2,1)S(1)} %get-tuple-element.137.w_ref, bf16[2,3,256,256]{3,2,1,0:T(8,128)(2,1)S(1)} %get-tuple-element.138.u_ref, bf16[256,256]{1,0:T(8,128)(2,1)S(1)} %get-tuple-element.139.ws_ref, ...), custom_call_target="tpu_custom_call" | custom-call | tf_op jit(solution)/shard_map/inputs_back/pallas_call | solution.py:586
  66.5 0.6 collective-permute-done.20.refs_2_
  67.1 2.5 %collective-permute-start.26 = (bf16[152,256]{1,0:T(8,128)(2,1)S(1)}, bf16[152,256]{1,0:T(8,128)(2,1)S(1)}, u32[]{:S(2)}, u32[]{:S(2)}) collective-permute-start(bf16[152,256]{1,0:T(8,128)(2,1)S(1)} %get-tuple-element.152), channel_id=1, source_target_pairs={{0,3},{1,2},{2,1},{3,0},{4,7},{5,6},{6,5},{7,4},{8,11},{9,10},{10,... | collective-permute-start | bytes 233480 | tf_op jit(solution)/shard_map/ppermute | solution.py:675
  69.6 2.0 %collective-permute-start.25 = (bf16[72,256]{1,0:T(8,128)(2,1)S(1)}, bf16[72,256]{1,0:T(8,128)(2,1)S(1)}, u32[]{:S(2)}, u32[]{:S(2)}) collective-permute-start(bf16[72,256]{1,0:T(8,128)(2,1)S(1)} %get-tuple-element.150), channel_id=1, source_target_pairs={{0,2},{1,3},{2,0},{3,1},{4,6},{5,7},{6,4},{7,5},{8,10},{9,11},{10,... | collective-permute-start | bytes 110600 | tf_op jit(solution)/shard_map/ppermute | solution.py:675
  71.5 2.5 %collective-permute-done.24.refs_1_ = bf16[72,256]{1,0:T(8,128)(2,1)S(1)} collective-permute-done((bf16[72,256]{1,0:T(8,128)(2,1)S(1)}, bf16[72,256]{1,0:T(8,128)(2,1)S(1)}, u32[]{:S(2)}, u32[]{:S(2)}) %collective-permute-start.24) | collective-permute-done | bytes 36896 | tf_op jit(solution)/shard_map/ppermute | solution.py:675
  74.0 0.4 collective-permute-done.25.refs_2_
  74.5 2.0 %collective-permute-start.29 = (bf16[152,256]{1,0:T(8,128)(2,1)S(1)}, bf16[152,256]{1,0:T(8,128)(2,1)S(1)}, u32[]{:S(2)}, u32[]{:S(2)}) collective-permute-start(bf16[152,256]{1,0:T(8,128)(2,1)S(1)} %rank_sums.1), channel_id=1, source_target_pairs={{0,24},{8,16},{16,8},{24,0},{1,25},{9,17},{17,9},{25,1},{2,26},{10... | collective-permute-start | bytes 233480 | tf_op jit(solution)/shard_map/ppermute | solution.py:675
  76.4 1.0 %collective-permute-start.28 = (bf16[152,256]{1,0:T(8,128)(2,1)S(1)}, bf16[152,256]{1,0:T(8,128)(2,1)S(1)}, u32[]{:S(2)}, u32[]{:S(2)}) collective-permute-start(bf16[152,256]{1,0:T(8,128)(2,1)S(1)} %rank_sums.1), channel_id=1, source_target_pairs={{0,16},{8,24},{16,0},{24,8},{1,17},{9,25},{17,1},{25,9},{2,18},{10... | collective-permute-start | bytes 233480 | tf_op jit(solution)/shard_map/ppermute | solution.py:675
  77.5 0.5 collective-permute-start.27
  78.0 2.5 %collective-permute-done.29 = bf16[152,256]{1,0:T(8,128)(2,1)S(1)} collective-permute-done((bf16[152,256]{1,0:T(8,128)(2,1)S(1)}, bf16[152,256]{1,0:T(8,128)(2,1)S(1)}, u32[]{:S(2)}, u32[]{:S(2)}) %collective-permute-start.29) | collective-permute-done | bytes 77856 | tf_op jit(solution)/shard_map/ppermute | solution.py:675
  80.5 0.6 collective-permute-done.28
  81.2 0.7 collective-permute-done.27
  82.1 2.2 %update.2 = (f32[576,256]{1,0:T(8,128)}, f32[576,256]{1,0:T(8,128)}, f32[576,256]{1,0:T(8,128)}, f32[576,256]{1,0:T(8,128)}, f32[576,256]{1,0:T(8,128)}, /*index...) custom-call(s32[52]{0:T(128)S(1)} %concatenate.4.ids_ref, ...), custom_call_target="tpu_custom_call" | custom-call | flops 2000000000 | bytes 9000000 | tf_op jit(solution)/shard_map/update/pallas_call | solution.py:657
  84.4 2.2 %update.3 = (f32[576,256]{1,0:T(8,128)}, f32[576,256]{1,0:T(8,128)}, f32[576,256]{1,0:T(8,128)}, f32[576,256]{1,0:T(8,128)}, f32[576,256]{1,0:T(8,128)}, /*index...) custom-call(s32[52]{0:T(128)S(1)} %concatenate.4.ids_ref, ...), custom_call_target="tpu_custom_call", output_to_operand_aliasing={{0}: (11, {}), {1}: (12, {}), {2}: (13, {}), {3}: (14, {}),... | custom-call | flops 2000000000 | bytes 9000000 | tf_op jit(solution)/shard_map/update/pallas_call | solution.py:657
  (53 shorter events, 0.8 us)
Async XLA Ops:
  0.6 17.5 %copy-start.9 = (s32[12,4]{0,1:T(4,128)S(1)}, s32[12,4]{0,1:T(4,128)}, u32[]{:S(2)}) copy-start(s32[12,4]{0,1:T(4,128)} %param.16) | copy-start | bytes 580
  2.2 11.7 %collective-permute-start.2 = (bf16[152,256]{1,0:T(8,128)(2,1)S(1)}, bf16[152,256]{1,0:T(8,128)(2,1)S(1)}, u32[]{:S(2)}, u32[]{:S(2)}) collective-permute-start(bf16[152,256]{1,0:T(8,128)(2,1)S(1)} %get-tuple-element.92), channel_id=1, source_target_pairs={{0,3},{1,2},{2,1},{3,0},{4,7},{5,6},{6,5},{7,4},{8,11},{9,10},{10,... | collective-permute-start | bytes 233480 | tf_op jit(solution)/shard_map/ppermute | solution.py:675
  7.4 6.6 %collective-permute-start.1 = (bf16[72,256]{1,0:T(8,128)(2,1)S(1)}, bf16[72,256]{1,0:T(8,128)(2,1)S(1)}, u32[]{:S(2)}, u32[]{:S(2)}) collective-permute-start(bf16[72,256]{1,0:T(8,128)(2,1)S(1)} %get-tuple-element.91), channel_id=1, source_target_pairs={{0,2},{1,3},{2,0},{3,1},{4,6},{5,7},{6,4},{7,5},{8,10},{9,11},{10,... | collective-permute-start | bytes 110600 | tf_op jit(solution)/shard_map/ppermute | solution.py:675
  7.4 6.6 %collective-permute-start = (bf16[72,256]{1,0:T(8,128)(2,1)S(1)}, bf16[72,256]{1,0:T(8,128)(2,1)S(1)}, u32[]{:S(2)}, u32[]{:S(2)}) collective-permute-start(bf16[72,256]{1,0:T(8,128)(2,1)S(1)} %get-tuple-element.91), channel_id=1, source_target_pairs={{0,1},{1,0},{2,3},{3,2},{4,5},{5,4},{6,7},{7,6},{8,9},{9,8},{10,11... | collective-permute-start | bytes 110600 | tf_op jit(solution)/shard_map/ppermute | solution.py:675
  9.6 12.3 %collective-permute-start.7 = (bf16[320,256]{1,0:T(8,128)(2,1)S(1)}, bf16[320,256]{1,0:T(8,128)(2,1)S(1)}, u32[]{:S(2)}, u32[]{:S(2)}) collective-permute-start(bf16[320,256]{1,0:T(8,128)(2,1)S(1)} %pack.3.refs_4_), channel_id=1, source_target_pairs={{0,2},{1,3},{2,0},{3,1},{4,6},{5,7},{6,4},{7,5},{8,10},{9,11},{10,... | collective-permute-start | bytes 491528 | tf_op jit(solution)/shard_map/ppermute | solution.py:675
  11.9 10.0 %collective-permute-start.6 = (bf16[320,256]{1,0:T(8,128)(2,1)S(1)}, bf16[320,256]{1,0:T(8,128)(2,1)S(1)}, u32[]{:S(2)}, u32[]{:S(2)}) collective-permute-start(bf16[320,256]{1,0:T(8,128)(2,1)S(1)} %pack.3.refs_4_), channel_id=1, source_target_pairs={{0,1},{1,0},{2,3},{3,2},{4,5},{5,4},{6,7},{7,6},{8,9},{9,8},{10,11... | collective-permute-start | bytes 491528 | tf_op jit(solution)/shard_map/ppermute | solution.py:675
  14.0 8.0 %collective-permute-start.5 = (bf16[296,256]{1,0:T(8,128)(2,1)S(1)}, bf16[296,256]{1,0:T(8,128)(2,1)S(1)}, u32[]{:S(2)}, u32[]{:S(2)}) collective-permute-start(bf16[296,256]{1,0:T(8,128)(2,1)S(1)} %below.1.refs_3_.refs_0_), channel_id=1, source_target_pairs={{0,24},{8,16},{16,8},{24,0},{1,25},{9,17},{17,9},{25,1},{2,26},{10... | collective-permute-start | bytes 454664 | tf_op jit(solution)/shard_map/ppermute | solution.py:675
  16.5 6.0 %collective-permute-start.4 = (bf16[296,256]{1,0:T(8,128)(2,1)S(1)}, bf16[296,256]{1,0:T(8,128)(2,1)S(1)}, u32[]{:S(2)}, u32[]{:S(2)}) collective-permute-start(bf16[296,256]{1,0:T(8,128)(2,1)S(1)} %below.1.refs_3_.refs_0_), channel_id=1, source_target_pairs={{0,16},{8,24},{16,0},{24,8},{1,17},{9,25},{17,1},{25,9},{2,18},{10... | collective-permute-start | bytes 454664 | tf_op jit(solution)/shard_map/ppermute | solution.py:675
  17.0 5.6 %collective-permute-start.3 = (bf16[296,256]{1,0:T(8,128)(2,1)S(1)}, bf16[296,256]{1,0:T(8,128)(2,1)S(1)}, u32[]{:S(2)}, u32[]{:S(2)}) collective-permute-start(bf16[296,256]{1,0:T(8,128)(2,1)S(1)} %below.1.refs_3_.refs_0_), channel_id=1, source_target_pairs={{0,8},{8,0},{16,24},{24,16},{1,9},{9,1},{17,25},{25,17},{2,10},{10... | collective-permute-start | bytes 454664 | tf_op jit(solution)/shard_map/ppermute | solution.py:675
  22.6 1.4 %collective-permute-start.8 = (bf16[296,256]{1,0:T(8,128)(2,1)S(1)}, bf16[296,256]{1,0:T(8,128)(2,1)S(1)}, u32[]{:S(2)}, u32[]{:S(2)}) collective-permute-start(bf16[296,256]{1,0:T(8,128)(2,1)S(1)} %below.1.refs_3_.refs_0_), channel_id=1, source_target_pairs={{0,4},{4,0},{1,5},{5,1},{2,6},{6,2},{3,7},{7,3},{8,12},{12,8},{9,1... | collective-permute-start | bytes 454664 | tf_op jit(solution)/shard_map/ppermute | solution.py:675
  22.6 8.1 %collective-permute-start.12 = (bf16[320,256]{1,0:T(8,128)(2,1)S(1)}, bf16[320,256]{1,0:T(8,128)(2,1)S(1)}, u32[]{:S(2)}, u32[]{:S(2)}) collective-permute-start(bf16[320,256]{1,0:T(8,128)(2,1)S(1)} %collective-permute-done.6.refs_8_), channel_id=1, source_target_pairs={{0,4},{4,0},{1,5},{5,1},{2,6},{6,2},{3,7},{7,3},{8,12},{12,8},{9,1... | collective-permute-start | bytes 491528 | tf_op jit(solution)/shard_map/ppermute | solution.py:675
  23.1 7.6 %collective-permute-start.13 = (bf16[320,256]{1,0:T(8,128)(2,1)S(1)}, bf16[320,256]{1,0:T(8,128)(2,1)S(1)}, u32[]{:S(2)}, u32[]{:S(2)}) collective-permute-start(bf16[320,256]{1,0:T(8,128)(2,1)S(1)} %collective-permute-done.7.refs_9_), channel_id=1, source_target_pairs={{0,4},{4,0},{1,5},{5,1},{2,6},{6,2},{3,7},{7,3},{8,12},{12,8},{9,1... | collective-permute-start | bytes 491528 | tf_op jit(solution)/shard_map/ppermute | solution.py:675
  23.1 1.6 %collective-permute-start.9 = (bf16[296,256]{1,0:T(8,128)(2,1)S(1)}, bf16[296,256]{1,0:T(8,128)(2,1)S(1)}, u32[]{:S(2)}, u32[]{:S(2)}) collective-permute-start(bf16[296,256]{1,0:T(8,128)(2,1)S(1)} %collective-permute-done.3.refs_1_), channel_id=1, source_target_pairs={{0,4},{4,0},{1,5},{5,1},{2,6},{6,2},{3,7},{7,3},{8,12},{12,8},{9,1... | collective-permute-start | bytes 454664 | tf_op jit(solution)/shard_map/ppermute | solution.py:675
  23.6 1.4 %collective-permute-start.10 = (bf16[296,256]{1,0:T(8,128)(2,1)S(1)}, bf16[296,256]{1,0:T(8,128)(2,1)S(1)}, u32[]{:S(2)}, u32[]{:S(2)}) collective-permute-start(bf16[296,256]{1,0:T(8,128)(2,1)S(1)} %collective-permute-done.4.refs_2_), channel_id=1, source_target_pairs={{0,4},{4,0},{1,5},{5,1},{2,6},{6,2},{3,7},{7,3},{8,12},{12,8},{9,1... | collective-permute-start | bytes 454664 | tf_op jit(solution)/shard_map/ppermute | solution.py:675
  23.9 1.4 %collective-permute-start.11 = (bf16[296,256]{1,0:T(8,128)(2,1)S(1)}, bf16[296,256]{1,0:T(8,128)(2,1)S(1)}, u32[]{:S(2)}, u32[]{:S(2)}) collective-permute-start(bf16[296,256]{1,0:T(8,128)(2,1)S(1)} %collective-permute-done.5.refs_3_), channel_id=1, source_target_pairs={{0,4},{4,0},{1,5},{5,1},{2,6},{6,2},{3,7},{7,3},{8,12},{12,8},{9,1... | collective-permute-start | bytes 454664 | tf_op jit(solution)/shard_map/ppermute | solution.py:675
  41.3 2.2 %collective-permute-start.14 = (bf16[4,4,80,256]{3,2,1,0:T(8,128)(2,1)S(1)}, bf16[4,4,80,256]{3,2,1,0:T(8,128)(2,1)S(1)}, u32[]{:S(2)}, u32[]{:S(2)}) collective-permute-start(bf16[4,4,80,256]{3,2,1,0:T(8,128)(2,1)S(1)} %get-tuple-element.116), channel_id=1, source_target_pairs={{0,4},{4,0},{1,5},{5,1},{2,6},{6,2},{3,7},{7,3},{8,12},{12,8},{9,1... | collective-permute-start | bytes 1966088 | tf_op jit(solution)/shard_map/ppermute | solution.py:675
  43.7 10.7 %collective-permute-start.17 = (bf16[4,80,256]{2,1,0:T(8,128)(2,1)S(1)}, bf16[4,80,256]{2,1,0:T(8,128)(2,1)S(1)}, u32[]{:S(2)}, u32[]{:S(2)}) collective-permute-start(bf16[4,80,256]{2,1,0:T(8,128)(2,1)S(1)} %get-tuple-element.171), channel_id=1, source_target_pairs={{0,24},{8,16},{16,8},{24,0},{1,25},{9,17},{17,9},{25,1},{2,26},{10... | collective-permute-start | bytes 491528 | tf_op jit(solution)/shard_map/ppermute | solution.py:675
  45.6 8.8 %collective-permute-start.16 = (bf16[4,80,256]{2,1,0:T(8,128)(2,1)S(1)}, bf16[4,80,256]{2,1,0:T(8,128)(2,1)S(1)}, u32[]{:S(2)}, u32[]{:S(2)}) collective-permute-start(bf16[4,80,256]{2,1,0:T(8,128)(2,1)S(1)} %get-tuple-element.172), channel_id=1, source_target_pairs={{0,16},{8,24},{16,0},{24,8},{1,17},{9,25},{17,1},{25,9},{2,18},{10... | collective-permute-start | bytes 491528 | tf_op jit(solution)/shard_map/ppermute | solution.py:675
  46.7 7.7 %collective-permute-start.15 = (bf16[4,80,256]{2,1,0:T(8,128)(2,1)S(1)}, bf16[4,80,256]{2,1,0:T(8,128)(2,1)S(1)}, u32[]{:S(2)}, u32[]{:S(2)}) collective-permute-start(bf16[4,80,256]{2,1,0:T(8,128)(2,1)S(1)} %get-tuple-element.173), channel_id=1, source_target_pairs={{0,8},{8,0},{16,24},{24,16},{1,9},{9,1},{17,25},{25,17},{2,10},{10... | collective-permute-start | bytes 491528 | tf_op jit(solution)/shard_map/ppermute | solution.py:675
  54.4 2.1 %collective-permute-start.18 = (bf16[4,4,72,256]{3,2,1,0:T(8,128)(2,1)S(1)}, bf16[4,4,72,256]{3,2,1,0:T(8,128)(2,1)S(1)}, u32[]{:S(2)}, u32[]{:S(2)}) collective-permute-start(bf16[4,4,72,256]{3,2,1,0:T(8,128)(2,1)S(1)} %get-tuple-element.120), channel_id=1, source_target_pairs={{0,4},{4,0},{1,5},{5,1},{2,6},{6,2},{3,7},{7,3},{8,12},{12,8},{9,1... | collective-permute-start | bytes 1769480 | tf_op jit(solution)/shard_map/ppermute | solution.py:675
  56.7 9.8 %collective-permute-start.19 = (bf16[4,72,256]{2,1,0:T(8,128)(2,1)S(1)}, bf16[4,72,256]{2,1,0:T(8,128)(2,1)S(1)}, u32[]{:S(2)}, u32[]{:S(2)}) collective-permute-start(bf16[4,72,256]{2,1,0:T(8,128)(2,1)S(1)} %get-tuple-element.130), channel_id=1, source_target_pairs={{0,8},{8,0},{16,24},{24,16},{1,9},{9,1},{17,25},{25,17},{2,10},{10... | collective-permute-start | bytes 442376 | tf_op jit(solution)/shard_map/ppermute | solution.py:675
  58.2 8.8 %collective-permute-start.20 = (bf16[4,72,256]{2,1,0:T(8,128)(2,1)S(1)}, bf16[4,72,256]{2,1,0:T(8,128)(2,1)S(1)}, u32[]{:S(2)}, u32[]{:S(2)}) collective-permute-start(bf16[4,72,256]{2,1,0:T(8,128)(2,1)S(1)} %get-tuple-element.131), channel_id=1, source_target_pairs={{0,16},{8,24},{16,0},{24,8},{1,17},{9,25},{17,1},{25,9},{2,18},{10... | collective-permute-start | bytes 442376 | tf_op jit(solution)/shard_map/ppermute | solution.py:675
  59.2 7.8 %collective-permute-start.21 = (bf16[4,72,256]{2,1,0:T(8,128)(2,1)S(1)}, bf16[4,72,256]{2,1,0:T(8,128)(2,1)S(1)}, u32[]{:S(2)}, u32[]{:S(2)}) collective-permute-start(bf16[4,72,256]{2,1,0:T(8,128)(2,1)S(1)} %get-tuple-element.132), channel_id=1, source_target_pairs={{0,24},{8,16},{16,8},{24,0},{1,25},{9,17},{17,9},{25,1},{2,26},{10... | collective-permute-start | bytes 442376 | tf_op jit(solution)/shard_map/ppermute | solution.py:675
  60.2 6.2 %collective-permute-start.22 = (bf16[80,256]{1,0:T(8,128)(2,1)S(1)}, bf16[80,256]{1,0:T(8,128)(2,1)S(1)}, u32[]{:S(2)}, u32[]{:S(2)}) collective-permute-start(bf16[80,256]{1,0:T(8,128)(2,1)S(1)} %get-tuple-element.134), channel_id=1, source_target_pairs={{0,1},{1,0},{2,3},{3,2},{4,5},{5,4},{6,7},{7,6},{8,9},{9,8},{10,11... | collective-permute-start | bytes 122888 | tf_op jit(solution)/shard_map/ppermute | solution.py:675
  60.5 6.0 %collective-permute-start.23 = (bf16[80,256]{1,0:T(8,128)(2,1)S(1)}, bf16[80,256]{1,0:T(8,128)(2,1)S(1)}, u32[]{:S(2)}, u32[]{:S(2)}) collective-permute-start(bf16[80,256]{1,0:T(8,128)(2,1)S(1)} %get-tuple-element.135), channel_id=1, source_target_pairs={{0,2},{1,3},{2,0},{3,1},{4,6},{5,7},{6,4},{7,5},{8,10},{9,11},{10,... | collective-permute-start | bytes 122888 | tf_op jit(solution)/shard_map/ppermute | solution.py:675
  61.7 20.3 %copy-start = (f32[576,256]{1,0:T(8,128)S(1)}, f32[576,256]{1,0:T(8,128)}, u32[]{:S(2)}) copy-start(f32[576,256]{1,0:T(8,128)} %refs_3_.3) | copy-start | bytes 1769476
  61.7 20.4 %copy-start.1 = (f32[576,256]{1,0:T(8,128)S(1)}, f32[576,256]{1,0:T(8,128)}, u32[]{:S(2)}) copy-start(f32[576,256]{1,0:T(8,128)} %refs_0_.9) | copy-start | bytes 1769476
  61.7 20.4 %copy-start.2 = (f32[64,256]{1,0:T(8,128)S(1)}, f32[64,256]{1,0:T(8,128)}, u32[]{:S(2)}) copy-start(f32[64,256]{1,0:T(8,128)} %refs_6_.3) | copy-start | bytes 196612
  61.7 20.4 %copy-start.3 = (f32[576,256]{1,0:T(8,128)S(1)}, f32[576,256]{1,0:T(8,128)}, u32[]{:S(2)}) copy-start(f32[576,256]{1,0:T(8,128)} %refs_1_.9) | copy-start | bytes 1769476
  61.7 20.4 %copy-start.4 = (f32[576,256]{1,0:T(8,128)S(1)}, f32[576,256]{1,0:T(8,128)}, u32[]{:S(2)}) copy-start(f32[576,256]{1,0:T(8,128)} %refs_2_.7) | copy-start | bytes 1769476
  61.7 20.4 %copy-start.5 = (f32[576,256]{1,0:T(8,128)S(1)}, f32[576,256]{1,0:T(8,128)}, u32[]{:S(2)}) copy-start(f32[576,256]{1,0:T(8,128)} %refs_4_.3) | copy-start | bytes 1769476
  61.7 20.4 %copy-start.6 = (f32[576,256]{1,0:T(8,128)S(1)}, f32[576,256]{1,0:T(8,128)}, u32[]{:S(2)}) copy-start(f32[576,256]{1,0:T(8,128)} %refs_5_.3) | copy-start | bytes 1769476
  61.7 20.4 %copy-start.7 = (f32[64,256]{1,0:T(8,128)S(1)}, f32[64,256]{1,0:T(8,128)}, u32[]{:S(2)}) copy-start(f32[64,256]{1,0:T(8,128)} %refs_7_.3) | copy-start | bytes 196612
  61.7 20.4 %copy-start.8 = (f32[64,256]{1,0:T(8,128)S(1)}, f32[64,256]{1,0:T(8,128)}, u32[]{:S(2)}) copy-start(f32[64,256]{1,0:T(8,128)} %refs_8_.3) | copy-start | bytes 196612
  67.1 7.3 %collective-permute-start.26 = (bf16[152,256]{1,0:T(8,128)(2,1)S(1)}, bf16[152,256]{1,0:T(8,128)(2,1)S(1)}, u32[]{:S(2)}, u32[]{:S(2)}) collective-permute-start(bf16[152,256]{1,0:T(8,128)(2,1)S(1)} %get-tuple-element.152), channel_id=1, source_target_pairs={{0,3},{1,2},{2,1},{3,0},{4,7},{5,6},{6,5},{7,4},{8,11},{9,10},{10,... | collective-permute-start | bytes 233480 | tf_op jit(solution)/shard_map/ppermute | solution.py:675
  69.6 4.4 %collective-permute-start.24 = (bf16[72,256]{1,0:T(8,128)(2,1)S(1)}, bf16[72,256]{1,0:T(8,128)(2,1)S(1)}, u32[]{:S(2)}, u32[]{:S(2)}) collective-permute-start(bf16[72,256]{1,0:T(8,128)(2,1)S(1)} %get-tuple-element.149), channel_id=1, source_target_pairs={{0,1},{1,0},{2,3},{3,2},{4,5},{5,4},{6,7},{7,6},{8,9},{9,8},{10,11... | collective-permute-start | bytes 110600 | tf_op jit(solution)/shard_map/ppermute | solution.py:675
  69.6 4.9 %collective-permute-start.25 = (bf16[72,256]{1,0:T(8,128)(2,1)S(1)}, bf16[72,256]{1,0:T(8,128)(2,1)S(1)}, u32[]{:S(2)}, u32[]{:S(2)}) collective-permute-start(bf16[72,256]{1,0:T(8,128)(2,1)S(1)} %get-tuple-element.150), channel_id=1, source_target_pairs={{0,2},{1,3},{2,0},{3,1},{4,6},{5,7},{6,4},{7,5},{8,10},{9,11},{10,... | collective-permute-start | bytes 110600 | tf_op jit(solution)/shard_map/ppermute | solution.py:675
  74.5 6.1 %collective-permute-start.29 = (bf16[152,256]{1,0:T(8,128)(2,1)S(1)}, bf16[152,256]{1,0:T(8,128)(2,1)S(1)}, u32[]{:S(2)}, u32[]{:S(2)}) collective-permute-start(bf16[152,256]{1,0:T(8,128)(2,1)S(1)} %rank_sums.1), channel_id=1, source_target_pairs={{0,24},{8,16},{16,8},{24,0},{1,25},{9,17},{17,9},{25,1},{2,26},{10... | collective-permute-start | bytes 233480 | tf_op jit(solution)/shard_map/ppermute | solution.py:675
  76.4 4.7 %collective-permute-start.28 = (bf16[152,256]{1,0:T(8,128)(2,1)S(1)}, bf16[152,256]{1,0:T(8,128)(2,1)S(1)}, u32[]{:S(2)}, u32[]{:S(2)}) collective-permute-start(bf16[152,256]{1,0:T(8,128)(2,1)S(1)} %rank_sums.1), channel_id=1, source_target_pairs={{0,16},{8,24},{16,0},{24,8},{1,17},{9,25},{17,1},{25,9},{2,18},{10... | collective-permute-start | bytes 233480 | tf_op jit(solution)/shard_map/ppermute | solution.py:675
  77.5 4.4 %collective-permute-start.27 = (bf16[152,256]{1,0:T(8,128)(2,1)S(1)}, bf16[152,256]{1,0:T(8,128)(2,1)S(1)}, u32[]{:S(2)}, u32[]{:S(2)}) collective-permute-start(bf16[152,256]{1,0:T(8,128)(2,1)S(1)} %rank_sums.1), channel_id=1, source_target_pairs={{0,8},{8,0},{16,24},{24,16},{1,9},{9,1},{17,25},{25,17},{2,10},{10... | collective-permute-start | bytes 233480 | tf_op jit(solution)/shard_map/ppermute | solution.py:675
  81.9 2.4 %collective-permute-start.30 = (bf16[4,152,256]{2,1,0:T(8,128)(2,1)S(1)}, bf16[4,152,256]{2,1,0:T(8,128)(2,1)S(1)}, u32[]{:S(2)}, u32[]{:S(2)}) collective-permute-start(bf16[4,152,256]{2,1,0:T(8,128)(2,1)S(1)} %pad_maximum_fusion.grads_ref), channel_id=1, source_target_pairs={{0,4},{4,0},{1,5},{5,1},{2,6},{6,2},{3,7},{7,3},{8,12},{12,8},{9,1... | collective-permute-start | bytes 933896 | tf_op jit(solution)/shard_map/ppermute | solution.py:675
